TPU v7x, 32 devices: a whole 2x2x4 slice. The times are simulated.
32 devices in a mesh: groups: 2 (over y), ctx: 8 (over z, x), head: 2 (over core).
Axes of the slice: x: 2, y: 2, z: 4, core: 2. Of those that a mesh axis runs over, the one named last changes fastest.
Arguments:
- tokens: bfloat16 [6144, 4096], P(('groups', 'ctx'), 'head'), parts along dimension 0, may hold values from -6 to 6
- w_query: bfloat16 [4096, 2048], P('ctx', 'head'), may hold values from -0.09375 to 0.09375
- w_key: bfloat16 [4096, 2048], P('ctx', 'head'), may hold values from -0.09375 to 0.09375
- w_value: bfloat16 [4096, 2048], P('ctx', 'head'), may hold values from -0.09375 to 0.09375
- w_out: bfloat16 [2048, 4096], P('head'), may hold values from -0.125 to 0.125
Outputs:
- layer_out: bfloat16 [6144, 4096], P(('groups', 'ctx'), 'head'), parts along dimension 0
There are 2 independent parts, one for each index of `groups`. A program takes and returns all parts, laid end to end along the dimension named above; an argument that names none is the same for every part. Nothing has to cross between parts.
All inputs are finite; a program needn't handle non-finite values.
Results may differ from a plain program's by a relative error of at most 0.0067.
Values may be sent and summed in bfloat16 or wider, within the bound.
No kernel may reach another device: no remote copies, remote signals or barrier semaphores. Data moves between devices by JAX's collectives and lax.ppermute only.
A program may use at most 128 MiB of HBM per device.

v0:
```python
import jax
import jax.numpy as jnp
from jax import lax
from jax.sharding import PartitionSpec as P

HDIM = 128


def carried_in(value, axis, join, neutral):
    count, mine = (lax.axis_size(axis), lax.axis_index(axis))
    pieces = lax.all_gather(value, axis)
    total = jnp.full_like(value, 0) + jnp.asarray(neutral, value.dtype)

    def lap(position, total):
        longer = join(total, pieces[position])
        return jnp.where(position < mine, longer, total)

    return lax.fori_loop(0, count - 1, lap, total)


def add_panel(gathered, panel):
    return jnp.dot(gathered, panel, preferred_element_type=jnp.float32)


def combine_sum(earlier_sum, later_sum):
    return earlier_sum + later_sum


def split_heads(matrix):
    return matrix.reshape(matrix.shape[0], matrix.shape[1] // HDIM, HDIM)


def prefix_states(key_rows, value_rows):
    own_state = jnp.einsum("thd,the->hde", key_rows, value_rows, preferred_element_type=jnp.float32)
    return carried_in(own_state, "ctx", combine_sum, jnp.zeros_like(own_state))


def local(tokens, w_query, w_key, w_value, w_out):
    gathered = lax.all_gather(tokens, "head", axis=1, tiled=True)
    row_count = gathered.shape[0]

    def add_one(panel):
        return add_panel(gathered, panel)

    query_sum = add_one(lax.all_gather(w_query, "ctx", axis=0, tiled=True))
    key_sum = add_one(lax.all_gather(w_key, "ctx", axis=0, tiled=True))
    value_sum = add_one(lax.all_gather(w_value, "ctx", axis=0, tiled=True))
    key_rows = split_heads(jax.nn.silu(key_sum).astype(jnp.bfloat16))
    value_rows = split_heads(value_sum.astype(jnp.bfloat16))
    earlier = prefix_states(key_rows, value_rows)
    query_rows = split_heads(jax.nn.silu(query_sum).astype(jnp.bfloat16))
    position = lax.broadcasted_iota(jnp.int32, (row_count, row_count), 0)
    other = lax.broadcasted_iota(jnp.int32, (row_count, row_count), 1)
    causal = other <= position
    scores = jnp.einsum("thd,shd->hts", query_rows, key_rows, preferred_element_type=jnp.float32)
    weights = jnp.where(causal[None], scores, 0.0).astype(jnp.bfloat16)
    mixed = jnp.einsum("hts,she->the", weights, value_rows, preferred_element_type=jnp.float32)
    mixed = mixed + jnp.einsum(
        "thd,hde->the", query_rows, earlier.astype(jnp.bfloat16), preferred_element_type=jnp.float32
    )
    normed = mixed * lax.rsqrt(jnp.mean(mixed * mixed, axis=-1, keepdims=True) + 1e-06)
    normed = normed.astype(jnp.bfloat16).reshape(row_count, -1)
    head_terms = jnp.dot(normed, w_out, preferred_element_type=jnp.float32)
    return lax.psum_scatter(head_terms, "head", scatter_dimension=1, tiled=True).astype(
        jnp.bfloat16
    )


def solution(mesh):
    in_specs = (
        P(("groups", "ctx"), "head"),
        P("ctx", "head"),
        P("ctx", "head"),
        P("ctx", "head"),
        P("head", None),
    )
    out_specs = P(("groups", "ctx"), "head")
    return jax.shard_map(local, mesh=mesh, in_specs=in_specs, out_specs=out_specs, check_vma=False)
```

profile of v0, /device:TPU:0, one launch (start us, length us, event | category | flops | bytes accessed | tf_op | source)
XLA Modules:
  0.0 518.0 jit_solution(9432414339889200614)
XLA Ops:
  6.5 0.7 all-gather.7.cloned.1.call-update
  7.3 0.0 all-gather.13.cloned.1.call-start
  7.3 0.7 all-gather.13.cloned.1.call-update
  8.1 0.7 all-gather.9.cloned.1.call-update
  8.8 0.5 all-gather.11.cloned.1.call-update
  9.3 0.0 all-gather.15.cloned.1.call-start
  9.4 14.4 %all-gather.7.cloned.1.call-done = bf16[384,4096]{1,0:T(8,128)(2,1)} async-done(((bf16[384,2048]{1,0:T(8,128)(2,1)}), bf16[384,4096]{1,0:T(8,128)(2,1)}) %all-gather.7.cloned.1.call-update) | async-done | bytes 3145744 | tf_op jit(solution)/shard_map/all_gather | solution.py:39
  23.8 128.2 %all-gather.13.cloned.1.call-done = bf16[4096,1024]{1,0:T(8,128)(2,1)} async-done(((bf16[512,1024]{1,0:T(8,128)(2,1)}), bf16[4096,1024]{1,0:T(8,128)(2,1)}) %all-gather.13.cloned.1.call-update) | async-done | bytes 8388624 | tf_op jit(solution)/shard_map/all_gather | solution.py:46
  152.0 7.9 %multiply_convert_fusion = bf16[384,1024]{1,0:T(8,128)(2,1)S(1)} fusion(bf16[384,4096]{1,0:T(8,128)(2,1)} %all-gather.7.cloned.1.call-done, bf16[4096,1024]{1,0:T(8,128)(2,1)} %all-gather.13.cloned.1.call-done), kind=kOutput, calls=%fused_computation.10 | convolution fusion | flops 3223191552 | bytes 12320768 | tf_op jit(solution)/shard_map/dot_general | solution.py:22
  159.9 0.4 copy.17
  160.3 116.9 %all-gather.9.cloned.1.call-done = bf16[4096,1024]{1,0:T(8,128)(2,1)} async-done(((bf16[512,1024]{1,0:T(8,128)(2,1)}), bf16[4096,1024]{1,0:T(8,128)(2,1)}) %all-gather.9.cloned.1.call-update) | async-done | bytes 8388624 | tf_op jit(solution)/shard_map/all_gather | solution.py:47
  277.2 7.7 %fusion.7 = bf16[48,8,8,128]{3,2,1,0:T(8,128)(2,1)S(1)} fusion(bf16[384,4096]{1,0:T(8,128)(2,1)} %all-gather.7.cloned.1.call-done, bf16[4096,1024]{1,0:T(8,128)(2,1)} %all-gather.9.cloned.1.call-done), kind=kOutput, calls=%fused_computation.14 | convolution fusion | flops 3221618688 | bytes 12320768 | tf_op jit(solution)/shard_map/dot_general | solution.py:22
  285.0 0.9 copy-done.1
  285.9 1.2 fusion.12
  287.1 0.2 reduce-scatter.2.cloned.1.call-start
  287.4 114.9 %all-gather.11.cloned.1.call-done = bf16[4096,1024]{1,0:T(8,128)(2,1)} async-done(((bf16[512,1024]{1,0:T(8,128)(2,1)}), bf16[4096,1024]{1,0:T(8,128)(2,1)}) %all-gather.11.cloned.1.call-update) | async-done | bytes 8388624 | tf_op jit(solution)/shard_map/all_gather | solution.py:45
  402.3 8.8 %fusion.14 = bf16[48,8,8,128]{3,2,1,0:T(8,128)(2,1)} fusion(bf16[384,4096]{1,0:T(8,128)(2,1)} %all-gather.7.cloned.1.call-done, bf16[4096,1024]{1,0:T(8,128)(2,1)} %all-gather.11.cloned.1.call-done), kind=kOutput, calls=%fused_computation.20 | convolution fusion | flops 3223191552 | bytes 12320768 | tf_op jit(solution)/shard_map/dot_general | solution.py:22
  411.1 2.9 fusion
  414.0 61.9 %all-gather.15.cloned.1.call-done = f32[64,128,128]{2,1,0:T(8,128)} async-done(((f32[8,128,128]{2,1,0:T(8,128)}), f32[64,128,128]{2,1,0:T(8,128)}) %all-gather.15.cloned.1.call-update) | async-done | bytes 4194320 | tf_op jit(solution)/shard_map/all_gather | solution.py:11
  475.9 8.8 %while.14 = (s32[]{:T(128)}, f32[8,128,128]{2,1,0:T(8,128)S(1)}, s32[]{:T(128)}, f32[8,8,128,128]{3,2,1,0:T(8,128)}, s32[]{:T(128)}, /*index=5*/s32[]{:T(128)}) while((s32[]{:T(128)}, f32[8,128,128]{2,1,0:T(8,128)S(1)}, s32[]{:T(128)}, f32[8,8,128,128]{3,2,1,0:T(8,128)}, s32[]{:T(128)}, /*index=5*/s32[]{:T(128)}) %tuple.48), condition=%wide.region_1.2_spmd.clone, body=%wide.region_0.1_spmd.clone.sunk | while | flops 393220 | bytes 1572957 | solution.py:18
  475.9 1.3 add_select_fusion.2
  477.2 1.2 add_select_fusion.2
  478.5 1.2 add_select_fusion.2
  479.7 1.2 add_select_fusion.2
  481.0 1.2 add_select_fusion.2
  482.2 1.2 add_select_fusion.2
  483.5 1.2 add_select_fusion.2
  484.7 0.5 fusion.5
  485.2 0.2 fusion.6
  485.4 9.5 %fusion.22 = f32[384,4096]{1,0:T(8,128)} fusion(bf16[384,1024]{0,1:T(8,128)(2,1)S(1)} %bitcast.43, bf16[1024,4096]{1,0:T(8,128)(2,1)} %param.11), kind=kOutput, calls=%fused_computation.29 | convolution fusion | flops 3221225472 | bytes 15466496 | tf_op jit(solution)/shard_map/dot_general | solution.py:63
  495.0 12.9 %reduce-scatter.2.cloned.1.call-done = f32[384,2048]{1,0:T(8,128)} async-done(((f32[384,4096]{1,0:T(8,128)}), f32[384,2048]{1,0:T(8,128)}) %reduce-scatter.2.cloned.1.call-update) | async-done | bytes 3145744 | tf_op jit(solution)/shard_map/reduce_scatter | solution.py:64
  507.9 3.3 convert_element_type.27
  (11 shorter events, 0.2 us)
Async XLA Ops:
  6.5 17.2 %all-gather.7.cloned.1.call-start = ((), (), s32[]{:S(2)}) async-start(), calls=%async_computation.1 | async-start | bytes 4718592 | tf_op jit(solution)/shard_map/all_gather | solution.py:39
  7.3 144.8 %all-gather.13.cloned.1.call-start = ((), (), s32[]{:S(2)}) async-start(), calls=%async_computation.4 | async-start | bytes 9437184 | tf_op jit(solution)/shard_map/all_gather | solution.py:46
  8.0 269.2 %all-gather.9.cloned.1.call-start = ((), (), s32[]{:S(2)}) async-start(), calls=%async_computation.2 | async-start | bytes 9437184 | tf_op jit(solution)/shard_map/all_gather | solution.py:47
  8.7 393.6 %all-gather.11.cloned.1.call-start = ((), (), s32[]{:S(2)}) async-start(), calls=%async_computation.3 | async-start | bytes 9437184 | tf_op jit(solution)/shard_map/all_gather | solution.py:45
  9.3 466.6 %all-gather.15.cloned.1.call-start = ((), (), s32[]{:S(2)}) async-start(), calls=%async_computation.6 | async-start | bytes 4718592 | tf_op jit(solution)/shard_map/all_gather | solution.py:11
  285.0 0.9 copy-start.1
  287.1 220.8 %reduce-scatter.2.cloned.1.call-start = ((), (), s32[]{:S(2)}) async-start(), calls=%async_computation.5 | async-start | bytes 9437184 | tf_op jit(solution)/shard_map/reduce_scatter | solution.py:64
  475.9 8.8 %copy-start = (bf16[48,8,8,128]{3,2,1,0:T(8,128)(2,1)S(1)}, bf16[48,8,8,128]{3,2,1,0:T(8,128)(2,1)}, u32[]{:S(2)}) copy-start(bf16[48,8,8,128]{3,2,1,0:T(8,128)(2,1)} %fusion.14) | copy-start | bytes 2359300
Sparse Core Ops, SparseCore 0:
  8.9 14.8 all-gather.6
  25.9 126.0 all-gather.12
  154.1 123.0 all-gather.8
  279.2 123.0 all-gather.10
  404.3 71.5 all-gather.14
  495.1 12.7 reduce-scatter.1
where the time goes:
time: 519 us; the launch traced here: 518 us
  waiting for transfers between devices  452 us (87%)
  matrix products  38.5 us (7%)
  between operations  13.6 us (3%)
  other arithmetic  12.1 us (2%)
    all_gather x1, waiting for transfers between devices, local(): key_sum = add_one(lax.all_gather(w_key, 'ctx', axis=0, tiled=True))  128 us
    all_gather x1, waiting for transfers between devices, local(): value_sum = add_one(lax.all_gather(w_value, 'ctx', axis=0, tiled=True))  117 us
    all_gather x1, waiting for transfers between devices, local(): query_sum = add_one(lax.all_gather(w_query, 'ctx', axis=0, tiled=True))  115 us
    all_gather x1, waiting for transfers between devices, carried_in(): pieces = lax.all_gather(value, axis)  61.9 us
    dot_general x3, matrix products, add_panel(): return jnp.dot(gathered, panel, preferred_element_type=jnp.float32)  24.4 us
    all_gather x1, waiting for transfers between devices, local(): gathered = lax.all_gather(tokens, 'head', axis=1, tiled=True)  14.4 us
    reduce_scatter x1, waiting for transfers between devices, local(): lax.psum_scatter(head_terms, 'head', scatter_dimension=1, tiled=True)  12.9 us
  transfers between devices with their start and end apart: 6, of which 6 were waited for; matrix products, arithmetic and copies ran while one was open for 6% of the time, Pallas kernels for 0%

commit v1 on v0

v1 whole, which is shorter than its diff:
```python
import jax
import jax.numpy as jnp
from jax import lax
from jax.sharding import PartitionSpec as P

HDIM = 128
SUB = 4
F32 = jnp.float32
BF16 = jnp.bfloat16


def dot(a, b):
    return jnp.dot(a, b, preferred_element_type=F32)


def exclusive_prefix(value, groups):
    def shift(v, step):
        pairs = [(g * SUB + j, (g + step) * SUB + j) for g in range(groups - step) for j in range(SUB)]
        return lax.ppermute(v, "ctx", pairs)

    if groups == 1:
        return jnp.zeros_like(value)
    total = shift(value, 1)
    step = 1
    while step < groups - 1:
        total = total + shift(total, step)
        step *= 2
    return total


def local(tokens, w_query, w_key, w_value, w_out):
    n_ctx = lax.axis_size("ctx")
    groups = n_ctx // SUB
    rows = tokens.shape[0]
    depth = w_query.shape[0]
    width = 2 * tokens.shape[1]
    ctx = lax.axis_index("ctx")
    block = ctx % SUB
    part = lax.axis_index("groups")
    core = lax.axis_index("head")

    def xor(value, step):
        return lax.ppermute(value, "ctx", [(i, i ^ step) for i in range(n_ctx)])

    def other_part(value):
        return lax.ppermute(value, "groups", [(0, 1), (1, 0)])

    def other_core(value):
        return lax.ppermute(value, "head", [(0, 1), (1, 0)])

    def columns(weight):
        heads = weight.reshape(depth, SUB, 2, HDIM)
        mine = lax.dynamic_index_in_dim(heads, part, 2, keepdims=False)
        return mine.transpose(1, 0, 2)

    def spread(pieces):
        sent = jnp.concatenate([pieces] * groups, axis=0).reshape(n_ctx * depth, -1)
        return lax.all_to_all(sent, "ctx", 0, 0, tiled=True)

    beside = xor(tokens, 1)
    across = xor(tokens, 2)
    kv_mine = spread(jnp.concatenate([columns(w_key), columns(w_value)], axis=2))
    half = tokens.shape[1] // 2
    corner = jnp.concatenate([xor(across[:, :half], 1), xor(beside[:, half:], 2)], axis=1)
    kv_other = other_part(kv_mine)
    q_mine = spread(columns(w_query))
    q_other = other_part(q_mine)

    out_cols = w_out.shape[1] // 2
    out_mine = lax.dynamic_slice_in_dim(w_out, core * out_cols, out_cols, 1)
    out_other = other_core(lax.dynamic_slice_in_dim(w_out, (1 - core) * out_cols, out_cols, 1))

    stream = jnp.zeros((SUB * rows, width), BF16)
    for step, piece in enumerate((tokens, beside, across, corner)):
        whole = lax.all_gather(piece, "head", axis=1, tiled=True)
        stream = lax.dynamic_update_slice(stream, whole, ((block ^ step) * rows, 0))

    position = lax.broadcasted_iota(jnp.int32, (rows, rows), 0)
    other = lax.broadcasted_iota(jnp.int32, (rows, rows), 1)
    causal = other <= position

    def attend(kv, q):
        both = dot(stream, kv)
        key = jax.nn.silu(both[:, :HDIM]).astype(BF16).reshape(SUB, rows, HDIM)
        value = both[:, HDIM:].astype(BF16).reshape(SUB, rows, HDIM)
        own = jnp.einsum("bsd,bse->bde", key, value, preferred_element_type=F32)
        carried = exclusive_prefix(own.sum(0), groups)
        prefixes = [carried]
        for b in range(SUB - 1):
            prefixes.append(prefixes[-1] + own[b])
        earlier = jnp.stack(prefixes).astype(BF16)
        query = jax.nn.silu(dot(stream, q)).astype(BF16).reshape(SUB, rows, HDIM)
        scores = jnp.einsum("btd,bsd->bts", query, key, preferred_element_type=F32)
        weights = jnp.where(causal[None], scores, 0.0).astype(BF16)
        mixed = jnp.einsum("bts,bse->bte", weights, value, preferred_element_type=F32)
        mixed = mixed + jnp.einsum("btd,bde->bte", query, earlier, preferred_element_type=F32)
        return (mixed * lax.rsqrt(jnp.mean(mixed * mixed, axis=-1, keepdims=True) + 1e-06)).astype(BF16)

    mine = attend(kv_mine, q_mine)
    theirs = attend(kv_other, q_other)
    first = jnp.where(part == 0, mine, theirs)
    second = jnp.where(part == 0, theirs, mine)
    normed = jnp.concatenate([first, second], axis=2)

    def block_for(step):
        return lax.dynamic_index_in_dim(normed, block ^ step, 0, keepdims=False)

    full = jnp.zeros((rows, SUB * 2 * HDIM), BF16)
    for step in range(SUB):
        piece = block_for(step)
        if step:
            piece = xor(piece, step)
        full = lax.dynamic_update_slice(full, piece, (0, (block ^ step) * 2 * HDIM))
    return (dot(full, out_mine) + dot(other_core(full), out_other)).astype(BF16)


def solution(mesh):
    in_specs = (
        P(("groups", "ctx"), "head"),
        P("ctx", "head"),
        P("ctx", "head"),
        P("ctx", "head"),
        P("head", None),
    )
    out_specs = P(("groups", "ctx"), "head")
    return jax.shard_map(local, mesh=mesh, in_specs=in_specs, out_specs=out_specs, check_vma=False)
```

time: 519 us -> 279 us (0.54)
  waiting for transfers between devices: 452 us -> 156 us
  starting transfers between devices: 0.38 us -> 34.9 us
  local copies, waits for them, and re-layouts: 1.3 us -> 33.1 us
  other arithmetic: 12.1 us -> 4.65 us
    all_gather x5 -> x4, waiting for transfers between devices: 436 us -> 0.01 us  [local(): whole = lax.all_gather(piece, 'head', axis=1, tiled=True)]
    ppermute x0 -> x13, waiting for transfers between devices: none -> 154 us  [the longest x7 125 us: xor(): return lax.ppermute(value, 'ctx', [(i, i ^ step) for i in range(n_ctx)])]
    ppermute x0 -> x13, starting transfers between devices: none -> 23.8 us  [the longest x7 12 us: xor(): return lax.ppermute(value, 'ctx', [(i, i ^ step) for i in range(n_ctx)])]
    dynamic_update_slice x0 -> x7, local copies, waits for them, and re-layouts: none -> 13.8 us  [the longest x4 13.7 us: local(): stream = lax.dynamic_update_slice(stream, whole, ((block ^ step) * rows, 0))]
    reduce_scatter x1 -> x0, waiting for transfers between devices: 12.9 us -> none  [local(): lax.psum_scatter(head_terms, 'head', scatter_dimension=1, tiled=True)]
    all_to_all x0 -> x2, starting transfers between devices: none -> 10.9 us  [spread(): return lax.all_to_all(sent, 'ctx', 0, 0, tiled=True)]
    select_n x7 -> x1, other arithmetic: 8.66 us -> 0.16 us  [local(): second = jnp.where(part == 0, theirs, mine)]
    broadcast_in_dim x0 -> x2, local copies, waits for them, and re-layouts: none -> 6.54 us  [the longest x1 6.47 us: local(): stream = jnp.zeros((SUB * rows, width), BF16)]
  transfers between devices with their start and end apart: 6 -> 19, of which waited for: 6 -> 11; matrix products, arithmetic and copies ran while one was open for 6% -> 22% of each run, Pallas kernels for 0% -> 0%
where the time goes in v1:
time: 279 us; the launch traced here: 278 us
  waiting for transfers between devices  156 us (56%)
  matrix products  36 us (13%)
  starting transfers between devices  34.9 us (13%)
  local copies, waits for them, and re-layouts  33.1 us (12%)
  between operations  13.5 us (5%)
  other arithmetic  4.65 us (2%)
    ppermute x7, waiting for transfers between devices, xor(): return lax.ppermute(value, 'ctx', [(i, i ^ step) for i in range(n_ctx)])  125 us
    dot_general x6, matrix products, dot(): return jnp.dot(a, b, preferred_element_type=F32)  32.1 us
    ppermute x2, waiting for transfers between devices, other_part(): return lax.ppermute(value, 'groups', [(0, 1), (1, 0)])  24.7 us
    dynamic_update_slice x4, local copies, waits for them, and re-layouts, local(): stream = lax.dynamic_update_slice(stream, whole, ((block ^ step) * rows, 0))  13.7 us
    ppermute x7, starting transfers between devices, xor(): return lax.ppermute(value, 'ctx', [(i, i ^ step) for i in range(n_ctx)])  12 us
    all_to_all x2, starting transfers between devices, spread(): return lax.all_to_all(sent, 'ctx', 0, 0, tiled=True)  10.9 us
    ppermute x2, starting transfers between devices, shift(): return lax.ppermute(v, 'ctx', pairs)  9.19 us
    unnamed x19, local copies, waits for them, and re-layouts  6.95 us
  transfers between devices with their start and end apart: 19, of which 11 were waited for; matrix products, arithmetic and copies ran while one was open for 22% of the time, Pallas kernels for 0%

profile of v1, /device:TPU:0, one launch (start us, length us, event | category | flops | bytes accessed | tf_op | source)
XLA Modules:
  0.0 278.2 jit_solution(17229874692633283822)
XLA Ops:
  7.3 3.0 %collective-permute-start = (bf16[384,2048]{1,0:T(8,128)(2,1)}, bf16[384,2048]{1,0:T(8,128)(2,1)S(1)}, u32[]{:S(2)}, u32[]{:S(2)}) collective-permute-start(bf16[384,2048]{1,0:T(8,128)(2,1)} %param.5), channel_id=1, source_target_pairs={{0,2},{2,0},{4,6},{6,4},{8,10},{10,8},{12,14},{14,12},{1,3},{3,1},... | collective-permute-start | bytes 4718600 | tf_op jit(solution)/shard_map/ppermute | solution.py:43
  10.3 34.6 %collective-permute-done = bf16[384,2048]{1,0:T(8,128)(2,1)S(1)} collective-permute-done((bf16[384,2048]{1,0:T(8,128)(2,1)}, bf16[384,2048]{1,0:T(8,128)(2,1)S(1)}, u32[]{:S(2)}, u32[]{:S(2)}) %collective-permute-start) | collective-permute-done | bytes 1572896 | tf_op jit(solution)/shard_map/ppermute | solution.py:43
  46.1 1.9 collective-permute-start.1
  50.9 4.8 %all-to-all-start = ((bf16[8,512,128]{2,1,0:T(8,128)(2,1)}), bf16[8,512,128]{2,1,0:T(8,128)(2,1)}, u32[]{:S(2)}, u32[]{:S(2)}) async-start(bf16[8,512,128]{2,1,0:T(8,128)(2,1)} %pad_maximum_fusion.1), calls=%async_computation | async-start | bytes 2097152 | tf_op jit(solution)/shard_map/all_to_all | solution.py:58
  55.7 37.8 %collective-permute-done.1 = bf16[384,2048]{1,0:T(8,128)(2,1)S(1)} collective-permute-done((bf16[384,2048]{1,0:T(8,128)(2,1)}, bf16[384,2048]{1,0:T(8,128)(2,1)S(1)}, u32[]{:S(2)}, u32[]{:S(2)}) %collective-permute-start.1) | collective-permute-done | bytes 1572896 | tf_op jit(solution)/shard_map/ppermute | solution.py:43
  100.4 6.1 %all-to-all-start.1 = ((bf16[8,512,256]{2,1,0:T(8,128)(2,1)}), bf16[8,512,256]{2,1,0:T(8,128)(2,1)}, u32[]{:S(2)}, u32[]{:S(2)}) async-start(bf16[8,512,256]{2,1,0:T(8,128)(2,1)} %maximum_maximum_fusion), calls=%async_computation.1 | async-start | bytes 4194304 | tf_op jit(solution)/shard_map/all_to_all | solution.py:58
  106.6 2.0 collective-permute-start.2
  108.8 1.5 collective-permute-start.3
  110.3 33.9 %collective-permute-done.2 = bf16[384,1024]{1,0:T(8,128)(2,1)S(1)} collective-permute-done((bf16[384,1024]{1,0:T(8,128)(2,1)S(1)}, bf16[384,1024]{1,0:T(8,128)(2,1)S(1)}, u32[]{:S(2)}, u32[]{:S(2)}) %collective-permute-start.2) | collective-permute-done | bytes 786464 | tf_op jit(solution)/shard_map/ppermute | solution.py:43
  144.2 11.3 %collective-permute-done.3 = bf16[384,1024]{1,0:T(8,128)(2,1)S(1)} collective-permute-done((bf16[384,1024]{1,0:T(8,128)(2,1)S(1)}, bf16[384,1024]{1,0:T(8,128)(2,1)S(1)}, u32[]{:S(2)}, u32[]{:S(2)}) %collective-permute-start.3) | collective-permute-done | bytes 786464 | tf_op jit(solution)/shard_map/ppermute | solution.py:43
  156.8 4.7 %constant_dynamic-slice_fusion = bf16[1024,2048]{1,0:T(8,128)(2,1)} fusion(bf16[1024,4096]{1,0:T(8,128)(2,1)} %param.9, s32[]{:T(128)S(6)} %select_n.95), kind=kLoop, calls=%fused_computation.89 | loop fusion | bytes 8388612 | tf_op jit(solution)/shard_map/dynamic_slice | solution.py:71
  161.6 1.6 collective-permute-start.5
  163.1 6.5 %broadcast_in_dim.30 = bf16[1536,4096]{1,0:T(8,128)(2,1)} broadcast(bf16[]{:T(256)} %constant.63.clone.1), dimensions={} | broadcast | bytes 12582914 | tf_op jit(solution)/shard_map/broadcast_in_dim | solution.py:73
  169.6 1.8 constant_dynamic-update-slice_fusion.6
  172.4 3.9 %constant_dynamic-update-slice_fusion.5 = bf16[1536,4096]{1,0:T(8,128)(2,1)} fusion(bf16[1536,4096]{1,0:T(8,128)(2,1)} %constant_dynamic-update-slice_fusion.6, bf16[384,4096]{1,0:T(8,128)(2,1)} %all-gather.7.cloned.1.call-done, s32[]{:T(128)S(6)} %select_n.78), kind=kLoop, calls=%fused_computation.96 | loop fusion | bytes 6291460 | tf_op jit(solution)/shard_map/dynamic_update_slice | solution.py:76
  176.3 4.0 %constant_dynamic-update-slice_fusion.4 = bf16[1536,4096]{1,0:T(8,128)(2,1)} fusion(bf16[1536,4096]{1,0:T(8,128)(2,1)} %constant_dynamic-update-slice_fusion.5, bf16[384,4096]{1,0:T(8,128)(2,1)} %all-gather.9.cloned.1.call-done, s32[]{:T(128)S(6)} %select_n.79), kind=kLoop, calls=%fused_computation.95 | loop fusion | bytes 6291460 | tf_op jit(solution)/shard_map/dynamic_update_slice | solution.py:76
  180.3 3.9 %constant_dynamic-update-slice_fusion.3 = bf16[1536,4096]{1,0:T(8,128)(2,1)} fusion(bf16[1536,4096]{1,0:T(8,128)(2,1)} %constant_dynamic-update-slice_fusion.4, bf16[384,4096]{1,0:T(8,128)(2,1)} %all-gather.11.cloned.1.call-done, s32[]{:T(128)S(6)} %select_n.80), kind=kLoop, calls=%fused_computation.94 | loop fusion | bytes 6291460 | tf_op jit(solution)/shard_map/dynamic_update_slice | solution.py:76
  184.2 7.7 %fusion.54 = f32[1536,256]{1,0:T(8,128)S(1)} fusion(bf16[1536,4096]{1,0:T(8,128)(2,1)} %constant_dynamic-update-slice_fusion.3, bf16[4096,256]{1,0:T(8,128)(2,1)} %bitcast.11), kind=kOutput, calls=%fused_computation.104 | convolution fusion | flops 3221225472 | bytes 16252928 | tf_op jit(solution)/shard_map/dot_general | solution.py:13
  193.0 4.7 %multiply_convert_fusion.5 = bf16[1536,128]{1,0:T(8,128)(2,1)S(1)} fusion(bf16[1536,4096]{1,0:T(8,128)(2,1)S(1)} %copy-done, bf16[4096,128]{1,0:T(8,128)(2,1)} %bitcast.3), kind=kOutput, calls=%fused_computation.33 | convolution fusion | flops 1611595776 | bytes 14024704 | tf_op jit(solution)/shard_map/dot_general | solution.py:13
  198.4 4.7 %collective-permute-start.4 = (f32[128,128]{1,0:T(8,128)S(1)}, f32[128,128]{1,0:T(8,128)S(1)}, u32[]{:S(2)}, u32[]{:S(2)}) collective-permute-start(f32[128,128]{1,0:T(8,128)S(1)} %get-tuple-element.18), channel_id=1, source_target_pairs={{0,8},{2,10},{4,12},{6,14},{1,9},{3,11},{5,13},{7,15},{16,24},{18,... | collective-permute-start | bytes 196616 | tf_op jit(solution)/shard_map/ppermute | solution.py:19
  203.1 3.5 %multiply_convert_fusion.2 = bf16[1536,128]{1,0:T(8,128)(2,1)S(1)} fusion(bf16[1536,4096]{1,0:T(8,128)(2,1)S(1)} %copy-done, bf16[4096,128]{1,0:T(8,128)(2,1)S(1)} %collective-permute-done.5), kind=kOutput, calls=%fused_computation.29 | convolution fusion | flops 1611595776 | bytes 14024704 | tf_op jit(solution)/shard_map/dot_general | solution.py:13
  207.8 24.7 %collective-permute-done.6 = bf16[4096,256]{1,0:T(8,128)(2,1)} collective-permute-done((bf16[4096,256]{1,0:T(8,128)(2,1)}, bf16[4096,256]{1,0:T(8,128)(2,1)}, u32[]{:S(2)}, u32[]{:S(2)}) %collective-permute-start.6) | collective-permute-done | bytes 2097184 | tf_op jit(solution)/shard_map/ppermute | solution.py:46
  232.5 7.0 %fusion.55 = f32[1536,256]{1,0:T(8,128)S(1)} fusion(bf16[1536,4096]{1,0:T(8,128)(2,1)} %constant_dynamic-update-slice_fusion.3, bf16[4096,256]{1,0:T(8,128)(2,1)} %collective-permute-done.6), kind=kOutput, calls=%fused_computation.105 | convolution fusion | flops 3221225472 | bytes 16252928 | tf_op jit(solution)/shard_map/dot_general | solution.py:13
  240.1 4.5 %collective-permute-start.7 = (f32[128,128]{1,0:T(8,128)S(1)}, f32[128,128]{1,0:T(8,128)S(1)}, u32[]{:S(2)}, u32[]{:S(2)}) collective-permute-start(f32[128,128]{1,0:T(8,128)S(1)} %get-tuple-element.22), channel_id=1, source_target_pairs={{0,8},{2,10},{4,12},{6,14},{1,9},{3,11},{5,13},{7,15},{16,24},{18,... | collective-permute-start | bytes 196616 | tf_op jit(solution)/shard_map/ppermute | solution.py:19
  244.7 1.9 collective-permute-done.7
  246.9 1.7 multiply_reduce_fusion
  252.6 3.3 %collective-permute-done.8 = bf16[384,256]{0,1:T(8,128)(2,1)S(1)} collective-permute-done((bf16[384,256]{0,1:T(8,128)(2,1)S(1)}, bf16[384,256]{0,1:T(8,128)(2,1)S(1)}, u32[]{:S(2)}, u32[]{:S(2)}) %collective-permute-start.8) | collective-permute-done | bytes 196640 | tf_op jit(solution)/shard_map/ppermute | solution.py:43
  255.9 1.8 collective-permute-done.9
  257.8 2.3 collective-permute-done.10
  260.2 2.3 collective-permute-done.11
  262.4 4.0 %fusion.56 = f32[384,2048]{1,0:T(8,128)S(1)} fusion(bf16[384,1024]{0,1:T(8,128)(2,1)S(1)} %collective-permute-done.11, bf16[1024,2048]{1,0:T(8,128)(2,1)} %collective-permute-done.12), kind=kOutput, calls=%fused_computation.106 | convolution fusion | flops 1610612736 | bytes 8126464 | tf_op jit(solution)/shard_map/dot_general | solution.py:13
  266.5 5.2 %add_convert_fusion = bf16[384,2048]{1,0:T(8,128)(2,1)} fusion(f32[384,2048]{1,0:T(8,128)S(1)} %fusion.56, bf16[384,1024]{0,1:T(8,128)(2,1)S(1)} %constant_dynamic-update-slice_fusion, bf16[1024,4096]{1,0:T(8,128)(2,1)} %param.9, s32[]{:T(128)S(6)} %select_n.94), kind=kOutput, calls=%fused_computation.2 | convolution fusion | flops 1612185600 | bytes 9699332 | tf_op jit(solution)/shard_map/dot_general | solution.py:13
  (73 shorter events, 22.0 us)
Async XLA Ops:
  6.5 156.6 %all-gather.5.cloned.1.call-start = ((), (), s32[]{:S(2)}) async-start(), calls=%async_computation.2 | async-start | bytes 4718592 | tf_op jit(solution)/shard_map/all_gather | solution.py:75
  7.3 165.2 %all-gather.7.cloned.1.call-start = ((), (), s32[]{:S(2)}) async-start(), calls=%async_computation.3 | async-start | bytes 4718592 | tf_op jit(solution)/shard_map/all_gather | solution.py:75
  7.3 37.6 %collective-permute-start = (bf16[384,2048]{1,0:T(8,128)(2,1)}, bf16[384,2048]{1,0:T(8,128)(2,1)S(1)}, u32[]{:S(2)}, u32[]{:S(2)}) collective-permute-start(bf16[384,2048]{1,0:T(8,128)(2,1)} %param.5), channel_id=1, source_target_pairs={{0,2},{2,0},{4,6},{6,4},{8,10},{10,8},{12,14},{14,12},{1,3},{3,1},... | collective-permute-start | bytes 4718600 | tf_op jit(solution)/shard_map/ppermute | solution.py:43
  44.9 1.1 copy-start.1
  46.1 47.4 %collective-permute-start.1 = (bf16[384,2048]{1,0:T(8,128)(2,1)}, bf16[384,2048]{1,0:T(8,128)(2,1)S(1)}, u32[]{:S(2)}, u32[]{:S(2)}) collective-permute-start(bf16[384,2048]{1,0:T(8,128)(2,1)} %param.5), channel_id=1, source_target_pairs={{0,4},{2,6},{4,0},{6,2},{8,12},{10,14},{12,8},{14,10},{1,5},{3,7},... | collective-permute-start | bytes 4718600 | tf_op jit(solution)/shard_map/ppermute | solution.py:43
  49.8 44.9 %copy-start.6 = (bf16[512,1024]{1,0:T(8,128)(2,1)S(1)}, bf16[512,1024]{1,0:T(8,128)(2,1)}, u32[]{:S(2)}) copy-start(bf16[512,1024]{1,0:T(8,128)(2,1)} %param.7) | copy-start | bytes 3145732
  50.9 49.5 %all-to-all-start = ((bf16[8,512,128]{2,1,0:T(8,128)(2,1)}), bf16[8,512,128]{2,1,0:T(8,128)(2,1)}, u32[]{:S(2)}, u32[]{:S(2)}) async-start(bf16[8,512,128]{2,1,0:T(8,128)(2,1)} %pad_maximum_fusion.1), calls=%async_computation | async-start | bytes 2097152 | tf_op jit(solution)/shard_map/all_to_all | solution.py:58
  55.7 120.6 %all-gather.9.cloned.1.call-start = ((), (), s32[]{:S(2)}) async-start(), calls=%async_computation.4 | async-start | bytes 4718592 | tf_op jit(solution)/shard_map/all_gather | solution.py:75
  93.5 1.2 copy-start.3
  97.4 9.2 %copy-start.4 = (bf16[384,2048]{1,0:T(8,128)(2,1)S(1)}, bf16[384,2048]{1,0:T(8,128)(2,1)}, u32[]{:S(2)}) copy-start(bf16[384,2048]{1,0:T(8,128)(2,1)} %copy-done.3) | copy-start | bytes 4718596
  98.9 9.8 %copy-start.2 = (bf16[384,2048]{1,0:T(8,128)(2,1)S(1)}, bf16[384,2048]{1,0:T(8,128)(2,1)}, u32[]{:S(2)}) copy-start(bf16[384,2048]{1,0:T(8,128)(2,1)} %copy-done.1) | copy-start | bytes 4718596
  100.4 71.1 %all-to-all-start.1 = ((bf16[8,512,256]{2,1,0:T(8,128)(2,1)}), bf16[8,512,256]{2,1,0:T(8,128)(2,1)}, u32[]{:S(2)}, u32[]{:S(2)}) async-start(bf16[8,512,256]{2,1,0:T(8,128)(2,1)} %maximum_maximum_fusion), calls=%async_computation.1 | async-start | bytes 4194304 | tf_op jit(solution)/shard_map/all_to_all | solution.py:58
  106.5 73.8 %all-gather.11.cloned.1.call-start = ((), (), s32[]{:S(2)}) async-start(), calls=%async_computation.5 | async-start | bytes 4718592 | tf_op jit(solution)/shard_map/all_gather | solution.py:75
  106.6 37.6 %collective-permute-start.2 = (bf16[384,1024]{1,0:T(8,128)(2,1)S(1)}, bf16[384,1024]{1,0:T(8,128)(2,1)S(1)}, u32[]{:S(2)}, u32[]{:S(2)}) collective-permute-start(bf16[384,1024]{1,0:T(8,128)(2,1)S(1)} %slice.50), channel_id=1, source_target_pairs={{0,2},{2,0},{4,6},{6,4},{8,10},{10,8},{12,14},{14,12},{1,3},{3,1},... | collective-permute-start | bytes 2359304 | tf_op jit(solution)/shard_map/ppermute | solution.py:43
  108.8 46.7 %collective-permute-start.3 = (bf16[384,1024]{1,0:T(8,128)(2,1)S(1)}, bf16[384,1024]{1,0:T(8,128)(2,1)S(1)}, u32[]{:S(2)}, u32[]{:S(2)}) collective-permute-start(bf16[384,1024]{1,0:T(8,128)(2,1)S(1)} %slice.51), channel_id=1, source_target_pairs={{0,4},{2,6},{4,0},{6,2},{8,12},{10,14},{12,8},{14,10},{1,5},{3,7},... | collective-permute-start | bytes 2359304 | tf_op jit(solution)/shard_map/ppermute | solution.py:43
  161.5 98.7 %collective-permute-start.12 = (bf16[1024,2048]{1,0:T(8,128)(2,1)}, bf16[1024,2048]{1,0:T(8,128)(2,1)}, u32[]{:S(2)}, u32[]{:S(2)}) collective-permute-start(bf16[1024,2048]{1,0:T(8,128)(2,1)} %constant_dynamic-slice_fusion), channel_id=1, source_target_pairs={{0,1},{1,0},{2,3},{3,2},{4,5},{5,4},{6,7},{7,6},{8,9},{9,8},{10,11... | collective-permute-start | bytes 12582920 | tf_op jit(solution)/shard_map/ppermute | solution.py:49
  161.5 45.4 %copy-start.7 = (pred[384,384]{1,0:T(8,128)(4,1)}, pred[384,384]{1,0:T(8,128)(4,1)S(1)}, u32[]{:S(2)}) copy-start(pred[384,384]{1,0:T(8,128)(4,1)S(1)} %iota_compare_fusion) | copy-start | bytes 442372
  161.6 41.5 %collective-permute-start.5 = (bf16[4096,128]{1,0:T(8,128)(2,1)}, bf16[4096,128]{1,0:T(8,128)(2,1)S(1)}, u32[]{:S(2)}, u32[]{:S(2)}) collective-permute-start(bf16[4096,128]{1,0:T(8,128)(2,1)} %bitcast.3), channel_id=1, source_target_pairs={{0,16},{16,0},{1,17},{17,1},{2,18},{18,2},{3,19},{19,3},{4,20},{20... | collective-permute-start | bytes 3145736 | tf_op jit(solution)/shard_map/ppermute | solution.py:46
  163.1 6.5 %copy-start.5 = (bf16[384,4096]{1,0:T(8,128)(2,1)S(1)}, bf16[384,4096]{1,0:T(8,128)(2,1)}, u32[]{:S(2)}) copy-start(bf16[384,4096]{1,0:T(8,128)(2,1)} %all-gather.5.cloned.1.call-done) | copy-start | bytes 9437188
  171.5 61.0 %collective-permute-start.6 = (bf16[4096,256]{1,0:T(8,128)(2,1)}, bf16[4096,256]{1,0:T(8,128)(2,1)}, u32[]{:S(2)}, u32[]{:S(2)}) collective-permute-start(bf16[4096,256]{1,0:T(8,128)(2,1)} %bitcast.11), channel_id=1, source_target_pairs={{0,16},{16,0},{1,17},{17,1},{2,18},{18,2},{3,19},{19,3},{4,20},{20... | collective-permute-start | bytes 6291464 | tf_op jit(solution)/shard_map/ppermute | solution.py:46
  184.2 8.8 %copy-start = (bf16[1536,4096]{1,0:T(8,128)(2,1)S(1)}, bf16[1536,4096]{1,0:T(8,128)(2,1)}, u32[]{:S(2)}) copy-start(bf16[1536,4096]{1,0:T(8,128)(2,1)} %constant_dynamic-update-slice_fusion.3) | copy-start | bytes 37748740
  198.4 8.2 %collective-permute-start.4 = (f32[128,128]{1,0:T(8,128)S(1)}, f32[128,128]{1,0:T(8,128)S(1)}, u32[]{:S(2)}, u32[]{:S(2)}) collective-permute-start(f32[128,128]{1,0:T(8,128)S(1)} %get-tuple-element.18), channel_id=1, source_target_pairs={{0,8},{2,10},{4,12},{6,14},{1,9},{3,11},{5,13},{7,15},{16,24},{18,... | collective-permute-start | bytes 196616 | tf_op jit(solution)/shard_map/ppermute | solution.py:19
  240.1 6.4 %collective-permute-start.7 = (f32[128,128]{1,0:T(8,128)S(1)}, f32[128,128]{1,0:T(8,128)S(1)}, u32[]{:S(2)}, u32[]{:S(2)}) collective-permute-start(f32[128,128]{1,0:T(8,128)S(1)} %get-tuple-element.22), channel_id=1, source_target_pairs={{0,8},{2,10},{4,12},{6,14},{1,9},{3,11},{5,13},{7,15},{16,24},{18,... | collective-permute-start | bytes 196616 | tf_op jit(solution)/shard_map/ppermute | solution.py:19
  248.9 7.0 %collective-permute-start.8 = (bf16[384,256]{0,1:T(8,128)(2,1)S(1)}, bf16[384,256]{0,1:T(8,128)(2,1)S(1)}, u32[]{:S(2)}, u32[]{:S(2)}) collective-permute-start(bf16[384,256]{0,1:T(8,128)(2,1)S(1)} %get-tuple-element.8), channel_id=1, source_target_pairs={{0,2},{2,0},{4,6},{6,4},{8,10},{10,8},{12,14},{14,12},{1,3},{3,1},... | collective-permute-start | bytes 589832 | tf_op jit(solution)/shard_map/ppermute | solution.py:43
  250.3 7.5 %collective-permute-start.9 = (bf16[384,256]{0,1:T(8,128)(2,1)S(1)}, bf16[384,256]{0,1:T(8,128)(2,1)S(1)}, u32[]{:S(2)}, u32[]{:S(2)}) collective-permute-start(bf16[384,256]{0,1:T(8,128)(2,1)S(1)} %get-tuple-element.9), channel_id=1, source_target_pairs={{0,4},{2,6},{4,0},{6,2},{8,12},{10,14},{12,8},{14,10},{1,5},{3,7},... | collective-permute-start | bytes 589832 | tf_op jit(solution)/shard_map/ppermute | solution.py:43
  251.1 9.0 %collective-permute-start.10 = (bf16[384,256]{0,1:T(8,128)(2,1)S(1)}, bf16[384,256]{0,1:T(8,128)(2,1)S(1)}, u32[]{:S(2)}, u32[]{:S(2)}) collective-permute-start(bf16[384,256]{0,1:T(8,128)(2,1)S(1)} %get-tuple-element.7), channel_id=1, source_target_pairs={{0,6},{2,4},{4,2},{6,0},{8,14},{10,12},{12,10},{14,8},{1,7},{3,5},... | collective-permute-start | bytes 589832 | tf_op jit(solution)/shard_map/ppermute | solution.py:43
  260.1 2.4 collective-permute-start.11
Sparse Core Ops, SparseCore 0:
  8.9 14.8 all-gather.4
  46.2 13.6 all-gather.6
  94.8 15.0 all-gather.8
  156.9 14.1 all-gather.10

commit v2 on v1

v2 whole, which is shorter than its diff:
```python
import functools

import jax
import jax.numpy as jnp
from jax import lax
from jax.experimental import pallas as pl
from jax.experimental.pallas import tpu as pltpu
from jax.sharding import PartitionSpec as P

HDIM = 128
SUB = 4
F32 = jnp.float32
BF16 = jnp.bfloat16
ANY = pl.BlockSpec(memory_space=pl.ANY)
VMEM = pl.BlockSpec(memory_space=pltpu.VMEM)


def dot(a, b, contract=((1,), (0,))):
    return lax.dot_general(a, b, (contract, ((), ())), preferred_element_type=F32)


def cost(flops, moved):
    return pl.CostEstimate(flops=int(flops), bytes_accessed=int(moved), transcendentals=0)


def silu(u):
    return u / (1.0 + jnp.exp(-u))


def pack_columns(place, weights, count):
    depth = weights[0].shape[0]
    width = HDIM * len(weights)

    def kernel(place_ref, *refs):
        *ins, out = refs
        for i, ref in enumerate(ins):
            out[:, i * HDIM : (i + 1) * HDIM] = ref[...]

    return pl.pallas_call(
        kernel,
        out_shape=jax.ShapeDtypeStruct((count * depth, width), BF16),
        grid_spec=pltpu.PrefetchScalarGridSpec(
            num_scalar_prefetch=1,
            grid=(count,),
            in_specs=[pl.BlockSpec((depth, HDIM), lambda i, s: (0, 2 * lax.rem(i, SUB) + s[1]))] * len(weights),
            out_specs=pl.BlockSpec((depth, width), lambda i, s: (i, 0)),
        ),
        cost_estimate=cost(0, 2 * count * depth * width * 2),
        name="pack_columns",
    )(place, *weights)


def pack_rows(place, w_out):
    rows, width = w_out.shape
    half = width // 2

    def kernel(place_ref, keep_in, send_in, keep, send):
        keep[...] = keep_in[...]
        send[...] = send_in[...]

    def head(i, s):
        return 2 * jnp.bitwise_xor(s[0], lax.rem(i, SUB)) + jnp.bitwise_xor(s[1], i // SUB)

    return pl.pallas_call(
        kernel,
        out_shape=[jax.ShapeDtypeStruct((rows, half), BF16)] * 2,
        grid_spec=pltpu.PrefetchScalarGridSpec(
            num_scalar_prefetch=1,
            grid=(rows // HDIM,),
            in_specs=[
                pl.BlockSpec((HDIM, half), lambda i, s: (head(i, s), s[2])),
                pl.BlockSpec((HDIM, half), lambda i, s: (head(i, s), 1 - s[2])),
            ],
            out_specs=[pl.BlockSpec((HDIM, half), lambda i, s: (i, 0))] * 2,
        ),
        cost_estimate=cost(0, 2 * rows * width * 2),
        name="pack_rows",
    )(place, w_out, w_out)


class Stream:
    def __init__(self, pieces, rows, half):
        self.pieces, self.rows, self.half = pieces, rows, half

    def scratch(self, width):
        return [
            pltpu.VMEM((SUB, self.rows, 2 * self.half), BF16),
            pltpu.VMEM((2 * self.half, width), BF16),
            pltpu.SemaphoreType.DMA((len(self.pieces) + 2,)),
        ]

    def copies(self, place_ref, refs, w_ref, held, w_held, sems):
        core = place_ref[2]
        by_block = [[] for _ in range(SUB)]
        weight = []
        for i in range(2):
            start = (core if i == 0 else 1 - core) * self.half
            weight.append(
                pltpu.make_async_copy(
                    w_ref.at[pl.ds(start, self.half), :], w_held.at[pl.ds(i * self.half, self.half), :], sems.at[i]
                )
            )
        for i, ((array, block, column), ref) in enumerate(zip(self.pieces, refs)):
            target = held.at[block, :, pl.ds(column, array.shape[1])]
            by_block[block].append(pltpu.make_async_copy(ref, target, sems.at[i + 2]))
        for copy in weight:
            copy.start()
        for group in by_block:
            for copy in group:
                copy.start()
        return weight, by_block

    def arrays(self):
        return [array for array, _, _ in self.pieces]


SMEM = pl.BlockSpec(memory_space=pltpu.SMEM)


def project(place, stream, kv):
    rows, count = stream.rows, len(stream.pieces)

    def kernel(place_ref, *refs):
        ins, w_ref = refs[:count], refs[count]
        key_ref, value_ref, state_ref, held, w_held, sems = refs[count + 1 :]
        weight, by_block = stream.copies(place_ref, ins, w_ref, held, w_held, sems)
        for copy in weight:
            copy.wait()
        state = jnp.zeros((HDIM, HDIM), F32)
        for r in range(SUB):
            for copy in by_block[r]:
                copy.wait()
            both = dot(held[r], w_held[...])
            key = silu(both[:, :HDIM]).astype(BF16)
            value = both[:, HDIM:].astype(BF16)
            key_ref[r] = key
            value_ref[r] = value
            state = state + dot(key, value, ((0,), (0,)))
        state_ref[...] = state

    shape = jax.ShapeDtypeStruct((SUB, rows, HDIM), BF16)
    return pl.pallas_call(
        kernel,
        out_shape=[shape, shape, jax.ShapeDtypeStruct((HDIM, HDIM), F32)],
        in_specs=[SMEM] + [ANY] * (count + 1),
        out_specs=[VMEM] * 3,
        scratch_shapes=stream.scratch(2 * HDIM),
        cost_estimate=cost(2 * SUB * rows * 2 * stream.half * 2 * HDIM, SUB * rows * 2 * stream.half * 2),
        name="project",
    )(place, *stream.arrays(), kv)


def finish(place, stream, w_q, key, value, carried):
    rows, count = stream.rows, len(stream.pieces)

    def kernel(place_ref, *refs):
        ins, w_ref = refs[:count], refs[count]
        key_ref, value_ref, carried_ref, out_ref, held, w_held, sems = refs[count + 1 :]
        weight, by_block = stream.copies(place_ref, ins, w_ref, held, w_held, sems)
        block = place_ref[0]
        states = [dot(key_ref[r], value_ref[r], ((0,), (0,))) for r in range(SUB)]
        causal = lax.broadcasted_iota(jnp.int32, (rows, rows), 1) <= lax.broadcasted_iota(
            jnp.int32, (rows, rows), 0
        )
        for copy in weight:
            copy.wait()
        for r in range(SUB):
            earlier = carried_ref[...]
            for other in range(SUB):
                if other != r:
                    before = jnp.bitwise_xor(block, other) < jnp.bitwise_xor(block, r)
                    earlier = earlier + jnp.where(before, states[other], 0.0)
            for copy in by_block[r]:
                copy.wait()
            query = silu(dot(held[r], w_held[...])).astype(BF16)
            scores = dot(query, key_ref[r], ((1,), (1,)))
            weights = jnp.where(causal, scores, 0.0).astype(BF16)
            mixed = dot(weights, value_ref[r]) + dot(query, earlier.astype(BF16))
            scale = lax.rsqrt(jnp.mean(mixed * mixed, axis=-1, keepdims=True) + 1e-06)
            out_ref[r] = (mixed * scale).astype(BF16)

    return pl.pallas_call(
        kernel,
        out_shape=jax.ShapeDtypeStruct((SUB, rows, HDIM), BF16),
        in_specs=[SMEM] + [ANY] * (count + 1) + [VMEM] * 3,
        out_specs=VMEM,
        scratch_shapes=stream.scratch(HDIM),
        cost_estimate=cost(2 * SUB * rows * 2 * stream.half * HDIM, SUB * rows * 2 * stream.half * 2),
        name="finish",
    )(place, *stream.arrays(), w_q, key, value, carried)


def add_features(mine, theirs, w_mine, w_theirs, first, partial=None):
    rows, depth = mine.shape
    width = w_mine.shape[1]
    tile = min(512, width)

    def kernel(*refs):
        m_ref, t_ref, wm_ref, wt_ref = refs[:4]
        total = dot(m_ref[...], wm_ref[...]) + dot(t_ref[...], wt_ref[...])
        if partial is not None:
            total = total + refs[4][...]
        refs[-1][...] = total.astype(refs[-1].dtype)

    w_spec = pl.BlockSpec((depth, tile), lambda i: (0 if first else 1, i))
    sum_spec = pl.BlockSpec((rows, tile), lambda i: (0, i))
    return pl.pallas_call(
        kernel,
        out_shape=jax.ShapeDtypeStruct((rows, width), F32 if partial is None else BF16),
        grid=(width // tile,),
        in_specs=[pl.BlockSpec((rows, depth), lambda i: (0, 0))] * 2
        + [w_spec] * 2
        + ([] if partial is None else [sum_spec]),
        out_specs=sum_spec,
        cost_estimate=cost(4 * rows * depth * width, 4 * depth * width + 4 * rows * width),
        name="add_features",
    )(mine, theirs, w_mine, w_theirs, *([] if partial is None else [partial]))


def exclusive_prefix(value, groups):
    def shift(v, step):
        pairs = [(g * SUB + j, (g + step) * SUB + j) for g in range(groups - step) for j in range(SUB)]
        return lax.ppermute(v, "ctx", pairs)

    if groups == 1:
        return jnp.zeros_like(value)
    total = shift(value, 1)
    step = 1
    while step < groups - 1:
        total = total + shift(total, step)
        step *= 2
    return total


def local(tokens, w_query, w_key, w_value, w_out):
    n_ctx = lax.axis_size("ctx")
    groups = n_ctx // SUB
    rows, half = tokens.shape
    block = lax.axis_index("ctx") % SUB
    place = jnp.stack([block, lax.axis_index("groups"), lax.axis_index("head")]).astype(jnp.int32)

    def xor(value, step):
        return lax.ppermute(value, "ctx", [(i, i ^ step) for i in range(n_ctx)])

    def other_part(value):
        return lax.ppermute(value, "groups", [(0, 1), (1, 0)])

    def other_core(value):
        return lax.ppermute(value, "head", [(0, 1), (1, 0)])

    def spread(packed):
        return lax.all_to_all(packed, "ctx", 0, 0, tiled=True)

    cut = half // 2
    across = xor(tokens, 2)
    beside = xor(tokens, 1)
    kv_mine = spread(pack_columns(place, [w_key, w_value], n_ctx))
    q_packed = pack_columns(place, [w_query], n_ctx)
    across, beside, kv_mine, q_packed = lax.optimization_barrier((across, beside, kv_mine, q_packed))
    kv_other = other_part(kv_mine)
    q_mine = spread(q_packed)
    left = xor(across[:, :cut], 1)
    right = xor(beside[:, cut:], 2)
    left, right, q_mine, kv_other = lax.optimization_barrier((left, right, q_mine, kv_other))
    q_other = other_part(q_mine)

    out_keep, out_send = pack_rows(place, w_out)
    out_other = other_core(out_send)

    pieces = []
    for array, r, column in ((tokens, 0, 0), (beside, 1, 0), (across, 2, 0), (left, 3, 0), (right, 3, cut)):
        pieces += [(array, r, column), (other_core(array), r, half + column)]
    stream = Stream(pieces, rows, half)

    def exchange(normed):
        return jnp.concatenate([normed[0]] + [xor(normed[r], r) for r in range(1, SUB)], axis=1)

    k_mine, v_mine, state_mine = project(place, stream, kv_mine)
    carried_mine = exclusive_prefix(state_mine, groups)
    k_other, v_other, state_other = project(place, stream, kv_other)
    carried_other = exclusive_prefix(state_other, groups)
    mine = exchange(finish(place, stream, q_mine, k_mine, v_mine, carried_mine))
    partial = add_features(mine, other_core(mine), out_keep, out_other, True)
    theirs = exchange(finish(place, stream, q_other, k_other, v_other, carried_other))
    return add_features(theirs, other_core(theirs), out_keep, out_other, False, partial)


def solution(mesh):
    in_specs = (
        P(("groups", "ctx"), "head"),
        P("ctx", "head"),
        P("ctx", "head"),
        P("ctx", "head"),
        P("head", None),
    )
    out_specs = P(("groups", "ctx"), "head")
    return jax.shard_map(local, mesh=mesh, in_specs=in_specs, out_specs=out_specs, check_vma=False)
```

time: 279 us -> 220 us (0.79)
  Pallas kernels: 0 us -> 83.8 us
  waiting for transfers between devices: 156 us -> 91 us
  matrix products: 36 us -> 0 us
  local copies, waits for them, and re-layouts: 33.1 us -> 7.23 us
  between operations: 13.5 us -> 0.19 us
  other arithmetic: 4.65 us -> 0.67 us
    pallas_call x0 -> x9, Pallas kernels: none -> 83.8 us  [the longest x2 26.4 us: finish(): pl.pallas_call(kernel, out_shape=jax.ShapeDtypeStruct((SUB, rows, HDIM),...]
    ppermute x7 -> x10, waiting for transfers between devices: 125 us -> 83.7 us  [xor(): return lax.ppermute(value, 'ctx', [(i, i ^ step) for i in range(n_ctx)])]
    dot_general x12 -> x0, matrix products: 36 us -> none  [the longest x6 32.1 us: dot(): return jnp.dot(a, b, preferred_element_type=F32)]
    ppermute x2, waiting for transfers between devices: 24.7 us -> 5.54 us  [other_part(): return lax.ppermute(value, 'groups', [(0, 1), (1, 0)])]
    dynamic_update_slice x7 -> x0, local copies, waits for them, and re-layouts: 13.8 us -> none  [the longest x4 13.7 us: local(): stream = lax.dynamic_update_slice(stream, whole, ((block ^ step) * rows, 0))]
    broadcast_in_dim x2 -> x0, local copies, waits for them, and re-layouts: 6.54 us -> none  [the longest x1 6.47 us: local(): stream = jnp.zeros((SUB * rows, width), BF16)]
    dynamic_slice x6 -> x0, local copies, waits for them, and re-layouts: 5.65 us -> none  [the longest x1 4.71 us: local(): lax.dynamic_slice_in_dim(w_out, (1 - core) * out_cols, out_cols, 1)]
    unnamed x19 -> x18, local copies, waits for them, and re-layouts: 6.95 us -> 3.19 us
  transfers between devices with their start and end apart: 19 -> 24, of which waited for: 11 -> 10; matrix products, arithmetic and copies ran while one was open for 22% -> 2% of each run, Pallas kernels for 0% -> 32%
where the time goes in v2:
time: 220 us; the launch traced here: 219 us
  waiting for transfers between devices  91 us (41%)
  Pallas kernels  83.8 us (38%)
  starting transfers between devices  36.1 us (16%)
  local copies, waits for them, and re-layouts  7.23 us (3%)
    ppermute x10, waiting for transfers between devices, xor(): return lax.ppermute(value, 'ctx', [(i, i ^ step) for i in range(n_ctx)])  83.7 us
    pallas_call x2, Pallas kernels, finish(): pl.pallas_call(kernel, out_shape=jax.ShapeDtypeStruct((SUB, rows, HDIM),...  26.4 us
    pallas_call x2, Pallas kernels, project(): pl.pallas_call(kernel, out_shape=[shape, shape, jax.ShapeDtypeStruct((HDI...  23.4 us
    ppermute x10, starting transfers between devices, xor(): return lax.ppermute(value, 'ctx', [(i, i ^ step) for i in range(n_ctx)])  14.1 us
    pallas_call x2, Pallas kernels, pack_columns(): pl.pallas_call(kernel, out_shape=jax.ShapeDtypeStruct((count * depth, wid...  12.4 us
    pallas_call x2, Pallas kernels, add_features(): pl.pallas_call(kernel, out_shape=jax.ShapeDtypeStruct((rows, width), F32...  12.1 us
    all_to_all x2, starting transfers between devices, spread(): return lax.all_to_all(packed, 'ctx', 0, 0, tiled=True)  11.9 us
    pallas_call x1, Pallas kernels, pack_rows(): pl.pallas_call(kernel, out_shape=[jax.ShapeDtypeStruct((rows, half), BF16...  9.53 us
  transfers between devices with their start and end apart: 24, of which 10 were waited for; matrix products, arithmetic and copies ran while one was open for 2% of the time, Pallas kernels for 32%

profile of v2, /device:TPU:0, one launch (start us, length us, event | category | flops | bytes accessed | tf_op | source)
XLA Modules:
  0.0 219.0 jit_solution(11367731191845741405)
XLA Ops:
  0.6 6.6 %pack_columns.2 = bf16[4096,256]{1,0:T(8,128)(2,1)} custom-call(s32[3]{0:T(128)} %pad_add_fusion.place_ref, bf16[512,1024]{1,0:T(8,128)(2,1)} %refs_0_.6, bf16[512,1024]{1,0:T(8,128)(2,1)} %refs_1_.1), custom_call_target="tpu_custom_call" | custom-call | bytes 4194304 | tf_op jit(solution)/shard_map/pack_columns/pallas_call | solution.py:39
  7.1 7.3 %all-to-all-start = ((bf16[8,512,256]{2,1,0:T(8,128)(2,1)}), bf16[8,512,256]{2,1,0:T(8,128)(2,1)}, u32[]{:S(2)}, u32[]{:S(2)}) async-start(bf16[8,512,256]{2,1,0:T(8,128)(2,1)} %bitcast.23), calls=%async_computation | async-start | bytes 4194304 | tf_op jit(solution)/shard_map/all_to_all | solution.py:252
  14.4 2.0 collective-permute-start.2
  16.4 1.5 collective-permute-start.1
  17.9 5.9 %pack_columns.3 = bf16[4096,128]{1,0:T(8,128)(2,1)} custom-call(s32[3]{0:T(128)} %pad_add_fusion.place_ref, bf16[512,1024]{1,0:T(8,128)(2,1)} %refs_0_.7), custom_call_target="tpu_custom_call" | custom-call | bytes 2097152 | tf_op jit(solution)/shard_map/pack_columns/pallas_call | solution.py:39
  23.7 49.2 %collective-permute-done.2.refs_2_ = bf16[384,2048]{1,0:T(8,128)(2,1)S(1)} collective-permute-done((bf16[384,2048]{1,0:T(8,128)(2,1)}, bf16[384,2048]{1,0:T(8,128)(2,1)S(1)}, u32[]{:S(2)}, u32[]{:S(2)}) %collective-permute-start.2) | collective-permute-done | bytes 1572896 | tf_op jit(solution)/shard_map/ppermute | solution.py:243
  72.9 11.3 %collective-permute-done.1.refs_4_ = bf16[384,2048]{1,0:T(8,128)(2,1)S(1)} collective-permute-done((bf16[384,2048]{1,0:T(8,128)(2,1)}, bf16[384,2048]{1,0:T(8,128)(2,1)S(1)}, u32[]{:S(2)}, u32[]{:S(2)}) %collective-permute-start.1) | collective-permute-done | bytes 1572896 | tf_op jit(solution)/shard_map/ppermute | solution.py:243
  84.2 1.5 collective-permute-start.7
  85.7 4.7 %all-to-all-start.1 = ((bf16[8,512,128]{2,1,0:T(8,128)(2,1)}), bf16[8,512,128]{2,1,0:T(8,128)(2,1)}, u32[]{:S(2)}, u32[]{:S(2)}) async-start(bf16[8,512,128]{2,1,0:T(8,128)(2,1)} %bitcast.24), calls=%async_computation.1 | async-start | bytes 2097152 | tf_op jit(solution)/shard_map/all_to_all | solution.py:252
  91.4 2.0 collective-permute-start.5
  94.3 1.5 collective-permute-start.6
  95.8 9.5 %pack_rows.1 = (bf16[1024,2048]{1,0:T(8,128)(2,1)}, bf16[1024,2048]{1,0:T(8,128)(2,1)}) custom-call(s32[3]{0:T(128)} %pad_add_fusion.place_ref, bf16[1024,4096]{1,0:T(8,128)(2,1)} %send_in.1, bf16[1024,4096]{1,0:T(8,128)(2,1)} %send_in.1), custom_call_target="tpu_custom_call" | custom-call | bytes 16777216 | tf_op jit(solution)/shard_map/pack_rows/pallas_call | solution.py:64
  105.8 13.7 %collective-permute-done.5.refs_6_ = bf16[384,1024]{1,0:T(8,128)(2,1)} collective-permute-done((bf16[384,1024]{1,0:T(8,128)(2,1)}, bf16[384,1024]{1,0:T(8,128)(2,1)}, u32[]{:S(2)}, u32[]{:S(2)}) %collective-permute-start.5) | collective-permute-done | bytes 786464 | tf_op jit(solution)/shard_map/ppermute | solution.py:243
  119.5 5.7 %collective-permute-done.6.refs_8_ = bf16[384,1024]{1,0:T(8,128)(2,1)} collective-permute-done((bf16[384,1024]{1,0:T(8,128)(2,1)}, bf16[384,1024]{1,0:T(8,128)(2,1)}, u32[]{:S(2)}, u32[]{:S(2)}) %collective-permute-start.6) | collective-permute-done | bytes 786464 | tf_op jit(solution)/shard_map/ppermute | solution.py:243
  125.2 5.5 %collective-permute-done.7.refs_10_ = bf16[4096,256]{1,0:T(8,128)(2,1)} collective-permute-done((bf16[4096,256]{1,0:T(8,128)(2,1)}, bf16[4096,256]{1,0:T(8,128)(2,1)}, u32[]{:S(2)}, u32[]{:S(2)}) %collective-permute-start.7) | collective-permute-done | bytes 2097184 | tf_op jit(solution)/shard_map/ppermute | solution.py:246
  131.3 1.5 collective-permute-start.10
  133.4 1.1 collective-permute-done.9.refs_9_
  134.5 11.7 %project.3 = (bf16[4,384,128]{2,1,0:T(8,128)(2,1)}, bf16[4,384,128]{2,1,0:T(8,128)(2,1)}, f32[128,128]{1,0:T(8,128)}) custom-call(s32[3]{0:T(128)} %pad_add_fusion.place_ref, bf16[384,2048]{1,0:T(8,128)(2,1)} %refs_0_.11, bf16[384,2048]{1,0:T(8,128)(2,1)} %collective-permute-done.refs_1_, bf16[384,2048]{1,0:T(8,128)(2,1)} %copy-done, ...), custom_call_target="tpu_custom_call" | custom-call | flops 3221225472 | bytes 12582912 | tf_op jit(solution)/shard_map/project/pallas_call | solution.py:142
  146.2 4.4 %collective-permute-start.17 = (f32[128,128]{1,0:T(8,128)}, f32[128,128]{1,0:T(8,128)S(1)}, u32[]{:S(2)}, u32[]{:S(2)}) collective-permute-start(f32[128,128]{1,0:T(8,128)} %get-tuple-element.36), channel_id=1, source_target_pairs={{0,8},{2,10},{4,12},{6,14},{1,9},{3,11},{5,13},{7,15},{16,24},{18,... | collective-permute-start | bytes 196616 | tf_op jit(solution)/shard_map/ppermute | solution.py:223
  150.6 11.7 %project.2 = (bf16[4,384,128]{2,1,0:T(8,128)(2,1)}, bf16[4,384,128]{2,1,0:T(8,128)(2,1)}, f32[128,128]{1,0:T(8,128)}) custom-call(s32[3]{0:T(128)} %pad_add_fusion.place_ref, bf16[384,2048]{1,0:T(8,128)(2,1)} %refs_0_.11, bf16[384,2048]{1,0:T(8,128)(2,1)} %collective-permute-done.refs_1_, bf16[384,2048]{1,0:T(8,128)(2,1)} %copy-done, ...), custom_call_target="tpu_custom_call" | custom-call | flops 3221225472 | bytes 12582912 | tf_op jit(solution)/shard_map/project/pallas_call | solution.py:142
  162.3 1.5 collective-permute-start.11
  164.4 13.2 %finish.3 = bf16[4,384,128]{2,1,0:T(8,128)(2,1)} custom-call(s32[3]{0:T(128)} %pad_add_fusion.place_ref, bf16[384,2048]{1,0:T(8,128)(2,1)} %refs_0_.11, bf16[384,2048]{1,0:T(8,128)(2,1)} %collective-permute-done.refs_1_, bf16[384,2048]{1,0:T(8,128)(2,1)} %copy-done, bf16[384,2048]{1,0:T(8,128)(2,1)} %collective-permute-done.3.refs_3_, ...), custom_call_target="tpu_custom_call" | custom-call | flops 1610612736 | bytes 12582912 | tf_op jit(solution)/shard_map/finish/pallas_call | solution.py:182
  177.6 1.1 slice_bitcast_fusion.3
  178.7 1.4 collective-permute-start.20
  180.1 1.5 collective-permute-start.19
  183.3 13.2 %finish.2 = bf16[4,384,128]{2,1,0:T(8,128)(2,1)} custom-call(s32[3]{0:T(128)} %pad_add_fusion.place_ref, bf16[384,2048]{1,0:T(8,128)(2,1)} %refs_0_.11, bf16[384,2048]{1,0:T(8,128)(2,1)} %collective-permute-done.refs_1_, bf16[384,2048]{1,0:T(8,128)(2,1)} %copy-done, bf16[384,2048]{1,0:T(8,128)(2,1)} %collective-permute-done.3.refs_3_, ...), custom_call_target="tpu_custom_call" | custom-call | flops 1610612736 | bytes 12582912 | tf_op jit(solution)/shard_map/finish/pallas_call | solution.py:182
  196.5 1.1 slice_bitcast_fusion.7
  197.6 1.4 collective-permute-start.14
  199.0 1.5 collective-permute-start.13
  201.3 2.2 %collective-permute-done.14 = bf16[384,128]{1,0:T(8,128)(2,1)S(1)} collective-permute-done((bf16[384,128]{1,0:T(8,128)(2,1)S(1)}, bf16[384,128]{1,0:T(8,128)(2,1)S(1)}, u32[]{:S(2)}, u32[]{:S(2)}) %collective-permute-start.14) | collective-permute-done | bytes 98336 | tf_op jit(solution)/shard_map/ppermute | solution.py:243
  206.1 5.8 %add_features.2.refs_4_ = f32[384,2048]{1,0:T(8,128)} custom-call(bf16[384,512]{1,0:T(8,128)(2,1)} %copy-done.2, bf16[384,512]{1,0:T(8,128)(2,1)} %copy-done.5, bf16[1024,2048]{1,0:T(8,128)(2,1)} %get-tuple-element.32.refs_2_, bf16[1024,2048]{1,0:T(8,128)(2,1)} %collective-permute-done.16.refs_3_), custom_call_target="tpu_custom_call" | custom-call | flops 1610612736 | bytes 7340032 | tf_op jit(solution)/shard_map/add_features/pallas_call | solution.py:207
  212.7 6.3 %add_features.3 = bf16[384,2048]{1,0:T(8,128)(2,1)} custom-call(bf16[384,512]{1,0:T(8,128)(2,1)} %copy-done.3, bf16[384,512]{1,0:T(8,128)(2,1)} %copy-done.6, bf16[1024,2048]{1,0:T(8,128)(2,1)} %get-tuple-element.32.refs_2_, bf16[1024,2048]{1,0:T(8,128)(2,1)} %collective-permute-done.16.refs_3_, f32[384,2048]{1,0:T(8,128)} %add_features.2.refs_4_), custom_call_target="tpu_custom_call" | custom-call | flops 1610612736 | bytes 7340032 | tf_op jit(solution)/shard_map/add_features/pallas_call | solution.py:207
  (50 shorter events, 10.4 us)
Async XLA Ops:
  7.1 77.1 %all-to-all-start = ((bf16[8,512,256]{2,1,0:T(8,128)(2,1)}), bf16[8,512,256]{2,1,0:T(8,128)(2,1)}, u32[]{:S(2)}, u32[]{:S(2)}) async-start(bf16[8,512,256]{2,1,0:T(8,128)(2,1)} %bitcast.23), calls=%async_computation | async-start | bytes 4194304 | tf_op jit(solution)/shard_map/all_to_all | solution.py:252
  14.4 58.5 %collective-permute-start.2 = (bf16[384,2048]{1,0:T(8,128)(2,1)}, bf16[384,2048]{1,0:T(8,128)(2,1)S(1)}, u32[]{:S(2)}, u32[]{:S(2)}) collective-permute-start(bf16[384,2048]{1,0:T(8,128)(2,1)} %refs_0_.11), channel_id=1, source_target_pairs={{0,2},{2,0},{4,6},{6,4},{8,10},{10,8},{12,14},{14,12},{1,3},{3,1},... | collective-permute-start | bytes 4718600 | tf_op jit(solution)/shard_map/ppermute | solution.py:243
  16.4 67.8 %collective-permute-start.1 = (bf16[384,2048]{1,0:T(8,128)(2,1)}, bf16[384,2048]{1,0:T(8,128)(2,1)S(1)}, u32[]{:S(2)}, u32[]{:S(2)}) collective-permute-start(bf16[384,2048]{1,0:T(8,128)(2,1)} %refs_0_.11), channel_id=1, source_target_pairs={{0,4},{2,6},{4,0},{6,2},{8,12},{10,14},{12,8},{14,10},{1,5},{3,7},... | collective-permute-start | bytes 4718600 | tf_op jit(solution)/shard_map/ppermute | solution.py:243
  72.9 46.6 %copy-start = (bf16[384,2048]{1,0:T(8,128)(2,1)}, bf16[384,2048]{1,0:T(8,128)(2,1)S(1)}, u32[]{:S(2)}) copy-start(bf16[384,2048]{1,0:T(8,128)(2,1)S(1)} %collective-permute-done.2.refs_2_) | copy-start | bytes 4718596
  84.2 41.0 %copy-start.1 = (bf16[384,2048]{1,0:T(8,128)(2,1)}, bf16[384,2048]{1,0:T(8,128)(2,1)S(1)}, u32[]{:S(2)}) copy-start(bf16[384,2048]{1,0:T(8,128)(2,1)S(1)} %collective-permute-done.1.refs_4_) | copy-start | bytes 4718596
  84.2 46.5 %collective-permute-start.7 = (bf16[4096,256]{1,0:T(8,128)(2,1)}, bf16[4096,256]{1,0:T(8,128)(2,1)}, u32[]{:S(2)}, u32[]{:S(2)}) collective-permute-start(bf16[4096,256]{1,0:T(8,128)(2,1)} %bitcast.4.refs_10_), channel_id=1, source_target_pairs={{0,16},{16,0},{1,17},{17,1},{2,18},{18,2},{3,19},{19,3},{4,20},{20... | collective-permute-start | bytes 6291464 | tf_op jit(solution)/shard_map/ppermute | solution.py:246
  85.7 39.5 %all-to-all-start.1 = ((bf16[8,512,128]{2,1,0:T(8,128)(2,1)}), bf16[8,512,128]{2,1,0:T(8,128)(2,1)}, u32[]{:S(2)}, u32[]{:S(2)}) async-start(bf16[8,512,128]{2,1,0:T(8,128)(2,1)} %bitcast.24), calls=%async_computation.1 | async-start | bytes 2097152 | tf_op jit(solution)/shard_map/all_to_all | solution.py:252
  91.4 28.2 %collective-permute-start.5 = (bf16[384,1024]{1,0:T(8,128)(2,1)}, bf16[384,1024]{1,0:T(8,128)(2,1)}, u32[]{:S(2)}, u32[]{:S(2)}) collective-permute-start(bf16[384,1024]{1,0:T(8,128)(2,1)} %slice.30), channel_id=1, source_target_pairs={{0,2},{2,0},{4,6},{6,4},{8,10},{10,8},{12,14},{14,12},{1,3},{3,1},... | collective-permute-start | bytes 2359304 | tf_op jit(solution)/shard_map/ppermute | solution.py:243
  94.3 30.9 %collective-permute-start.6 = (bf16[384,1024]{1,0:T(8,128)(2,1)}, bf16[384,1024]{1,0:T(8,128)(2,1)}, u32[]{:S(2)}, u32[]{:S(2)}) collective-permute-start(bf16[384,1024]{1,0:T(8,128)(2,1)} %slice.31), channel_id=1, source_target_pairs={{0,4},{2,6},{4,0},{6,2},{8,12},{10,14},{12,8},{14,10},{1,5},{3,7},... | collective-permute-start | bytes 2359304 | tf_op jit(solution)/shard_map/ppermute | solution.py:243
  95.8 35.0 %collective-permute-start = (bf16[384,2048]{1,0:T(8,128)(2,1)}, bf16[384,2048]{1,0:T(8,128)(2,1)}, u32[]{:S(2)}, u32[]{:S(2)}) collective-permute-start(bf16[384,2048]{1,0:T(8,128)(2,1)} %refs_0_.11), channel_id=1, source_target_pairs={{0,1},{1,0},{2,3},{3,2},{4,5},{5,4},{6,7},{7,6},{8,9},{9,8},{10,11... | collective-permute-start | bytes 4718600 | tf_op jit(solution)/shard_map/ppermute | solution.py:249
  105.3 100.0 %collective-permute-start.16 = (bf16[1024,2048]{1,0:T(8,128)(2,1)}, bf16[1024,2048]{1,0:T(8,128)(2,1)}, u32[]{:S(2)}, u32[]{:S(2)}) collective-permute-start(bf16[1024,2048]{1,0:T(8,128)(2,1)} %get-tuple-element.33), channel_id=1, source_target_pairs={{0,1},{1,0},{2,3},{3,2},{4,5},{5,4},{6,7},{7,6},{8,9},{9,8},{10,11... | collective-permute-start | bytes 12582920 | tf_op jit(solution)/shard_map/ppermute | solution.py:249
  119.5 11.7 %collective-permute-start.3 = (bf16[384,2048]{1,0:T(8,128)(2,1)S(1)}, bf16[384,2048]{1,0:T(8,128)(2,1)}, u32[]{:S(2)}, u32[]{:S(2)}) collective-permute-start(bf16[384,2048]{1,0:T(8,128)(2,1)S(1)} %collective-permute-done.2.refs_2_), channel_id=1, source_target_pairs={{0,1},{1,0},{2,3},{3,2},{4,5},{5,4},{6,7},{7,6},{8,9},{9,8},{10,11... | collective-permute-start | bytes 4718600 | tf_op jit(solution)/shard_map/ppermute | solution.py:249
  125.2 7.6 %collective-permute-start.4 = (bf16[384,2048]{1,0:T(8,128)(2,1)S(1)}, bf16[384,2048]{1,0:T(8,128)(2,1)}, u32[]{:S(2)}, u32[]{:S(2)}) collective-permute-start(bf16[384,2048]{1,0:T(8,128)(2,1)S(1)} %collective-permute-done.1.refs_4_), channel_id=1, source_target_pairs={{0,1},{1,0},{2,3},{3,2},{4,5},{5,4},{6,7},{7,6},{8,9},{9,8},{10,11... | collective-permute-start | bytes 4718600 | tf_op jit(solution)/shard_map/ppermute | solution.py:249
  130.7 2.6 %collective-permute-start.8 = (bf16[384,1024]{1,0:T(8,128)(2,1)}, bf16[384,1024]{1,0:T(8,128)(2,1)}, u32[]{:S(2)}, u32[]{:S(2)}) collective-permute-start(bf16[384,1024]{1,0:T(8,128)(2,1)} %collective-permute-done.5.refs_6_), channel_id=1, source_target_pairs={{0,1},{1,0},{2,3},{3,2},{4,5},{5,4},{6,7},{7,6},{8,9},{9,8},{10,11... | collective-permute-start | bytes 2359304 | tf_op jit(solution)/shard_map/ppermute | solution.py:249
  130.7 3.7 %collective-permute-start.9 = (bf16[384,1024]{1,0:T(8,128)(2,1)}, bf16[384,1024]{1,0:T(8,128)(2,1)}, u32[]{:S(2)}, u32[]{:S(2)}) collective-permute-start(bf16[384,1024]{1,0:T(8,128)(2,1)} %collective-permute-done.6.refs_8_), channel_id=1, source_target_pairs={{0,1},{1,0},{2,3},{3,2},{4,5},{5,4},{6,7},{7,6},{8,9},{9,8},{10,11... | collective-permute-start | bytes 2359304 | tf_op jit(solution)/shard_map/ppermute | solution.py:249
  131.3 51.0 %collective-permute-start.10 = (bf16[4096,128]{1,0:T(8,128)(2,1)}, bf16[4096,128]{1,0:T(8,128)(2,1)S(1)}, u32[]{:S(2)}, u32[]{:S(2)}) collective-permute-start(bf16[4096,128]{1,0:T(8,128)(2,1)} %bitcast.6.refs_10_), channel_id=1, source_target_pairs={{0,16},{16,0},{1,17},{17,1},{2,18},{18,2},{3,19},{19,3},{4,20},{20... | collective-permute-start | bytes 3145736 | tf_op jit(solution)/shard_map/ppermute | solution.py:246
  146.2 17.6 %collective-permute-start.17 = (f32[128,128]{1,0:T(8,128)}, f32[128,128]{1,0:T(8,128)S(1)}, u32[]{:S(2)}, u32[]{:S(2)}) collective-permute-start(f32[128,128]{1,0:T(8,128)} %get-tuple-element.36), channel_id=1, source_target_pairs={{0,8},{2,10},{4,12},{6,14},{1,9},{3,11},{5,13},{7,15},{16,24},{18,... | collective-permute-start | bytes 196616 | tf_op jit(solution)/shard_map/ppermute | solution.py:223
  162.3 19.4 %collective-permute-start.11 = (f32[128,128]{1,0:T(8,128)}, f32[128,128]{1,0:T(8,128)S(1)}, u32[]{:S(2)}, u32[]{:S(2)}) collective-permute-start(f32[128,128]{1,0:T(8,128)} %get-tuple-element.31), channel_id=1, source_target_pairs={{0,8},{2,10},{4,12},{6,14},{1,9},{3,11},{5,13},{7,15},{16,24},{18,... | collective-permute-start | bytes 196616 | tf_op jit(solution)/shard_map/ppermute | solution.py:223
  163.8 0.6 copy-start.8
  178.7 20.3 %collective-permute-start.20 = (bf16[384,128]{1,0:T(8,128)(2,1)S(1)}, bf16[384,128]{1,0:T(8,128)(2,1)S(1)}, u32[]{:S(2)}, u32[]{:S(2)}) collective-permute-start(bf16[384,128]{1,0:T(8,128)(2,1)S(1)} %get-tuple-element.38), channel_id=1, source_target_pairs={{0,6},{2,4},{4,2},{6,0},{8,14},{10,12},{12,10},{14,8},{1,7},{3,5},... | collective-permute-start | bytes 294920 | tf_op jit(solution)/shard_map/ppermute | solution.py:243
  180.1 20.4 %collective-permute-start.19 = (bf16[384,128]{1,0:T(8,128)(2,1)S(1)}, bf16[384,128]{1,0:T(8,128)(2,1)S(1)}, u32[]{:S(2)}, u32[]{:S(2)}) collective-permute-start(bf16[384,128]{1,0:T(8,128)(2,1)S(1)} %get-tuple-element.39), channel_id=1, source_target_pairs={{0,4},{2,6},{4,0},{6,2},{8,12},{10,14},{12,8},{14,10},{1,5},{3,7},... | collective-permute-start | bytes 294920 | tf_op jit(solution)/shard_map/ppermute | solution.py:243
  181.7 19.5 %collective-permute-start.18 = (bf16[384,128]{1,0:T(8,128)(2,1)S(1)}, bf16[384,128]{1,0:T(8,128)(2,1)S(1)}, u32[]{:S(2)}, u32[]{:S(2)}) collective-permute-start(bf16[384,128]{1,0:T(8,128)(2,1)S(1)} %get-tuple-element.40), channel_id=1, source_target_pairs={{0,2},{2,0},{4,6},{6,4},{8,10},{10,8},{12,14},{14,12},{1,3},{3,1},... | collective-permute-start | bytes 294920 | tf_op jit(solution)/shard_map/ppermute | solution.py:243
  182.3 1.0 copy-start.4
  197.6 5.9 %collective-permute-start.14 = (bf16[384,128]{1,0:T(8,128)(2,1)S(1)}, bf16[384,128]{1,0:T(8,128)(2,1)S(1)}, u32[]{:S(2)}, u32[]{:S(2)}) collective-permute-start(bf16[384,128]{1,0:T(8,128)(2,1)S(1)} %get-tuple-element.42), channel_id=1, source_target_pairs={{0,6},{2,4},{4,2},{6,0},{8,14},{10,12},{12,10},{14,8},{1,7},{3,5},... | collective-permute-start | bytes 294920 | tf_op jit(solution)/shard_map/ppermute | solution.py:243
  199.0 5.3 %collective-permute-start.13 = (bf16[384,128]{1,0:T(8,128)(2,1)S(1)}, bf16[384,128]{1,0:T(8,128)(2,1)S(1)}, u32[]{:S(2)}, u32[]{:S(2)}) collective-permute-start(bf16[384,128]{1,0:T(8,128)(2,1)S(1)} %get-tuple-element.43), channel_id=1, source_target_pairs={{0,4},{2,6},{4,0},{6,2},{8,12},{10,14},{12,8},{14,10},{1,5},{3,7},... | collective-permute-start | bytes 294920 | tf_op jit(solution)/shard_map/ppermute | solution.py:243
  200.6 4.6 %collective-permute-start.12 = (bf16[384,128]{1,0:T(8,128)(2,1)S(1)}, bf16[384,128]{1,0:T(8,128)(2,1)S(1)}, u32[]{:S(2)}, u32[]{:S(2)}) collective-permute-start(bf16[384,128]{1,0:T(8,128)(2,1)S(1)} %get-tuple-element.44), channel_id=1, source_target_pairs={{0,2},{2,0},{4,6},{6,4},{8,10},{10,8},{12,14},{14,12},{1,3},{3,1},... | collective-permute-start | bytes 294920 | tf_op jit(solution)/shard_map/ppermute | solution.py:243
  201.2 4.1 %copy-start.2 = (bf16[384,512]{1,0:T(8,128)(2,1)}, bf16[384,512]{1,0:T(8,128)(2,1)S(1)}, u32[]{:S(2)}) copy-start(bf16[384,512]{1,0:T(8,128)(2,1)S(1)} %pad_maximum_fusion.1.refs_0_) | copy-start | bytes 1179652
  201.2 4.1 %collective-permute-start.21 = (bf16[384,512]{1,0:T(8,128)(2,1)S(1)}, bf16[384,512]{1,0:T(8,128)(2,1)S(1)}, u32[]{:S(2)}, u32[]{:S(2)}) collective-permute-start(bf16[384,512]{1,0:T(8,128)(2,1)S(1)} %pad_maximum_fusion.1.refs_0_), channel_id=1, source_target_pairs={{0,1},{1,0},{2,3},{3,2},{4,5},{5,4},{6,7},{7,6},{8,9},{9,8},{10,11... | collective-permute-start | bytes 1179656 | tf_op jit(solution)/shard_map/ppermute | solution.py:249
  205.2 6.7 %copy-start.3 = (bf16[384,512]{1,0:T(8,128)(2,1)}, bf16[384,512]{1,0:T(8,128)(2,1)S(1)}, u32[]{:S(2)}) copy-start(bf16[384,512]{1,0:T(8,128)(2,1)S(1)} %pad_maximum_fusion.refs_0_) | copy-start | bytes 1179652
  205.2 6.7 %collective-permute-start.15 = (bf16[384,512]{1,0:T(8,128)(2,1)S(1)}, bf16[384,512]{1,0:T(8,128)(2,1)S(1)}, u32[]{:S(2)}, u32[]{:S(2)}) collective-permute-start(bf16[384,512]{1,0:T(8,128)(2,1)S(1)} %pad_maximum_fusion.refs_0_), channel_id=1, source_target_pairs={{0,1},{1,0},{2,3},{3,2},{4,5},{5,4},{6,7},{7,6},{8,9},{9,8},{10,11... | collective-permute-start | bytes 1179656 | tf_op jit(solution)/shard_map/ppermute | solution.py:249
  205.3 0.8 copy-start.5
  211.9 0.8 copy-start.6
  (1 other events, 0.6 us)

commit v3 on v1

v3 whole, which is shorter than its diff:
```python
import jax
import jax.numpy as jnp
from jax import lax
from jax.experimental import pallas as pl
from jax.experimental.pallas import tpu as pltpu
from jax.sharding import PartitionSpec as P

HDIM = 128
SUB = 4
F32 = jnp.float32
BF16 = jnp.bfloat16
MIB = 1 << 20
LIMIT = 8
ANY = pl.BlockSpec(memory_space=pl.ANY)
VMEM = pl.BlockSpec(memory_space=pltpu.VMEM)
SMEM = pl.BlockSpec(memory_space=pltpu.SMEM)


def dot(a, b, contract=((1,), (0,))):
    return lax.dot_general(a, b, (contract, ((), ())), preferred_element_type=F32)


def silu(u):
    return u / (1.0 + jnp.exp(-u))


def call(kernel, name, out_shape, in_specs, out_specs, limit, flops, moved, scratch=()):
    return pl.pallas_call(
        kernel,
        out_shape=out_shape,
        in_specs=in_specs,
        out_specs=out_specs,
        scratch_shapes=list(scratch),
        compiler_params=pltpu.CompilerParams(vmem_limit_bytes=limit * MIB),
        cost_estimate=pl.CostEstimate(flops=int(flops), bytes_accessed=int(moved), transcendentals=0),
        name=name,
    )


def pack_keys_values(place, w_key, w_value, count):
    depth = w_key.shape[0]

    def kernel(place_ref, key_ref, value_ref, out):
        for j in range(SUB):
            start = pl.multiple_of((2 * j + place_ref[1]) * HDIM, HDIM)
            key = key_ref[:, pl.ds(start, HDIM)]
            value = value_ref[:, pl.ds(start, HDIM)]
            for i in range(j, count, SUB):
                out[i * depth : (i + 1) * depth, :HDIM] = key
                out[i * depth : (i + 1) * depth, HDIM:] = value

    shape = jax.ShapeDtypeStruct((count * depth, 2 * HDIM), BF16)
    moved = count * depth * 2 * HDIM * 4
    return call(kernel, "pack_keys_values", shape, [SMEM, VMEM, VMEM], VMEM, LIMIT, 0, moved)(place, w_key, w_value)


def pack_queries(place, w_query):
    depth = w_query.shape[0]

    def kernel(place_ref, query_ref, *outs):
        for r, out in enumerate(outs):
            start = pl.multiple_of(jnp.bitwise_xor(place_ref[0], r) * 2 * HDIM, 2 * HDIM)
            out[...] = query_ref[:, pl.ds(start, 2 * HDIM)]

    shapes = [jax.ShapeDtypeStruct((depth, 2 * HDIM), BF16)] * SUB
    moved = SUB * depth * 2 * HDIM * 4
    return call(kernel, "pack_queries", shapes, [SMEM, VMEM], [VMEM] * SUB, LIMIT, 0, moved)(place, w_query)


def take_rows(place, w_out):
    rows, width = w_out.shape
    half = width // 2
    return lax.dynamic_slice(w_out, (0, (1 - place[2]) * half), (rows, half))


def stage_rows(place, w_out, w_far):
    rows, half = w_far.shape
    depth = rows // SUB

    def kernel(place_ref, out_ref, far_ref, keep, far, sems):
        column = pl.multiple_of(place_ref[2] * half, half)
        copies = []
        for r in range(SUB):
            row = pl.multiple_of(jnp.bitwise_xor(place_ref[0], r) * depth, depth)
            copies.append(
                pltpu.make_async_copy(out_ref.at[pl.ds(row, depth), pl.ds(column, half)], keep.at[r], sems.at[r])
            )
            copies.append(pltpu.make_async_copy(far_ref.at[pl.ds(row, depth), :], far.at[r], sems.at[SUB + r]))
        for copy in copies:
            copy.start()
        for copy in copies:
            copy.wait()

    shapes = [pltpu.VMEM((SUB, depth, half), BF16)] * 2
    sems = pltpu.SemaphoreType.DMA((2 * SUB,))
    return call(kernel, "stage_rows", shapes, [SMEM, ANY, ANY], [VMEM] * 2, 40, 0, rows * half * 8, [sems])(
        place, w_out, w_far
    )


def stage(pieces, rows, width):
    count = len(pieces)

    def kernel(*refs):
        out, sems = refs[count], refs[count + 1]
        copies = [
            pltpu.make_async_copy(ref, out.at[r, :, pl.ds(column, array.shape[1])], sems.at[i])
            for i, ((array, r, column), ref) in enumerate(zip(pieces, refs))
        ]
        for copy in copies:
            copy.start()
        for copy in copies:
            copy.wait()

    shape = pltpu.VMEM((SUB, rows, width), BF16)
    sems = pltpu.SemaphoreType.DMA((count,))
    return call(kernel, "stage", shape, [ANY] * count, VMEM, LIMIT, 0, SUB * rows * width * 4, [sems])(
        *[array for array, _, _ in pieces]
    )


def by_halves(place_ref, stream_ref, r, w_ref):
    half = w_ref.shape[0] // 2
    own = pl.multiple_of(place_ref[2] * half, half)
    far = pl.multiple_of((1 - place_ref[2]) * half, half)
    return dot(stream_ref[r, :, :half], w_ref[pl.ds(own, half), :]) + dot(
        stream_ref[r, :, half:], w_ref[pl.ds(far, half), :]
    )


def project(place, stream, kv):
    _, rows, width = stream.shape

    def kernel(place_ref, stream_ref, w_ref, key_ref, value_ref, before_ref, total_ref):
        states = []
        for r in range(SUB):
            both = by_halves(place_ref, stream_ref, r, w_ref)
            key = silu(both[:, :HDIM]).astype(BF16)
            value = both[:, HDIM:].astype(BF16)
            key_ref[r] = key
            value_ref[r] = value
            states.append(dot(key, value, ((0,), (0,))))
        total_ref[...] = (states[0] + states[1]) + (states[2] + states[3])
        block = place_ref[0]
        for r in range(SUB):
            before = jnp.zeros((HDIM, HDIM), F32)
            for other in range(SUB):
                if other != r:
                    is_before = jnp.bitwise_xor(block, other) < jnp.bitwise_xor(block, r)
                    before = before + jnp.where(is_before, states[other], 0.0)
            before_ref[r] = before

    shape = jax.ShapeDtypeStruct((SUB, rows, HDIM), BF16)
    shapes = [shape, shape, jax.ShapeDtypeStruct((SUB, HDIM, HDIM), F32), jax.ShapeDtypeStruct((HDIM, HDIM), F32)]
    flops = 4 * SUB * rows * width * HDIM
    return call(kernel, "project", shapes, [SMEM, VMEM, VMEM], [VMEM] * 4, LIMIT, flops, 2 * MIB)(place, stream, kv)


def queries(place, stream, pieces):
    _, rows, width = stream.shape
    count = len(pieces)
    depth = pieces[0].shape[0]
    half = width // 2

    def kernel(place_ref, stream_ref, *refs):
        ins, out, w_held = refs[:count], refs[count], refs[count + 1]
        for m, piece in enumerate(ins):
            row = jnp.bitwise_xor(place_ref[3], m) * depth
            far = jnp.where(row >= half, 1, 0) != place_ref[2]
            row = pl.multiple_of(lax.rem(row, half) + jnp.where(far, half, 0), depth)
            w_held[pl.ds(row, depth), :] = piece[...]
        swap = place_ref[1] == 1
        for r in range(SUB):
            both = silu(dot(stream_ref[r], w_held[...])).astype(BF16)
            out[r, :, :HDIM] = jnp.where(swap, both[:, HDIM:], both[:, :HDIM])
            out[r, :, HDIM:] = jnp.where(swap, both[:, :HDIM], both[:, HDIM:])

    shape = jax.ShapeDtypeStruct((SUB, rows, 2 * HDIM), BF16)
    flops = 4 * SUB * rows * width * HDIM
    held = pltpu.VMEM((width, 2 * HDIM), BF16)
    return call(
        kernel, "queries", shape, [SMEM, VMEM] + [VMEM] * count, VMEM, LIMIT, flops, 2 * MIB, [held]
    )(place, stream, *pieces)


def attend(place, blocks, query, parts):
    rows = query.shape[1]
    count = len(blocks)

    def kernel(place_ref, query_ref, *refs):
        ins, outs = refs[:8], refs[8:]
        causal = lax.broadcasted_iota(jnp.int32, (rows, rows), 1) <= lax.broadcasted_iota(
            jnp.int32, (rows, rows), 0
        )
        for i, r in enumerate(blocks):
            for h in range(2):
                key_ref, value_ref, before_ref, carried_ref = ins[4 * h : 4 * h + 4]
                columns = slice(h * HDIM, (h + 1) * HDIM)
                q = query_ref[r, :, columns]
                earlier = (before_ref[r] + carried_ref[...]).astype(BF16)
                scores = dot(q, key_ref[r], ((1,), (1,)))
                weights = jnp.where(causal, scores, 0.0).astype(BF16)
                mixed = dot(weights, value_ref[r]) + dot(q, earlier)
                scale = lax.rsqrt(jnp.mean(mixed * mixed, axis=-1, keepdims=True) + 1e-06)
                target = pl.multiple_of(jnp.bitwise_xor(place_ref[1], h) * HDIM, HDIM)
                outs[i][:, pl.ds(target, HDIM)] = (mixed * scale).astype(BF16)

    shapes = [jax.ShapeDtypeStruct((rows, 2 * HDIM), BF16)] * count
    flops = count * 4 * rows * HDIM * (2 * rows + HDIM)
    return call(kernel, "attend", shapes, [SMEM] + [VMEM] * 9, [VMEM] * count, LIMIT, flops, 2 * MIB)(
        place, query, *parts[0], *parts[1]
    )


def add_features(pieces, weight, partial=None):
    rows, depth = pieces[0].shape
    width = weight.shape[2]
    count = len(pieces)
    tile = min(512, width)

    def kernel(*refs):
        w_ref, out = refs[count], refs[-1]
        for start in range(0, width, tile):
            columns = slice(start, start + tile)
            total = refs[count + 1][:, columns] if partial is not None else jnp.zeros((rows, tile), F32)
            for i in range(count):
                total = total + dot(refs[i][...], w_ref[i, :, columns])
            out[:, columns] = total.astype(out.dtype)

    shape = pltpu.VMEM((rows, width), F32) if partial is None else jax.ShapeDtypeStruct((rows, width), BF16)
    args = [*pieces, weight] + ([] if partial is None else [partial])
    flops = 2 * count * depth * rows * width
    return call(kernel, "add_features", shape, [VMEM] * len(args), VMEM, LIMIT, flops, 8 * MIB)(*args)


def exclusive_prefix(value, groups):
    def shift(v, step):
        pairs = [(g * SUB + j, (g + step) * SUB + j) for g in range(groups - step) for j in range(SUB)]
        return lax.ppermute(v, "ctx", pairs)

    if groups == 1:
        return jnp.zeros_like(value)
    total = shift(value, 1)
    step = 1
    while step < groups - 1:
        total = total + shift(total, step)
        step *= 2
    return total


def local(tokens, w_query, w_key, w_value, w_out):
    n_ctx = lax.axis_size("ctx")
    groups = n_ctx // SUB
    rows, half = tokens.shape
    ctx = lax.axis_index("ctx")
    place = jnp.stack([ctx % SUB, lax.axis_index("groups"), lax.axis_index("head"), ctx]).astype(jnp.int32)

    def xor(value, step):
        return lax.ppermute(value, "ctx", [(i, i ^ step) for i in range(n_ctx)])

    def other_part(value):
        return lax.ppermute(value, "groups", [(0, 1), (1, 0)])

    def other_core(value):
        return lax.ppermute(value, "head", [(0, 1), (1, 0)])

    def spread(packed):
        return lax.all_to_all(packed, "ctx", 0, 0, tiled=True)

    def gather_queries(sent):
        block = ctx % SUB
        ordered = [lax.dynamic_index_in_dim(jnp.stack(sent), block ^ j, keepdims=False) for j in range(SUB)]
        whole = spread(jnp.concatenate(ordered * groups, axis=0)).reshape(n_ctx, -1, 2 * HDIM)
        return [lax.dynamic_index_in_dim(whole, ctx ^ m, keepdims=False) for m in range(n_ctx)]

    across = xor(tokens, 2)
    beside = xor(tokens, 1)
    kv_mine = spread(pack_keys_values(place, w_key, w_value, n_ctx))
    q_sent = pack_queries(place, w_query)
    across, beside, kv_mine, q_sent = lax.optimization_barrier((across, beside, kv_mine, q_sent))
    cut = half * 11 // 16 // HDIM * HDIM
    left = xor(across[:, :cut], 1)
    right = xor(beside[:, cut:], 2)
    kv_other = other_part(kv_mine)
    arrived = {m: xor(q_sent[m % SUB], m) for m in (4, 6, 5, 7, 2, 3, 1)} if n_ctx == 2 * SUB else {}
    if arrived:
        q_pieces = [q_sent[0]] + [arrived[m] for m in range(1, n_ctx)]
    else:
        q_pieces = gather_queries(q_sent)

    w_far = other_core(take_rows(place, w_out))

    pieces = []
    for array, r, column in ((tokens, 0, 0), (beside, 1, 0), (across, 2, 0), (left, 3, 0), (right, 3, cut)):
        pieces += [(array, r, column), (other_core(array), r, half + column)]
    stream = stage(pieces, rows, 2 * half)

    def keys_values(kv):
        key, value, before, total = project(place, stream, kv)
        return key, value, before, exclusive_prefix(total, groups)

    parts = [keys_values(kv_mine), keys_values(kv_other)]
    query = queries(place, stream, q_pieces)
    away = attend(place, (3, 1, 2), query, parts)
    home = attend(place, (0,), query, parts)
    normed = [home[0], xor(away[1], 1), xor(away[2], 2), xor(away[0], 3)]
    home_0, w_far = lax.optimization_barrier((home[0], w_far))
    out_keep, out_far = stage_rows(place, w_out, w_far)
    out_keep, out_far, *normed = lax.optimization_barrier((out_keep, out_far, home_0, *normed[1:]))
    partial = add_features(normed, out_keep)
    return add_features([other_core(n) for n in normed], out_far, partial)


def solution(mesh):
    in_specs = (
        P(("groups", "ctx"), "head"),
        P("ctx", "head"),
        P("ctx", "head"),
        P("ctx", "head"),
        P("head", None),
    )
    out_specs = P(("groups", "ctx"), "head")
    return jax.shard_map(local, mesh=mesh, in_specs=in_specs, out_specs=out_specs, check_vma=False)
```

time: 279 us -> 194 us (0.70)
  waiting for transfers between devices: 156 us -> 111 us
  Pallas kernels: 0 us -> 37.3 us
  matrix products: 36 us -> 0 us
  local copies, waits for them, and re-layouts: 33.1 us -> 9.8 us
  between operations: 13.5 us -> 0.22 us
  other arithmetic: 4.65 us -> 0.08 us
    pallas_call x0 -> x11, Pallas kernels: none -> 37.3 us  [the longest x2 15.6 us: project(): call(kernel, 'project', shapes, [SMEM, VMEM, VMEM], [VMEM] * 4, LIMIT, fl...]
    dot_general x12 -> x0, matrix products: 36 us -> none  [the longest x6 32.1 us: dot(): return jnp.dot(a, b, preferred_element_type=F32)]
    ppermute x7 -> x14, waiting for transfers between devices: 125 us -> 101 us  [xor(): return lax.ppermute(value, 'ctx', [(i, i ^ step) for i in range(n_ctx)])]
    ppermute x2 -> x1, waiting for transfers between devices: 24.7 us -> 9.11 us  [other_part(): return lax.ppermute(value, 'groups', [(0, 1), (1, 0)])]
    dynamic_update_slice x7 -> x0, local copies, waits for them, and re-layouts: 13.8 us -> none  [the longest x4 13.7 us: local(): stream = lax.dynamic_update_slice(stream, whole, ((block ^ step) * rows, 0))]
    ppermute x7 -> x14, starting transfers between devices: 12 us -> 21.8 us  [xor(): return lax.ppermute(value, 'ctx', [(i, i ^ step) for i in range(n_ctx)])]
    broadcast_in_dim x2 -> x0, local copies, waits for them, and re-layouts: 6.54 us -> none  [the longest x1 6.47 us: local(): stream = jnp.zeros((SUB * rows, width), BF16)]
    ppermute x2, starting transfers between devices: 9.19 us -> 3.01 us  [shift(): return lax.ppermute(v, 'ctx', pairs)]
  transfers between devices with their start and end apart: 19 -> 28, of which waited for: 11 -> 9; matrix products, arithmetic and copies ran while one was open for 22% -> 4% of each run, Pallas kernels for 0% -> 17%
where the time goes in v3:
time: 194 us
  waiting for transfers between devices  111 us (57%)
  Pallas kernels  37.3 us (19%)
  starting transfers between devices  35.6 us (18%)
  local copies, waits for them, and re-layouts  9.8 us (5%)
    ppermute x14, waiting for transfers between devices, xor(): return lax.ppermute(value, 'ctx', [(i, i ^ step) for i in range(n_ctx)])  101 us
    ppermute x14, starting transfers between devices, xor(): return lax.ppermute(value, 'ctx', [(i, i ^ step) for i in range(n_ctx)])  21.8 us
    pallas_call x2, Pallas kernels, project(): call(kernel, 'project', shapes, [SMEM, VMEM, VMEM], [VMEM] * 4, LIMIT, fl...  15.6 us
    ppermute x1, waiting for transfers between devices, other_part(): return lax.ppermute(value, 'groups', [(0, 1), (1, 0)])  9.11 us
    all_to_all x1, starting transfers between devices, spread(): return lax.all_to_all(packed, 'ctx', 0, 0, tiled=True)  7.25 us
    dynamic_slice x1, local copies, waits for them, and re-layouts, take_rows(): return lax.dynamic_slice(w_out, (0, (1 - place[2]) * half), (rows, half))  4.84 us
    pallas_call x2, Pallas kernels, add_features(): call(kernel, 'add_features', shape, [VMEM] * len(args), VMEM, LIMIT, flop...  4.72 us
    pallas_call x1, Pallas kernels, queries(): call(kernel, 'queries', shape, [SMEM, VMEM] + [VMEM] * count, VMEM, LIMIT...  4.31 us
  transfers between devices with their start and end apart: 28, of which 9 were waited for; matrix products, arithmetic and copies ran while one was open for 4% of the time, Pallas kernels for 17%

profile of v3, /device:TPU:0, one launch (start us, length us, event | category | flops | bytes accessed | tf_op | source)
XLA Modules:
  0.0 193.9 jit_solution(7147741647133703651)
XLA Ops:
  2.5 2.2 %pack_keys_values.1 = bf16[4096,256]{1,0:T(8,128)(2,1)} custom-call(s32[4]{0:T(128)S(1)} %pad_add_fusion.place_ref, bf16[512,1024]{1,0:T(8,128)(2,1)S(1)} %copy-done.1, bf16[512,1024]{1,0:T(8,128)(2,1)S(1)} %copy-done.2), custom_call_target="tpu_custom_call" | custom-call | bytes 4194304 | tf_op jit(solution)/shard_map/pack_keys_values/pallas_call | solution.py:54
  4.7 7.3 %all-to-all-start = ((bf16[8,512,256]{2,1,0:T(8,128)(2,1)}), bf16[8,512,256]{2,1,0:T(8,128)(2,1)S(1)}, u32[]{:S(2)}, u32[]{:S(2)}) async-start(bf16[8,512,256]{2,1,0:T(8,128)(2,1)} %bitcast.4), calls=%async_computation | async-start | bytes 4194304 | tf_op jit(solution)/shard_map/all_to_all | solution.py:268
  12.0 2.0 %collective-permute-start.1 = (bf16[384,2048]{1,0:T(8,128)(2,1)}, bf16[384,2048]{1,0:T(8,128)(2,1)}, u32[]{:S(2)}, u32[]{:S(2)}) collective-permute-start(bf16[384,2048]{1,0:T(8,128)(2,1)} %refs_0_.1), channel_id=1, source_target_pairs={{0,4},{2,6},{4,0},{6,2},{8,12},{10,14},{12,8},{14,10},{1,5},{3,7},... | collective-permute-start | bytes 4718600 | tf_op jit(solution)/shard_map/ppermute | solution.py:259
  14.0 1.5 collective-permute-start.2
  15.5 4.8 %constant_dynamic-slice_fusion = bf16[1024,2048]{1,0:T(8,128)(2,1)} fusion(bf16[1024,4096]{1,0:T(8,128)(2,1)} %out_ref.1, s32[]{:T(128)S(6)} %select_n.11), kind=kLoop, calls=%fused_computation.1 | loop fusion | bytes 8388612 | tf_op jit(solution)/shard_map/dynamic_slice | solution.py:73
  21.5 60.4 %collective-permute-done.1.refs_4_ = bf16[384,2048]{1,0:T(8,128)(2,1)} collective-permute-done((bf16[384,2048]{1,0:T(8,128)(2,1)}, bf16[384,2048]{1,0:T(8,128)(2,1)}, u32[]{:S(2)}, u32[]{:S(2)}) %collective-permute-start.1) | collective-permute-done | bytes 1572896 | tf_op jit(solution)/shard_map/ppermute | solution.py:259
  83.1 1.4 collective-permute-start.7
  85.8 1.3 collective-permute-start.5
  87.2 7.8 %collective-permute-done.7.refs_8_ = bf16[384,640]{1,0:T(8,128)(2,1)S(1)} collective-permute-done((bf16[384,640]{1,0:T(8,128)(2,1)S(1)}, bf16[384,640]{1,0:T(8,128)(2,1)S(1)}, u32[]{:S(2)}, u32[]{:S(2)}) %collective-permute-start.7) | collective-permute-done | bytes 491552 | tf_op jit(solution)/shard_map/ppermute | solution.py:259
  95.0 1.5 collective-permute-start.17
  97.0 13.3 %collective-permute-done.5.refs_6_ = bf16[384,1408]{1,0:T(8,128)(2,1)S(1)} collective-permute-done((bf16[384,1408]{1,0:T(8,128)(2,1)S(1)}, bf16[384,1408]{1,0:T(8,128)(2,1)S(1)}, u32[]{:S(2)}, u32[]{:S(2)}) %collective-permute-start.5) | collective-permute-done | bytes 1081376 | tf_op jit(solution)/shard_map/ppermute | solution.py:259
  110.9 1.9 collective-permute-start.11
  113.1 2.3 %collective-permute-start.12 = (bf16[512,256]{1,0:T(8,128)(2,1)S(1)}, bf16[512,256]{1,0:T(8,128)(2,1)S(1)}, u32[]{:S(2)}, u32[]{:S(2)}) collective-permute-start(bf16[512,256]{1,0:T(8,128)(2,1)S(1)} %get-tuple-element.43.refs_0_), channel_id=1, source_target_pairs={{0,8},{2,10},{4,12},{6,14},{8,0},{10,2},{12,4},{14,6},{1,9},{3,11}... | collective-permute-start | bytes 786440 | tf_op jit(solution)/shard_map/ppermute | solution.py:259
  115.4 2.7 %stage.1.stream_ref = bf16[4,384,4096]{2,1,0:T(8,128)(2,1)S(1)} custom-call(bf16[384,2048]{1,0:T(8,128)(2,1)S(1)} %copy-done, bf16[384,2048]{1,0:T(8,128)(2,1)} %collective-permute-done.refs_1_, bf16[384,2048]{1,0:T(8,128)(2,1)} %collective-permute-done.2.refs_2_, bf16[384,2048]{1,0:T(8,128)(2,1)S(1)} %collective-permute-done.3.refs_3_, ...), custom_call_target="tpu_custom_call" | custom-call | bytes 25165824 | tf_op jit(solution)/shard_map/stage/pallas_call | solution.py:117
  118.1 7.8 %project.2 = (bf16[4,384,128]{2,1,0:T(8,128)(2,1)S(1)}, bf16[4,384,128]{2,1,0:T(8,128)(2,1)S(1)}, f32[4,128,128]{2,1,0:T(8,128)S(1)}, f32[128,128]{1,0:T(8,128)S(1)}) custom-call(s32[4]{0:T(128)S(1)} %pad_add_fusion.place_ref, bf16[4,384,4096]{2,1,0:T(8,128)(2,1)S(1)} %stage.1.stream_ref, bf16[4096,256]{1,0:T(8,128)(2,1)S(1)} %bitcast.7), custom_call_target="tpu_custom_call" | custom-call | flops 3221225472 | bytes 2097152 | tf_op jit(solution)/shard_map/project/pallas_call | solution.py:156
  125.9 1.5 collective-permute-start.14
  127.4 3.3 %collective-permute-done.11.refs_3_ = bf16[512,256]{1,0:T(8,128)(2,1)S(1)} collective-permute-done((bf16[512,256]{1,0:T(8,128)(2,1)S(1)}, bf16[512,256]{1,0:T(8,128)(2,1)S(1)}, u32[]{:S(2)}, u32[]{:S(2)}) %collective-permute-start.11) | collective-permute-done | bytes 262176 | tf_op jit(solution)/shard_map/ppermute | solution.py:259
  130.7 3.2 %collective-permute-start.15 = (bf16[512,256]{1,0:T(8,128)(2,1)S(1)}, bf16[512,256]{1,0:T(8,128)(2,1)S(1)}, u32[]{:S(2)}, u32[]{:S(2)}) collective-permute-start(bf16[512,256]{1,0:T(8,128)(2,1)S(1)} %get-tuple-element.46), channel_id=1, source_target_pairs={{0,14},{2,12},{4,10},{6,8},{8,6},{10,4},{12,2},{14,0},{1,15},{3,13... | collective-permute-start | bytes 786440 | tf_op jit(solution)/shard_map/ppermute | solution.py:259
  133.9 9.1 %collective-permute-done.17.w_ref = bf16[4096,256]{1,0:T(8,128)(2,1)S(1)} collective-permute-done((bf16[4096,256]{1,0:T(8,128)(2,1)S(1)}, bf16[4096,256]{1,0:T(8,128)(2,1)S(1)}, u32[]{:S(2)}, u32[]{:S(2)}) %collective-permute-start.17) | collective-permute-done | bytes 2097184 | tf_op jit(solution)/shard_map/ppermute | solution.py:262
  143.0 1.8 collective-permute-start.9
  144.9 7.8 %project.3 = (bf16[4,384,128]{2,1,0:T(8,128)(2,1)S(1)}, bf16[4,384,128]{2,1,0:T(8,128)(2,1)S(1)}, f32[4,128,128]{2,1,0:T(8,128)S(1)}, f32[128,128]{1,0:T(8,128)S(1)}) custom-call(s32[4]{0:T(128)S(1)} %pad_add_fusion.place_ref, bf16[4,384,4096]{2,1,0:T(8,128)(2,1)S(1)} %stage.1.stream_ref, bf16[4096,256]{1,0:T(8,128)(2,1)S(1)} %collective-permute-done.17.w_ref), custom_call_target="tpu_custom_call" | custom-call | flops 3221225472 | bytes 2097152 | tf_op jit(solution)/shard_map/project/pallas_call | solution.py:156
  152.6 13.1 %collective-permute-done.13.refs_5_ = bf16[512,256]{1,0:T(8,128)(2,1)S(1)} collective-permute-done((bf16[512,256]{1,0:T(8,128)(2,1)S(1)}, bf16[512,256]{1,0:T(8,128)(2,1)S(1)}, u32[]{:S(2)}, u32[]{:S(2)}) %collective-permute-start.13) | collective-permute-done | bytes 262176 | tf_op jit(solution)/shard_map/ppermute | solution.py:259
  165.7 1.5 collective-permute-start.18
  167.3 1.5 collective-permute-start.16
  168.8 4.3 %queries.1.query_ref = bf16[4,384,256]{2,1,0:T(8,128)(2,1)S(1)} custom-call(s32[4]{0:T(128)S(1)} %pad_add_fusion.place_ref, bf16[4,384,4096]{2,1,0:T(8,128)(2,1)S(1)} %stage.1.stream_ref, bf16[512,256]{1,0:T(8,128)(2,1)S(1)} %get-tuple-element.43.refs_0_, bf16[512,256]{1,0:T(8,128)(2,1)S(1)} %collective-permute-done.9.refs_1_, ...), custom_call_target="tpu_custom_call" | custom-call | flops 3221225472 | bytes 2097152 | tf_op jit(solution)/shard_map/queries/pallas_call | solution.py:181
  173.1 2.0 %attend.3 = (bf16[384,256]{1,0:T(8,128)(2,1)S(1)}, bf16[384,256]{1,0:T(8,128)(2,1)S(1)}, bf16[384,256]{1,0:T(8,128)(2,1)S(1)}) custom-call(s32[4]{0:T(128)S(1)} %pad_add_fusion.place_ref, bf16[4,384,256]{2,1,0:T(8,128)(2,1)S(1)} %queries.1.query_ref, bf16[4,384,128]{2,1,0:T(8,128)(2,1)S(1)} %get-tuple-element.48.refs_0_, ...), custom_call_target="tpu_custom_call" | custom-call | flops 528482304 | bytes 2097152 | tf_op jit(solution)/shard_map/attend/pallas_call | solution.py:210
  175.1 1.4 collective-permute-start.20
  176.5 1.7 collective-permute-start.21
  180.6 4.0 %stage_rows.1 = (bf16[4,256,2048]{2,1,0:T(8,128)(2,1)S(1)}, bf16[4,256,2048]{2,1,0:T(8,128)(2,1)S(1)}) custom-call(s32[4]{0:T(128)S(1)} %pad_add_fusion.place_ref, bf16[1024,4096]{1,0:T(8,128)(2,1)} %out_ref.1, bf16[1024,2048]{1,0:T(8,128)(2,1)} %collective-permute-done.19.far_ref), custom_call_target="tpu_custom_call" | custom-call | bytes 16777216 | tf_op jit(solution)/shard_map/stage_rows/pallas_call | solution.py:96
  184.6 3.5 %collective-permute-done.22.refs_3_ = bf16[384,256]{1,0:T(8,128)(2,1)S(1)} collective-permute-done((bf16[384,256]{1,0:T(8,128)(2,1)S(1)}, bf16[384,256]{1,0:T(8,128)(2,1)S(1)}, u32[]{:S(2)}, u32[]{:S(2)}) %collective-permute-start.22) | collective-permute-done | bytes 196640 | tf_op jit(solution)/shard_map/ppermute | solution.py:259
  189.2 1.8 add_features.2.refs_5_
  191.0 2.9 %add_features.3 = bf16[384,2048]{1,0:T(8,128)(2,1)} custom-call(bf16[384,256]{1,0:T(8,128)(2,1)S(1)} %collective-permute-done.23.refs_0_, bf16[384,256]{1,0:T(8,128)(2,1)S(1)} %collective-permute-done.24.refs_1_, bf16[384,256]{1,0:T(8,128)(2,1)S(1)} %collective-permute-done.25.refs_2_, bf16[384,256]{1,0:T(8,128)(2,1)S(1)} %collective-permute-done.26.refs_3_, ...), custom_call_target="tpu_custom_call" | custom-call | flops 1610612736 | bytes 8388608 | tf_op jit(solution)/shard_map/add_features/pallas_call | solution.py:233
  (47 shorter events, 11.0 us)
Async XLA Ops:
  0.1 1.2 copy-start.1
  1.3 1.2 copy-start.2
  4.7 77.2 %all-to-all-start = ((bf16[8,512,256]{2,1,0:T(8,128)(2,1)}), bf16[8,512,256]{2,1,0:T(8,128)(2,1)S(1)}, u32[]{:S(2)}, u32[]{:S(2)}) async-start(bf16[8,512,256]{2,1,0:T(8,128)(2,1)} %bitcast.4), calls=%async_computation | async-start | bytes 4194304 | tf_op jit(solution)/shard_map/all_to_all | solution.py:268
  12.0 69.9 %collective-permute-start.1 = (bf16[384,2048]{1,0:T(8,128)(2,1)}, bf16[384,2048]{1,0:T(8,128)(2,1)}, u32[]{:S(2)}, u32[]{:S(2)}) collective-permute-start(bf16[384,2048]{1,0:T(8,128)(2,1)} %refs_0_.1), channel_id=1, source_target_pairs={{0,4},{2,6},{4,0},{6,2},{8,12},{10,14},{12,8},{14,10},{1,5},{3,7},... | collective-permute-start | bytes 4718600 | tf_op jit(solution)/shard_map/ppermute | solution.py:259
  14.0 67.9 %collective-permute-start.2 = (bf16[384,2048]{1,0:T(8,128)(2,1)}, bf16[384,2048]{1,0:T(8,128)(2,1)}, u32[]{:S(2)}, u32[]{:S(2)}) collective-permute-start(bf16[384,2048]{1,0:T(8,128)(2,1)} %refs_0_.1), channel_id=1, source_target_pairs={{0,2},{2,0},{4,6},{6,4},{8,10},{10,8},{12,14},{14,12},{1,3},{3,1},... | collective-permute-start | bytes 4718600 | tf_op jit(solution)/shard_map/ppermute | solution.py:259
  15.5 81.0 %collective-permute-start = (bf16[384,2048]{1,0:T(8,128)(2,1)}, bf16[384,2048]{1,0:T(8,128)(2,1)}, u32[]{:S(2)}, u32[]{:S(2)}) collective-permute-start(bf16[384,2048]{1,0:T(8,128)(2,1)} %refs_0_.1), channel_id=1, source_target_pairs={{0,1},{1,0},{2,3},{3,2},{4,5},{5,4},{6,7},{7,6},{8,9},{9,8},{10,11... | collective-permute-start | bytes 4718600 | tf_op jit(solution)/shard_map/ppermute | solution.py:265
  15.5 5.3 %copy-start.3 = (bf16[512,1024]{1,0:T(8,128)(2,1)S(1)}, bf16[512,1024]{1,0:T(8,128)(2,1)}, u32[]{:S(2)}) copy-start(bf16[512,1024]{1,0:T(8,128)(2,1)} %query_ref.1) | copy-start | bytes 3145732
  20.3 160.3 %collective-permute-start.19 = (bf16[1024,2048]{1,0:T(8,128)(2,1)}, bf16[1024,2048]{1,0:T(8,128)(2,1)}, u32[]{:S(2)}, u32[]{:S(2)}) collective-permute-start(bf16[1024,2048]{1,0:T(8,128)(2,1)} %constant_dynamic-slice_fusion), channel_id=1, source_target_pairs={{0,1},{1,0},{2,3},{3,2},{4,5},{5,4},{6,7},{7,6},{8,9},{9,8},{10,11... | collective-permute-start | bytes 12582920 | tf_op jit(solution)/shard_map/ppermute | solution.py:265
  81.9 33.5 %copy-start = (bf16[384,2048]{1,0:T(8,128)(2,1)S(1)}, bf16[384,2048]{1,0:T(8,128)(2,1)}, u32[]{:S(2)}) copy-start(bf16[384,2048]{1,0:T(8,128)(2,1)} %refs_0_.1) | copy-start | bytes 4718596
  83.1 11.9 %collective-permute-start.7 = (bf16[384,640]{1,0:T(8,128)(2,1)S(1)}, bf16[384,640]{1,0:T(8,128)(2,1)S(1)}, u32[]{:S(2)}, u32[]{:S(2)}) collective-permute-start(bf16[384,640]{1,0:T(8,128)(2,1)S(1)} %slice.7), channel_id=1, source_target_pairs={{0,4},{2,6},{4,0},{6,2},{8,12},{10,14},{12,8},{14,10},{1,5},{3,7},... | collective-permute-start | bytes 1474568 | tf_op jit(solution)/shard_map/ppermute | solution.py:259
  85.8 24.5 %collective-permute-start.5 = (bf16[384,1408]{1,0:T(8,128)(2,1)S(1)}, bf16[384,1408]{1,0:T(8,128)(2,1)S(1)}, u32[]{:S(2)}, u32[]{:S(2)}) collective-permute-start(bf16[384,1408]{1,0:T(8,128)(2,1)S(1)} %slice.6), channel_id=1, source_target_pairs={{0,2},{2,0},{4,6},{6,4},{8,10},{10,8},{12,14},{14,12},{1,3},{3,1},... | collective-permute-start | bytes 3244040 | tf_op jit(solution)/shard_map/ppermute | solution.py:259
  95.0 1.9 collective-permute-start.8
  95.0 48.0 %collective-permute-start.17 = (bf16[4096,256]{1,0:T(8,128)(2,1)S(1)}, bf16[4096,256]{1,0:T(8,128)(2,1)S(1)}, u32[]{:S(2)}, u32[]{:S(2)}) collective-permute-start(bf16[4096,256]{1,0:T(8,128)(2,1)S(1)} %bitcast.6), channel_id=1, source_target_pairs={{0,16},{16,0},{1,17},{17,1},{2,18},{18,2},{3,19},{19,3},{4,20},{20... | collective-permute-start | bytes 6291464 | tf_op jit(solution)/shard_map/ppermute | solution.py:262
  96.5 13.8 %collective-permute-start.3 = (bf16[384,2048]{1,0:T(8,128)(2,1)}, bf16[384,2048]{1,0:T(8,128)(2,1)S(1)}, u32[]{:S(2)}, u32[]{:S(2)}) collective-permute-start(bf16[384,2048]{1,0:T(8,128)(2,1)} %collective-permute-done.2.refs_2_), channel_id=1, source_target_pairs={{0,1},{1,0},{2,3},{3,2},{4,5},{5,4},{6,7},{7,6},{8,9},{9,8},{10,11... | collective-permute-start | bytes 4718600 | tf_op jit(solution)/shard_map/ppermute | solution.py:265
  96.8 14.0 %collective-permute-start.4 = (bf16[384,2048]{1,0:T(8,128)(2,1)}, bf16[384,2048]{1,0:T(8,128)(2,1)S(1)}, u32[]{:S(2)}, u32[]{:S(2)}) collective-permute-start(bf16[384,2048]{1,0:T(8,128)(2,1)} %collective-permute-done.1.refs_4_), channel_id=1, source_target_pairs={{0,1},{1,0},{2,3},{3,2},{4,5},{5,4},{6,7},{7,6},{8,9},{9,8},{10,11... | collective-permute-start | bytes 4718600 | tf_op jit(solution)/shard_map/ppermute | solution.py:265
  110.3 2.7 %collective-permute-start.6 = (bf16[384,1408]{1,0:T(8,128)(2,1)S(1)}, bf16[384,1408]{1,0:T(8,128)(2,1)S(1)}, u32[]{:S(2)}, u32[]{:S(2)}) collective-permute-start(bf16[384,1408]{1,0:T(8,128)(2,1)S(1)} %collective-permute-done.5.refs_6_), channel_id=1, source_target_pairs={{0,1},{1,0},{2,3},{3,2},{4,5},{5,4},{6,7},{7,6},{8,9},{9,8},{10,11... | collective-permute-start | bytes 3244040 | tf_op jit(solution)/shard_map/ppermute | solution.py:265
  110.4 15.5 %collective-permute-start.10 = (bf16[512,256]{1,0:T(8,128)(2,1)S(1)}, bf16[512,256]{1,0:T(8,128)(2,1)S(1)}, u32[]{:S(2)}, u32[]{:S(2)}) collective-permute-start(bf16[512,256]{1,0:T(8,128)(2,1)S(1)} %get-tuple-element.45), channel_id=1, source_target_pairs={{0,4},{2,6},{4,0},{6,2},{8,12},{10,14},{12,8},{14,10},{1,5},{3,7},... | collective-permute-start | bytes 786440 | tf_op jit(solution)/shard_map/ppermute | solution.py:259
  110.9 19.8 %collective-permute-start.11 = (bf16[512,256]{1,0:T(8,128)(2,1)S(1)}, bf16[512,256]{1,0:T(8,128)(2,1)S(1)}, u32[]{:S(2)}, u32[]{:S(2)}) collective-permute-start(bf16[512,256]{1,0:T(8,128)(2,1)S(1)} %get-tuple-element.46), channel_id=1, source_target_pairs={{0,6},{2,4},{4,2},{6,0},{8,14},{10,12},{12,10},{14,8},{1,7},{3,5},... | collective-permute-start | bytes 786440 | tf_op jit(solution)/shard_map/ppermute | solution.py:259
  113.1 20.9 %collective-permute-start.12 = (bf16[512,256]{1,0:T(8,128)(2,1)S(1)}, bf16[512,256]{1,0:T(8,128)(2,1)S(1)}, u32[]{:S(2)}, u32[]{:S(2)}) collective-permute-start(bf16[512,256]{1,0:T(8,128)(2,1)S(1)} %get-tuple-element.43.refs_0_), channel_id=1, source_target_pairs={{0,8},{2,10},{4,12},{6,14},{8,0},{10,2},{12,4},{14,6},{1,9},{3,11}... | collective-permute-start | bytes 786440 | tf_op jit(solution)/shard_map/ppermute | solution.py:259
  125.9 41.4 %collective-permute-start.14 = (bf16[512,256]{1,0:T(8,128)(2,1)S(1)}, bf16[512,256]{1,0:T(8,128)(2,1)S(1)}, u32[]{:S(2)}, u32[]{:S(2)}) collective-permute-start(bf16[512,256]{1,0:T(8,128)(2,1)S(1)} %get-tuple-element.45), channel_id=1, source_target_pairs={{0,12},{2,14},{4,8},{6,10},{8,4},{10,6},{12,0},{14,2},{1,13},{3,15... | collective-permute-start | bytes 786440 | tf_op jit(solution)/shard_map/ppermute | solution.py:259
  130.7 38.1 %collective-permute-start.15 = (bf16[512,256]{1,0:T(8,128)(2,1)S(1)}, bf16[512,256]{1,0:T(8,128)(2,1)S(1)}, u32[]{:S(2)}, u32[]{:S(2)}) collective-permute-start(bf16[512,256]{1,0:T(8,128)(2,1)S(1)} %get-tuple-element.46), channel_id=1, source_target_pairs={{0,14},{2,12},{4,10},{6,8},{8,6},{10,4},{12,2},{14,0},{1,15},{3,13... | collective-permute-start | bytes 786440 | tf_op jit(solution)/shard_map/ppermute | solution.py:259
  133.9 31.8 %collective-permute-start.13 = (bf16[512,256]{1,0:T(8,128)(2,1)S(1)}, bf16[512,256]{1,0:T(8,128)(2,1)S(1)}, u32[]{:S(2)}, u32[]{:S(2)}) collective-permute-start(bf16[512,256]{1,0:T(8,128)(2,1)S(1)} %get-tuple-element.44), channel_id=1, source_target_pairs={{0,10},{2,8},{4,14},{6,12},{8,2},{10,0},{12,6},{14,4},{1,11},{3,9}... | collective-permute-start | bytes 786440 | tf_op jit(solution)/shard_map/ppermute | solution.py:259
  143.0 25.8 %collective-permute-start.9 = (bf16[512,256]{1,0:T(8,128)(2,1)S(1)}, bf16[512,256]{1,0:T(8,128)(2,1)S(1)}, u32[]{:S(2)}, u32[]{:S(2)}) collective-permute-start(bf16[512,256]{1,0:T(8,128)(2,1)S(1)} %get-tuple-element.44), channel_id=1, source_target_pairs={{0,2},{2,0},{4,6},{6,4},{8,10},{10,8},{12,14},{14,12},{1,3},{3,1},... | collective-permute-start | bytes 786440 | tf_op jit(solution)/shard_map/ppermute | solution.py:259
  165.7 7.4 %collective-permute-start.18 = (f32[128,128]{1,0:T(8,128)S(1)}, f32[128,128]{1,0:T(8,128)S(1)}, u32[]{:S(2)}, u32[]{:S(2)}) collective-permute-start(f32[128,128]{1,0:T(8,128)S(1)} %get-tuple-element.55), channel_id=1, source_target_pairs={{0,8},{2,10},{4,12},{6,14},{1,9},{3,11},{5,13},{7,15},{16,24},{18,... | collective-permute-start | bytes 196616 | tf_op jit(solution)/shard_map/ppermute | solution.py:239
  167.3 5.8 %collective-permute-start.16 = (f32[128,128]{1,0:T(8,128)S(1)}, f32[128,128]{1,0:T(8,128)S(1)}, u32[]{:S(2)}, u32[]{:S(2)}) collective-permute-start(f32[128,128]{1,0:T(8,128)S(1)} %get-tuple-element.51), channel_id=1, source_target_pairs={{0,8},{2,10},{4,12},{6,14},{1,9},{3,11},{5,13},{7,15},{16,24},{18,... | collective-permute-start | bytes 196616 | tf_op jit(solution)/shard_map/ppermute | solution.py:239
  175.1 9.5 %collective-permute-start.20 = (bf16[384,256]{1,0:T(8,128)(2,1)S(1)}, bf16[384,256]{1,0:T(8,128)(2,1)S(1)}, u32[]{:S(2)}, u32[]{:S(2)}) collective-permute-start(bf16[384,256]{1,0:T(8,128)(2,1)S(1)} %get-tuple-element.60), channel_id=1, source_target_pairs={{0,2},{2,0},{4,6},{6,4},{8,10},{10,8},{12,14},{14,12},{1,3},{3,1},... | collective-permute-start | bytes 589832 | tf_op jit(solution)/shard_map/ppermute | solution.py:259
  176.5 8.1 %collective-permute-start.21 = (bf16[384,256]{1,0:T(8,128)(2,1)S(1)}, bf16[384,256]{1,0:T(8,128)(2,1)S(1)}, u32[]{:S(2)}, u32[]{:S(2)}) collective-permute-start(bf16[384,256]{1,0:T(8,128)(2,1)S(1)} %get-tuple-element.61), channel_id=1, source_target_pairs={{0,4},{2,6},{4,0},{6,2},{8,12},{10,14},{12,8},{14,10},{1,5},{3,7},... | collective-permute-start | bytes 589832 | tf_op jit(solution)/shard_map/ppermute | solution.py:259
  178.2 9.9 %collective-permute-start.22 = (bf16[384,256]{1,0:T(8,128)(2,1)S(1)}, bf16[384,256]{1,0:T(8,128)(2,1)S(1)}, u32[]{:S(2)}, u32[]{:S(2)}) collective-permute-start(bf16[384,256]{1,0:T(8,128)(2,1)S(1)} %get-tuple-element.62), channel_id=1, source_target_pairs={{0,6},{2,4},{4,2},{6,0},{8,14},{10,12},{12,10},{14,8},{1,7},{3,5},... | collective-permute-start | bytes 589832 | tf_op jit(solution)/shard_map/ppermute | solution.py:259
  188.1 2.8 %collective-permute-start.23 = (bf16[384,256]{1,0:T(8,128)(2,1)S(1)}, bf16[384,256]{1,0:T(8,128)(2,1)S(1)}, u32[]{:S(2)}, u32[]{:S(2)}) collective-permute-start(bf16[384,256]{1,0:T(8,128)(2,1)S(1)} %attend.2.refs_0_), channel_id=1, source_target_pairs={{0,1},{1,0},{2,3},{3,2},{4,5},{5,4},{6,7},{7,6},{8,9},{9,8},{10,11... | collective-permute-start | bytes 589832 | tf_op jit(solution)/shard_map/ppermute | solution.py:265
  188.1 2.8 %collective-permute-start.24 = (bf16[384,256]{1,0:T(8,128)(2,1)S(1)}, bf16[384,256]{1,0:T(8,128)(2,1)S(1)}, u32[]{:S(2)}, u32[]{:S(2)}) collective-permute-start(bf16[384,256]{1,0:T(8,128)(2,1)S(1)} %collective-permute-done.20.refs_1_), channel_id=1, source_target_pairs={{0,1},{1,0},{2,3},{3,2},{4,5},{5,4},{6,7},{7,6},{8,9},{9,8},{10,11... | collective-permute-start | bytes 589832 | tf_op jit(solution)/shard_map/ppermute | solution.py:265
  188.6 2.3 %collective-permute-start.25 = (bf16[384,256]{1,0:T(8,128)(2,1)S(1)}, bf16[384,256]{1,0:T(8,128)(2,1)S(1)}, u32[]{:S(2)}, u32[]{:S(2)}) collective-permute-start(bf16[384,256]{1,0:T(8,128)(2,1)S(1)} %collective-permute-done.21.refs_2_), channel_id=1, source_target_pairs={{0,1},{1,0},{2,3},{3,2},{4,5},{5,4},{6,7},{7,6},{8,9},{9,8},{10,11... | collective-permute-start | bytes 589832 | tf_op jit(solution)/shard_map/ppermute | solution.py:265
  188.6 2.3 %collective-permute-start.26 = (bf16[384,256]{1,0:T(8,128)(2,1)S(1)}, bf16[384,256]{1,0:T(8,128)(2,1)S(1)}, u32[]{:S(2)}, u32[]{:S(2)}) collective-permute-start(bf16[384,256]{1,0:T(8,128)(2,1)S(1)} %collective-permute-done.22.refs_3_), channel_id=1, source_target_pairs={{0,1},{1,0},{2,3},{3,2},{4,5},{5,4},{6,7},{7,6},{8,9},{9,8},{10,11... | collective-permute-start | bytes 589832 | tf_op jit(solution)/shard_map/ppermute | solution.py:265

commit v4 on v3

--- a/solution.py
+++ b/solution.py
@@ -98,15 +98,17 @@
     )
 
 
-def stage(pieces, rows, width):
+def stage(place, pieces, rows, width):
     count = len(pieces)
-
-    def kernel(*refs):
+    half = width // 2
+
+    def kernel(place_ref, *refs):
         out, sems = refs[count], refs[count + 1]
-        copies = [
-            pltpu.make_async_copy(ref, out.at[r, :, pl.ds(column, array.shape[1])], sems.at[i])
-            for i, ((array, r, column), ref) in enumerate(zip(pieces, refs))
-        ]
+        copies = []
+        for i, ((array, r, column, far), ref) in enumerate(zip(pieces, refs)):
+            core = 1 - place_ref[2] if far else place_ref[2]
+            start = pl.multiple_of(core * half + column, HDIM)
+            copies.append(pltpu.make_async_copy(ref, out.at[r, :, pl.ds(start, array.shape[1])], sems.at[i]))
         for copy in copies:
             copy.start()
         for copy in copies:
@@ -114,18 +116,9 @@
 
     shape = pltpu.VMEM((SUB, rows, width), BF16)
     sems = pltpu.SemaphoreType.DMA((count,))
-    return call(kernel, "stage", shape, [ANY] * count, VMEM, LIMIT, 0, SUB * rows * width * 4, [sems])(
-        *[array for array, _, _ in pieces]
-    )
-
-
-def by_halves(place_ref, stream_ref, r, w_ref):
-    half = w_ref.shape[0] // 2
-    own = pl.multiple_of(place_ref[2] * half, half)
-    far = pl.multiple_of((1 - place_ref[2]) * half, half)
-    return dot(stream_ref[r, :, :half], w_ref[pl.ds(own, half), :]) + dot(
-        stream_ref[r, :, half:], w_ref[pl.ds(far, half), :]
-    )
+    return call(
+        kernel, "stage", shape, [SMEM] + [ANY] * count, VMEM, LIMIT, 0, SUB * rows * width * 4, [sems]
+    )(place, *[piece[0] for piece in pieces])
 
 
 def project(place, stream, kv):
@@ -134,7 +127,7 @@
     def kernel(place_ref, stream_ref, w_ref, key_ref, value_ref, before_ref, total_ref):
         states = []
         for r in range(SUB):
-            both = by_halves(place_ref, stream_ref, r, w_ref)
+            both = dot(stream_ref[r], w_ref[...])
             key = silu(both[:, :HDIM]).astype(BF16)
             value = both[:, HDIM:].astype(BF16)
             key_ref[r] = key
@@ -160,14 +153,11 @@
     _, rows, width = stream.shape
     count = len(pieces)
     depth = pieces[0].shape[0]
-    half = width // 2
 
     def kernel(place_ref, stream_ref, *refs):
         ins, out, w_held = refs[:count], refs[count], refs[count + 1]
         for m, piece in enumerate(ins):
-            row = jnp.bitwise_xor(place_ref[3], m) * depth
-            far = jnp.where(row >= half, 1, 0) != place_ref[2]
-            row = pl.multiple_of(lax.rem(row, half) + jnp.where(far, half, 0), depth)
+            row = pl.multiple_of(jnp.bitwise_xor(place_ref[3], m) * depth, depth)
             w_held[pl.ds(row, depth), :] = piece[...]
         swap = place_ref[1] == 1
         for r in range(SUB):
@@ -273,27 +263,34 @@
         whole = spread(jnp.concatenate(ordered * groups, axis=0)).reshape(n_ctx, -1, 2 * HDIM)
         return [lax.dynamic_index_in_dim(whole, ctx ^ m, keepdims=False) for m in range(n_ctx)]
 
+    cut = half * 11 // 16 // HDIM * HDIM
     across = xor(tokens, 2)
     beside = xor(tokens, 1)
     kv_mine = spread(pack_keys_values(place, w_key, w_value, n_ctx))
     q_sent = pack_queries(place, w_query)
-    across, beside, kv_mine, q_sent = lax.optimization_barrier((across, beside, kv_mine, q_sent))
-    cut = half * 11 // 16 // HDIM * HDIM
+    w_far = other_core(take_rows(place, w_out))
+    far_tokens = other_core(tokens)
+    far_beside = other_core(beside)
+    across, beside, kv_mine, q_sent, w_far, far_tokens, far_beside = lax.optimization_barrier(
+        (across, beside, kv_mine, q_sent, w_far, far_tokens, far_beside)
+    )
     left = xor(across[:, :cut], 1)
     right = xor(beside[:, cut:], 2)
     kv_other = other_part(kv_mine)
-    arrived = {m: xor(q_sent[m % SUB], m) for m in (4, 6, 5, 7, 2, 3, 1)} if n_ctx == 2 * SUB else {}
-    if arrived:
-        q_pieces = [q_sent[0]] + [arrived[m] for m in range(1, n_ctx)]
+    far_across = other_core(across)
+    if n_ctx == 2 * SUB:
+        arrived = {0: q_sent[0]} | {m: xor(q_sent[m % SUB], m) for m in (4, 6)}
+        left, right, arrived, q_sent = lax.optimization_barrier((left, right, arrived, q_sent))
+        arrived = arrived | {m: xor(q_sent[m % SUB], m) for m in (5, 7, 2, 3, 1)}
+        q_pieces = [arrived[m] for m in range(n_ctx)]
     else:
         q_pieces = gather_queries(q_sent)
 
-    w_far = other_core(take_rows(place, w_out))
-
-    pieces = []
-    for array, r, column in ((tokens, 0, 0), (beside, 1, 0), (across, 2, 0), (left, 3, 0), (right, 3, cut)):
-        pieces += [(array, r, column), (other_core(array), r, half + column)]
-    stream = stage(pieces, rows, 2 * half)
+    pieces = [(tokens, 0, 0, False), (far_tokens, 0, 0, True), (beside, 1, 0, False), (far_beside, 1, 0, True)]
+    pieces += [(across, 2, 0, False), (far_across, 2, 0, True)]
+    for array, column in ((left, 0), (right, cut)):
+        pieces += [(array, 3, column, False), (other_core(array), 3, column, True)]
+    stream = stage(place, pieces, rows, 2 * half)
 
     def keys_values(kv):
         key, value, before, total = project(place, stream, kv)

time: 194 us -> 177 us (0.912)
  waiting for transfers between devices: 111 us -> 86.7 us
  local copies, waits for them, and re-layouts: 9.8 us -> 17.3 us
    ppermute x14, waiting for transfers between devices: 101 us -> 85.2 us  [xor(): return lax.ppermute(value, 'ctx', [(i, i ^ step) for i in range(n_ctx)])]
    ppermute x1, waiting for transfers between devices: 9.11 us -> 0.01 us  [other_part(): return lax.ppermute(value, 'groups', [(0, 1), (1, 0)])]
    unnamed x8 -> x32, local copies, waits for them, and re-layouts: 2.46 us -> 9.84 us
    ppermute x2, starting transfers between devices: 3.01 us -> 5.77 us  [shift(): return lax.ppermute(v, 'ctx', pairs)]
    ppermute x14, starting transfers between devices: 21.8 us -> 19.6 us  [xor(): return lax.ppermute(value, 'ctx', [(i, i ^ step) for i in range(n_ctx)])]
  transfers between devices with their start and end apart: 28 -> 28, of which waited for: 9 -> 7; matrix products, arithmetic and copies ran while one was open for 4% -> 1% of each run, Pallas kernels for 17% -> 18%
where the time goes in v4:
time: 177 us
  waiting for transfers between devices  86.7 us (49%)
  Pallas kernels  36.7 us (21%)
  starting transfers between devices  35.8 us (20%)
  local copies, waits for them, and re-layouts  17.3 us (10%)
    ppermute x14, waiting for transfers between devices, xor(): return lax.ppermute(value, 'ctx', [(i, i ^ step) for i in range(n_ctx)])  85.2 us
    ppermute x14, starting transfers between devices, xor(): return lax.ppermute(value, 'ctx', [(i, i ^ step) for i in range(n_ctx)])  19.6 us
    pallas_call x2, Pallas kernels, project(): call(kernel, 'project', shapes, [SMEM, VMEM, VMEM], [VMEM] * 4, LIMIT, fl...  15.6 us
    unnamed x32, local copies, waits for them, and re-layouts  9.84 us
    all_to_all x1, starting transfers between devices, spread(): return lax.all_to_all(packed, 'ctx', 0, 0, tiled=True)  6.93 us
    ppermute x2, starting transfers between devices, shift(): return lax.ppermute(v, 'ctx', pairs)  5.77 us
    dynamic_slice x1, local copies, waits for them, and re-layouts, take_rows(): return lax.dynamic_slice(w_out, (0, (1 - place[2]) * half), (rows, half))  4.94 us
    pallas_call x2, Pallas kernels, add_features(): call(kernel, 'add_features', shape, [VMEM] * len(args), VMEM, LIMIT, flop...  4.72 us
  transfers between devices with their start and end apart: 28, of which 7 were waited for; matrix products, arithmetic and copies ran while one was open for 1% of the time, Pallas kernels for 18%

profile of v4, /device:TPU:0, one launch (start us, length us, event | category | flops | bytes accessed | tf_op | source)
XLA Modules:
  0.0 176.9 jit_solution(1868268840388407252)
XLA Ops:
  0.0 4.9 %constant_dynamic-slice_fusion = bf16[1024,2048]{1,0:T(8,128)(2,1)} fusion(bf16[1024,4096]{1,0:T(8,128)(2,1)} %out_ref.1, s32[]{:T(128)S(6)} %select_n.11), kind=kLoop, calls=%fused_computation.1 | loop fusion | bytes 8388612 | tf_op jit(solution)/shard_map/dynamic_slice | solution.py:73
  5.5 2.1 %pack_keys_values.1 = bf16[4096,256]{1,0:T(8,128)(2,1)} custom-call(s32[4]{0:T(128)S(1)} %pad_add_fusion.place_ref, bf16[512,1024]{1,0:T(8,128)(2,1)S(1)} %copy-done.9, bf16[512,1024]{1,0:T(8,128)(2,1)S(1)} %copy-done.10), custom_call_target="tpu_custom_call" | custom-call | bytes 4194304 | tf_op jit(solution)/shard_map/pack_keys_values/pallas_call | solution.py:54
  7.6 6.9 %all-to-all-start = ((bf16[8,512,256]{2,1,0:T(8,128)(2,1)}), bf16[8,512,256]{2,1,0:T(8,128)(2,1)S(1)}, u32[]{:S(2)}, u32[]{:S(2)}) async-start(bf16[8,512,256]{2,1,0:T(8,128)(2,1)} %bitcast.4), calls=%async_computation | async-start | bytes 4194304 | tf_op jit(solution)/shard_map/all_to_all | solution.py:258
  14.6 2.0 %collective-permute-start.1 = (bf16[384,2048]{1,0:T(8,128)(2,1)}, bf16[384,2048]{1,0:T(8,128)(2,1)S(1)}, u32[]{:S(2)}, u32[]{:S(2)}) collective-permute-start(bf16[384,2048]{1,0:T(8,128)(2,1)} %refs_0_.1), channel_id=1, source_target_pairs={{0,2},{2,0},{4,6},{6,4},{8,10},{10,8},{12,14},{14,12},{1,3},{3,1},... | collective-permute-start | bytes 4718600 | tf_op jit(solution)/shard_map/ppermute | solution.py:249
  16.6 1.5 collective-permute-start
  18.0 55.7 %collective-permute-done.1.refs_2_ = bf16[384,2048]{1,0:T(8,128)(2,1)S(1)} collective-permute-done((bf16[384,2048]{1,0:T(8,128)(2,1)}, bf16[384,2048]{1,0:T(8,128)(2,1)S(1)}, u32[]{:S(2)}, u32[]{:S(2)}) %collective-permute-start.1) | collective-permute-done | bytes 1572896 | tf_op jit(solution)/shard_map/ppermute | solution.py:249
  76.6 8.5 %collective-permute-done.refs_4_ = bf16[384,2048]{1,0:T(8,128)(2,1)S(1)} collective-permute-done((bf16[384,2048]{1,0:T(8,128)(2,1)}, bf16[384,2048]{1,0:T(8,128)(2,1)S(1)}, u32[]{:S(2)}, u32[]{:S(2)}) %collective-permute-start) | collective-permute-done | bytes 1572896 | tf_op jit(solution)/shard_map/ppermute | solution.py:249
  88.5 1.5 slice.6
  90.0 1.5 collective-permute-start.6
  91.5 1.5 collective-permute-start.18
  93.1 2.5 %collective-permute-start.8 = (bf16[512,256]{1,0:T(8,128)(2,1)S(1)}, bf16[512,256]{1,0:T(8,128)(2,1)S(1)}, u32[]{:S(2)}, u32[]{:S(2)}) collective-permute-start(bf16[512,256]{1,0:T(8,128)(2,1)S(1)} %get-tuple-element.62.refs_0_), channel_id=1, source_target_pairs={{0,8},{2,10},{4,12},{6,14},{8,0},{10,2},{12,4},{14,6},{1,9},{3,11}... | collective-permute-start | bytes 786440 | tf_op jit(solution)/shard_map/ppermute | solution.py:249
  97.1 9.6 %collective-permute-done.8.refs_4_ = bf16[512,256]{1,0:T(8,128)(2,1)S(1)} collective-permute-done((bf16[512,256]{1,0:T(8,128)(2,1)S(1)}, bf16[512,256]{1,0:T(8,128)(2,1)S(1)}, u32[]{:S(2)}, u32[]{:S(2)}) %collective-permute-start.8) | collective-permute-done | bytes 262176 | tf_op jit(solution)/shard_map/ppermute | solution.py:249
  106.7 2.5 %collective-permute-start.9 = (bf16[512,256]{1,0:T(8,128)(2,1)}, bf16[512,256]{1,0:T(8,128)(2,1)S(1)}, u32[]{:S(2)}, u32[]{:S(2)}) collective-permute-start(bf16[512,256]{1,0:T(8,128)(2,1)} %copy-done.14), channel_id=1, source_target_pairs={{0,12},{2,14},{4,8},{6,10},{8,4},{10,6},{12,0},{14,2},{1,13},{3,15... | collective-permute-start | bytes 786440 | tf_op jit(solution)/shard_map/ppermute | solution.py:249
  109.3 9.1 %collective-permute-done.9.refs_6_ = bf16[512,256]{1,0:T(8,128)(2,1)S(1)} collective-permute-done((bf16[512,256]{1,0:T(8,128)(2,1)}, bf16[512,256]{1,0:T(8,128)(2,1)S(1)}, u32[]{:S(2)}, u32[]{:S(2)}) %collective-permute-start.9) | collective-permute-done | bytes 262176 | tf_op jit(solution)/shard_map/ppermute | solution.py:249
  120.4 1.5 collective-permute-done.11.refs_9_
  122.0 1.3 collective-permute-start.14
  123.3 2.5 %collective-permute-start.16 = (bf16[512,256]{1,0:T(8,128)(2,1)}, bf16[512,256]{1,0:T(8,128)(2,1)S(1)}, u32[]{:S(2)}, u32[]{:S(2)}) collective-permute-start(bf16[512,256]{1,0:T(8,128)(2,1)} %copy-done.12), channel_id=1, source_target_pairs={{0,14},{2,12},{4,10},{6,8},{8,6},{10,4},{12,2},{14,0},{1,15},{3,13... | collective-permute-start | bytes 786440 | tf_op jit(solution)/shard_map/ppermute | solution.py:249
  125.8 1.4 copy-done.4
  127.2 1.4 copy-done.6
  128.7 1.4 copy-done.8
  130.1 2.1 %stage.1.stream_ref = bf16[4,384,4096]{2,1,0:T(8,128)(2,1)S(1)} custom-call(s32[4]{0:T(128)S(1)} %pad_add_fusion.place_ref, bf16[384,2048]{1,0:T(8,128)(2,1)S(1)} %copy-done.4, bf16[384,2048]{1,0:T(8,128)(2,1)S(1)} %copy-done.6, bf16[384,2048]{1,0:T(8,128)(2,1)S(1)} %copy-done.3, bf16[384,2048]{1,0:T(8,128)(2,1)S(1)} %copy-done.8, ...), custom_call_target="tpu_custom_call" | custom-call | bytes 25165824 | tf_op jit(solution)/shard_map/stage/pallas_call | solution.py:119
  132.2 7.8 %project.2 = (bf16[4,384,128]{2,1,0:T(8,128)(2,1)S(1)}, bf16[4,384,128]{2,1,0:T(8,128)(2,1)S(1)}, f32[4,128,128]{2,1,0:T(8,128)S(1)}, f32[128,128]{1,0:T(8,128)S(1)}) custom-call(s32[4]{0:T(128)S(1)} %pad_add_fusion.place_ref, bf16[4,384,4096]{2,1,0:T(8,128)(2,1)S(1)} %stage.1.stream_ref, bf16[4096,256]{1,0:T(8,128)(2,1)S(1)} %bitcast.7), custom_call_target="tpu_custom_call" | custom-call | flops 3221225472 | bytes 2097152 | tf_op jit(solution)/shard_map/project/pallas_call | solution.py:149
  140.3 7.8 %project.3 = (bf16[4,384,128]{2,1,0:T(8,128)(2,1)S(1)}, bf16[4,384,128]{2,1,0:T(8,128)(2,1)S(1)}, f32[4,128,128]{2,1,0:T(8,128)S(1)}, f32[128,128]{1,0:T(8,128)S(1)}) custom-call(s32[4]{0:T(128)S(1)} %pad_add_fusion.place_ref, bf16[4,384,4096]{2,1,0:T(8,128)(2,1)S(1)} %stage.1.stream_ref, bf16[4096,256]{1,0:T(8,128)(2,1)S(1)} %collective-permute-done.18.w_ref), custom_call_target="tpu_custom_call" | custom-call | flops 3221225472 | bytes 2097152 | tf_op jit(solution)/shard_map/project/pallas_call | solution.py:149
  148.1 4.3 %collective-permute-start.19 = (f32[128,128]{1,0:T(8,128)S(1)}, f32[128,128]{1,0:T(8,128)S(1)}, u32[]{:S(2)}, u32[]{:S(2)}) collective-permute-start(f32[128,128]{1,0:T(8,128)S(1)} %get-tuple-element.76), channel_id=1, source_target_pairs={{0,8},{2,10},{4,12},{6,14},{1,9},{3,11},{5,13},{7,15},{16,24},{18,... | collective-permute-start | bytes 196616 | tf_op jit(solution)/shard_map/ppermute | solution.py:229
  152.4 1.5 collective-permute-start.17
  153.9 4.3 %queries.1.query_ref = bf16[4,384,256]{2,1,0:T(8,128)(2,1)S(1)} custom-call(s32[4]{0:T(128)S(1)} %pad_add_fusion.place_ref, bf16[4,384,4096]{2,1,0:T(8,128)(2,1)S(1)} %stage.1.stream_ref, bf16[512,256]{1,0:T(8,128)(2,1)S(1)} %get-tuple-element.62.refs_0_, bf16[512,256]{1,0:T(8,128)(2,1)S(1)} %collective-permute-done.12.refs_1_, ...), custom_call_target="tpu_custom_call" | custom-call | flops 3221225472 | bytes 2097152 | tf_op jit(solution)/shard_map/queries/pallas_call | solution.py:171
  158.2 2.0 %attend.3 = (bf16[384,256]{1,0:T(8,128)(2,1)S(1)}, bf16[384,256]{1,0:T(8,128)(2,1)S(1)}, bf16[384,256]{1,0:T(8,128)(2,1)S(1)}) custom-call(s32[4]{0:T(128)S(1)} %pad_add_fusion.place_ref, bf16[4,384,256]{2,1,0:T(8,128)(2,1)S(1)} %queries.1.query_ref, bf16[4,384,128]{2,1,0:T(8,128)(2,1)S(1)} %get-tuple-element.69.refs_0_, ...), custom_call_target="tpu_custom_call" | custom-call | flops 528482304 | bytes 2097152 | tf_op jit(solution)/shard_map/attend/pallas_call | solution.py:200
  161.0 2.8 %collective-permute-start.22 = (bf16[384,256]{1,0:T(8,128)(2,1)S(1)}, bf16[384,256]{1,0:T(8,128)(2,1)S(1)}, u32[]{:S(2)}, u32[]{:S(2)}) collective-permute-start(bf16[384,256]{1,0:T(8,128)(2,1)S(1)} %get-tuple-element.84), channel_id=1, source_target_pairs={{0,6},{2,4},{4,2},{6,0},{8,14},{10,12},{12,10},{14,8},{1,7},{3,5},... | collective-permute-start | bytes 589832 | tf_op jit(solution)/shard_map/ppermute | solution.py:249
  165.0 4.0 %stage_rows.1 = (bf16[4,256,2048]{2,1,0:T(8,128)(2,1)S(1)}, bf16[4,256,2048]{2,1,0:T(8,128)(2,1)S(1)}) custom-call(s32[4]{0:T(128)S(1)} %pad_add_fusion.place_ref, bf16[1024,4096]{1,0:T(8,128)(2,1)} %out_ref.1, bf16[1024,2048]{1,0:T(8,128)(2,1)} %collective-permute-done.2.far_ref), custom_call_target="tpu_custom_call" | custom-call | bytes 16777216 | tf_op jit(solution)/shard_map/stage_rows/pallas_call | solution.py:96
  169.0 2.1 %collective-permute-done.22.refs_3_ = bf16[384,256]{1,0:T(8,128)(2,1)S(1)} collective-permute-done((bf16[384,256]{1,0:T(8,128)(2,1)S(1)}, bf16[384,256]{1,0:T(8,128)(2,1)S(1)}, u32[]{:S(2)}, u32[]{:S(2)}) %collective-permute-start.22) | collective-permute-done | bytes 196640 | tf_op jit(solution)/shard_map/ppermute | solution.py:249
  172.1 1.8 %add_features.2.refs_5_ = f32[384,2048]{1,0:T(8,128)S(1)} custom-call(bf16[384,256]{1,0:T(8,128)(2,1)S(1)} %attend.2.refs_0_, bf16[384,256]{1,0:T(8,128)(2,1)S(1)} %collective-permute-done.20.refs_1_, bf16[384,256]{1,0:T(8,128)(2,1)S(1)} %collective-permute-done.21.refs_2_, bf16[384,256]{1,0:T(8,128)(2,1)S(1)} %collective-permute-done.22.refs_3_, ...), custom_call_target="tpu_custom_call" | custom-call | flops 1610612736 | bytes 8388608 | tf_op jit(solution)/shard_map/add_features/pallas_call | solution.py:223
  173.9 2.9 %add_features.3 = bf16[384,2048]{1,0:T(8,128)(2,1)} custom-call(bf16[384,256]{1,0:T(8,128)(2,1)S(1)} %collective-permute-done.23.refs_0_, bf16[384,256]{1,0:T(8,128)(2,1)S(1)} %collective-permute-done.24.refs_1_, bf16[384,256]{1,0:T(8,128)(2,1)S(1)} %collective-permute-done.25.refs_2_, bf16[384,256]{1,0:T(8,128)(2,1)S(1)} %collective-permute-done.26.refs_3_, ...), custom_call_target="tpu_custom_call" | custom-call | flops 1610612736 | bytes 8388608 | tf_op jit(solution)/shard_map/add_features/pallas_call | solution.py:223
  (71 shorter events, 13.8 us)
Async XLA Ops:
  4.9 83.6 %collective-permute-start.2 = (bf16[1024,2048]{1,0:T(8,128)(2,1)}, bf16[1024,2048]{1,0:T(8,128)(2,1)}, u32[]{:S(2)}, u32[]{:S(2)}) collective-permute-start(bf16[1024,2048]{1,0:T(8,128)(2,1)} %constant_dynamic-slice_fusion), channel_id=1, source_target_pairs={{0,1},{1,0},{2,3},{3,2},{4,5},{5,4},{6,7},{7,6},{8,9},{9,8},{10,11... | collective-permute-start | bytes 12582920 | tf_op jit(solution)/shard_map/ppermute | solution.py:255
  7.6 66.1 %copy-start.11 = (bf16[512,1024]{1,0:T(8,128)(2,1)S(1)}, bf16[512,1024]{1,0:T(8,128)(2,1)}, u32[]{:S(2)}) copy-start(bf16[512,1024]{1,0:T(8,128)(2,1)} %query_ref.1) | copy-start | bytes 3145732
  7.6 80.9 %all-to-all-start = ((bf16[8,512,256]{2,1,0:T(8,128)(2,1)}), bf16[8,512,256]{2,1,0:T(8,128)(2,1)S(1)}, u32[]{:S(2)}, u32[]{:S(2)}) async-start(bf16[8,512,256]{2,1,0:T(8,128)(2,1)} %bitcast.4), calls=%async_computation | async-start | bytes 4194304 | tf_op jit(solution)/shard_map/all_to_all | solution.py:258
  14.6 59.2 %collective-permute-start.1 = (bf16[384,2048]{1,0:T(8,128)(2,1)}, bf16[384,2048]{1,0:T(8,128)(2,1)S(1)}, u32[]{:S(2)}, u32[]{:S(2)}) collective-permute-start(bf16[384,2048]{1,0:T(8,128)(2,1)} %refs_0_.1), channel_id=1, source_target_pairs={{0,2},{2,0},{4,6},{6,4},{8,10},{10,8},{12,14},{14,12},{1,3},{3,1},... | collective-permute-start | bytes 4718600 | tf_op jit(solution)/shard_map/ppermute | solution.py:249
  16.6 68.5 %collective-permute-start = (bf16[384,2048]{1,0:T(8,128)(2,1)}, bf16[384,2048]{1,0:T(8,128)(2,1)S(1)}, u32[]{:S(2)}, u32[]{:S(2)}) collective-permute-start(bf16[384,2048]{1,0:T(8,128)(2,1)} %refs_0_.1), channel_id=1, source_target_pairs={{0,4},{2,6},{4,0},{6,2},{8,12},{10,14},{12,8},{14,10},{1,5},{3,7},... | collective-permute-start | bytes 4718600 | tf_op jit(solution)/shard_map/ppermute | solution.py:249
  18.0 67.0 %collective-permute-start.3 = (bf16[384,2048]{1,0:T(8,128)(2,1)}, bf16[384,2048]{1,0:T(8,128)(2,1)S(1)}, u32[]{:S(2)}, u32[]{:S(2)}) collective-permute-start(bf16[384,2048]{1,0:T(8,128)(2,1)} %refs_0_.1), channel_id=1, source_target_pairs={{0,1},{1,0},{2,3},{3,2},{4,5},{5,4},{6,7},{7,6},{8,9},{9,8},{10,11... | collective-permute-start | bytes 4718600 | tf_op jit(solution)/shard_map/ppermute | solution.py:255
  73.8 11.3 %copy-start.2 = (bf16[384,2048]{1,0:T(8,128)(2,1)}, bf16[384,2048]{1,0:T(8,128)(2,1)S(1)}, u32[]{:S(2)}) copy-start(bf16[384,2048]{1,0:T(8,128)(2,1)S(1)} %collective-permute-done.1.refs_2_) | copy-start | bytes 4718596
  73.8 13.6 %collective-permute-start.4 = (bf16[384,2048]{1,0:T(8,128)(2,1)S(1)}, bf16[384,2048]{1,0:T(8,128)(2,1)S(1)}, u32[]{:S(2)}, u32[]{:S(2)}) collective-permute-start(bf16[384,2048]{1,0:T(8,128)(2,1)S(1)} %collective-permute-done.1.refs_2_), channel_id=1, source_target_pairs={{0,1},{1,0},{2,3},{3,2},{4,5},{5,4},{6,7},{7,6},{8,9},{9,8},{10,11... | collective-permute-start | bytes 4718600 | tf_op jit(solution)/shard_map/ppermute | solution.py:255
  88.5 8.6 %copy-start.1 = (bf16[384,2048]{1,0:T(8,128)(2,1)S(1)}, bf16[384,2048]{1,0:T(8,128)(2,1)}, u32[]{:S(2)}) copy-start(bf16[384,2048]{1,0:T(8,128)(2,1)} %copy-done) | copy-start | bytes 4718596
  88.5 37.3 %copy-start.3 = (bf16[384,2048]{1,0:T(8,128)(2,1)S(1)}, bf16[384,2048]{1,0:T(8,128)(2,1)}, u32[]{:S(2)}) copy-start(bf16[384,2048]{1,0:T(8,128)(2,1)} %copy-done.2) | copy-start | bytes 4718596
  90.0 28.5 %collective-permute-start.6 = (bf16[384,1408]{1,0:T(8,128)(2,1)S(1)}, bf16[384,1408]{1,0:T(8,128)(2,1)S(1)}, u32[]{:S(2)}, u32[]{:S(2)}) collective-permute-start(bf16[384,1408]{1,0:T(8,128)(2,1)S(1)} %slice.6), channel_id=1, source_target_pairs={{0,2},{2,0},{4,6},{6,4},{8,10},{10,8},{12,14},{14,12},{1,3},{3,1},... | collective-permute-start | bytes 3244040 | tf_op jit(solution)/shard_map/ppermute | solution.py:249
  91.5 48.4 %collective-permute-start.18 = (bf16[4096,256]{1,0:T(8,128)(2,1)S(1)}, bf16[4096,256]{1,0:T(8,128)(2,1)S(1)}, u32[]{:S(2)}, u32[]{:S(2)}) collective-permute-start(bf16[4096,256]{1,0:T(8,128)(2,1)S(1)} %bitcast.6), channel_id=1, source_target_pairs={{0,16},{16,0},{1,17},{17,1},{2,18},{18,2},{3,19},{19,3},{4,20},{20... | collective-permute-start | bytes 6291464 | tf_op jit(solution)/shard_map/ppermute | solution.py:252
  93.1 13.7 %collective-permute-start.8 = (bf16[512,256]{1,0:T(8,128)(2,1)S(1)}, bf16[512,256]{1,0:T(8,128)(2,1)S(1)}, u32[]{:S(2)}, u32[]{:S(2)}) collective-permute-start(bf16[512,256]{1,0:T(8,128)(2,1)S(1)} %get-tuple-element.62.refs_0_), channel_id=1, source_target_pairs={{0,8},{2,10},{4,12},{6,14},{8,0},{10,2},{12,4},{14,6},{1,9},{3,11}... | collective-permute-start | bytes 786440 | tf_op jit(solution)/shard_map/ppermute | solution.py:249
  96.6 21.9 %collective-permute-start.7 = (bf16[384,640]{1,0:T(8,128)(2,1)S(1)}, bf16[384,640]{1,0:T(8,128)(2,1)S(1)}, u32[]{:S(2)}, u32[]{:S(2)}) collective-permute-start(bf16[384,640]{1,0:T(8,128)(2,1)S(1)} %slice.7), channel_id=1, source_target_pairs={{0,4},{2,6},{4,0},{6,2},{8,12},{10,14},{12,8},{14,10},{1,5},{3,7},... | collective-permute-start | bytes 1474568 | tf_op jit(solution)/shard_map/ppermute | solution.py:249
  97.1 22.6 %collective-permute-start.5 = (bf16[384,2048]{1,0:T(8,128)(2,1)S(1)}, bf16[384,2048]{1,0:T(8,128)(2,1)S(1)}, u32[]{:S(2)}, u32[]{:S(2)}) collective-permute-start(bf16[384,2048]{1,0:T(8,128)(2,1)S(1)} %copy-done.1), channel_id=1, source_target_pairs={{0,1},{1,0},{2,3},{3,2},{4,5},{5,4},{6,7},{7,6},{8,9},{9,8},{10,11... | collective-permute-start | bytes 4718600 | tf_op jit(solution)/shard_map/ppermute | solution.py:255
  106.7 11.6 %collective-permute-start.9 = (bf16[512,256]{1,0:T(8,128)(2,1)}, bf16[512,256]{1,0:T(8,128)(2,1)S(1)}, u32[]{:S(2)}, u32[]{:S(2)}) collective-permute-start(bf16[512,256]{1,0:T(8,128)(2,1)} %copy-done.14), channel_id=1, source_target_pairs={{0,12},{2,14},{4,8},{6,10},{8,4},{10,6},{12,0},{14,2},{1,13},{3,15... | collective-permute-start | bytes 786440 | tf_op jit(solution)/shard_map/ppermute | solution.py:249
  118.6 4.7 %collective-permute-start.10 = (bf16[384,1408]{1,0:T(8,128)(2,1)S(1)}, bf16[384,1408]{1,0:T(8,128)(2,1)S(1)}, u32[]{:S(2)}, u32[]{:S(2)}) collective-permute-start(bf16[384,1408]{1,0:T(8,128)(2,1)S(1)} %collective-permute-done.6.refs_6_), channel_id=1, source_target_pairs={{0,1},{1,0},{2,3},{3,2},{4,5},{5,4},{6,7},{7,6},{8,9},{9,8},{10,11... | collective-permute-start | bytes 3244040 | tf_op jit(solution)/shard_map/ppermute | solution.py:255
  118.6 3.4 %collective-permute-start.11 = (bf16[384,640]{1,0:T(8,128)(2,1)S(1)}, bf16[384,640]{1,0:T(8,128)(2,1)S(1)}, u32[]{:S(2)}, u32[]{:S(2)}) collective-permute-start(bf16[384,640]{1,0:T(8,128)(2,1)S(1)} %collective-permute-done.7.refs_8_), channel_id=1, source_target_pairs={{0,1},{1,0},{2,3},{3,2},{4,5},{5,4},{6,7},{7,6},{8,9},{9,8},{10,11... | collective-permute-start | bytes 1474568 | tf_op jit(solution)/shard_map/ppermute | solution.py:255
  119.1 29.0 %collective-permute-start.12 = (bf16[512,256]{1,0:T(8,128)(2,1)}, bf16[512,256]{1,0:T(8,128)(2,1)S(1)}, u32[]{:S(2)}, u32[]{:S(2)}) collective-permute-start(bf16[512,256]{1,0:T(8,128)(2,1)} %copy-done.13), channel_id=1, source_target_pairs={{0,2},{2,0},{4,6},{6,4},{8,10},{10,8},{12,14},{14,12},{1,3},{3,1},... | collective-permute-start | bytes 786440 | tf_op jit(solution)/shard_map/ppermute | solution.py:249
  119.7 34.2 %collective-permute-start.15 = (bf16[512,256]{1,0:T(8,128)(2,1)}, bf16[512,256]{1,0:T(8,128)(2,1)S(1)}, u32[]{:S(2)}, u32[]{:S(2)}) collective-permute-start(bf16[512,256]{1,0:T(8,128)(2,1)} %copy-done.13), channel_id=1, source_target_pairs={{0,10},{2,8},{4,14},{6,12},{8,2},{10,0},{12,6},{14,4},{1,11},{3,9}... | collective-permute-start | bytes 786440 | tf_op jit(solution)/shard_map/ppermute | solution.py:249
  122.0 31.9 %collective-permute-start.14 = (bf16[512,256]{1,0:T(8,128)(2,1)}, bf16[512,256]{1,0:T(8,128)(2,1)S(1)}, u32[]{:S(2)}, u32[]{:S(2)}) collective-permute-start(bf16[512,256]{1,0:T(8,128)(2,1)} %copy-done.12), channel_id=1, source_target_pairs={{0,6},{2,4},{4,2},{6,0},{8,14},{10,12},{12,10},{14,8},{1,7},{3,5},... | collective-permute-start | bytes 786440 | tf_op jit(solution)/shard_map/ppermute | solution.py:249
  123.3 30.6 %collective-permute-start.16 = (bf16[512,256]{1,0:T(8,128)(2,1)}, bf16[512,256]{1,0:T(8,128)(2,1)S(1)}, u32[]{:S(2)}, u32[]{:S(2)}) collective-permute-start(bf16[512,256]{1,0:T(8,128)(2,1)} %copy-done.12), channel_id=1, source_target_pairs={{0,14},{2,12},{4,10},{6,8},{8,6},{10,4},{12,2},{14,0},{1,15},{3,13... | collective-permute-start | bytes 786440 | tf_op jit(solution)/shard_map/ppermute | solution.py:249
  140.0 12.4 %collective-permute-start.13 = (bf16[512,256]{1,0:T(8,128)(2,1)S(1)}, bf16[512,256]{1,0:T(8,128)(2,1)S(1)}, u32[]{:S(2)}, u32[]{:S(2)}) collective-permute-start(bf16[512,256]{1,0:T(8,128)(2,1)S(1)} %copy-done.15), channel_id=1, source_target_pairs={{0,4},{2,6},{4,0},{6,2},{8,12},{10,14},{12,8},{14,10},{1,5},{3,7},... | collective-permute-start | bytes 786440 | tf_op jit(solution)/shard_map/ppermute | solution.py:249
  148.1 10.1 %collective-permute-start.19 = (f32[128,128]{1,0:T(8,128)S(1)}, f32[128,128]{1,0:T(8,128)S(1)}, u32[]{:S(2)}, u32[]{:S(2)}) collective-permute-start(f32[128,128]{1,0:T(8,128)S(1)} %get-tuple-element.76), channel_id=1, source_target_pairs={{0,8},{2,10},{4,12},{6,14},{1,9},{3,11},{5,13},{7,15},{16,24},{18,... | collective-permute-start | bytes 196616 | tf_op jit(solution)/shard_map/ppermute | solution.py:229
  152.4 5.8 %collective-permute-start.17 = (f32[128,128]{1,0:T(8,128)S(1)}, f32[128,128]{1,0:T(8,128)S(1)}, u32[]{:S(2)}, u32[]{:S(2)}) collective-permute-start(f32[128,128]{1,0:T(8,128)S(1)} %get-tuple-element.72), channel_id=1, source_target_pairs={{0,8},{2,10},{4,12},{6,14},{1,9},{3,11},{5,13},{7,15},{16,24},{18,... | collective-permute-start | bytes 196616 | tf_op jit(solution)/shard_map/ppermute | solution.py:229
  160.2 8.8 %collective-permute-start.20 = (bf16[384,256]{1,0:T(8,128)(2,1)S(1)}, bf16[384,256]{1,0:T(8,128)(2,1)S(1)}, u32[]{:S(2)}, u32[]{:S(2)}) collective-permute-start(bf16[384,256]{1,0:T(8,128)(2,1)S(1)} %get-tuple-element.82), channel_id=1, source_target_pairs={{0,2},{2,0},{4,6},{6,4},{8,10},{10,8},{12,14},{14,12},{1,3},{3,1},... | collective-permute-start | bytes 589832 | tf_op jit(solution)/shard_map/ppermute | solution.py:249
  161.0 8.0 %collective-permute-start.21 = (bf16[384,256]{1,0:T(8,128)(2,1)S(1)}, bf16[384,256]{1,0:T(8,128)(2,1)S(1)}, u32[]{:S(2)}, u32[]{:S(2)}) collective-permute-start(bf16[384,256]{1,0:T(8,128)(2,1)S(1)} %get-tuple-element.83), channel_id=1, source_target_pairs={{0,4},{2,6},{4,0},{6,2},{8,12},{10,14},{12,8},{14,10},{1,5},{3,7},... | collective-permute-start | bytes 589832 | tf_op jit(solution)/shard_map/ppermute | solution.py:249
  161.0 10.1 %collective-permute-start.22 = (bf16[384,256]{1,0:T(8,128)(2,1)S(1)}, bf16[384,256]{1,0:T(8,128)(2,1)S(1)}, u32[]{:S(2)}, u32[]{:S(2)}) collective-permute-start(bf16[384,256]{1,0:T(8,128)(2,1)S(1)} %get-tuple-element.84), channel_id=1, source_target_pairs={{0,6},{2,4},{4,2},{6,0},{8,14},{10,12},{12,10},{14,8},{1,7},{3,5},... | collective-permute-start | bytes 589832 | tf_op jit(solution)/shard_map/ppermute | solution.py:249
  171.1 2.8 %collective-permute-start.23 = (bf16[384,256]{1,0:T(8,128)(2,1)S(1)}, bf16[384,256]{1,0:T(8,128)(2,1)S(1)}, u32[]{:S(2)}, u32[]{:S(2)}) collective-permute-start(bf16[384,256]{1,0:T(8,128)(2,1)S(1)} %attend.2.refs_0_), channel_id=1, source_target_pairs={{0,1},{1,0},{2,3},{3,2},{4,5},{5,4},{6,7},{7,6},{8,9},{9,8},{10,11... | collective-permute-start | bytes 589832 | tf_op jit(solution)/shard_map/ppermute | solution.py:255
  171.1 2.8 %collective-permute-start.24 = (bf16[384,256]{1,0:T(8,128)(2,1)S(1)}, bf16[384,256]{1,0:T(8,128)(2,1)S(1)}, u32[]{:S(2)}, u32[]{:S(2)}) collective-permute-start(bf16[384,256]{1,0:T(8,128)(2,1)S(1)} %collective-permute-done.20.refs_1_), channel_id=1, source_target_pairs={{0,1},{1,0},{2,3},{3,2},{4,5},{5,4},{6,7},{7,6},{8,9},{9,8},{10,11... | collective-permute-start | bytes 589832 | tf_op jit(solution)/shard_map/ppermute | solution.py:255
  171.6 2.3 %collective-permute-start.25 = (bf16[384,256]{1,0:T(8,128)(2,1)S(1)}, bf16[384,256]{1,0:T(8,128)(2,1)S(1)}, u32[]{:S(2)}, u32[]{:S(2)}) collective-permute-start(bf16[384,256]{1,0:T(8,128)(2,1)S(1)} %collective-permute-done.21.refs_2_), channel_id=1, source_target_pairs={{0,1},{1,0},{2,3},{3,2},{4,5},{5,4},{6,7},{7,6},{8,9},{9,8},{10,11... | collective-permute-start | bytes 589832 | tf_op jit(solution)/shard_map/ppermute | solution.py:255
  171.6 2.3 %collective-permute-start.26 = (bf16[384,256]{1,0:T(8,128)(2,1)S(1)}, bf16[384,256]{1,0:T(8,128)(2,1)S(1)}, u32[]{:S(2)}, u32[]{:S(2)}) collective-permute-start(bf16[384,256]{1,0:T(8,128)(2,1)S(1)} %collective-permute-done.22.refs_3_), channel_id=1, source_target_pairs={{0,1},{1,0},{2,3},{3,2},{4,5},{5,4},{6,7},{7,6},{8,9},{9,8},{10,11... | collective-permute-start | bytes 589832 | tf_op jit(solution)/shard_map/ppermute | solution.py:255
  (12 other events, 28.6 us)

commit v5 on v4

--- a/solution.py
+++ b/solution.py
@@ -98,7 +98,7 @@
     )
 
 
-def stage(place, pieces, rows, width):
+def stage(place, pieces, blocks, rows, width):
     count = len(pieces)
     half = width // 2
 
@@ -106,100 +106,117 @@
         out, sems = refs[count], refs[count + 1]
         copies = []
         for i, ((array, r, column, far), ref) in enumerate(zip(pieces, refs)):
-            core = 1 - place_ref[2] if far else place_ref[2]
-            start = pl.multiple_of(core * half + column, HDIM)
-            copies.append(pltpu.make_async_copy(ref, out.at[r, :, pl.ds(start, array.shape[1])], sems.at[i]))
+            if far is None:
+                target = out.at[r]
+            else:
+                core = 1 - place_ref[2] if far else place_ref[2]
+                start = pl.multiple_of(core * half + column, HDIM)
+                target = out.at[r, :, pl.ds(start, array.shape[1])]
+            copies.append(pltpu.make_async_copy(ref, target, sems.at[i]))
         for copy in copies:
             copy.start()
         for copy in copies:
             copy.wait()
 
-    shape = pltpu.VMEM((SUB, rows, width), BF16)
+    shape = pltpu.VMEM((blocks, rows, width), BF16)
     sems = pltpu.SemaphoreType.DMA((count,))
-    return call(
-        kernel, "stage", shape, [SMEM] + [ANY] * count, VMEM, LIMIT, 0, SUB * rows * width * 4, [sems]
-    )(place, *[piece[0] for piece in pieces])
-
-
-def project(place, stream, kv):
-    _, rows, width = stream.shape
-
-    def kernel(place_ref, stream_ref, w_ref, key_ref, value_ref, before_ref, total_ref):
-        states = []
-        for r in range(SUB):
-            both = dot(stream_ref[r], w_ref[...])
-            key = silu(both[:, :HDIM]).astype(BF16)
-            value = both[:, HDIM:].astype(BF16)
-            key_ref[r] = key
-            value_ref[r] = value
-            states.append(dot(key, value, ((0,), (0,))))
-        total_ref[...] = (states[0] + states[1]) + (states[2] + states[3])
-        block = place_ref[0]
-        for r in range(SUB):
-            before = jnp.zeros((HDIM, HDIM), F32)
-            for other in range(SUB):
-                if other != r:
-                    is_before = jnp.bitwise_xor(block, other) < jnp.bitwise_xor(block, r)
-                    before = before + jnp.where(is_before, states[other], 0.0)
-            before_ref[r] = before
-
-    shape = jax.ShapeDtypeStruct((SUB, rows, HDIM), BF16)
-    shapes = [shape, shape, jax.ShapeDtypeStruct((SUB, HDIM, HDIM), F32), jax.ShapeDtypeStruct((HDIM, HDIM), F32)]
-    flops = 4 * SUB * rows * width * HDIM
-    return call(kernel, "project", shapes, [SMEM, VMEM, VMEM], [VMEM] * 4, LIMIT, flops, 2 * MIB)(place, stream, kv)
-
-
-def queries(place, stream, pieces):
-    _, rows, width = stream.shape
+    moved = blocks * rows * width * 4
+    return call(kernel, "stage", shape, [SMEM] + [ANY] * count, VMEM, LIMIT, 0, moved, [sems])(
+        place, *[piece[0] for piece in pieces]
+    )
+
+
+def project(stream, kv, total=None):
+    blocks, rows, width = stream.shape
+    kv = kv if isinstance(kv, list) else [kv]
+    cuts = [sum(w.shape[0] for w in kv[:i]) for i in range(len(kv) + 1)]
+
+    def kernel(stream_ref, *refs):
+        key_ref, value_ref, state_ref, total_ref = refs[-4:]
+        for r in range(blocks):
+            both = sum(dot(stream_ref[r, :, cuts[i] : cuts[i + 1]], refs[i][...]) for i in range(len(kv)))
+            key_ref[r] = silu(both[:, :HDIM]).astype(BF16)
+            value_ref[r] = both[:, HDIM:].astype(BF16)
+        added = jnp.zeros((HDIM, HDIM), F32) if total is None else refs[len(kv)][...]
+        for r in range(blocks):
+            state = dot(key_ref[r], value_ref[r], ((0,), (0,)))
+            state_ref[r] = state
+            added = added + state
+        total_ref[...] = added
+
+    shape = jax.ShapeDtypeStruct((blocks, rows, HDIM), BF16)
+    state = jax.ShapeDtypeStruct((blocks, HDIM, HDIM), F32)
+    shapes = [shape, shape, state, jax.ShapeDtypeStruct((HDIM, HDIM), F32)]
+    args = [stream, *kv] + ([] if total is None else [total])
+    flops = 4 * blocks * rows * width * HDIM
+    return call(kernel, "project", shapes, [VMEM] * len(args), [VMEM] * 4, LIMIT, flops, 2 * MIB)(*args)
+
+
+def queries(place, streams, pieces):
+    _, rows, width = streams[0].shape
     count = len(pieces)
     depth = pieces[0].shape[0]
 
-    def kernel(place_ref, stream_ref, *refs):
-        ins, out, w_held = refs[:count], refs[count], refs[count + 1]
+    def kernel(place_ref, *refs):
+        sources, ins = refs[: len(streams)], refs[len(streams) : len(streams) + count]
+        out, w_held = refs[-2:]
         for m, piece in enumerate(ins):
             row = pl.multiple_of(jnp.bitwise_xor(place_ref[3], m) * depth, depth)
             w_held[pl.ds(row, depth), :] = piece[...]
         swap = place_ref[1] == 1
-        for r in range(SUB):
-            both = silu(dot(stream_ref[r], w_held[...])).astype(BF16)
-            out[r, :, :HDIM] = jnp.where(swap, both[:, HDIM:], both[:, :HDIM])
-            out[r, :, HDIM:] = jnp.where(swap, both[:, :HDIM], both[:, HDIM:])
+        blocks = [(source, r) for source in sources for r in range(source.shape[0])]
+        for i, (source, r) in enumerate(blocks):
+            both = silu(dot(source[r], w_held[...])).astype(BF16)
+            out[i, :, :HDIM] = jnp.where(swap, both[:, HDIM:], both[:, :HDIM])
+            out[i, :, HDIM:] = jnp.where(swap, both[:, :HDIM], both[:, HDIM:])
 
     shape = jax.ShapeDtypeStruct((SUB, rows, 2 * HDIM), BF16)
     flops = 4 * SUB * rows * width * HDIM
     held = pltpu.VMEM((width, 2 * HDIM), BF16)
-    return call(
-        kernel, "queries", shape, [SMEM, VMEM] + [VMEM] * count, VMEM, LIMIT, flops, 2 * MIB, [held]
-    )(place, stream, *pieces)
-
-
-def attend(place, blocks, query, parts):
+    specs = [SMEM] + [VMEM] * (len(streams) + count)
+    return call(kernel, "queries", shape, specs, VMEM, LIMIT, flops, 2 * MIB, [held])(place, *streams, *pieces)
+
+
+def attend(place, blocks, query, heads):
     rows = query.shape[1]
     count = len(blocks)
+    flat, where = [], []
+    for parts, carried in heads:
+        index = []
+        for part in parts:
+            index += [(len(flat), r) for r in range(part[0].shape[0])]
+            flat += part
+        where.append((index, len(flat)))
+        flat.append(carried)
 
     def kernel(place_ref, query_ref, *refs):
-        ins, outs = refs[:8], refs[8:]
+        ins, outs = refs[: len(flat)], refs[len(flat) :]
         causal = lax.broadcasted_iota(jnp.int32, (rows, rows), 1) <= lax.broadcasted_iota(
             jnp.int32, (rows, rows), 0
         )
+        block = place_ref[0]
         for i, r in enumerate(blocks):
-            for h in range(2):
-                key_ref, value_ref, before_ref, carried_ref = ins[4 * h : 4 * h + 4]
-                columns = slice(h * HDIM, (h + 1) * HDIM)
-                q = query_ref[r, :, columns]
-                earlier = (before_ref[r] + carried_ref[...]).astype(BF16)
-                scores = dot(q, key_ref[r], ((1,), (1,)))
+            for h, (index, carried) in enumerate(where):
+                earlier = ins[carried][...]
+                for other in range(SUB):
+                    if other != r:
+                        is_before = jnp.bitwise_xor(block, other) < jnp.bitwise_xor(block, r)
+                        slot, j = index[other]
+                        earlier = earlier + jnp.where(is_before, ins[slot + 2][j], 0.0)
+                slot, j = index[r]
+                key, value = ins[slot][j], ins[slot + 1][j]
+                q = query_ref[r, :, h * HDIM : (h + 1) * HDIM]
+                scores = dot(q, key, ((1,), (1,)))
                 weights = jnp.where(causal, scores, 0.0).astype(BF16)
-                mixed = dot(weights, value_ref[r]) + dot(q, earlier)
+                mixed = dot(weights, value) + dot(q, earlier.astype(BF16))
                 scale = lax.rsqrt(jnp.mean(mixed * mixed, axis=-1, keepdims=True) + 1e-06)
                 target = pl.multiple_of(jnp.bitwise_xor(place_ref[1], h) * HDIM, HDIM)
                 outs[i][:, pl.ds(target, HDIM)] = (mixed * scale).astype(BF16)
 
     shapes = [jax.ShapeDtypeStruct((rows, 2 * HDIM), BF16)] * count
     flops = count * 4 * rows * HDIM * (2 * rows + HDIM)
-    return call(kernel, "attend", shapes, [SMEM] + [VMEM] * 9, [VMEM] * count, LIMIT, flops, 2 * MIB)(
-        place, query, *parts[0], *parts[1]
-    )
+    specs = [SMEM] + [VMEM] * (1 + len(flat))
+    return call(kernel, "attend", shapes, specs, [VMEM] * count, LIMIT, flops, 2 * MIB)(place, query, *flat)
 
 
 def add_features(pieces, weight, partial=None):
@@ -263,43 +280,52 @@
         whole = spread(jnp.concatenate(ordered * groups, axis=0)).reshape(n_ctx, -1, 2 * HDIM)
         return [lax.dynamic_index_in_dim(whole, ctx ^ m, keepdims=False) for m in range(n_ctx)]
 
+    def both_cores(value):
+        return lax.all_gather(value, "head", axis=1, tiled=True)
+
     cut = half * 11 // 16 // HDIM * HDIM
     across = xor(tokens, 2)
     beside = xor(tokens, 1)
+    far_tokens = other_core(tokens)
+    far_tokens, w_key, w_value = lax.optimization_barrier((far_tokens, w_key, w_value))
     kv_mine = spread(pack_keys_values(place, w_key, w_value, n_ctx))
-    q_sent = pack_queries(place, w_query)
-    w_far = other_core(take_rows(place, w_out))
-    far_tokens = other_core(tokens)
-    far_beside = other_core(beside)
-    across, beside, kv_mine, q_sent, w_far, far_tokens, far_beside = lax.optimization_barrier(
-        (across, beside, kv_mine, q_sent, w_far, far_tokens, far_beside)
-    )
+    across, beside, kv_mine, w_query, w_out = lax.optimization_barrier((across, beside, kv_mine, w_query, w_out))
+    middle = kv_mine.shape[0] // 2
+    kv_upper = other_part(kv_mine[:middle])
     left = xor(across[:, :cut], 1)
     right = xor(beside[:, cut:], 2)
-    kv_other = other_part(kv_mine)
-    far_across = other_core(across)
+    q_sent = pack_queries(place, w_query)
+    near = [(tokens, 0, 0, 0), (far_tokens, 0, 0, 1), (both_cores(beside), 1, 0, None), (both_cores(across), 2, 0, None)]
+    near = stage(place, near, SUB - 1, rows, 2 * half)
+    first = project(near, kv_mine)
+    arrived = {m: xor(q_sent[m % SUB], m) for m in (4, 6)} if n_ctx == 2 * SUB else {}
+    w_sent = take_rows(place, w_out)
+    left, right, arrived, q_sent, w_sent, kv_upper, kv_mine, first = lax.optimization_barrier(
+        (left, right, arrived, q_sent, w_sent, kv_upper, kv_mine, first)
+    )
+    kv_lower = other_part(kv_mine[middle:])
+    corner = []
+    for array, column in ((left, 0), (right, cut)):
+        corner += [(array, 0, column, 0), (other_core(array), 0, column, 1)]
+    corner = stage(place, corner, 1, rows, 2 * half)
+    last = project(corner, kv_mine, first[3])
     if n_ctx == 2 * SUB:
-        arrived = {0: q_sent[0]} | {m: xor(q_sent[m % SUB], m) for m in (4, 6)}
-        left, right, arrived, q_sent = lax.optimization_barrier((left, right, arrived, q_sent))
         arrived = arrived | {m: xor(q_sent[m % SUB], m) for m in (5, 7, 2, 3, 1)}
-        q_pieces = [arrived[m] for m in range(n_ctx)]
+        arrived, kv_lower, last, w_sent = lax.optimization_barrier((arrived, kv_lower, last, w_sent))
+        q_pieces = [q_sent[0]] + [arrived[m] for m in range(1, n_ctx)]
     else:
         q_pieces = gather_queries(q_sent)
-
-    pieces = [(tokens, 0, 0, False), (far_tokens, 0, 0, True), (beside, 1, 0, False), (far_beside, 1, 0, True)]
-    pieces += [(across, 2, 0, False), (far_across, 2, 0, True)]
-    for array, column in ((left, 0), (right, cut)):
-        pieces += [(array, 3, column, False), (other_core(array), 3, column, True)]
-    stream = stage(place, pieces, rows, 2 * half)
-
-    def keys_values(kv):
-        key, value, before, total = project(place, stream, kv)
-        return key, value, before, exclusive_prefix(total, groups)
-
-    parts = [keys_values(kv_mine), keys_values(kv_other)]
-    query = queries(place, stream, q_pieces)
-    away = attend(place, (3, 1, 2), query, parts)
-    home = attend(place, (0,), query, parts)
+    w_far = other_core(w_sent)
+
+    def head(near_part, corner_part):
+        return [near_part[:3], corner_part[:3]], exclusive_prefix(corner_part[3], groups)
+
+    kv_other = [kv_upper, kv_lower]
+    second = project(near, kv_other)
+    heads = [head(first, last), head(second, project(corner, kv_other, second[3]))]
+    query = queries(place, [near, corner], q_pieces)
+    away = attend(place, (3, 1, 2), query, heads)
+    home = attend(place, (0,), query, heads)
     normed = [home[0], xor(away[1], 1), xor(away[2], 2), xor(away[0], 3)]
     home_0, w_far = lax.optimization_barrier((home[0], w_far))
     out_keep, out_far = stage_rows(place, w_out, w_far)

time: 177 us -> 212 us (1.20)
  waiting for transfers between devices: 86.7 us -> 104 us
  between operations: 0.27 us -> 13.7 us
  Pallas kernels: 36.7 us -> 29.5 us
  local copies, waits for them, and re-layouts: 17.3 us -> 23.2 us
  starting transfers between devices: 35.8 us -> 40.7 us
    ppermute x14, waiting for transfers between devices: 85.2 us -> 94.4 us  [xor(): return lax.ppermute(value, 'ctx', [(i, i ^ step) for i in range(n_ctx)])]
    ppermute x14, starting transfers between devices: 19.6 us -> 26 us  [xor(): return lax.ppermute(value, 'ctx', [(i, i ^ step) for i in range(n_ctx)])]
    all_gather x0 -> x2, waiting for transfers between devices: none -> 5.74 us  [both_cores(): return lax.all_gather(value, 'head', axis=1, tiled=True)]
    pallas_call x6 -> x9, Pallas kernels: 25.1 us -> 19.8 us  [the longest x4 8.5 us: project(): call(kernel, 'project', shapes, [VMEM] * len(args), [VMEM] * 4, LIMIT, fl...]
    unnamed x32 -> x28, local copies, waits for them, and re-layouts: 9.84 us -> 13.1 us
    ppermute x2, starting transfers between devices: 5.77 us -> 2.77 us  [shift(): return lax.ppermute(v, 'ctx', pairs)]
  transfers between devices with their start and end apart: 28 -> 29, of which waited for: 7 -> 10; matrix products, arithmetic and copies ran while one was open for 1% -> 5% of each run, Pallas kernels for 18% -> 12%
where the time goes in v5:
time: 212 us; the launch traced here: 211 us
  waiting for transfers between devices  104 us (49%)
  starting transfers between devices  40.7 us (19%)
  Pallas kernels  29.5 us (14%)
  local copies, waits for them, and re-layouts  23.2 us (11%)
  between operations  13.7 us (6%)
    ppermute x14, waiting for transfers between devices, xor(): return lax.ppermute(value, 'ctx', [(i, i ^ step) for i in range(n_ctx)])  94.4 us
    ppermute x14, starting transfers between devices, xor(): return lax.ppermute(value, 'ctx', [(i, i ^ step) for i in range(n_ctx)])  26 us
    unnamed x28, local copies, waits for them, and re-layouts  13.1 us
    pallas_call x4, Pallas kernels, project(): call(kernel, 'project', shapes, [VMEM] * len(args), [VMEM] * 4, LIMIT, fl...  8.5 us
    all_to_all x1, starting transfers between devices, spread(): return lax.all_to_all(packed, 'ctx', 0, 0, tiled=True)  7.17 us
    all_gather x2, waiting for transfers between devices, both_cores(): return lax.all_gather(value, 'head', axis=1, tiled=True)  5.74 us
    pallas_call x1, Pallas kernels, queries(): call(kernel, 'queries', shape, specs, VMEM, LIMIT, flops, 2 * MIB, [held])  4.83 us
    dynamic_slice x1, local copies, waits for them, and re-layouts, take_rows(): return lax.dynamic_slice(w_out, (0, (1 - place[2]) * half), (rows, half))  4.76 us
  transfers between devices with their start and end apart: 29, of which 10 were waited for; matrix products, arithmetic and copies ran while one was open for 5% of the time, Pallas kernels for 12%

profile of v5, /device:TPU:0, one launch (start us, length us, event | category | flops | bytes accessed | tf_op | source)
XLA Modules:
  0.0 211.2 jit_solution(9916920934530789552)
XLA Ops:
  7.1 3.2 %collective-permute-done.2.refs_1_ = bf16[384,2048]{1,0:T(8,128)(2,1)S(1)} collective-permute-done((bf16[384,2048]{1,0:T(8,128)(2,1)}, bf16[384,2048]{1,0:T(8,128)(2,1)S(1)}, u32[]{:S(2)}, u32[]{:S(2)}) %collective-permute-start.2) | collective-permute-done | bytes 1572896 | tf_op jit(solution)/shard_map/ppermute | solution.py:272
  14.9 7.2 %all-to-all-start = ((bf16[8,512,256]{2,1,0:T(8,128)(2,1)}), bf16[8,512,256]{2,1,0:T(8,128)(2,1)S(1)}, u32[]{:S(2)}, u32[]{:S(2)}) async-start(bf16[8,512,256]{2,1,0:T(8,128)(2,1)} %bitcast.10), calls=%async_computation | async-start | bytes 4194304 | tf_op jit(solution)/shard_map/all_to_all | solution.py:275
  22.1 2.0 collective-permute-start
  25.5 66.7 %collective-permute-done = bf16[384,2048]{1,0:T(8,128)(2,1)} collective-permute-done((bf16[384,2048]{1,0:T(8,128)(2,1)}, bf16[384,2048]{1,0:T(8,128)(2,1)}, u32[]{:S(2)}, u32[]{:S(2)}) %collective-permute-start) | collective-permute-done | bytes 1572896 | tf_op jit(solution)/shard_map/ppermute | solution.py:266
  93.0 2.3 %slice.12 = bf16[384,1408]{1,0:T(8,128)(2,1)} slice(bf16[384,2048]{1,0:T(8,128)(2,1)} %collective-permute-done), slice={[0:384], [0:1408]} | slice | bytes 2162688 | tf_op jit(solution)/shard_map/slice | solution.py:295
  95.4 1.5 collective-permute-start.3
  97.9 1.5 collective-permute-start.7
  99.4 1.9 slice.13
  105.4 2.5 %collective-permute-start.5 = (bf16[512,256]{1,0:T(8,128)(2,1)S(1)}, bf16[512,256]{1,0:T(8,128)(2,1)}, u32[]{:S(2)}, u32[]{:S(2)}) collective-permute-start(bf16[512,256]{1,0:T(8,128)(2,1)S(1)} %get-tuple-element.92.refs_2_), channel_id=1, source_target_pairs={{0,8},{2,10},{4,12},{6,14},{8,0},{10,2},{12,4},{14,6},{1,9},{3,11}... | collective-permute-start | bytes 786440 | tf_op jit(solution)/shard_map/ppermute | solution.py:266
  109.1 4.8 %constant_dynamic-slice_fusion = bf16[1024,2048]{1,0:T(8,128)(2,1)} fusion(bf16[1024,4096]{1,0:T(8,128)(2,1)} %out_ref, s32[]{:T(128)S(6)} %select_n.11), kind=kLoop, calls=%fused_computation.1 | loop fusion | bytes 8388612 | tf_op jit(solution)/shard_map/dynamic_slice | solution.py:73
  113.8 5.7 %all-gather.5.cloned.1.call-done.refs_3_ = bf16[384,4096]{1,0:T(8,128)(2,1)} async-done(((bf16[384,2048]{1,0:T(8,128)(2,1)}), bf16[384,4096]{1,0:T(8,128)(2,1)}) %all-gather.5.cloned.1.call-update) | async-done | bytes 3145744 | tf_op jit(solution)/shard_map/all_gather | solution.py:284
  119.6 1.9 copy-done.1
  121.5 1.9 copy-done.2
  127.5 3.0 %project.4 = (bf16[3,384,128]{2,1,0:T(8,128)(2,1)S(1)}, bf16[3,384,128]{2,1,0:T(8,128)(2,1)S(1)}, f32[3,128,128]{2,1,0:T(8,128)S(1)}, f32[128,128]{1,0:T(8,128)S(1)}) custom-call(bf16[3,384,4096]{2,1,0:T(8,128)(2,1)S(1)} %stage.2.stream_ref.refs_0_, bf16[4096,256]{1,0:T(8,128)(2,1)S(1)} %bitcast.7), custom_call_target="tpu_custom_call" | custom-call | flops 2415919104 | bytes 2097152 | tf_op jit(solution)/shard_map/project/pallas_call | solution.py:152
  131.1 1.7 collective-permute-start.15
  132.8 1.5 collective-permute-start.10
  134.2 2.4 %collective-permute-start.13 = (bf16[512,256]{1,0:T(8,128)(2,1)S(1)}, bf16[512,256]{1,0:T(8,128)(2,1)S(1)}, u32[]{:S(2)}, u32[]{:S(2)}) collective-permute-start(bf16[512,256]{1,0:T(8,128)(2,1)S(1)} %copy-done.12), channel_id=1, source_target_pairs={{0,10},{2,8},{4,14},{6,12},{8,2},{10,0},{12,6},{14,4},{1,11},{3,9}... | collective-permute-start | bytes 786440 | tf_op jit(solution)/shard_map/ppermute | solution.py:266
  136.6 5.9 %collective-permute-done.10.refs_3_ = bf16[512,256]{1,0:T(8,128)(2,1)S(1)} collective-permute-done((bf16[512,256]{1,0:T(8,128)(2,1)S(1)}, bf16[512,256]{1,0:T(8,128)(2,1)S(1)}, u32[]{:S(2)}, u32[]{:S(2)}) %collective-permute-start.10) | collective-permute-done | bytes 262176 | tf_op jit(solution)/shard_map/ppermute | solution.py:266
  142.5 6.1 %collective-permute-start.11 = (bf16[512,256]{1,0:T(8,128)(2,1)}, bf16[512,256]{1,0:T(8,128)(2,1)S(1)}, u32[]{:S(2)}, u32[]{:S(2)}) collective-permute-start(bf16[512,256]{1,0:T(8,128)(2,1)} %get-tuple-element.94), channel_id=1, source_target_pairs={{0,4},{2,6},{4,0},{6,2},{8,12},{10,14},{12,8},{14,10},{1,5},{3,7},... | collective-permute-start | bytes 786440 | tf_op jit(solution)/shard_map/ppermute | solution.py:266
  149.6 2.4 %collective-permute-start.14 = (bf16[512,256]{1,0:T(8,128)(2,1)S(1)}, bf16[512,256]{1,0:T(8,128)(2,1)S(1)}, u32[]{:S(2)}, u32[]{:S(2)}) collective-permute-start(bf16[512,256]{1,0:T(8,128)(2,1)S(1)} %copy-done.10), channel_id=1, source_target_pairs={{0,14},{2,12},{4,10},{6,8},{8,6},{10,4},{12,2},{14,0},{1,15},{3,13... | collective-permute-start | bytes 786440 | tf_op jit(solution)/shard_map/ppermute | solution.py:266
  152.0 2.0 stage.3.stream_ref.refs_1_
  155.9 7.3 %collective-permute-done.12.refs_5_ = bf16[512,256]{1,0:T(8,128)(2,1)S(1)} collective-permute-done((bf16[512,256]{1,0:T(8,128)(2,1)S(1)}, bf16[512,256]{1,0:T(8,128)(2,1)S(1)}, u32[]{:S(2)}, u32[]{:S(2)}) %collective-permute-start.12) | collective-permute-done | bytes 262176 | tf_op jit(solution)/shard_map/ppermute | solution.py:266
  163.2 8.1 %collective-permute-done.14.refs_9_ = bf16[512,256]{1,0:T(8,128)(2,1)S(1)} collective-permute-done((bf16[512,256]{1,0:T(8,128)(2,1)S(1)}, bf16[512,256]{1,0:T(8,128)(2,1)S(1)}, u32[]{:S(2)}, u32[]{:S(2)}) %collective-permute-start.14) | collective-permute-done | bytes 262176 | tf_op jit(solution)/shard_map/ppermute | solution.py:266
  171.4 3.0 %project.6 = (bf16[3,384,128]{2,1,0:T(8,128)(2,1)S(1)}, bf16[3,384,128]{2,1,0:T(8,128)(2,1)S(1)}, f32[3,128,128]{2,1,0:T(8,128)S(1)}, f32[128,128]{1,0:T(8,128)S(1)}) custom-call(bf16[3,384,4096]{2,1,0:T(8,128)(2,1)S(1)} %stage.2.stream_ref.refs_0_, bf16[2048,256]{1,0:T(8,128)(2,1)S(1)} %collective-permute-done.7.refs_0_, ...), custom_call_target="tpu_custom_call" | custom-call | flops 2415919104 | bytes 2097152 | tf_op jit(solution)/shard_map/project/pallas_call | solution.py:152
  176.9 1.5 collective-permute-start.16
  178.4 4.8 %queries.1.query_ref = bf16[4,384,256]{2,1,0:T(8,128)(2,1)S(1)} custom-call(s32[4]{0:T(128)S(1)} %pad_add_fusion.place_ref, bf16[3,384,4096]{2,1,0:T(8,128)(2,1)S(1)} %stage.2.stream_ref.refs_0_, bf16[1,384,4096]{2,1,0:T(8,128)(2,1)S(1)} %stage.3.stream_ref.refs_1_, bf16[512,256]{1,0:T(8,128)(2,1)S(1)} %get-tuple-element.92.refs_2_, ...), custom_call_target="tpu_custom_call" | custom-call | flops 3221225472 | bytes 2097152 | tf_op jit(solution)/shard_map/queries/pallas_call | solution.py:177
  183.3 2.0 attend.3
  185.9 2.6 %collective-permute-start.20 = (bf16[384,256]{1,0:T(8,128)(2,1)S(1)}, bf16[384,256]{1,0:T(8,128)(2,1)S(1)}, u32[]{:S(2)}, u32[]{:S(2)}) collective-permute-start(bf16[384,256]{1,0:T(8,128)(2,1)S(1)} %get-tuple-element.135), channel_id=1, source_target_pairs={{0,4},{2,6},{4,0},{6,2},{8,12},{10,14},{12,8},{14,10},{1,5},{3,7},... | collective-permute-start | bytes 589832 | tf_op jit(solution)/shard_map/ppermute | solution.py:266
  190.6 2.8 %stage_rows.1 = (bf16[4,256,2048]{2,1,0:T(8,128)(2,1)S(1)}, bf16[4,256,2048]{2,1,0:T(8,128)(2,1)S(1)}) custom-call(s32[4]{0:T(128)S(1)} %pad_add_fusion.place_ref, bf16[1024,4096]{1,0:T(8,128)(2,1)} %out_ref, bf16[1024,2048]{1,0:T(8,128)(2,1)S(1)} %collective-permute-done.18.far_ref), custom_call_target="tpu_custom_call" | custom-call | bytes 16777216 | tf_op jit(solution)/shard_map/stage_rows/pallas_call | solution.py:96
  194.2 4.4 %collective-permute-done.21.refs_3_ = bf16[384,256]{1,0:T(8,128)(2,1)S(1)} collective-permute-done((bf16[384,256]{1,0:T(8,128)(2,1)S(1)}, bf16[384,256]{1,0:T(8,128)(2,1)S(1)}, u32[]{:S(2)}, u32[]{:S(2)}) %collective-permute-start.21) | collective-permute-done | bytes 196640 | tf_op jit(solution)/shard_map/ppermute | solution.py:266
  199.6 1.8 add_features.2.refs_5_
  201.5 2.9 %add_features.3 = bf16[384,2048]{1,0:T(8,128)(2,1)} custom-call(bf16[384,256]{1,0:T(8,128)(2,1)S(1)} %collective-permute-done.22.refs_0_, bf16[384,256]{1,0:T(8,128)(2,1)S(1)} %collective-permute-done.23.refs_1_, bf16[384,256]{1,0:T(8,128)(2,1)S(1)} %collective-permute-done.24.refs_2_, bf16[384,256]{1,0:T(8,128)(2,1)S(1)} %collective-permute-done.25.refs_3_, ...), custom_call_target="tpu_custom_call" | custom-call | flops 1610612736 | bytes 8388608 | tf_op jit(solution)/shard_map/add_features/pallas_call | solution.py:240
  (76 shorter events, 28.4 us)
Async XLA Ops:
  6.5 3.7 %collective-permute-start.2 = (bf16[384,2048]{1,0:T(8,128)(2,1)}, bf16[384,2048]{1,0:T(8,128)(2,1)S(1)}, u32[]{:S(2)}, u32[]{:S(2)}) collective-permute-start(bf16[384,2048]{1,0:T(8,128)(2,1)} %refs_0_.1), channel_id=1, source_target_pairs={{0,1},{1,0},{2,3},{3,2},{4,5},{5,4},{6,7},{7,6},{8,9},{9,8},{10,11... | collective-permute-start | bytes 4718600 | tf_op jit(solution)/shard_map/ppermute | solution.py:272
  14.9 77.4 %all-to-all-start = ((bf16[8,512,256]{2,1,0:T(8,128)(2,1)}), bf16[8,512,256]{2,1,0:T(8,128)(2,1)S(1)}, u32[]{:S(2)}, u32[]{:S(2)}) async-start(bf16[8,512,256]{2,1,0:T(8,128)(2,1)} %bitcast.10), calls=%async_computation | async-start | bytes 4194304 | tf_op jit(solution)/shard_map/all_to_all | solution.py:275
  22.0 91.8 %all-gather.3.cloned.1.call-start = ((), (), s32[]{:S(2)}) async-start(), calls=%async_computation.1 | async-start | bytes 4718592 | tf_op jit(solution)/shard_map/all_gather | solution.py:284
  22.1 70.2 %collective-permute-start = (bf16[384,2048]{1,0:T(8,128)(2,1)}, bf16[384,2048]{1,0:T(8,128)(2,1)}, u32[]{:S(2)}, u32[]{:S(2)}) collective-permute-start(bf16[384,2048]{1,0:T(8,128)(2,1)} %refs_0_.1), channel_id=1, source_target_pairs={{0,4},{2,6},{4,0},{6,2},{8,12},{10,14},{12,8},{14,10},{1,5},{3,7},... | collective-permute-start | bytes 4718600 | tf_op jit(solution)/shard_map/ppermute | solution.py:266
  24.1 68.2 %collective-permute-start.1 = (bf16[384,2048]{1,0:T(8,128)(2,1)}, bf16[384,2048]{1,0:T(8,128)(2,1)}, u32[]{:S(2)}, u32[]{:S(2)}) collective-permute-start(bf16[384,2048]{1,0:T(8,128)(2,1)} %refs_0_.1), channel_id=1, source_target_pairs={{0,2},{2,0},{4,6},{6,4},{8,10},{10,8},{12,14},{14,12},{1,3},{3,1},... | collective-permute-start | bytes 4718600 | tf_op jit(solution)/shard_map/ppermute | solution.py:266
  92.3 27.3 %all-gather.5.cloned.1.call-start = ((), (), s32[]{:S(2)}) async-start(), calls=%async_computation.2 | async-start | bytes 4718592 | tf_op jit(solution)/shard_map/all_gather | solution.py:284
  95.4 35.6 %collective-permute-start.3 = (bf16[384,1408]{1,0:T(8,128)(2,1)}, bf16[384,1408]{1,0:T(8,128)(2,1)}, u32[]{:S(2)}, u32[]{:S(2)}) collective-permute-start(bf16[384,1408]{1,0:T(8,128)(2,1)} %slice.12), channel_id=1, source_target_pairs={{0,2},{2,0},{4,6},{6,4},{8,10},{10,8},{12,14},{14,12},{1,3},{3,1},... | collective-permute-start | bytes 3244040 | tf_op jit(solution)/shard_map/ppermute | solution.py:266
  97.9 33.1 %collective-permute-start.7 = (bf16[2048,256]{1,0:T(8,128)(2,1)}, bf16[2048,256]{1,0:T(8,128)(2,1)S(1)}, u32[]{:S(2)}, u32[]{:S(2)}) collective-permute-start(bf16[2048,256]{1,0:T(8,128)(2,1)} %slice.14), channel_id=1, source_target_pairs={{0,16},{16,0},{1,17},{17,1},{2,18},{18,2},{3,19},{19,3},{4,20},{20... | collective-permute-start | bytes 3145736 | tf_op jit(solution)/shard_map/ppermute | solution.py:269
  105.4 25.0 %collective-permute-start.5 = (bf16[512,256]{1,0:T(8,128)(2,1)S(1)}, bf16[512,256]{1,0:T(8,128)(2,1)}, u32[]{:S(2)}, u32[]{:S(2)}) collective-permute-start(bf16[512,256]{1,0:T(8,128)(2,1)S(1)} %get-tuple-element.92.refs_2_), channel_id=1, source_target_pairs={{0,8},{2,10},{4,12},{6,14},{8,0},{10,2},{12,4},{14,6},{1,9},{3,11}... | collective-permute-start | bytes 786440 | tf_op jit(solution)/shard_map/ppermute | solution.py:266
  107.9 22.5 %collective-permute-start.6 = (bf16[512,256]{1,0:T(8,128)(2,1)}, bf16[512,256]{1,0:T(8,128)(2,1)}, u32[]{:S(2)}, u32[]{:S(2)}) collective-permute-start(bf16[512,256]{1,0:T(8,128)(2,1)} %get-tuple-element.94), channel_id=1, source_target_pairs={{0,12},{2,14},{4,8},{6,10},{8,4},{10,6},{12,0},{14,2},{1,13},{3,15... | collective-permute-start | bytes 786440 | tf_op jit(solution)/shard_map/ppermute | solution.py:266
  109.1 21.9 %collective-permute-start.4 = (bf16[384,640]{1,0:T(8,128)(2,1)}, bf16[384,640]{1,0:T(8,128)(2,1)}, u32[]{:S(2)}, u32[]{:S(2)}) collective-permute-start(bf16[384,640]{1,0:T(8,128)(2,1)} %slice.13), channel_id=1, source_target_pairs={{0,4},{2,6},{4,0},{6,2},{8,12},{10,14},{12,8},{14,10},{1,5},{3,7},... | collective-permute-start | bytes 1474568 | tf_op jit(solution)/shard_map/ppermute | solution.py:266
  127.5 5.3 %copy-start.12 = (bf16[512,256]{1,0:T(8,128)(2,1)S(1)}, bf16[512,256]{1,0:T(8,128)(2,1)}, u32[]{:S(2)}) copy-start(bf16[512,256]{1,0:T(8,128)(2,1)} %copy-done.11) | copy-start | bytes 786436
  127.5 21.1 %copy-start.10 = (bf16[512,256]{1,0:T(8,128)(2,1)S(1)}, bf16[512,256]{1,0:T(8,128)(2,1)}, u32[]{:S(2)}) copy-start(bf16[512,256]{1,0:T(8,128)(2,1)} %copy-done.9) | copy-start | bytes 786436
  131.0 18.6 %collective-permute-start.8 = (bf16[384,1408]{1,0:T(8,128)(2,1)}, bf16[384,1408]{1,0:T(8,128)(2,1)S(1)}, u32[]{:S(2)}, u32[]{:S(2)}) collective-permute-start(bf16[384,1408]{1,0:T(8,128)(2,1)} %collective-permute-done.3.refs_0_), channel_id=1, source_target_pairs={{0,1},{1,0},{2,3},{3,2},{4,5},{5,4},{6,7},{7,6},{8,9},{9,8},{10,11... | collective-permute-start | bytes 3244040 | tf_op jit(solution)/shard_map/ppermute | solution.py:272
  131.1 40.3 %collective-permute-start.15 = (bf16[2048,256]{1,0:T(8,128)(2,1)S(1)}, bf16[2048,256]{1,0:T(8,128)(2,1)S(1)}, u32[]{:S(2)}, u32[]{:S(2)}) collective-permute-start(bf16[2048,256]{1,0:T(8,128)(2,1)S(1)} %slice.15), channel_id=1, source_target_pairs={{0,16},{16,0},{1,17},{17,1},{2,18},{18,2},{3,19},{19,3},{4,20},{20... | collective-permute-start | bytes 3145736 | tf_op jit(solution)/shard_map/ppermute | solution.py:269
  132.8 15.8 %collective-permute-start.9 = (bf16[384,640]{1,0:T(8,128)(2,1)}, bf16[384,640]{1,0:T(8,128)(2,1)S(1)}, u32[]{:S(2)}, u32[]{:S(2)}) collective-permute-start(bf16[384,640]{1,0:T(8,128)(2,1)} %collective-permute-done.4.refs_2_), channel_id=1, source_target_pairs={{0,1},{1,0},{2,3},{3,2},{4,5},{5,4},{6,7},{7,6},{8,9},{9,8},{10,11... | collective-permute-start | bytes 1474568 | tf_op jit(solution)/shard_map/ppermute | solution.py:272
  132.8 9.7 %collective-permute-start.10 = (bf16[512,256]{1,0:T(8,128)(2,1)S(1)}, bf16[512,256]{1,0:T(8,128)(2,1)S(1)}, u32[]{:S(2)}, u32[]{:S(2)}) collective-permute-start(bf16[512,256]{1,0:T(8,128)(2,1)S(1)} %copy-done.12), channel_id=1, source_target_pairs={{0,2},{2,0},{4,6},{6,4},{8,10},{10,8},{12,14},{14,12},{1,3},{3,1},... | collective-permute-start | bytes 786440 | tf_op jit(solution)/shard_map/ppermute | solution.py:266
  134.2 29.0 %collective-permute-start.13 = (bf16[512,256]{1,0:T(8,128)(2,1)S(1)}, bf16[512,256]{1,0:T(8,128)(2,1)S(1)}, u32[]{:S(2)}, u32[]{:S(2)}) collective-permute-start(bf16[512,256]{1,0:T(8,128)(2,1)S(1)} %copy-done.12), channel_id=1, source_target_pairs={{0,10},{2,8},{4,14},{6,12},{8,2},{10,0},{12,6},{14,4},{1,11},{3,9}... | collective-permute-start | bytes 786440 | tf_op jit(solution)/shard_map/ppermute | solution.py:266
  142.5 13.4 %collective-permute-start.11 = (bf16[512,256]{1,0:T(8,128)(2,1)}, bf16[512,256]{1,0:T(8,128)(2,1)S(1)}, u32[]{:S(2)}, u32[]{:S(2)}) collective-permute-start(bf16[512,256]{1,0:T(8,128)(2,1)} %get-tuple-element.94), channel_id=1, source_target_pairs={{0,4},{2,6},{4,0},{6,2},{8,12},{10,14},{12,8},{14,10},{1,5},{3,7},... | collective-permute-start | bytes 786440 | tf_op jit(solution)/shard_map/ppermute | solution.py:266
  148.6 14.7 %collective-permute-start.12 = (bf16[512,256]{1,0:T(8,128)(2,1)S(1)}, bf16[512,256]{1,0:T(8,128)(2,1)S(1)}, u32[]{:S(2)}, u32[]{:S(2)}) collective-permute-start(bf16[512,256]{1,0:T(8,128)(2,1)S(1)} %copy-done.10), channel_id=1, source_target_pairs={{0,6},{2,4},{4,2},{6,0},{8,14},{10,12},{12,10},{14,8},{1,7},{3,5},... | collective-permute-start | bytes 786440 | tf_op jit(solution)/shard_map/ppermute | solution.py:266
  149.6 21.8 %collective-permute-start.14 = (bf16[512,256]{1,0:T(8,128)(2,1)S(1)}, bf16[512,256]{1,0:T(8,128)(2,1)S(1)}, u32[]{:S(2)}, u32[]{:S(2)}) collective-permute-start(bf16[512,256]{1,0:T(8,128)(2,1)S(1)} %copy-done.10), channel_id=1, source_target_pairs={{0,14},{2,12},{4,10},{6,8},{8,6},{10,4},{12,2},{14,0},{1,15},{3,13... | collective-permute-start | bytes 786440 | tf_op jit(solution)/shard_map/ppermute | solution.py:266
  153.9 17.4 %copy-start.13 = (bf16[1024,2048]{1,0:T(8,128)(2,1)S(1)}, bf16[1024,2048]{1,0:T(8,128)(2,1)}, u32[]{:S(2)}) copy-start(bf16[1024,2048]{1,0:T(8,128)(2,1)} %constant_dynamic-slice_fusion) | copy-start | bytes 12582916
  171.3 19.3 %collective-permute-start.18 = (bf16[1024,2048]{1,0:T(8,128)(2,1)S(1)}, bf16[1024,2048]{1,0:T(8,128)(2,1)S(1)}, u32[]{:S(2)}, u32[]{:S(2)}) collective-permute-start(bf16[1024,2048]{1,0:T(8,128)(2,1)S(1)} %copy-done.13), channel_id=1, source_target_pairs={{0,1},{1,0},{2,3},{3,2},{4,5},{5,4},{6,7},{7,6},{8,9},{9,8},{10,11... | collective-permute-start | bytes 12582920 | tf_op jit(solution)/shard_map/ppermute | solution.py:272
  175.6 7.6 %collective-permute-start.17 = (f32[128,128]{1,0:T(8,128)S(1)}, f32[128,128]{1,0:T(8,128)S(1)}, u32[]{:S(2)}, u32[]{:S(2)}) collective-permute-start(f32[128,128]{1,0:T(8,128)S(1)} %get-tuple-element.128), channel_id=1, source_target_pairs={{0,8},{2,10},{4,12},{6,14},{1,9},{3,11},{5,13},{7,15},{16,24},{18,... | collective-permute-start | bytes 196616 | tf_op jit(solution)/shard_map/ppermute | solution.py:246
  176.9 6.3 %collective-permute-start.16 = (f32[128,128]{1,0:T(8,128)S(1)}, f32[128,128]{1,0:T(8,128)S(1)}, u32[]{:S(2)}, u32[]{:S(2)}) collective-permute-start(f32[128,128]{1,0:T(8,128)S(1)} %get-tuple-element.118), channel_id=1, source_target_pairs={{0,8},{2,10},{4,12},{6,14},{1,9},{3,11},{5,13},{7,15},{16,24},{18,... | collective-permute-start | bytes 196616 | tf_op jit(solution)/shard_map/ppermute | solution.py:246
  185.3 8.2 %collective-permute-start.19 = (bf16[384,256]{1,0:T(8,128)(2,1)S(1)}, bf16[384,256]{1,0:T(8,128)(2,1)S(1)}, u32[]{:S(2)}, u32[]{:S(2)}) collective-permute-start(bf16[384,256]{1,0:T(8,128)(2,1)S(1)} %get-tuple-element.134), channel_id=1, source_target_pairs={{0,2},{2,0},{4,6},{6,4},{8,10},{10,8},{12,14},{14,12},{1,3},{3,1},... | collective-permute-start | bytes 589832 | tf_op jit(solution)/shard_map/ppermute | solution.py:266
  185.9 8.3 %collective-permute-start.20 = (bf16[384,256]{1,0:T(8,128)(2,1)S(1)}, bf16[384,256]{1,0:T(8,128)(2,1)S(1)}, u32[]{:S(2)}, u32[]{:S(2)}) collective-permute-start(bf16[384,256]{1,0:T(8,128)(2,1)S(1)} %get-tuple-element.135), channel_id=1, source_target_pairs={{0,4},{2,6},{4,0},{6,2},{8,12},{10,14},{12,8},{14,10},{1,5},{3,7},... | collective-permute-start | bytes 589832 | tf_op jit(solution)/shard_map/ppermute | solution.py:266
  188.5 10.1 %collective-permute-start.21 = (bf16[384,256]{1,0:T(8,128)(2,1)S(1)}, bf16[384,256]{1,0:T(8,128)(2,1)S(1)}, u32[]{:S(2)}, u32[]{:S(2)}) collective-permute-start(bf16[384,256]{1,0:T(8,128)(2,1)S(1)} %get-tuple-element.136), channel_id=1, source_target_pairs={{0,6},{2,4},{4,2},{6,0},{8,14},{10,12},{12,10},{14,8},{1,7},{3,5},... | collective-permute-start | bytes 589832 | tf_op jit(solution)/shard_map/ppermute | solution.py:266
  198.6 2.8 %collective-permute-start.22 = (bf16[384,256]{1,0:T(8,128)(2,1)S(1)}, bf16[384,256]{1,0:T(8,128)(2,1)S(1)}, u32[]{:S(2)}, u32[]{:S(2)}) collective-permute-start(bf16[384,256]{1,0:T(8,128)(2,1)S(1)} %attend.2.refs_0_), channel_id=1, source_target_pairs={{0,1},{1,0},{2,3},{3,2},{4,5},{5,4},{6,7},{7,6},{8,9},{9,8},{10,11... | collective-permute-start | bytes 589832 | tf_op jit(solution)/shard_map/ppermute | solution.py:272
  198.6 2.8 %collective-permute-start.23 = (bf16[384,256]{1,0:T(8,128)(2,1)S(1)}, bf16[384,256]{1,0:T(8,128)(2,1)S(1)}, u32[]{:S(2)}, u32[]{:S(2)}) collective-permute-start(bf16[384,256]{1,0:T(8,128)(2,1)S(1)} %collective-permute-done.19.refs_1_), channel_id=1, source_target_pairs={{0,1},{1,0},{2,3},{3,2},{4,5},{5,4},{6,7},{7,6},{8,9},{9,8},{10,11... | collective-permute-start | bytes 589832 | tf_op jit(solution)/shard_map/ppermute | solution.py:272
  199.1 2.3 %collective-permute-start.24 = (bf16[384,256]{1,0:T(8,128)(2,1)S(1)}, bf16[384,256]{1,0:T(8,128)(2,1)S(1)}, u32[]{:S(2)}, u32[]{:S(2)}) collective-permute-start(bf16[384,256]{1,0:T(8,128)(2,1)S(1)} %collective-permute-done.20.refs_2_), channel_id=1, source_target_pairs={{0,1},{1,0},{2,3},{3,2},{4,5},{5,4},{6,7},{7,6},{8,9},{9,8},{10,11... | collective-permute-start | bytes 589832 | tf_op jit(solution)/shard_map/ppermute | solution.py:272
  199.1 2.3 %collective-permute-start.25 = (bf16[384,256]{1,0:T(8,128)(2,1)S(1)}, bf16[384,256]{1,0:T(8,128)(2,1)S(1)}, u32[]{:S(2)}, u32[]{:S(2)}) collective-permute-start(bf16[384,256]{1,0:T(8,128)(2,1)S(1)} %collective-permute-done.21.refs_3_), channel_id=1, source_target_pairs={{0,1},{1,0},{2,3},{3,2},{4,5},{5,4},{6,7},{7,6},{8,9},{9,8},{10,11... | collective-permute-start | bytes 589832 | tf_op jit(solution)/shard_map/ppermute | solution.py:272
  (11 other events, 15.3 us)
Sparse Core Ops, SparseCore 0:
  92.4 12.2 all-gather.2
  106.2 13.2 all-gather.4

commit v6 on v5

--- a/solution.py
+++ b/solution.py
@@ -67,25 +67,18 @@
     return call(kernel, "pack_queries", shapes, [SMEM, VMEM], [VMEM] * SUB, LIMIT, 0, moved)(place, w_query)
 
 
-def take_rows(place, w_out):
+def stage_rows(place, w_out, w_far):
     rows, width = w_out.shape
-    half = width // 2
-    return lax.dynamic_slice(w_out, (0, (1 - place[2]) * half), (rows, half))
-
-
-def stage_rows(place, w_out, w_far):
-    rows, half = w_far.shape
-    depth = rows // SUB
+    depth, half = rows // SUB, width // 2
 
     def kernel(place_ref, out_ref, far_ref, keep, far, sems):
         column = pl.multiple_of(place_ref[2] * half, half)
         copies = []
         for r in range(SUB):
             row = pl.multiple_of(jnp.bitwise_xor(place_ref[0], r) * depth, depth)
-            copies.append(
-                pltpu.make_async_copy(out_ref.at[pl.ds(row, depth), pl.ds(column, half)], keep.at[r], sems.at[r])
-            )
-            copies.append(pltpu.make_async_copy(far_ref.at[pl.ds(row, depth), :], far.at[r], sems.at[SUB + r]))
+            for i, (source, target) in enumerate(((out_ref, keep), (far_ref, far))):
+                block = source.at[pl.ds(row, depth), pl.ds(column, half)]
+                copies.append(pltpu.make_async_copy(block, target.at[r], sems.at[2 * r + i]))
         for copy in copies:
             copy.start()
         for copy in copies:
@@ -93,7 +86,7 @@
 
     shapes = [pltpu.VMEM((SUB, depth, half), BF16)] * 2
     sems = pltpu.SemaphoreType.DMA((2 * SUB,))
-    return call(kernel, "stage_rows", shapes, [SMEM, ANY, ANY], [VMEM] * 2, 40, 0, rows * half * 8, [sems])(
+    return call(kernel, "stage_rows", shapes, [SMEM, ANY, ANY], [VMEM] * 2, 40, 0, rows * width * 4, [sems])(
         place, w_out, w_far
     )
 
@@ -121,7 +114,7 @@
     shape = pltpu.VMEM((blocks, rows, width), BF16)
     sems = pltpu.SemaphoreType.DMA((count,))
     moved = blocks * rows * width * 4
-    return call(kernel, "stage", shape, [SMEM] + [ANY] * count, VMEM, LIMIT, 0, moved, [sems])(
+    return call(kernel, "stage", shape, [SMEM] + [ANY] * count, VMEM, 36 if blocks > 1 else LIMIT, 0, moved, [sems])(
         place, *[piece[0] for piece in pieces]
     )
 
@@ -280,49 +273,45 @@
         whole = spread(jnp.concatenate(ordered * groups, axis=0)).reshape(n_ctx, -1, 2 * HDIM)
         return [lax.dynamic_index_in_dim(whole, ctx ^ m, keepdims=False) for m in range(n_ctx)]
 
-    def both_cores(value):
-        return lax.all_gather(value, "head", axis=1, tiled=True)
-
     cut = half * 11 // 16 // HDIM * HDIM
     across = xor(tokens, 2)
     beside = xor(tokens, 1)
+    kv_mine = spread(pack_keys_values(place, w_key, w_value, n_ctx))
+    q_sent = pack_queries(place, w_query)
     far_tokens = other_core(tokens)
-    far_tokens, w_key, w_value = lax.optimization_barrier((far_tokens, w_key, w_value))
-    kv_mine = spread(pack_keys_values(place, w_key, w_value, n_ctx))
-    across, beside, kv_mine, w_query, w_out = lax.optimization_barrier((across, beside, kv_mine, w_query, w_out))
-    middle = kv_mine.shape[0] // 2
-    kv_upper = other_part(kv_mine[:middle])
+    far_beside = other_core(beside)
+    w_far = other_core(w_out)
+    across, beside, kv_mine, q_sent, far_tokens, far_beside, w_far = lax.optimization_barrier(
+        (across, beside, kv_mine, q_sent, far_tokens, far_beside, w_far)
+    )
+    kv_other = other_part(kv_mine)
     left = xor(across[:, :cut], 1)
     right = xor(beside[:, cut:], 2)
-    q_sent = pack_queries(place, w_query)
-    near = [(tokens, 0, 0, 0), (far_tokens, 0, 0, 1), (both_cores(beside), 1, 0, None), (both_cores(across), 2, 0, None)]
+    near = [(tokens, 0, 0, 0), (far_tokens, 0, 0, 1), (beside, 1, 0, 0), (far_beside, 1, 0, 1)]
+    near += [(lax.all_gather(across, "head", axis=1, tiled=True), 2, 0, None)]
     near = stage(place, near, SUB - 1, rows, 2 * half)
-    first = project(near, kv_mine)
-    arrived = {m: xor(q_sent[m % SUB], m) for m in (4, 6)} if n_ctx == 2 * SUB else {}
-    w_sent = take_rows(place, w_out)
-    left, right, arrived, q_sent, w_sent, kv_upper, kv_mine, first = lax.optimization_barrier(
-        (left, right, arrived, q_sent, w_sent, kv_upper, kv_mine, first)
-    )
-    kv_lower = other_part(kv_mine[middle:])
-    corner = []
-    for array, column in ((left, 0), (right, cut)):
-        corner += [(array, 0, column, 0), (other_core(array), 0, column, 1)]
-    corner = stage(place, corner, 1, rows, 2 * half)
-    last = project(corner, kv_mine, first[3])
     if n_ctx == 2 * SUB:
-        arrived = arrived | {m: xor(q_sent[m % SUB], m) for m in (5, 7, 2, 3, 1)}
-        arrived, kv_lower, last, w_sent = lax.optimization_barrier((arrived, kv_lower, last, w_sent))
-        q_pieces = [q_sent[0]] + [arrived[m] for m in range(1, n_ctx)]
+        arrived = {0: q_sent[0]} | {m: xor(q_sent[m % SUB], m) for m in (4, 6)}
+        left, right, arrived, q_sent = lax.optimization_barrier((left, right, arrived, q_sent))
+        arrived = arrived | {m: xor(q_sent[m % SUB], m) for m in (5, 7)}
+    far_left, far_right = other_core(left), other_core(right)
+    if n_ctx == 2 * SUB:
+        far_left, q_sent = lax.optimization_barrier((far_left, q_sent))
+        arrived = arrived | {m: xor(q_sent[m % SUB], m) for m in (3, 2, 1)}
+        q_pieces = [arrived[m] for m in range(n_ctx)]
     else:
         q_pieces = gather_queries(q_sent)
-    w_far = other_core(w_sent)
-
-    def head(near_part, corner_part):
-        return [near_part[:3], corner_part[:3]], exclusive_prefix(corner_part[3], groups)
-
-    kv_other = [kv_upper, kv_lower]
+    corner = [(left, 0, 0, 0), (far_left, 0, 0, 1), (right, 0, cut, 0), (far_right, 0, cut, 1)]
+    corner = stage(place, corner, 1, rows, 2 * half)
+
+    def head(parts):
+        return [part[:3] for part in parts], exclusive_prefix(parts[-1][3], groups)
+
+    first = project(near, kv_mine)
+    last = project(corner, kv_mine, first[3])
+    kv_other, last = lax.optimization_barrier((kv_other, last))
     second = project(near, kv_other)
-    heads = [head(first, last), head(second, project(corner, kv_other, second[3]))]
+    heads = [head([first, last]), head([second, project(corner, kv_other, second[3])])]
     query = queries(place, [near, corner], q_pieces)
     away = attend(place, (3, 1, 2), query, heads)
     home = attend(place, (0,), query, heads)

time: 212 us -> 187 us (0.88)
  waiting for transfers between devices: 104 us -> 86.1 us
  local copies, waits for them, and re-layouts: 23.2 us -> 9.88 us
  Pallas kernels: 29.5 us -> 40.2 us
  starting transfers between devices: 40.7 us -> 36.1 us
    ppermute x14, waiting for transfers between devices: 94.4 us -> 86 us  [xor(): return lax.ppermute(value, 'ctx', [(i, i ^ step) for i in range(n_ctx)])]
    pallas_call x4, Pallas kernels: 8.5 us -> 15 us  [project(): call(kernel, 'project', shapes, [VMEM] * len(args), [VMEM] * 4, LIMIT, fl...]
    all_gather x2 -> x1, waiting for transfers between devices: 5.74 us -> 0.02 us  [local(): near += [(lax.all_gather(across, 'head', axis=1, tiled=True), 2, 0, None)]]
    dynamic_slice x1 -> x0, local copies, waits for them, and re-layouts: 4.76 us -> none  [take_rows(): return lax.dynamic_slice(w_out, (0, (1 - place[2]) * half), (rows, half))]
    ppermute x14, starting transfers between devices: 26 us -> 21.3 us  [xor(): return lax.ppermute(value, 'ctx', [(i, i ^ step) for i in range(n_ctx)])]
    unnamed x28 -> x22, local copies, waits for them, and re-layouts: 13.1 us -> 8.51 us
    ppermute x8 -> x9, waiting for transfers between devices: 3.19 us -> 0.02 us  [other_core(): return lax.ppermute(value, 'head', [(0, 1), (1, 0)])]
  transfers between devices with their start and end apart: 29 -> 28, of which waited for: 10 -> 5; matrix products, arithmetic and copies ran while one was open for 5% -> 1% of each run, Pallas kernels for 12% -> 19%
where the time goes in v6:
time: 187 us; the launch traced here: 186 us
  waiting for transfers between devices  86.1 us (46%)
  Pallas kernels  40.2 us (21%)
  starting transfers between devices  36.1 us (19%)
  between operations  13.7 us (7%)
  local copies, waits for them, and re-layouts  9.88 us (5%)
    ppermute x14, waiting for transfers between devices, xor(): return lax.ppermute(value, 'ctx', [(i, i ^ step) for i in range(n_ctx)])  86 us
    ppermute x14, starting transfers between devices, xor(): return lax.ppermute(value, 'ctx', [(i, i ^ step) for i in range(n_ctx)])  21.3 us
    pallas_call x4, Pallas kernels, project(): call(kernel, 'project', shapes, [VMEM] * len(args), [VMEM] * 4, LIMIT, fl...  15 us
    unnamed x22, local copies, waits for them, and re-layouts  8.51 us
    all_to_all x1, starting transfers between devices, spread(): return lax.all_to_all(packed, 'ctx', 0, 0, tiled=True)  6.93 us
    pallas_call x1, Pallas kernels, queries(): call(kernel, 'queries', shape, specs, VMEM, LIMIT, flops, 2 * MIB, [held])  4.98 us
    pallas_call x2, Pallas kernels, add_features(): call(kernel, 'add_features', shape, [VMEM] * len(args), VMEM, LIMIT, flop...  4.77 us
    pallas_call x2, Pallas kernels, stage(): call(kernel, 'stage', shape, [SMEM] + [ANY] * count, VMEM, 36 if blocks >...  4.59 us
  transfers between devices with their start and end apart: 28, of which 5 were waited for; matrix products, arithmetic and copies ran while one was open for 1% of the time, Pallas kernels for 19%

profile of v6, /device:TPU:0, one launch (start us, length us, event | category | flops | bytes accessed | tf_op | source)
XLA Modules:
  0.0 186.1 jit_solution(522360919319627322)
XLA Ops:
  9.5 2.1 %pack_keys_values.1 = bf16[4096,256]{1,0:T(8,128)(2,1)} custom-call(s32[4]{0:T(128)S(1)} %pad_add_fusion.place_ref, bf16[512,1024]{1,0:T(8,128)(2,1)S(1)} %copy-done.4, bf16[512,1024]{1,0:T(8,128)(2,1)S(1)} %copy-done.5), custom_call_target="tpu_custom_call" | custom-call | bytes 4194304 | tf_op jit(solution)/shard_map/pack_keys_values/pallas_call | solution.py:54
  11.7 6.9 %all-to-all-start = ((bf16[8,512,256]{2,1,0:T(8,128)(2,1)}), bf16[8,512,256]{2,1,0:T(8,128)(2,1)}, u32[]{:S(2)}, u32[]{:S(2)}) async-start(bf16[8,512,256]{2,1,0:T(8,128)(2,1)} %bitcast.4), calls=%async_computation | async-start | bytes 4194304 | tf_op jit(solution)/shard_map/all_to_all | solution.py:268
  18.6 2.0 %collective-permute-start.1 = (bf16[384,2048]{1,0:T(8,128)(2,1)S(1)}, bf16[384,2048]{1,0:T(8,128)(2,1)S(1)}, u32[]{:S(2)}, u32[]{:S(2)}) collective-permute-start(bf16[384,2048]{1,0:T(8,128)(2,1)S(1)} %copy-done.2), channel_id=1, source_target_pairs={{0,2},{2,0},{4,6},{6,4},{8,10},{10,8},{12,14},{14,12},{1,3},{3,1},... | collective-permute-start | bytes 4718600 | tf_op jit(solution)/shard_map/ppermute | solution.py:259
  20.7 1.5 collective-permute-start
  22.1 55.6 %collective-permute-done.1.refs_2_ = bf16[384,2048]{1,0:T(8,128)(2,1)S(1)} collective-permute-done((bf16[384,2048]{1,0:T(8,128)(2,1)S(1)}, bf16[384,2048]{1,0:T(8,128)(2,1)S(1)}, u32[]{:S(2)}, u32[]{:S(2)}) %collective-permute-start.1) | collective-permute-done | bytes 1572896 | tf_op jit(solution)/shard_map/ppermute | solution.py:259
  77.8 1.8 copy-done.6
  79.6 1.5 pack_queries.1
  81.1 8.1 %collective-permute-done = bf16[384,2048]{1,0:T(8,128)(2,1)} collective-permute-done((bf16[384,2048]{1,0:T(8,128)(2,1)S(1)}, bf16[384,2048]{1,0:T(8,128)(2,1)}, u32[]{:S(2)}, u32[]{:S(2)}) %collective-permute-start) | collective-permute-done | bytes 1572896 | tf_op jit(solution)/shard_map/ppermute | solution.py:259
  90.5 1.5 collective-permute-start.5
  92.1 1.5 collective-permute-start.16
  93.7 1.6 collective-permute-start.6
  96.6 1.5 collective-permute-start.8
  98.1 14.5 %collective-permute-done.7.refs_6_ = bf16[512,256]{1,0:T(8,128)(2,1)S(1)} collective-permute-done((bf16[512,256]{1,0:T(8,128)(2,1)S(1)}, bf16[512,256]{1,0:T(8,128)(2,1)S(1)}, u32[]{:S(2)}, u32[]{:S(2)}) %collective-permute-start.7) | collective-permute-done | bytes 262176 | tf_op jit(solution)/shard_map/ppermute | solution.py:259
  113.3 5.7 %collective-permute-done.8.refs_8_ = bf16[512,256]{1,0:T(8,128)(2,1)S(1)} collective-permute-done((bf16[512,256]{1,0:T(8,128)(2,1)}, bf16[512,256]{1,0:T(8,128)(2,1)S(1)}, u32[]{:S(2)}, u32[]{:S(2)}) %collective-permute-start.8) | collective-permute-done | bytes 262176 | tf_op jit(solution)/shard_map/ppermute | solution.py:259
  120.2 2.4 %collective-permute-start.14 = (bf16[512,256]{1,0:T(8,128)(2,1)}, bf16[512,256]{1,0:T(8,128)(2,1)}, u32[]{:S(2)}, u32[]{:S(2)}) collective-permute-start(bf16[512,256]{1,0:T(8,128)(2,1)} %get-tuple-element.84), channel_id=1, source_target_pairs={{0,10},{2,8},{4,14},{6,12},{8,2},{10,0},{12,6},{14,4},{1,11},{3,9}... | collective-permute-start | bytes 786440 | tf_op jit(solution)/shard_map/ppermute | solution.py:259
  122.6 2.3 %collective-permute-start.15 = (bf16[512,256]{1,0:T(8,128)(2,1)}, bf16[512,256]{1,0:T(8,128)(2,1)}, u32[]{:S(2)}, u32[]{:S(2)}) collective-permute-start(bf16[512,256]{1,0:T(8,128)(2,1)} %get-tuple-element.86), channel_id=1, source_target_pairs={{0,14},{2,12},{4,10},{6,8},{8,6},{10,4},{12,2},{14,0},{1,15},{3,13... | collective-permute-start | bytes 786440 | tf_op jit(solution)/shard_map/ppermute | solution.py:259
  128.2 1.4 copy-done.3
  129.6 3.7 %stage.2.refs_0_.stream_ref = bf16[3,384,4096]{2,1,0:T(8,128)(2,1)S(1)} custom-call(s32[4]{0:T(128)S(1)} %pad_add_fusion.place_ref, bf16[384,2048]{1,0:T(8,128)(2,1)S(1)} %copy-done.3, bf16[384,2048]{1,0:T(8,128)(2,1)} %collective-permute-done.2.refs_1_, bf16[384,2048]{1,0:T(8,128)(2,1)S(1)} %copy-done.1, bf16[384,2048]{1,0:T(8,128)(2,1)} %collective-permute-done.3.refs_3_, ...), custom_call_target="tpu_custom_call" | custom-call | bytes 18874368 | tf_op jit(solution)/shard_map/stage/pallas_call | solution.py:117
  133.3 4.6 %project.4 = (bf16[3,384,128]{2,1,0:T(8,128)(2,1)S(1)}, bf16[3,384,128]{2,1,0:T(8,128)(2,1)S(1)}, f32[3,128,128]{2,1,0:T(8,128)S(1)}, f32[128,128]{1,0:T(8,128)S(1)}) custom-call(bf16[3,384,4096]{2,1,0:T(8,128)(2,1)S(1)} %stage.2.refs_0_.stream_ref, bf16[4096,256]{1,0:T(8,128)(2,1)} %bitcast.5.refs_0_), custom_call_target="tpu_custom_call" | custom-call | flops 2415919104 | bytes 2097152 | tf_op jit(solution)/shard_map/project/pallas_call | solution.py:145
  137.9 2.9 %project.5 = (bf16[1,384,128]{2,1,0:T(8,128)(2,1)S(1)}, bf16[1,384,128]{2,1,0:T(8,128)(2,1)S(1)}, f32[1,128,128]{2,1,0:T(8,128)S(1)}, f32[128,128]{1,0:T(8,128)S(1)}) custom-call(bf16[1,384,4096]{2,1,0:T(8,128)(2,1)S(1)} %stage.3.refs_1_.stream_ref, bf16[4096,256]{1,0:T(8,128)(2,1)} %bitcast.5.refs_0_, f32[128,128]{1,0:T(8,128)S(1)} %get-tuple-element.93.refs_1_), custom_call_target="tpu_custom_call" | custom-call | flops 805306368 | bytes 2097152 | tf_op jit(solution)/shard_map/project/pallas_call | solution.py:145
  140.8 2.7 %collective-permute-start.13 = (bf16[512,256]{1,0:T(8,128)(2,1)}, bf16[512,256]{1,0:T(8,128)(2,1)S(1)}, u32[]{:S(2)}, u32[]{:S(2)}) collective-permute-start(bf16[512,256]{1,0:T(8,128)(2,1)} %get-tuple-element.86), channel_id=1, source_target_pairs={{0,6},{2,4},{4,2},{6,0},{8,14},{10,12},{12,10},{14,8},{1,7},{3,5},... | collective-permute-start | bytes 786440 | tf_op jit(solution)/shard_map/ppermute | solution.py:259
  143.4 4.6 %project.6 = (bf16[3,384,128]{2,1,0:T(8,128)(2,1)S(1)}, bf16[3,384,128]{2,1,0:T(8,128)(2,1)S(1)}, f32[3,128,128]{2,1,0:T(8,128)S(1)}, f32[128,128]{1,0:T(8,128)S(1)}) custom-call(bf16[3,384,4096]{2,1,0:T(8,128)(2,1)S(1)} %stage.2.refs_0_.stream_ref, bf16[4096,256]{1,0:T(8,128)(2,1)} %collective-permute-done.16.refs_0_), custom_call_target="tpu_custom_call" | custom-call | flops 2415919104 | bytes 2097152 | tf_op jit(solution)/shard_map/project/pallas_call | solution.py:145
  148.1 2.9 %project.7 = (bf16[1,384,128]{2,1,0:T(8,128)(2,1)S(1)}, bf16[1,384,128]{2,1,0:T(8,128)(2,1)S(1)}, f32[1,128,128]{2,1,0:T(8,128)S(1)}, f32[128,128]{1,0:T(8,128)S(1)}) custom-call(bf16[1,384,4096]{2,1,0:T(8,128)(2,1)S(1)} %stage.3.refs_1_.stream_ref, bf16[4096,256]{1,0:T(8,128)(2,1)} %collective-permute-done.16.refs_0_, f32[128,128]{1,0:T(8,128)S(1)} %get-tuple-element.106.refs_1_), custom_call_target="tpu_custom_call" | custom-call | flops 805306368 | bytes 2097152 | tf_op jit(solution)/shard_map/project/pallas_call | solution.py:145
  151.0 2.9 %collective-permute-start.18 = (f32[128,128]{1,0:T(8,128)S(1)}, f32[128,128]{1,0:T(8,128)S(1)}, u32[]{:S(2)}, u32[]{:S(2)}) collective-permute-start(f32[128,128]{1,0:T(8,128)S(1)} %get-tuple-element.110), channel_id=1, source_target_pairs={{0,8},{2,10},{4,12},{6,14},{1,9},{3,11},{5,13},{7,15},{16,24},{18,... | collective-permute-start | bytes 196616 | tf_op jit(solution)/shard_map/ppermute | solution.py:239
  153.9 1.5 collective-permute-start.17
  155.4 5.0 %queries.1.query_ref = bf16[4,384,256]{2,1,0:T(8,128)(2,1)S(1)} custom-call(s32[4]{0:T(128)S(1)} %pad_add_fusion.place_ref, bf16[3,384,4096]{2,1,0:T(8,128)(2,1)S(1)} %stage.2.refs_0_.stream_ref, bf16[1,384,4096]{2,1,0:T(8,128)(2,1)S(1)} %stage.3.refs_1_.stream_ref, bf16[512,256]{1,0:T(8,128)(2,1)S(1)} %get-tuple-element.83.refs_2_, ...), custom_call_target="tpu_custom_call" | custom-call | flops 3221225472 | bytes 2097152 | tf_op jit(solution)/shard_map/queries/pallas_call | solution.py:170
  160.4 2.0 %attend.3 = (bf16[384,256]{1,0:T(8,128)(2,1)S(1)}, bf16[384,256]{1,0:T(8,128)(2,1)S(1)}, bf16[384,256]{1,0:T(8,128)(2,1)S(1)}) custom-call(s32[4]{0:T(128)S(1)} %pad_add_fusion.place_ref, bf16[4,384,256]{2,1,0:T(8,128)(2,1)S(1)} %queries.1.query_ref, bf16[3,384,128]{2,1,0:T(8,128)(2,1)S(1)} %get-tuple-element.90.refs_0_, ...), custom_call_target="tpu_custom_call" | custom-call | flops 528482304 | bytes 2097152 | tf_op jit(solution)/shard_map/attend/pallas_call | solution.py:212
  163.1 2.0 %collective-permute-start.20 = (bf16[384,256]{1,0:T(8,128)(2,1)S(1)}, bf16[384,256]{1,0:T(8,128)(2,1)S(1)}, u32[]{:S(2)}, u32[]{:S(2)}) collective-permute-start(bf16[384,256]{1,0:T(8,128)(2,1)S(1)} %get-tuple-element.117), channel_id=1, source_target_pairs={{0,4},{2,6},{4,0},{6,2},{8,12},{10,14},{12,8},{14,10},{1,5},{3,7},... | collective-permute-start | bytes 589832 | tf_op jit(solution)/shard_map/ppermute | solution.py:259
  167.2 4.0 %stage_rows.1 = (bf16[4,256,2048]{2,1,0:T(8,128)(2,1)S(1)}, bf16[4,256,2048]{2,1,0:T(8,128)(2,1)S(1)}) custom-call(s32[4]{0:T(128)S(1)} %pad_add_fusion.place_ref, bf16[1024,4096]{1,0:T(8,128)(2,1)} %out_ref.1, bf16[1024,4096]{1,0:T(8,128)(2,1)} %collective-permute-done.4.far_ref), custom_call_target="tpu_custom_call" | custom-call | bytes 16777216 | tf_op jit(solution)/shard_map/stage_rows/pallas_call | solution.py:89
  171.2 2.1 %collective-permute-done.21.refs_3_ = bf16[384,256]{1,0:T(8,128)(2,1)S(1)} collective-permute-done((bf16[384,256]{1,0:T(8,128)(2,1)S(1)}, bf16[384,256]{1,0:T(8,128)(2,1)S(1)}, u32[]{:S(2)}, u32[]{:S(2)}) %collective-permute-start.21) | collective-permute-done | bytes 196640 | tf_op jit(solution)/shard_map/ppermute | solution.py:259
  174.4 1.8 add_features.2.refs_5_
  176.2 3.0 %add_features.3 = bf16[384,2048]{1,0:T(8,128)(2,1)} custom-call(bf16[384,256]{1,0:T(8,128)(2,1)S(1)} %collective-permute-done.22.refs_0_, bf16[384,256]{1,0:T(8,128)(2,1)S(1)} %collective-permute-done.23.refs_1_, bf16[384,256]{1,0:T(8,128)(2,1)S(1)} %collective-permute-done.24.refs_2_, bf16[384,256]{1,0:T(8,128)(2,1)S(1)} %collective-permute-done.25.refs_3_, ...), custom_call_target="tpu_custom_call" | custom-call | flops 1610612736 | bytes 8388608 | tf_op jit(solution)/shard_map/add_features/pallas_call | solution.py:233
  (64 shorter events, 14.8 us)
Async XLA Ops:
  6.5 82.7 %collective-permute-start.4 = (bf16[1024,4096]{1,0:T(8,128)(2,1)}, bf16[1024,4096]{1,0:T(8,128)(2,1)}, u32[]{:S(2)}, u32[]{:S(2)}) collective-permute-start(bf16[1024,4096]{1,0:T(8,128)(2,1)} %out_ref.1), channel_id=1, source_target_pairs={{0,1},{1,0},{2,3},{3,2},{4,5},{5,4},{6,7},{7,6},{8,9},{9,8},{10,11... | collective-permute-start | bytes 25165832 | tf_op jit(solution)/shard_map/ppermute | solution.py:265
  11.6 7.0 %copy-start.2 = (bf16[384,2048]{1,0:T(8,128)(2,1)S(1)}, bf16[384,2048]{1,0:T(8,128)(2,1)}, u32[]{:S(2)}) copy-start(bf16[384,2048]{1,0:T(8,128)(2,1)} %refs_0_.1) | copy-start | bytes 4718596
  11.7 77.5 %all-to-all-start = ((bf16[8,512,256]{2,1,0:T(8,128)(2,1)}), bf16[8,512,256]{2,1,0:T(8,128)(2,1)}, u32[]{:S(2)}, u32[]{:S(2)}) async-start(bf16[8,512,256]{2,1,0:T(8,128)(2,1)} %bitcast.4), calls=%async_computation | async-start | bytes 4194304 | tf_op jit(solution)/shard_map/all_to_all | solution.py:268
  18.6 108.2 %all-gather.2.cloned.1.call-start = ((), (), s32[]{:S(2)}) async-start(), calls=%async_computation.1 | async-start | bytes 4718592 | tf_op jit(solution)/shard_map/all_gather | solution.py:291
  18.6 59.1 %collective-permute-start.1 = (bf16[384,2048]{1,0:T(8,128)(2,1)S(1)}, bf16[384,2048]{1,0:T(8,128)(2,1)S(1)}, u32[]{:S(2)}, u32[]{:S(2)}) collective-permute-start(bf16[384,2048]{1,0:T(8,128)(2,1)S(1)} %copy-done.2), channel_id=1, source_target_pairs={{0,2},{2,0},{4,6},{6,4},{8,10},{10,8},{12,14},{14,12},{1,3},{3,1},... | collective-permute-start | bytes 4718600 | tf_op jit(solution)/shard_map/ppermute | solution.py:259
  20.7 68.5 %collective-permute-start = (bf16[384,2048]{1,0:T(8,128)(2,1)S(1)}, bf16[384,2048]{1,0:T(8,128)(2,1)}, u32[]{:S(2)}, u32[]{:S(2)}) collective-permute-start(bf16[384,2048]{1,0:T(8,128)(2,1)S(1)} %copy-done.2), channel_id=1, source_target_pairs={{0,4},{2,6},{4,0},{6,2},{8,12},{10,14},{12,8},{14,10},{1,5},{3,7},... | collective-permute-start | bytes 4718600 | tf_op jit(solution)/shard_map/ppermute | solution.py:259
  22.1 67.0 %collective-permute-start.2 = (bf16[384,2048]{1,0:T(8,128)(2,1)S(1)}, bf16[384,2048]{1,0:T(8,128)(2,1)}, u32[]{:S(2)}, u32[]{:S(2)}) collective-permute-start(bf16[384,2048]{1,0:T(8,128)(2,1)S(1)} %copy-done.2), channel_id=1, source_target_pairs={{0,1},{1,0},{2,3},{3,2},{4,5},{5,4},{6,7},{7,6},{8,9},{9,8},{10,11... | collective-permute-start | bytes 4718600 | tf_op jit(solution)/shard_map/ppermute | solution.py:265
  77.8 15.8 %copy-start = (bf16[384,2048]{1,0:T(8,128)(2,1)}, bf16[384,2048]{1,0:T(8,128)(2,1)S(1)}, u32[]{:S(2)}) copy-start(bf16[384,2048]{1,0:T(8,128)(2,1)S(1)} %collective-permute-done.1.refs_2_) | copy-start | bytes 4718596
  77.8 11.4 %collective-permute-start.3 = (bf16[384,2048]{1,0:T(8,128)(2,1)S(1)}, bf16[384,2048]{1,0:T(8,128)(2,1)}, u32[]{:S(2)}, u32[]{:S(2)}) collective-permute-start(bf16[384,2048]{1,0:T(8,128)(2,1)S(1)} %collective-permute-done.1.refs_2_), channel_id=1, source_target_pairs={{0,1},{1,0},{2,3},{3,2},{4,5},{5,4},{6,7},{7,6},{8,9},{9,8},{10,11... | collective-permute-start | bytes 4718600 | tf_op jit(solution)/shard_map/ppermute | solution.py:265
  90.5 29.2 %collective-permute-start.5 = (bf16[384,1408]{1,0:T(8,128)(2,1)S(1)}, bf16[384,1408]{1,0:T(8,128)(2,1)S(1)}, u32[]{:S(2)}, u32[]{:S(2)}) collective-permute-start(bf16[384,1408]{1,0:T(8,128)(2,1)S(1)} %slice.6), channel_id=1, source_target_pairs={{0,2},{2,0},{4,6},{6,4},{8,10},{10,8},{12,14},{14,12},{1,3},{3,1},... | collective-permute-start | bytes 3244040 | tf_op jit(solution)/shard_map/ppermute | solution.py:259
  92.1 48.7 %collective-permute-start.16 = (bf16[4096,256]{1,0:T(8,128)(2,1)}, bf16[4096,256]{1,0:T(8,128)(2,1)}, u32[]{:S(2)}, u32[]{:S(2)}) collective-permute-start(bf16[4096,256]{1,0:T(8,128)(2,1)} %bitcast.5.refs_0_), channel_id=1, source_target_pairs={{0,16},{16,0},{1,17},{17,1},{2,18},{18,2},{3,19},{19,3},{4,20},{20... | collective-permute-start | bytes 6291464 | tf_op jit(solution)/shard_map/ppermute | solution.py:262
  93.7 26.0 %collective-permute-start.6 = (bf16[384,640]{1,0:T(8,128)(2,1)S(1)}, bf16[384,640]{1,0:T(8,128)(2,1)S(1)}, u32[]{:S(2)}, u32[]{:S(2)}) collective-permute-start(bf16[384,640]{1,0:T(8,128)(2,1)S(1)} %slice.7), channel_id=1, source_target_pairs={{0,4},{2,6},{4,0},{6,2},{8,12},{10,14},{12,8},{14,10},{1,5},{3,7},... | collective-permute-start | bytes 1474568 | tf_op jit(solution)/shard_map/ppermute | solution.py:259
  95.3 17.3 %collective-permute-start.7 = (bf16[512,256]{1,0:T(8,128)(2,1)S(1)}, bf16[512,256]{1,0:T(8,128)(2,1)S(1)}, u32[]{:S(2)}, u32[]{:S(2)}) collective-permute-start(bf16[512,256]{1,0:T(8,128)(2,1)S(1)} %get-tuple-element.83.refs_2_), channel_id=1, source_target_pairs={{0,8},{2,10},{4,12},{6,14},{8,0},{10,2},{12,4},{14,6},{1,9},{3,11}... | collective-permute-start | bytes 786440 | tf_op jit(solution)/shard_map/ppermute | solution.py:259
  96.6 22.3 %collective-permute-start.8 = (bf16[512,256]{1,0:T(8,128)(2,1)}, bf16[512,256]{1,0:T(8,128)(2,1)S(1)}, u32[]{:S(2)}, u32[]{:S(2)}) collective-permute-start(bf16[512,256]{1,0:T(8,128)(2,1)} %get-tuple-element.85), channel_id=1, source_target_pairs={{0,12},{2,14},{4,8},{6,10},{8,4},{10,6},{12,0},{14,2},{1,13},{3,15... | collective-permute-start | bytes 786440 | tf_op jit(solution)/shard_map/ppermute | solution.py:259
  119.7 5.2 %collective-permute-start.9 = (bf16[384,1408]{1,0:T(8,128)(2,1)S(1)}, bf16[384,1408]{1,0:T(8,128)(2,1)S(1)}, u32[]{:S(2)}, u32[]{:S(2)}) collective-permute-start(bf16[384,1408]{1,0:T(8,128)(2,1)S(1)} %collective-permute-done.5.refs_0_), channel_id=1, source_target_pairs={{0,1},{1,0},{2,3},{3,2},{4,5},{5,4},{6,7},{7,6},{8,9},{9,8},{10,11... | collective-permute-start | bytes 3244040 | tf_op jit(solution)/shard_map/ppermute | solution.py:265
  119.7 6.1 %collective-permute-start.10 = (bf16[384,640]{1,0:T(8,128)(2,1)S(1)}, bf16[384,640]{1,0:T(8,128)(2,1)S(1)}, u32[]{:S(2)}, u32[]{:S(2)}) collective-permute-start(bf16[384,640]{1,0:T(8,128)(2,1)S(1)} %collective-permute-done.6.refs_2_), channel_id=1, source_target_pairs={{0,1},{1,0},{2,3},{3,2},{4,5},{5,4},{6,7},{7,6},{8,9},{9,8},{10,11... | collective-permute-start | bytes 1474568 | tf_op jit(solution)/shard_map/ppermute | solution.py:265
  120.2 30.8 %collective-permute-start.14 = (bf16[512,256]{1,0:T(8,128)(2,1)}, bf16[512,256]{1,0:T(8,128)(2,1)}, u32[]{:S(2)}, u32[]{:S(2)}) collective-permute-start(bf16[512,256]{1,0:T(8,128)(2,1)} %get-tuple-element.84), channel_id=1, source_target_pairs={{0,10},{2,8},{4,14},{6,12},{8,2},{10,0},{12,6},{14,4},{1,11},{3,9}... | collective-permute-start | bytes 786440 | tf_op jit(solution)/shard_map/ppermute | solution.py:259
  122.6 31.3 %collective-permute-start.15 = (bf16[512,256]{1,0:T(8,128)(2,1)}, bf16[512,256]{1,0:T(8,128)(2,1)}, u32[]{:S(2)}, u32[]{:S(2)}) collective-permute-start(bf16[512,256]{1,0:T(8,128)(2,1)} %get-tuple-element.86), channel_id=1, source_target_pairs={{0,14},{2,12},{4,10},{6,8},{8,6},{10,4},{12,2},{14,0},{1,15},{3,13... | collective-permute-start | bytes 786440 | tf_op jit(solution)/shard_map/ppermute | solution.py:259
  124.9 30.5 %collective-permute-start.11 = (bf16[512,256]{1,0:T(8,128)(2,1)}, bf16[512,256]{1,0:T(8,128)(2,1)}, u32[]{:S(2)}, u32[]{:S(2)}) collective-permute-start(bf16[512,256]{1,0:T(8,128)(2,1)} %get-tuple-element.84), channel_id=1, source_target_pairs={{0,2},{2,0},{4,6},{6,4},{8,10},{10,8},{12,14},{14,12},{1,3},{3,1},... | collective-permute-start | bytes 786440 | tf_op jit(solution)/shard_map/ppermute | solution.py:259
  125.8 29.6 %collective-permute-start.12 = (bf16[512,256]{1,0:T(8,128)(2,1)}, bf16[512,256]{1,0:T(8,128)(2,1)}, u32[]{:S(2)}, u32[]{:S(2)}) collective-permute-start(bf16[512,256]{1,0:T(8,128)(2,1)} %get-tuple-element.85), channel_id=1, source_target_pairs={{0,4},{2,6},{4,0},{6,2},{8,12},{10,14},{12,8},{14,10},{1,5},{3,7},... | collective-permute-start | bytes 786440 | tf_op jit(solution)/shard_map/ppermute | solution.py:259
  140.8 14.6 %collective-permute-start.13 = (bf16[512,256]{1,0:T(8,128)(2,1)}, bf16[512,256]{1,0:T(8,128)(2,1)S(1)}, u32[]{:S(2)}, u32[]{:S(2)}) collective-permute-start(bf16[512,256]{1,0:T(8,128)(2,1)} %get-tuple-element.86), channel_id=1, source_target_pairs={{0,6},{2,4},{4,2},{6,0},{8,14},{10,12},{12,10},{14,8},{1,7},{3,5},... | collective-permute-start | bytes 786440 | tf_op jit(solution)/shard_map/ppermute | solution.py:259
  148.0 7.4 %copy-start.8 = (bf16[512,256]{1,0:T(8,128)(2,1)S(1)}, bf16[512,256]{1,0:T(8,128)(2,1)}, u32[]{:S(2)}) copy-start(bf16[512,256]{1,0:T(8,128)(2,1)} %copy-done.7) | copy-start | bytes 786436
  148.0 7.4 %copy-start.10 = (bf16[512,256]{1,0:T(8,128)(2,1)S(1)}, bf16[512,256]{1,0:T(8,128)(2,1)}, u32[]{:S(2)}) copy-start(bf16[512,256]{1,0:T(8,128)(2,1)} %copy-done.9) | copy-start | bytes 786436
  151.0 9.4 %collective-permute-start.18 = (f32[128,128]{1,0:T(8,128)S(1)}, f32[128,128]{1,0:T(8,128)S(1)}, u32[]{:S(2)}, u32[]{:S(2)}) collective-permute-start(f32[128,128]{1,0:T(8,128)S(1)} %get-tuple-element.110), channel_id=1, source_target_pairs={{0,8},{2,10},{4,12},{6,14},{1,9},{3,11},{5,13},{7,15},{16,24},{18,... | collective-permute-start | bytes 196616 | tf_op jit(solution)/shard_map/ppermute | solution.py:239
  153.9 6.5 %collective-permute-start.17 = (f32[128,128]{1,0:T(8,128)S(1)}, f32[128,128]{1,0:T(8,128)S(1)}, u32[]{:S(2)}, u32[]{:S(2)}) collective-permute-start(f32[128,128]{1,0:T(8,128)S(1)} %get-tuple-element.101), channel_id=1, source_target_pairs={{0,8},{2,10},{4,12},{6,14},{1,9},{3,11},{5,13},{7,15},{16,24},{18,... | collective-permute-start | bytes 196616 | tf_op jit(solution)/shard_map/ppermute | solution.py:239
  162.4 8.8 %collective-permute-start.19 = (bf16[384,256]{1,0:T(8,128)(2,1)S(1)}, bf16[384,256]{1,0:T(8,128)(2,1)S(1)}, u32[]{:S(2)}, u32[]{:S(2)}) collective-permute-start(bf16[384,256]{1,0:T(8,128)(2,1)S(1)} %get-tuple-element.116), channel_id=1, source_target_pairs={{0,2},{2,0},{4,6},{6,4},{8,10},{10,8},{12,14},{14,12},{1,3},{3,1},... | collective-permute-start | bytes 589832 | tf_op jit(solution)/shard_map/ppermute | solution.py:259
  163.1 8.2 %collective-permute-start.20 = (bf16[384,256]{1,0:T(8,128)(2,1)S(1)}, bf16[384,256]{1,0:T(8,128)(2,1)S(1)}, u32[]{:S(2)}, u32[]{:S(2)}) collective-permute-start(bf16[384,256]{1,0:T(8,128)(2,1)S(1)} %get-tuple-element.117), channel_id=1, source_target_pairs={{0,4},{2,6},{4,0},{6,2},{8,12},{10,14},{12,8},{14,10},{1,5},{3,7},... | collective-permute-start | bytes 589832 | tf_op jit(solution)/shard_map/ppermute | solution.py:259
  165.1 8.3 %collective-permute-start.21 = (bf16[384,256]{1,0:T(8,128)(2,1)S(1)}, bf16[384,256]{1,0:T(8,128)(2,1)S(1)}, u32[]{:S(2)}, u32[]{:S(2)}) collective-permute-start(bf16[384,256]{1,0:T(8,128)(2,1)S(1)} %get-tuple-element.118), channel_id=1, source_target_pairs={{0,6},{2,4},{4,2},{6,0},{8,14},{10,12},{12,10},{14,8},{1,7},{3,5},... | collective-permute-start | bytes 589832 | tf_op jit(solution)/shard_map/ppermute | solution.py:259
  173.4 2.8 %collective-permute-start.22 = (bf16[384,256]{1,0:T(8,128)(2,1)S(1)}, bf16[384,256]{1,0:T(8,128)(2,1)S(1)}, u32[]{:S(2)}, u32[]{:S(2)}) collective-permute-start(bf16[384,256]{1,0:T(8,128)(2,1)S(1)} %attend.2.refs_0_), channel_id=1, source_target_pairs={{0,1},{1,0},{2,3},{3,2},{4,5},{5,4},{6,7},{7,6},{8,9},{9,8},{10,11... | collective-permute-start | bytes 589832 | tf_op jit(solution)/shard_map/ppermute | solution.py:265
  173.4 2.8 %collective-permute-start.23 = (bf16[384,256]{1,0:T(8,128)(2,1)S(1)}, bf16[384,256]{1,0:T(8,128)(2,1)S(1)}, u32[]{:S(2)}, u32[]{:S(2)}) collective-permute-start(bf16[384,256]{1,0:T(8,128)(2,1)S(1)} %collective-permute-done.19.refs_1_), channel_id=1, source_target_pairs={{0,1},{1,0},{2,3},{3,2},{4,5},{5,4},{6,7},{7,6},{8,9},{9,8},{10,11... | collective-permute-start | bytes 589832 | tf_op jit(solution)/shard_map/ppermute | solution.py:265
  173.9 2.3 %collective-permute-start.24 = (bf16[384,256]{1,0:T(8,128)(2,1)S(1)}, bf16[384,256]{1,0:T(8,128)(2,1)S(1)}, u32[]{:S(2)}, u32[]{:S(2)}) collective-permute-start(bf16[384,256]{1,0:T(8,128)(2,1)S(1)} %collective-permute-done.20.refs_2_), channel_id=1, source_target_pairs={{0,1},{1,0},{2,3},{3,2},{4,5},{5,4},{6,7},{7,6},{8,9},{9,8},{10,11... | collective-permute-start | bytes 589832 | tf_op jit(solution)/shard_map/ppermute | solution.py:265
  173.9 2.3 %collective-permute-start.25 = (bf16[384,256]{1,0:T(8,128)(2,1)S(1)}, bf16[384,256]{1,0:T(8,128)(2,1)S(1)}, u32[]{:S(2)}, u32[]{:S(2)}) collective-permute-start(bf16[384,256]{1,0:T(8,128)(2,1)S(1)} %collective-permute-done.21.refs_3_), channel_id=1, source_target_pairs={{0,1},{1,0},{2,3},{3,2},{4,5},{5,4},{6,7},{7,6},{8,9},{9,8},{10,11... | collective-permute-start | bytes 589832 | tf_op jit(solution)/shard_map/ppermute | solution.py:265
  (7 other events, 8.5 us)
Sparse Core Ops, SparseCore 0:
  89.3 12.2 all-gather.1

commit v7 on v6

--- a/solution.py
+++ b/solution.py
@@ -114,7 +114,7 @@
     shape = pltpu.VMEM((blocks, rows, width), BF16)
     sems = pltpu.SemaphoreType.DMA((count,))
     moved = blocks * rows * width * 4
-    return call(kernel, "stage", shape, [SMEM] + [ANY] * count, VMEM, 36 if blocks > 1 else LIMIT, 0, moved, [sems])(
+    return call(kernel, "stage", shape, [SMEM] + [ANY] * count, VMEM, 20 if blocks > 1 else LIMIT, 0, moved, [sems])(
         place, *[piece[0] for piece in pieces]
     )
 
@@ -288,16 +288,18 @@
     left = xor(across[:, :cut], 1)
     right = xor(beside[:, cut:], 2)
     near = [(tokens, 0, 0, 0), (far_tokens, 0, 0, 1), (beside, 1, 0, 0), (far_beside, 1, 0, 1)]
-    near += [(lax.all_gather(across, "head", axis=1, tiled=True), 2, 0, None)]
+    near += [(across, 2, 0, 0), (other_core(across), 2, 0, 1)]
     near = stage(place, near, SUB - 1, rows, 2 * half)
+    first = project(near, kv_mine)
     if n_ctx == 2 * SUB:
         arrived = {0: q_sent[0]} | {m: xor(q_sent[m % SUB], m) for m in (4, 6)}
-        left, right, arrived, q_sent = lax.optimization_barrier((left, right, arrived, q_sent))
+        left, right, arrived, q_sent, first = lax.optimization_barrier((left, right, arrived, q_sent, first))
         arrived = arrived | {m: xor(q_sent[m % SUB], m) for m in (5, 7)}
     far_left, far_right = other_core(left), other_core(right)
     if n_ctx == 2 * SUB:
         far_left, q_sent = lax.optimization_barrier((far_left, q_sent))
         arrived = arrived | {m: xor(q_sent[m % SUB], m) for m in (3, 2, 1)}
+        arrived, kv_other = lax.optimization_barrier((arrived, kv_other))
         q_pieces = [arrived[m] for m in range(n_ctx)]
     else:
         q_pieces = gather_queries(q_sent)
@@ -307,7 +309,6 @@
     def head(parts):
         return [part[:3] for part in parts], exclusive_prefix(parts[-1][3], groups)
 
-    first = project(near, kv_mine)
     last = project(corner, kv_mine, first[3])
     kv_other, last = lax.optimization_barrier((kv_other, last))
     second = project(near, kv_other)

time: 187 us -> 183 us (0.979)
  waiting for transfers between devices: 86.1 us -> 103 us
  between operations: 13.7 us -> 0.32 us
  Pallas kernels: 40.2 us -> 28.9 us
  local copies, waits for them, and re-layouts: 9.88 us -> 16.1 us
    ppermute x14, waiting for transfers between devices: 86 us -> 103 us  [xor(): return lax.ppermute(value, 'ctx', [(i, i ^ step) for i in range(n_ctx)])]
    pallas_call x4, Pallas kernels: 15 us -> 8.51 us  [project(): call(kernel, 'project', shapes, [VMEM] * len(args), [VMEM] * 4, LIMIT, fl...]
    unnamed x22 -> x38, local copies, waits for them, and re-layouts: 8.51 us -> 13.6 us
    pallas_call x2, Pallas kernels: 4.59 us -> 2.62 us  [stage(): call(kernel, 'stage', shape, [SMEM] + [ANY] * count, VMEM, 20 if blocks >...]
  transfers between devices with their start and end apart: 28 -> 28, of which waited for: 5 -> 8; matrix products, arithmetic and copies ran while one was open for 1% -> 1% of each run, Pallas kernels for 19% -> 11%
where the time goes in v7:
time: 183 us
  waiting for transfers between devices  103 us (56%)
  starting transfers between devices  34.6 us (19%)
  Pallas kernels  28.9 us (16%)
  local copies, waits for them, and re-layouts  16.1 us (9%)
    ppermute x14, waiting for transfers between devices, xor(): return lax.ppermute(value, 'ctx', [(i, i ^ step) for i in range(n_ctx)])  103 us
    ppermute x14, starting transfers between devices, xor(): return lax.ppermute(value, 'ctx', [(i, i ^ step) for i in range(n_ctx)])  20.4 us
    unnamed x38, local copies, waits for them, and re-layouts  13.6 us
    pallas_call x4, Pallas kernels, project(): call(kernel, 'project', shapes, [VMEM] * len(args), [VMEM] * 4, LIMIT, fl...  8.51 us
    all_to_all x1, starting transfers between devices, spread(): return lax.all_to_all(packed, 'ctx', 0, 0, tiled=True)  6.93 us
    pallas_call x2, Pallas kernels, add_features(): call(kernel, 'add_features', shape, [VMEM] * len(args), VMEM, LIMIT, flop...  4.74 us
    pallas_call x1, Pallas kernels, queries(): call(kernel, 'queries', shape, specs, VMEM, LIMIT, flops, 2 * MIB, [held])  4.31 us
    pallas_call x1, Pallas kernels, stage_rows(): call(kernel, 'stage_rows', shapes, [SMEM, ANY, ANY], [VMEM] * 2, 40, 0, r...  4.02 us
  transfers between devices with their start and end apart: 28, of which 8 were waited for; matrix products, arithmetic and copies ran while one was open for 1% of the time, Pallas kernels for 11%

profile of v7, /device:TPU:0, one launch (start us, length us, event | category | flops | bytes accessed | tf_op | source)
XLA Modules:
  0.0 182.8 jit_solution(11680997389490264348)
XLA Ops:
  5.1 6.9 %all-to-all-start = ((bf16[8,512,256]{2,1,0:T(8,128)(2,1)}), bf16[8,512,256]{2,1,0:T(8,128)(2,1)S(1)}, u32[]{:S(2)}, u32[]{:S(2)}) async-start(bf16[8,512,256]{2,1,0:T(8,128)(2,1)} %bitcast.9), calls=%async_computation | async-start | bytes 4194304 | tf_op jit(solution)/shard_map/all_to_all | solution.py:268
  12.1 2.0 %collective-permute-start.1 = (bf16[384,2048]{1,0:T(8,128)(2,1)}, bf16[384,2048]{1,0:T(8,128)(2,1)S(1)}, u32[]{:S(2)}, u32[]{:S(2)}) collective-permute-start(bf16[384,2048]{1,0:T(8,128)(2,1)} %refs_0_.1), channel_id=1, source_target_pairs={{0,2},{2,0},{4,6},{6,4},{8,10},{10,8},{12,14},{14,12},{1,3},{3,1},... | collective-permute-start | bytes 4718600 | tf_op jit(solution)/shard_map/ppermute | solution.py:259
  14.1 1.5 collective-permute-start
  15.6 55.7 %collective-permute-done.1.refs_2_ = bf16[384,2048]{1,0:T(8,128)(2,1)S(1)} collective-permute-done((bf16[384,2048]{1,0:T(8,128)(2,1)}, bf16[384,2048]{1,0:T(8,128)(2,1)S(1)}, u32[]{:S(2)}, u32[]{:S(2)}) %collective-permute-start.1) | collective-permute-done | bytes 1572896 | tf_op jit(solution)/shard_map/ppermute | solution.py:259
  74.1 8.5 %collective-permute-done.refs_4_ = bf16[384,2048]{1,0:T(8,128)(2,1)S(1)} collective-permute-done((bf16[384,2048]{1,0:T(8,128)(2,1)}, bf16[384,2048]{1,0:T(8,128)(2,1)S(1)}, u32[]{:S(2)}, u32[]{:S(2)}) %collective-permute-start) | collective-permute-done | bytes 1572896 | tf_op jit(solution)/shard_map/ppermute | solution.py:259
  86.1 1.5 slice.6
  87.6 1.5 collective-permute-start.6
  89.1 1.5 collective-permute-start.17
  91.7 1.6 collective-permute-start.7
  94.7 1.5 collective-permute-start.9
  96.2 1.4 copy-done.5
  97.6 1.4 copy-done.7
  100.4 1.7 stage.2.stream_ref.refs_0_
  102.1 3.0 %project.4 = (bf16[3,384,128]{2,1,0:T(8,128)(2,1)S(1)}, bf16[3,384,128]{2,1,0:T(8,128)(2,1)S(1)}, f32[3,128,128]{2,1,0:T(8,128)S(1)}, f32[128,128]{1,0:T(8,128)S(1)}) custom-call(bf16[3,384,4096]{2,1,0:T(8,128)(2,1)S(1)} %stage.2.stream_ref.refs_0_, bf16[4096,256]{1,0:T(8,128)(2,1)S(1)} %bitcast.7), custom_call_target="tpu_custom_call" | custom-call | flops 2415919104 | bytes 2097152 | tf_op jit(solution)/shard_map/project/pallas_call | solution.py:145
  105.1 5.5 %collective-permute-done.8.refs_6_ = bf16[512,256]{1,0:T(8,128)(2,1)S(1)} collective-permute-done((bf16[512,256]{1,0:T(8,128)(2,1)S(1)}, bf16[512,256]{1,0:T(8,128)(2,1)S(1)}, u32[]{:S(2)}, u32[]{:S(2)}) %collective-permute-start.8) | collective-permute-done | bytes 262176 | tf_op jit(solution)/shard_map/ppermute | solution.py:259
  110.6 7.4 %collective-permute-done.9.refs_8_ = bf16[512,256]{1,0:T(8,128)(2,1)S(1)} collective-permute-done((bf16[512,256]{1,0:T(8,128)(2,1)}, bf16[512,256]{1,0:T(8,128)(2,1)S(1)}, u32[]{:S(2)}, u32[]{:S(2)}) %collective-permute-start.9) | collective-permute-done | bytes 262176 | tf_op jit(solution)/shard_map/ppermute | solution.py:259
  118.5 2.4 %collective-permute-start.15 = (bf16[512,256]{1,0:T(8,128)(2,1)S(1)}, bf16[512,256]{1,0:T(8,128)(2,1)S(1)}, u32[]{:S(2)}, u32[]{:S(2)}) collective-permute-start(bf16[512,256]{1,0:T(8,128)(2,1)S(1)} %copy-done.18), channel_id=1, source_target_pairs={{0,10},{2,8},{4,14},{6,12},{8,2},{10,0},{12,6},{14,4},{1,11},{3,9}... | collective-permute-start | bytes 786440 | tf_op jit(solution)/shard_map/ppermute | solution.py:259
  120.9 2.3 %collective-permute-start.16 = (bf16[512,256]{1,0:T(8,128)(2,1)S(1)}, bf16[512,256]{1,0:T(8,128)(2,1)S(1)}, u32[]{:S(2)}, u32[]{:S(2)}) collective-permute-start(bf16[512,256]{1,0:T(8,128)(2,1)S(1)} %copy-done.14), channel_id=1, source_target_pairs={{0,14},{2,12},{4,10},{6,8},{8,6},{10,4},{12,2},{14,0},{1,15},{3,13... | collective-permute-start | bytes 786440 | tf_op jit(solution)/shard_map/ppermute | solution.py:259
  123.9 16.8 %collective-permute-done.15.refs_7_ = bf16[512,256]{1,0:T(8,128)(2,1)S(1)} collective-permute-done((bf16[512,256]{1,0:T(8,128)(2,1)S(1)}, bf16[512,256]{1,0:T(8,128)(2,1)S(1)}, u32[]{:S(2)}, u32[]{:S(2)}) %collective-permute-start.15) | collective-permute-done | bytes 262176 | tf_op jit(solution)/shard_map/ppermute | solution.py:259
  140.7 2.0 %collective-permute-start.14 = (bf16[512,256]{1,0:T(8,128)(2,1)S(1)}, bf16[512,256]{1,0:T(8,128)(2,1)S(1)}, u32[]{:S(2)}, u32[]{:S(2)}) collective-permute-start(bf16[512,256]{1,0:T(8,128)(2,1)S(1)} %copy-done.14), channel_id=1, source_target_pairs={{0,6},{2,4},{4,2},{6,0},{8,14},{10,12},{12,10},{14,8},{1,7},{3,5},... | collective-permute-start | bytes 786440 | tf_op jit(solution)/shard_map/ppermute | solution.py:259
  145.0 5.0 %collective-permute-done.13.refs_4_ = bf16[512,256]{1,0:T(8,128)(2,1)S(1)} collective-permute-done((bf16[512,256]{1,0:T(8,128)(2,1)S(1)}, bf16[512,256]{1,0:T(8,128)(2,1)S(1)}, u32[]{:S(2)}, u32[]{:S(2)}) %collective-permute-start.13) | collective-permute-done | bytes 262176 | tf_op jit(solution)/shard_map/ppermute | solution.py:259
  149.9 2.9 %collective-permute-done.14.refs_5_ = bf16[512,256]{1,0:T(8,128)(2,1)S(1)} collective-permute-done((bf16[512,256]{1,0:T(8,128)(2,1)S(1)}, bf16[512,256]{1,0:T(8,128)(2,1)S(1)}, u32[]{:S(2)}, u32[]{:S(2)}) %collective-permute-start.14) | collective-permute-done | bytes 262176 | tf_op jit(solution)/shard_map/ppermute | solution.py:259
  152.9 3.0 %project.6 = (bf16[3,384,128]{2,1,0:T(8,128)(2,1)S(1)}, bf16[3,384,128]{2,1,0:T(8,128)(2,1)S(1)}, f32[3,128,128]{2,1,0:T(8,128)S(1)}, f32[128,128]{1,0:T(8,128)S(1)}) custom-call(bf16[3,384,4096]{2,1,0:T(8,128)(2,1)S(1)} %stage.2.stream_ref.refs_0_, bf16[4096,256]{1,0:T(8,128)(2,1)S(1)} %collective-permute-done.17.refs_0_), custom_call_target="tpu_custom_call" | custom-call | flops 2415919104 | bytes 2097152 | tf_op jit(solution)/shard_map/project/pallas_call | solution.py:145
  157.1 2.2 %collective-permute-start.19 = (f32[128,128]{1,0:T(8,128)S(1)}, f32[128,128]{1,0:T(8,128)S(1)}, u32[]{:S(2)}, u32[]{:S(2)}) collective-permute-start(f32[128,128]{1,0:T(8,128)S(1)} %get-tuple-element.136), channel_id=1, source_target_pairs={{0,8},{2,10},{4,12},{6,14},{1,9},{3,11},{5,13},{7,15},{16,24},{18,... | collective-permute-start | bytes 196616 | tf_op jit(solution)/shard_map/ppermute | solution.py:239
  159.4 1.5 collective-permute-start.18
  160.9 4.3 %queries.1.query_ref = bf16[4,384,256]{2,1,0:T(8,128)(2,1)S(1)} custom-call(s32[4]{0:T(128)S(1)} %pad_add_fusion.place_ref, bf16[3,384,4096]{2,1,0:T(8,128)(2,1)S(1)} %stage.2.stream_ref.refs_0_, bf16[1,384,4096]{2,1,0:T(8,128)(2,1)S(1)} %stage.3.refs_1_.stream_ref, bf16[512,256]{1,0:T(8,128)(2,1)S(1)} %get-tuple-element.107.refs_2_, ...), custom_call_target="tpu_custom_call" | custom-call | flops 3221225472 | bytes 2097152 | tf_op jit(solution)/shard_map/queries/pallas_call | solution.py:170
  165.2 2.0 %attend.3 = (bf16[384,256]{1,0:T(8,128)(2,1)S(1)}, bf16[384,256]{1,0:T(8,128)(2,1)S(1)}, bf16[384,256]{1,0:T(8,128)(2,1)S(1)}) custom-call(s32[4]{0:T(128)S(1)} %pad_add_fusion.place_ref, bf16[4,384,256]{2,1,0:T(8,128)(2,1)S(1)} %queries.1.query_ref, bf16[3,384,128]{2,1,0:T(8,128)(2,1)S(1)} %get-tuple-element.115.refs_0_, ...), custom_call_target="tpu_custom_call" | custom-call | flops 528482304 | bytes 2097152 | tf_op jit(solution)/shard_map/attend/pallas_call | solution.py:212
  167.2 1.4 collective-permute-start.20
  168.6 1.7 collective-permute-start.21
  172.0 4.0 %stage_rows.1 = (bf16[4,256,2048]{2,1,0:T(8,128)(2,1)S(1)}, bf16[4,256,2048]{2,1,0:T(8,128)(2,1)S(1)}) custom-call(s32[4]{0:T(128)S(1)} %pad_add_fusion.place_ref, bf16[1024,4096]{1,0:T(8,128)(2,1)} %out_ref.1, bf16[1024,4096]{1,0:T(8,128)(2,1)} %collective-permute-done.4.far_ref), custom_call_target="tpu_custom_call" | custom-call | bytes 16777216 | tf_op jit(solution)/shard_map/stage_rows/pallas_call | solution.py:89
  178.0 1.8 add_features.2.refs_5_
  179.8 2.9 %add_features.3 = bf16[384,2048]{1,0:T(8,128)(2,1)} custom-call(bf16[384,256]{1,0:T(8,128)(2,1)S(1)} %collective-permute-done.23.refs_0_, bf16[384,256]{1,0:T(8,128)(2,1)S(1)} %collective-permute-done.24.refs_1_, bf16[384,256]{1,0:T(8,128)(2,1)S(1)} %collective-permute-done.25.refs_2_, bf16[384,256]{1,0:T(8,128)(2,1)S(1)} %collective-permute-done.26.refs_3_, ...), custom_call_target="tpu_custom_call" | custom-call | flops 1610612736 | bytes 8388608 | tf_op jit(solution)/shard_map/add_features/pallas_call | solution.py:233
  (79 shorter events, 23.6 us)
Async XLA Ops:
  0.0 86.0 %collective-permute-start.4 = (bf16[1024,4096]{1,0:T(8,128)(2,1)}, bf16[1024,4096]{1,0:T(8,128)(2,1)}, u32[]{:S(2)}, u32[]{:S(2)}) collective-permute-start(bf16[1024,4096]{1,0:T(8,128)(2,1)} %out_ref.1), channel_id=1, source_target_pairs={{0,1},{1,0},{2,3},{3,2},{4,5},{5,4},{6,7},{7,6},{8,9},{9,8},{10,11... | collective-permute-start | bytes 25165832 | tf_op jit(solution)/shard_map/ppermute | solution.py:265
  5.1 66.1 %copy-start.12 = (bf16[512,1024]{1,0:T(8,128)(2,1)S(1)}, bf16[512,1024]{1,0:T(8,128)(2,1)}, u32[]{:S(2)}) copy-start(bf16[512,1024]{1,0:T(8,128)(2,1)} %query_ref.1) | copy-start | bytes 3145732
  5.1 80.9 %all-to-all-start = ((bf16[8,512,256]{2,1,0:T(8,128)(2,1)}), bf16[8,512,256]{2,1,0:T(8,128)(2,1)S(1)}, u32[]{:S(2)}, u32[]{:S(2)}) async-start(bf16[8,512,256]{2,1,0:T(8,128)(2,1)} %bitcast.9), calls=%async_computation | async-start | bytes 4194304 | tf_op jit(solution)/shard_map/all_to_all | solution.py:268
  12.1 59.2 %collective-permute-start.1 = (bf16[384,2048]{1,0:T(8,128)(2,1)}, bf16[384,2048]{1,0:T(8,128)(2,1)S(1)}, u32[]{:S(2)}, u32[]{:S(2)}) collective-permute-start(bf16[384,2048]{1,0:T(8,128)(2,1)} %refs_0_.1), channel_id=1, source_target_pairs={{0,2},{2,0},{4,6},{6,4},{8,10},{10,8},{12,14},{14,12},{1,3},{3,1},... | collective-permute-start | bytes 4718600 | tf_op jit(solution)/shard_map/ppermute | solution.py:259
  14.1 68.5 %collective-permute-start = (bf16[384,2048]{1,0:T(8,128)(2,1)}, bf16[384,2048]{1,0:T(8,128)(2,1)S(1)}, u32[]{:S(2)}, u32[]{:S(2)}) collective-permute-start(bf16[384,2048]{1,0:T(8,128)(2,1)} %refs_0_.1), channel_id=1, source_target_pairs={{0,4},{2,6},{4,0},{6,2},{8,12},{10,14},{12,8},{14,10},{1,5},{3,7},... | collective-permute-start | bytes 4718600 | tf_op jit(solution)/shard_map/ppermute | solution.py:259
  15.5 67.0 %collective-permute-start.2 = (bf16[384,2048]{1,0:T(8,128)(2,1)}, bf16[384,2048]{1,0:T(8,128)(2,1)S(1)}, u32[]{:S(2)}, u32[]{:S(2)}) collective-permute-start(bf16[384,2048]{1,0:T(8,128)(2,1)} %refs_0_.1), channel_id=1, source_target_pairs={{0,1},{1,0},{2,3},{3,2},{4,5},{5,4},{6,7},{7,6},{8,9},{9,8},{10,11... | collective-permute-start | bytes 4718600 | tf_op jit(solution)/shard_map/ppermute | solution.py:265
  71.3 13.6 %collective-permute-start.3 = (bf16[384,2048]{1,0:T(8,128)(2,1)S(1)}, bf16[384,2048]{1,0:T(8,128)(2,1)S(1)}, u32[]{:S(2)}, u32[]{:S(2)}) collective-permute-start(bf16[384,2048]{1,0:T(8,128)(2,1)S(1)} %collective-permute-done.1.refs_2_), channel_id=1, source_target_pairs={{0,1},{1,0},{2,3},{3,2},{4,5},{5,4},{6,7},{7,6},{8,9},{9,8},{10,11... | collective-permute-start | bytes 4718600 | tf_op jit(solution)/shard_map/ppermute | solution.py:265
  86.0 8.7 %collective-permute-start.5 = (bf16[384,2048]{1,0:T(8,128)(2,1)}, bf16[384,2048]{1,0:T(8,128)(2,1)S(1)}, u32[]{:S(2)}, u32[]{:S(2)}) collective-permute-start(bf16[384,2048]{1,0:T(8,128)(2,1)} %copy-done.1), channel_id=1, source_target_pairs={{0,1},{1,0},{2,3},{3,2},{4,5},{5,4},{6,7},{7,6},{8,9},{9,8},{10,11... | collective-permute-start | bytes 4718600 | tf_op jit(solution)/shard_map/ppermute | solution.py:265
  87.6 30.4 %collective-permute-start.6 = (bf16[384,1408]{1,0:T(8,128)(2,1)S(1)}, bf16[384,1408]{1,0:T(8,128)(2,1)S(1)}, u32[]{:S(2)}, u32[]{:S(2)}) collective-permute-start(bf16[384,1408]{1,0:T(8,128)(2,1)S(1)} %slice.6), channel_id=1, source_target_pairs={{0,2},{2,0},{4,6},{6,4},{8,10},{10,8},{12,14},{14,12},{1,3},{3,1},... | collective-permute-start | bytes 3244040 | tf_op jit(solution)/shard_map/ppermute | solution.py:259
  89.1 55.8 %collective-permute-start.17 = (bf16[4096,256]{1,0:T(8,128)(2,1)S(1)}, bf16[4096,256]{1,0:T(8,128)(2,1)S(1)}, u32[]{:S(2)}, u32[]{:S(2)}) collective-permute-start(bf16[4096,256]{1,0:T(8,128)(2,1)S(1)} %bitcast.6), channel_id=1, source_target_pairs={{0,16},{16,0},{1,17},{17,1},{2,18},{18,2},{3,19},{19,3},{4,20},{20... | collective-permute-start | bytes 6291464 | tf_op jit(solution)/shard_map/ppermute | solution.py:262
  91.7 26.3 %collective-permute-start.7 = (bf16[384,640]{1,0:T(8,128)(2,1)S(1)}, bf16[384,640]{1,0:T(8,128)(2,1)S(1)}, u32[]{:S(2)}, u32[]{:S(2)}) collective-permute-start(bf16[384,640]{1,0:T(8,128)(2,1)S(1)} %slice.7), channel_id=1, source_target_pairs={{0,4},{2,6},{4,0},{6,2},{8,12},{10,14},{12,8},{14,10},{1,5},{3,7},... | collective-permute-start | bytes 1474568 | tf_op jit(solution)/shard_map/ppermute | solution.py:259
  93.3 17.3 %collective-permute-start.8 = (bf16[512,256]{1,0:T(8,128)(2,1)S(1)}, bf16[512,256]{1,0:T(8,128)(2,1)S(1)}, u32[]{:S(2)}, u32[]{:S(2)}) collective-permute-start(bf16[512,256]{1,0:T(8,128)(2,1)S(1)} %get-tuple-element.107.refs_2_), channel_id=1, source_target_pairs={{0,8},{2,10},{4,12},{6,14},{8,0},{10,2},{12,4},{14,6},{1,9},{3,11}... | collective-permute-start | bytes 786440 | tf_op jit(solution)/shard_map/ppermute | solution.py:259
  94.7 23.3 %collective-permute-start.9 = (bf16[512,256]{1,0:T(8,128)(2,1)}, bf16[512,256]{1,0:T(8,128)(2,1)S(1)}, u32[]{:S(2)}, u32[]{:S(2)}) collective-permute-start(bf16[512,256]{1,0:T(8,128)(2,1)} %copy-done.15), channel_id=1, source_target_pairs={{0,12},{2,14},{4,8},{6,10},{8,4},{10,6},{12,0},{14,2},{1,13},{3,15... | collective-permute-start | bytes 786440 | tf_op jit(solution)/shard_map/ppermute | solution.py:259
  102.1 16.4 %copy-start.18 = (bf16[512,256]{1,0:T(8,128)(2,1)S(1)}, bf16[512,256]{1,0:T(8,128)(2,1)}, u32[]{:S(2)}) copy-start(bf16[512,256]{1,0:T(8,128)(2,1)} %copy-done.17) | copy-start | bytes 786436
  102.1 18.8 %copy-start.14 = (bf16[512,256]{1,0:T(8,128)(2,1)S(1)}, bf16[512,256]{1,0:T(8,128)(2,1)}, u32[]{:S(2)}) copy-start(bf16[512,256]{1,0:T(8,128)(2,1)} %copy-done.13) | copy-start | bytes 786436
  102.1 38.6 %copy-start.16 = (bf16[512,256]{1,0:T(8,128)(2,1)S(1)}, bf16[512,256]{1,0:T(8,128)(2,1)}, u32[]{:S(2)}) copy-start(bf16[512,256]{1,0:T(8,128)(2,1)} %copy-done.15) | copy-start | bytes 786436
  118.0 5.2 %collective-permute-start.10 = (bf16[384,1408]{1,0:T(8,128)(2,1)S(1)}, bf16[384,1408]{1,0:T(8,128)(2,1)S(1)}, u32[]{:S(2)}, u32[]{:S(2)}) collective-permute-start(bf16[384,1408]{1,0:T(8,128)(2,1)S(1)} %collective-permute-done.6.refs_0_), channel_id=1, source_target_pairs={{0,1},{1,0},{2,3},{3,2},{4,5},{5,4},{6,7},{7,6},{8,9},{9,8},{10,11... | collective-permute-start | bytes 3244040 | tf_op jit(solution)/shard_map/ppermute | solution.py:265
  118.0 22.7 %collective-permute-start.11 = (bf16[384,640]{1,0:T(8,128)(2,1)S(1)}, bf16[384,640]{1,0:T(8,128)(2,1)S(1)}, u32[]{:S(2)}, u32[]{:S(2)}) collective-permute-start(bf16[384,640]{1,0:T(8,128)(2,1)S(1)} %collective-permute-done.7.refs_2_), channel_id=1, source_target_pairs={{0,1},{1,0},{2,3},{3,2},{4,5},{5,4},{6,7},{7,6},{8,9},{9,8},{10,11... | collective-permute-start | bytes 1474568 | tf_op jit(solution)/shard_map/ppermute | solution.py:265
  118.5 22.2 %collective-permute-start.15 = (bf16[512,256]{1,0:T(8,128)(2,1)S(1)}, bf16[512,256]{1,0:T(8,128)(2,1)S(1)}, u32[]{:S(2)}, u32[]{:S(2)}) collective-permute-start(bf16[512,256]{1,0:T(8,128)(2,1)S(1)} %copy-done.18), channel_id=1, source_target_pairs={{0,10},{2,8},{4,14},{6,12},{8,2},{10,0},{12,6},{14,4},{1,11},{3,9}... | collective-permute-start | bytes 786440 | tf_op jit(solution)/shard_map/ppermute | solution.py:259
  120.9 24.1 %collective-permute-start.16 = (bf16[512,256]{1,0:T(8,128)(2,1)S(1)}, bf16[512,256]{1,0:T(8,128)(2,1)S(1)}, u32[]{:S(2)}, u32[]{:S(2)}) collective-permute-start(bf16[512,256]{1,0:T(8,128)(2,1)S(1)} %copy-done.14), channel_id=1, source_target_pairs={{0,14},{2,12},{4,10},{6,8},{8,6},{10,4},{12,2},{14,0},{1,15},{3,13... | collective-permute-start | bytes 786440 | tf_op jit(solution)/shard_map/ppermute | solution.py:259
  123.2 21.8 %collective-permute-start.12 = (bf16[512,256]{1,0:T(8,128)(2,1)S(1)}, bf16[512,256]{1,0:T(8,128)(2,1)S(1)}, u32[]{:S(2)}, u32[]{:S(2)}) collective-permute-start(bf16[512,256]{1,0:T(8,128)(2,1)S(1)} %copy-done.18), channel_id=1, source_target_pairs={{0,2},{2,0},{4,6},{6,4},{8,10},{10,8},{12,14},{14,12},{1,3},{3,1},... | collective-permute-start | bytes 786440 | tf_op jit(solution)/shard_map/ppermute | solution.py:259
  140.7 9.2 %collective-permute-start.13 = (bf16[512,256]{1,0:T(8,128)(2,1)S(1)}, bf16[512,256]{1,0:T(8,128)(2,1)S(1)}, u32[]{:S(2)}, u32[]{:S(2)}) collective-permute-start(bf16[512,256]{1,0:T(8,128)(2,1)S(1)} %copy-done.16), channel_id=1, source_target_pairs={{0,4},{2,6},{4,0},{6,2},{8,12},{10,14},{12,8},{14,10},{1,5},{3,7},... | collective-permute-start | bytes 786440 | tf_op jit(solution)/shard_map/ppermute | solution.py:259
  140.7 12.2 %collective-permute-start.14 = (bf16[512,256]{1,0:T(8,128)(2,1)S(1)}, bf16[512,256]{1,0:T(8,128)(2,1)S(1)}, u32[]{:S(2)}, u32[]{:S(2)}) collective-permute-start(bf16[512,256]{1,0:T(8,128)(2,1)S(1)} %copy-done.14), channel_id=1, source_target_pairs={{0,6},{2,4},{4,2},{6,0},{8,14},{10,12},{12,10},{14,8},{1,7},{3,5},... | collective-permute-start | bytes 786440 | tf_op jit(solution)/shard_map/ppermute | solution.py:259
  157.1 8.0 %collective-permute-start.19 = (f32[128,128]{1,0:T(8,128)S(1)}, f32[128,128]{1,0:T(8,128)S(1)}, u32[]{:S(2)}, u32[]{:S(2)}) collective-permute-start(f32[128,128]{1,0:T(8,128)S(1)} %get-tuple-element.136), channel_id=1, source_target_pairs={{0,8},{2,10},{4,12},{6,14},{1,9},{3,11},{5,13},{7,15},{16,24},{18,... | collective-permute-start | bytes 196616 | tf_op jit(solution)/shard_map/ppermute | solution.py:239
  159.4 5.8 %collective-permute-start.18 = (f32[128,128]{1,0:T(8,128)S(1)}, f32[128,128]{1,0:T(8,128)S(1)}, u32[]{:S(2)}, u32[]{:S(2)}) collective-permute-start(f32[128,128]{1,0:T(8,128)S(1)} %get-tuple-element.127), channel_id=1, source_target_pairs={{0,8},{2,10},{4,12},{6,14},{1,9},{3,11},{5,13},{7,15},{16,24},{18,... | collective-permute-start | bytes 196616 | tf_op jit(solution)/shard_map/ppermute | solution.py:239
  167.2 8.8 %collective-permute-start.20 = (bf16[384,256]{1,0:T(8,128)(2,1)S(1)}, bf16[384,256]{1,0:T(8,128)(2,1)S(1)}, u32[]{:S(2)}, u32[]{:S(2)}) collective-permute-start(bf16[384,256]{1,0:T(8,128)(2,1)S(1)} %get-tuple-element.142), channel_id=1, source_target_pairs={{0,2},{2,0},{4,6},{6,4},{8,10},{10,8},{12,14},{14,12},{1,3},{3,1},... | collective-permute-start | bytes 589832 | tf_op jit(solution)/shard_map/ppermute | solution.py:259
  168.6 7.4 %collective-permute-start.21 = (bf16[384,256]{1,0:T(8,128)(2,1)S(1)}, bf16[384,256]{1,0:T(8,128)(2,1)S(1)}, u32[]{:S(2)}, u32[]{:S(2)}) collective-permute-start(bf16[384,256]{1,0:T(8,128)(2,1)S(1)} %get-tuple-element.143), channel_id=1, source_target_pairs={{0,4},{2,6},{4,0},{6,2},{8,12},{10,14},{12,8},{14,10},{1,5},{3,7},... | collective-permute-start | bytes 589832 | tf_op jit(solution)/shard_map/ppermute | solution.py:259
  170.4 6.6 %collective-permute-start.22 = (bf16[384,256]{1,0:T(8,128)(2,1)S(1)}, bf16[384,256]{1,0:T(8,128)(2,1)S(1)}, u32[]{:S(2)}, u32[]{:S(2)}) collective-permute-start(bf16[384,256]{1,0:T(8,128)(2,1)S(1)} %get-tuple-element.144), channel_id=1, source_target_pairs={{0,6},{2,4},{4,2},{6,0},{8,14},{10,12},{12,10},{14,8},{1,7},{3,5},... | collective-permute-start | bytes 589832 | tf_op jit(solution)/shard_map/ppermute | solution.py:259
  176.9 2.8 %collective-permute-start.23 = (bf16[384,256]{1,0:T(8,128)(2,1)S(1)}, bf16[384,256]{1,0:T(8,128)(2,1)S(1)}, u32[]{:S(2)}, u32[]{:S(2)}) collective-permute-start(bf16[384,256]{1,0:T(8,128)(2,1)S(1)} %attend.2.refs_0_), channel_id=1, source_target_pairs={{0,1},{1,0},{2,3},{3,2},{4,5},{5,4},{6,7},{7,6},{8,9},{9,8},{10,11... | collective-permute-start | bytes 589832 | tf_op jit(solution)/shard_map/ppermute | solution.py:265
  176.9 2.8 %collective-permute-start.24 = (bf16[384,256]{1,0:T(8,128)(2,1)S(1)}, bf16[384,256]{1,0:T(8,128)(2,1)S(1)}, u32[]{:S(2)}, u32[]{:S(2)}) collective-permute-start(bf16[384,256]{1,0:T(8,128)(2,1)S(1)} %collective-permute-done.20.refs_1_), channel_id=1, source_target_pairs={{0,1},{1,0},{2,3},{3,2},{4,5},{5,4},{6,7},{7,6},{8,9},{9,8},{10,11... | collective-permute-start | bytes 589832 | tf_op jit(solution)/shard_map/ppermute | solution.py:265
  177.5 2.3 %collective-permute-start.25 = (bf16[384,256]{1,0:T(8,128)(2,1)S(1)}, bf16[384,256]{1,0:T(8,128)(2,1)S(1)}, u32[]{:S(2)}, u32[]{:S(2)}) collective-permute-start(bf16[384,256]{1,0:T(8,128)(2,1)S(1)} %collective-permute-done.21.refs_2_), channel_id=1, source_target_pairs={{0,1},{1,0},{2,3},{3,2},{4,5},{5,4},{6,7},{7,6},{8,9},{9,8},{10,11... | collective-permute-start | bytes 589832 | tf_op jit(solution)/shard_map/ppermute | solution.py:265
  177.5 2.4 %collective-permute-start.26 = (bf16[384,256]{1,0:T(8,128)(2,1)S(1)}, bf16[384,256]{1,0:T(8,128)(2,1)S(1)}, u32[]{:S(2)}, u32[]{:S(2)}) collective-permute-start(bf16[384,256]{1,0:T(8,128)(2,1)S(1)} %collective-permute-done.22.refs_3_), channel_id=1, source_target_pairs={{0,1},{1,0},{2,3},{3,2},{4,5},{5,4},{6,7},{7,6},{8,9},{9,8},{10,11... | collective-permute-start | bytes 589832 | tf_op jit(solution)/shard_map/ppermute | solution.py:265
  (15 other events, 45.2 us)

commit v8 on v7

--- a/solution.py
+++ b/solution.py
@@ -274,43 +274,50 @@
         return [lax.dynamic_index_in_dim(whole, ctx ^ m, keepdims=False) for m in range(n_ctx)]
 
     cut = half * 11 // 16 // HDIM * HDIM
+    pieced = n_ctx == 2 * SUB
+    ob = lax.optimization_barrier
+
     across = xor(tokens, 2)
     beside = xor(tokens, 1)
     kv_mine = spread(pack_keys_values(place, w_key, w_value, n_ctx))
+    far_tokens = other_core(tokens)
+    w_far = other_core(w_out)
+    beside, far_tokens, w_far, w_query = ob((beside, far_tokens, w_far, w_query))
     q_sent = pack_queries(place, w_query)
-    far_tokens = other_core(tokens)
     far_beside = other_core(beside)
-    w_far = other_core(w_out)
-    across, beside, kv_mine, q_sent, far_tokens, far_beside, w_far = lax.optimization_barrier(
-        (across, beside, kv_mine, q_sent, far_tokens, far_beside, w_far)
-    )
-    kv_other = other_part(kv_mine)
+
+    def fetch(sent, *steps):
+        if pieced:
+            arrived.update({m: xor(sent[m % SUB], m) for m in steps})
+
+    across, kv_mine, beside, far_beside, q_sent = ob((across, kv_mine, beside, far_beside, q_sent))
+    arrived = {0: q_sent[0]}
+    middle = kv_mine.shape[0] // 2
+    kv_upper = other_part(kv_mine[:middle])
     left = xor(across[:, :cut], 1)
     right = xor(beside[:, cut:], 2)
+    fetch(q_sent, 4, 6)
+    left, right, arrived, kv_upper, kv_mine, across, q_sent = ob(
+        (left, right, arrived, kv_upper, kv_mine, across, q_sent)
+    )
+    kv_lower = other_part(kv_mine[middle:])
+    fetch(q_sent, 5, 7, 3, 2, 1)
     near = [(tokens, 0, 0, 0), (far_tokens, 0, 0, 1), (beside, 1, 0, 0), (far_beside, 1, 0, 1)]
     near += [(across, 2, 0, 0), (other_core(across), 2, 0, 1)]
     near = stage(place, near, SUB - 1, rows, 2 * half)
-    first = project(near, kv_mine)
-    if n_ctx == 2 * SUB:
-        arrived = {0: q_sent[0]} | {m: xor(q_sent[m % SUB], m) for m in (4, 6)}
-        left, right, arrived, q_sent, first = lax.optimization_barrier((left, right, arrived, q_sent, first))
-        arrived = arrived | {m: xor(q_sent[m % SUB], m) for m in (5, 7)}
-    far_left, far_right = other_core(left), other_core(right)
-    if n_ctx == 2 * SUB:
-        far_left, q_sent = lax.optimization_barrier((far_left, q_sent))
-        arrived = arrived | {m: xor(q_sent[m % SUB], m) for m in (3, 2, 1)}
-        arrived, kv_other = lax.optimization_barrier((arrived, kv_other))
-        q_pieces = [arrived[m] for m in range(n_ctx)]
-    else:
-        q_pieces = gather_queries(q_sent)
-    corner = [(left, 0, 0, 0), (far_left, 0, 0, 1), (right, 0, cut, 0), (far_right, 0, cut, 1)]
+    corner = []
+    for array, column in ((left, 0), (right, cut)):
+        corner += [(array, 0, column, 0), (other_core(array), 0, column, 1)]
     corner = stage(place, corner, 1, rows, 2 * half)
 
     def head(parts):
         return [part[:3] for part in parts], exclusive_prefix(parts[-1][3], groups)
 
+    first = project(near, kv_mine)
     last = project(corner, kv_mine, first[3])
-    kv_other, last = lax.optimization_barrier((kv_other, last))
+    arrived, kv_lower, last = ob((arrived, kv_lower, last))
+    q_pieces = [arrived[m] for m in range(n_ctx)] if pieced else gather_queries(q_sent)
+    kv_other = [kv_upper, kv_lower]
     second = project(near, kv_other)
     heads = [head([first, last]), head([second, project(corner, kv_other, second[3])])]
     query = queries(place, [near, corner], q_pieces)

time: 183 us -> 180 us (0.984)
  local copies, waits for them, and re-layouts: 16.1 us -> 9.58 us
    unnamed x38 -> x26, local copies, waits for them, and re-layouts: 13.6 us -> 7.05 us
    ppermute x14, waiting for transfers between devices: 103 us -> 98.6 us  [xor(): return lax.ppermute(value, 'ctx', [(i, i ^ step) for i in range(n_ctx)])]
    ppermute x10, waiting for transfers between devices: 0.03 us -> 3.93 us  [other_core(): return lax.ppermute(value, 'head', [(0, 1), (1, 0)])]
  transfers between devices with their start and end apart: 28 -> 29, of which waited for: 8 -> 8; matrix products, arithmetic and copies ran while one was open for 1% -> 1% of each run, Pallas kernels for 11% -> 12%
where the time goes in v8:
time: 180 us; the launch traced here: 179 us
  waiting for transfers between devices  103 us (57%)
  starting transfers between devices  36.3 us (20%)
  Pallas kernels  30.5 us (17%)
  local copies, waits for them, and re-layouts  9.58 us (5%)
    ppermute x14, waiting for transfers between devices, xor(): return lax.ppermute(value, 'ctx', [(i, i ^ step) for i in range(n_ctx)])  98.6 us
    ppermute x14, starting transfers between devices, xor(): return lax.ppermute(value, 'ctx', [(i, i ^ step) for i in range(n_ctx)])  19.9 us
    pallas_call x4, Pallas kernels, project(): call(kernel, 'project', shapes, [VMEM] * len(args), [VMEM] * 4, LIMIT, fl...  8.51 us
    unnamed x26, local copies, waits for them, and re-layouts  7.05 us
    all_to_all x1, starting transfers between devices, spread(): return lax.all_to_all(packed, 'ctx', 0, 0, tiled=True)  6.93 us
    ppermute x2, starting transfers between devices, shift(): return lax.ppermute(v, 'ctx', pairs)  5.29 us
    pallas_call x2, Pallas kernels, add_features(): call(kernel, 'add_features', shape, [VMEM] * len(args), VMEM, LIMIT, flop...  4.74 us
    pallas_call x1, Pallas kernels, queries(): call(kernel, 'queries', shape, specs, VMEM, LIMIT, flops, 2 * MIB, [held])  4.31 us
  transfers between devices with their start and end apart: 29, of which 8 were waited for; matrix products, arithmetic and copies ran while one was open for 1% of the time, Pallas kernels for 12%

profile of v8, /device:TPU:0, one launch (start us, length us, event | category | flops | bytes accessed | tf_op | source)
XLA Modules:
  0.0 179.3 jit_solution(7961529418542976552)
XLA Ops:
  3.8 1.3 copy-done
  5.1 6.9 %all-to-all-start = ((bf16[8,512,256]{2,1,0:T(8,128)(2,1)}), bf16[8,512,256]{2,1,0:T(8,128)(2,1)S(1)}, u32[]{:S(2)}, u32[]{:S(2)}) async-start(bf16[8,512,256]{2,1,0:T(8,128)(2,1)} %bitcast.10), calls=%async_computation | async-start | bytes 4194304 | tf_op jit(solution)/shard_map/all_to_all | solution.py:268
  12.1 2.0 %collective-permute-start = (bf16[384,2048]{1,0:T(8,128)(2,1)}, bf16[384,2048]{1,0:T(8,128)(2,1)}, u32[]{:S(2)}, u32[]{:S(2)}) collective-permute-start(bf16[384,2048]{1,0:T(8,128)(2,1)} %refs_0_.1), channel_id=1, source_target_pairs={{0,2},{2,0},{4,6},{6,4},{8,10},{10,8},{12,14},{14,12},{1,3},{3,1},... | collective-permute-start | bytes 4718600 | tf_op jit(solution)/shard_map/ppermute | solution.py:259
  14.1 1.5 collective-permute-start.3
  15.6 55.8 %collective-permute-done.refs_2_ = bf16[384,2048]{1,0:T(8,128)(2,1)} collective-permute-done((bf16[384,2048]{1,0:T(8,128)(2,1)}, bf16[384,2048]{1,0:T(8,128)(2,1)}, u32[]{:S(2)}, u32[]{:S(2)}) %collective-permute-start) | collective-permute-done | bytes 1572896 | tf_op jit(solution)/shard_map/ppermute | solution.py:259
  75.3 7.3 %collective-permute-done.3.refs_4_ = bf16[384,2048]{1,0:T(8,128)(2,1)} collective-permute-done((bf16[384,2048]{1,0:T(8,128)(2,1)}, bf16[384,2048]{1,0:T(8,128)(2,1)}, u32[]{:S(2)}, u32[]{:S(2)}) %collective-permute-start.3) | collective-permute-done | bytes 1572896 | tf_op jit(solution)/shard_map/ppermute | solution.py:259
  82.7 1.3 slice.12
  84.0 1.5 collective-permute-start.5
  85.6 1.6 collective-permute-start.9
  88.3 1.6 collective-permute-start.6
  89.9 1.4 collective-permute-start.7
  91.3 1.5 collective-permute-start.8
  92.7 14.5 %collective-permute-done.7.refs_6_ = bf16[512,256]{1,0:T(8,128)(2,1)S(1)} collective-permute-done((bf16[512,256]{1,0:T(8,128)(2,1)S(1)}, bf16[512,256]{1,0:T(8,128)(2,1)S(1)}, u32[]{:S(2)}, u32[]{:S(2)}) %collective-permute-start.7) | collective-permute-done | bytes 262176 | tf_op jit(solution)/shard_map/ppermute | solution.py:259
  107.2 6.4 %collective-permute-done.8.refs_8_ = bf16[512,256]{1,0:T(8,128)(2,1)S(1)} collective-permute-done((bf16[512,256]{1,0:T(8,128)(2,1)S(1)}, bf16[512,256]{1,0:T(8,128)(2,1)S(1)}, u32[]{:S(2)}, u32[]{:S(2)}) %collective-permute-start.8) | collective-permute-done | bytes 262176 | tf_op jit(solution)/shard_map/ppermute | solution.py:259
  115.4 3.9 %collective-permute-done.12.refs_3_ = bf16[384,640]{1,0:T(8,128)(2,1)S(1)} collective-permute-done((bf16[384,640]{1,0:T(8,128)(2,1)S(1)}, bf16[384,640]{1,0:T(8,128)(2,1)S(1)}, u32[]{:S(2)}, u32[]{:S(2)}) %collective-permute-start.12) | collective-permute-done | bytes 491552 | tf_op jit(solution)/shard_map/ppermute | solution.py:265
  119.3 2.4 %collective-permute-start.16 = (bf16[512,256]{1,0:T(8,128)(2,1)S(1)}, bf16[512,256]{1,0:T(8,128)(2,1)S(1)}, u32[]{:S(2)}, u32[]{:S(2)}) collective-permute-start(bf16[512,256]{1,0:T(8,128)(2,1)S(1)} %copy-done.10), channel_id=1, source_target_pairs={{0,10},{2,8},{4,14},{6,12},{8,2},{10,0},{12,6},{14,4},{1,11},{3,9}... | collective-permute-start | bytes 786440 | tf_op jit(solution)/shard_map/ppermute | solution.py:259
  123.1 2.5 %collective-permute-start.17 = (bf16[512,256]{1,0:T(8,128)(2,1)S(1)}, bf16[512,256]{1,0:T(8,128)(2,1)S(1)}, u32[]{:S(2)}, u32[]{:S(2)}) collective-permute-start(bf16[512,256]{1,0:T(8,128)(2,1)S(1)} %copy-done.8), channel_id=1, source_target_pairs={{0,14},{2,12},{4,10},{6,8},{8,6},{10,4},{12,2},{14,0},{1,15},{3,13... | collective-permute-start | bytes 786440 | tf_op jit(solution)/shard_map/ppermute | solution.py:259
  125.6 3.3 %stage.2.stream_ref.refs_0_ = bf16[3,384,4096]{2,1,0:T(8,128)(2,1)S(1)} custom-call(s32[4]{0:T(128)S(1)} %pad_add_fusion.place_ref, bf16[384,2048]{1,0:T(8,128)(2,1)S(1)} %copy-done.1, bf16[384,2048]{1,0:T(8,128)(2,1)S(1)} %copy-done.3, bf16[384,2048]{1,0:T(8,128)(2,1)} %collective-permute-done.refs_2_, bf16[384,2048]{1,0:T(8,128)(2,1)} %collective-permute-done.4.refs_3_, ...), custom_call_target="tpu_custom_call" | custom-call | bytes 18874368 | tf_op jit(solution)/shard_map/stage/pallas_call | solution.py:117
  129.9 3.0 %project.4 = (bf16[3,384,128]{2,1,0:T(8,128)(2,1)S(1)}, bf16[3,384,128]{2,1,0:T(8,128)(2,1)S(1)}, f32[3,128,128]{2,1,0:T(8,128)S(1)}, f32[128,128]{1,0:T(8,128)S(1)}) custom-call(bf16[3,384,4096]{2,1,0:T(8,128)(2,1)S(1)} %stage.2.stream_ref.refs_0_, bf16[4096,256]{1,0:T(8,128)(2,1)S(1)} %bitcast.8), custom_call_target="tpu_custom_call" | custom-call | flops 2415919104 | bytes 2097152 | tf_op jit(solution)/shard_map/project/pallas_call | solution.py:145
  134.2 12.1 %collective-permute-done.14.refs_4_ = bf16[512,256]{1,0:T(8,128)(2,1)S(1)} collective-permute-done((bf16[512,256]{1,0:T(8,128)(2,1)S(1)}, bf16[512,256]{1,0:T(8,128)(2,1)S(1)}, u32[]{:S(2)}, u32[]{:S(2)}) %collective-permute-start.14) | collective-permute-done | bytes 262176 | tf_op jit(solution)/shard_map/ppermute | solution.py:259
  146.3 3.0 %project.6 = (bf16[3,384,128]{2,1,0:T(8,128)(2,1)S(1)}, bf16[3,384,128]{2,1,0:T(8,128)(2,1)S(1)}, f32[3,128,128]{2,1,0:T(8,128)S(1)}, f32[128,128]{1,0:T(8,128)S(1)}) custom-call(bf16[3,384,4096]{2,1,0:T(8,128)(2,1)S(1)} %stage.2.stream_ref.refs_0_, bf16[2048,256]{1,0:T(8,128)(2,1)S(1)} %collective-permute-done.9.refs_0_, ...), custom_call_target="tpu_custom_call" | custom-call | flops 2415919104 | bytes 2097152 | tf_op jit(solution)/shard_map/project/pallas_call | solution.py:145
  149.3 1.3 project.7
  150.6 3.8 %collective-permute-start.20 = (f32[128,128]{1,0:T(8,128)S(1)}, f32[128,128]{1,0:T(8,128)S(1)}, u32[]{:S(2)}, u32[]{:S(2)}) collective-permute-start(f32[128,128]{1,0:T(8,128)S(1)} %get-tuple-element.128), channel_id=1, source_target_pairs={{0,8},{2,10},{4,12},{6,14},{1,9},{3,11},{5,13},{7,15},{16,24},{18,... | collective-permute-start | bytes 196616 | tf_op jit(solution)/shard_map/ppermute | solution.py:239
  154.4 1.5 collective-permute-start.19
  155.9 4.3 %queries.1.query_ref = bf16[4,384,256]{2,1,0:T(8,128)(2,1)S(1)} custom-call(s32[4]{0:T(128)S(1)} %pad_add_fusion.place_ref, bf16[3,384,4096]{2,1,0:T(8,128)(2,1)S(1)} %stage.2.stream_ref.refs_0_, bf16[1,384,4096]{2,1,0:T(8,128)(2,1)S(1)} %stage.3.stream_ref.refs_1_, bf16[512,256]{1,0:T(8,128)(2,1)S(1)} %get-tuple-element.104.refs_2_, ...), custom_call_target="tpu_custom_call" | custom-call | flops 3221225472 | bytes 2097152 | tf_op jit(solution)/shard_map/queries/pallas_call | solution.py:170
  160.2 2.0 %attend.3 = (bf16[384,256]{1,0:T(8,128)(2,1)S(1)}, bf16[384,256]{1,0:T(8,128)(2,1)S(1)}, bf16[384,256]{1,0:T(8,128)(2,1)S(1)}) custom-call(s32[4]{0:T(128)S(1)} %pad_add_fusion.place_ref, bf16[4,384,256]{2,1,0:T(8,128)(2,1)S(1)} %queries.1.query_ref, bf16[3,384,128]{2,1,0:T(8,128)(2,1)S(1)} %get-tuple-element.112.refs_0_, ...), custom_call_target="tpu_custom_call" | custom-call | flops 528482304 | bytes 2097152 | tf_op jit(solution)/shard_map/attend/pallas_call | solution.py:212
  162.2 1.7 collective-permute-start.21
  163.9 1.8 %collective-permute-start.23 = (bf16[384,256]{1,0:T(8,128)(2,1)S(1)}, bf16[384,256]{1,0:T(8,128)(2,1)S(1)}, u32[]{:S(2)}, u32[]{:S(2)}) collective-permute-start(bf16[384,256]{1,0:T(8,128)(2,1)S(1)} %get-tuple-element.136), channel_id=1, source_target_pairs={{0,6},{2,4},{4,2},{6,0},{8,14},{10,12},{12,10},{14,8},{1,7},{3,5},... | collective-permute-start | bytes 589832 | tf_op jit(solution)/shard_map/ppermute | solution.py:259
  167.0 4.0 %stage_rows.1 = (bf16[4,256,2048]{2,1,0:T(8,128)(2,1)S(1)}, bf16[4,256,2048]{2,1,0:T(8,128)(2,1)S(1)}) custom-call(s32[4]{0:T(128)S(1)} %pad_add_fusion.place_ref, bf16[1024,4096]{1,0:T(8,128)(2,1)} %out_ref.1, bf16[1024,4096]{1,0:T(8,128)(2,1)} %collective-permute-done.2.far_ref), custom_call_target="tpu_custom_call" | custom-call | bytes 16777216 | tf_op jit(solution)/shard_map/stage_rows/pallas_call | solution.py:89
  171.6 1.9 %collective-permute-done.23.refs_3_ = bf16[384,256]{1,0:T(8,128)(2,1)S(1)} collective-permute-done((bf16[384,256]{1,0:T(8,128)(2,1)S(1)}, bf16[384,256]{1,0:T(8,128)(2,1)S(1)}, u32[]{:S(2)}, u32[]{:S(2)}) %collective-permute-start.23) | collective-permute-done | bytes 196640 | tf_op jit(solution)/shard_map/ppermute | solution.py:259
  174.5 1.8 %add_features.2.refs_5_ = f32[384,2048]{1,0:T(8,128)S(1)} custom-call(bf16[384,256]{1,0:T(8,128)(2,1)S(1)} %attend.2.refs_0_, bf16[384,256]{1,0:T(8,128)(2,1)S(1)} %collective-permute-done.21.refs_1_, bf16[384,256]{1,0:T(8,128)(2,1)S(1)} %collective-permute-done.22.refs_2_, bf16[384,256]{1,0:T(8,128)(2,1)S(1)} %collective-permute-done.23.refs_3_, ...), custom_call_target="tpu_custom_call" | custom-call | flops 1610612736 | bytes 8388608 | tf_op jit(solution)/shard_map/add_features/pallas_call | solution.py:233
  176.4 2.9 %add_features.3 = bf16[384,2048]{1,0:T(8,128)(2,1)} custom-call(bf16[384,256]{1,0:T(8,128)(2,1)S(1)} %collective-permute-done.24.refs_0_, bf16[384,256]{1,0:T(8,128)(2,1)S(1)} %collective-permute-done.25.refs_1_, bf16[384,256]{1,0:T(8,128)(2,1)S(1)} %collective-permute-done.26.refs_2_, bf16[384,256]{1,0:T(8,128)(2,1)S(1)} %collective-permute-done.27.refs_3_, ...), custom_call_target="tpu_custom_call" | custom-call | flops 1610612736 | bytes 8388608 | tf_op jit(solution)/shard_map/add_features/pallas_call | solution.py:233
  (71 shorter events, 17.1 us)
Async XLA Ops:
  0.0 72.5 %collective-permute-start.2 = (bf16[1024,4096]{1,0:T(8,128)(2,1)}, bf16[1024,4096]{1,0:T(8,128)(2,1)}, u32[]{:S(2)}, u32[]{:S(2)}) collective-permute-start(bf16[1024,4096]{1,0:T(8,128)(2,1)} %out_ref.1), channel_id=1, source_target_pairs={{0,1},{1,0},{2,3},{3,2},{4,5},{5,4},{6,7},{7,6},{8,9},{9,8},{10,11... | collective-permute-start | bytes 25165832 | tf_op jit(solution)/shard_map/ppermute | solution.py:265
  5.1 67.4 %copy-start.6 = (bf16[512,1024]{1,0:T(8,128)(2,1)S(1)}, bf16[512,1024]{1,0:T(8,128)(2,1)}, u32[]{:S(2)}) copy-start(bf16[512,1024]{1,0:T(8,128)(2,1)} %query_ref) | copy-start | bytes 3145732
  5.1 77.5 %all-to-all-start = ((bf16[8,512,256]{2,1,0:T(8,128)(2,1)}), bf16[8,512,256]{2,1,0:T(8,128)(2,1)S(1)}, u32[]{:S(2)}, u32[]{:S(2)}) async-start(bf16[8,512,256]{2,1,0:T(8,128)(2,1)} %bitcast.10), calls=%async_computation | async-start | bytes 4194304 | tf_op jit(solution)/shard_map/all_to_all | solution.py:268
  12.1 59.3 %collective-permute-start = (bf16[384,2048]{1,0:T(8,128)(2,1)}, bf16[384,2048]{1,0:T(8,128)(2,1)}, u32[]{:S(2)}, u32[]{:S(2)}) collective-permute-start(bf16[384,2048]{1,0:T(8,128)(2,1)} %refs_0_.1), channel_id=1, source_target_pairs={{0,2},{2,0},{4,6},{6,4},{8,10},{10,8},{12,14},{14,12},{1,3},{3,1},... | collective-permute-start | bytes 4718600 | tf_op jit(solution)/shard_map/ppermute | solution.py:259
  14.1 57.3 %collective-permute-start.1 = (bf16[384,2048]{1,0:T(8,128)(2,1)}, bf16[384,2048]{1,0:T(8,128)(2,1)S(1)}, u32[]{:S(2)}, u32[]{:S(2)}) collective-permute-start(bf16[384,2048]{1,0:T(8,128)(2,1)} %refs_0_.1), channel_id=1, source_target_pairs={{0,1},{1,0},{2,3},{3,2},{4,5},{5,4},{6,7},{7,6},{8,9},{9,8},{10,11... | collective-permute-start | bytes 4718600 | tf_op jit(solution)/shard_map/ppermute | solution.py:265
  14.1 68.6 %collective-permute-start.3 = (bf16[384,2048]{1,0:T(8,128)(2,1)}, bf16[384,2048]{1,0:T(8,128)(2,1)}, u32[]{:S(2)}, u32[]{:S(2)}) collective-permute-start(bf16[384,2048]{1,0:T(8,128)(2,1)} %refs_0_.1), channel_id=1, source_target_pairs={{0,4},{2,6},{4,0},{6,2},{8,12},{10,14},{12,8},{14,10},{1,5},{3,7},... | collective-permute-start | bytes 4718600 | tf_op jit(solution)/shard_map/ppermute | solution.py:259
  72.5 10.1 %collective-permute-start.4 = (bf16[384,2048]{1,0:T(8,128)(2,1)}, bf16[384,2048]{1,0:T(8,128)(2,1)}, u32[]{:S(2)}, u32[]{:S(2)}) collective-permute-start(bf16[384,2048]{1,0:T(8,128)(2,1)} %collective-permute-done.refs_2_), channel_id=1, source_target_pairs={{0,1},{1,0},{2,3},{3,2},{4,5},{5,4},{6,7},{7,6},{8,9},{9,8},{10,11... | collective-permute-start | bytes 4718600 | tf_op jit(solution)/shard_map/ppermute | solution.py:265
  84.0 29.6 %collective-permute-start.5 = (bf16[384,1408]{1,0:T(8,128)(2,1)S(1)}, bf16[384,1408]{1,0:T(8,128)(2,1)S(1)}, u32[]{:S(2)}, u32[]{:S(2)}) collective-permute-start(bf16[384,1408]{1,0:T(8,128)(2,1)S(1)} %slice.12), channel_id=1, source_target_pairs={{0,2},{2,0},{4,6},{6,4},{8,10},{10,8},{12,14},{14,12},{1,3},{3,1},... | collective-permute-start | bytes 3244040 | tf_op jit(solution)/shard_map/ppermute | solution.py:259
  85.6 29.3 %copy-start.10 = (bf16[512,256]{1,0:T(8,128)(2,1)S(1)}, bf16[512,256]{1,0:T(8,128)(2,1)}, u32[]{:S(2)}) copy-start(bf16[512,256]{1,0:T(8,128)(2,1)} %copy-done.9) | copy-start | bytes 786436
  85.6 36.1 %copy-start.8 = (bf16[512,256]{1,0:T(8,128)(2,1)S(1)}, bf16[512,256]{1,0:T(8,128)(2,1)}, u32[]{:S(2)}) copy-start(bf16[512,256]{1,0:T(8,128)(2,1)} %copy-done.7) | copy-start | bytes 786436
  85.6 28.0 %collective-permute-start.9 = (bf16[2048,256]{1,0:T(8,128)(2,1)S(1)}, bf16[2048,256]{1,0:T(8,128)(2,1)S(1)}, u32[]{:S(2)}, u32[]{:S(2)}) collective-permute-start(bf16[2048,256]{1,0:T(8,128)(2,1)S(1)} %slice.14), channel_id=1, source_target_pairs={{0,16},{16,0},{1,17},{17,1},{2,18},{18,2},{3,19},{19,3},{4,20},{20... | collective-permute-start | bytes 3145736 | tf_op jit(solution)/shard_map/ppermute | solution.py:262
  88.3 25.3 %collective-permute-start.6 = (bf16[384,640]{1,0:T(8,128)(2,1)S(1)}, bf16[384,640]{1,0:T(8,128)(2,1)S(1)}, u32[]{:S(2)}, u32[]{:S(2)}) collective-permute-start(bf16[384,640]{1,0:T(8,128)(2,1)S(1)} %slice.13), channel_id=1, source_target_pairs={{0,4},{2,6},{4,0},{6,2},{8,12},{10,14},{12,8},{14,10},{1,5},{3,7},... | collective-permute-start | bytes 1474568 | tf_op jit(solution)/shard_map/ppermute | solution.py:259
  89.9 17.3 %collective-permute-start.7 = (bf16[512,256]{1,0:T(8,128)(2,1)S(1)}, bf16[512,256]{1,0:T(8,128)(2,1)S(1)}, u32[]{:S(2)}, u32[]{:S(2)}) collective-permute-start(bf16[512,256]{1,0:T(8,128)(2,1)S(1)} %get-tuple-element.104.refs_2_), channel_id=1, source_target_pairs={{0,8},{2,10},{4,12},{6,14},{8,0},{10,2},{12,4},{14,6},{1,9},{3,11}... | collective-permute-start | bytes 786440 | tf_op jit(solution)/shard_map/ppermute | solution.py:259
  91.3 22.3 %collective-permute-start.8 = (bf16[512,256]{1,0:T(8,128)(2,1)S(1)}, bf16[512,256]{1,0:T(8,128)(2,1)S(1)}, u32[]{:S(2)}, u32[]{:S(2)}) collective-permute-start(bf16[512,256]{1,0:T(8,128)(2,1)S(1)} %copy-done.12), channel_id=1, source_target_pairs={{0,12},{2,14},{4,8},{6,10},{8,4},{10,6},{12,0},{14,2},{1,13},{3,15... | collective-permute-start | bytes 786440 | tf_op jit(solution)/shard_map/ppermute | solution.py:259
  113.6 9.5 %collective-permute-start.10 = (bf16[384,2048]{1,0:T(8,128)(2,1)}, bf16[384,2048]{1,0:T(8,128)(2,1)S(1)}, u32[]{:S(2)}, u32[]{:S(2)}) collective-permute-start(bf16[384,2048]{1,0:T(8,128)(2,1)} %collective-permute-done.3.refs_4_), channel_id=1, source_target_pairs={{0,1},{1,0},{2,3},{3,2},{4,5},{5,4},{6,7},{7,6},{8,9},{9,8},{10,11... | collective-permute-start | bytes 4718600 | tf_op jit(solution)/shard_map/ppermute | solution.py:265
  113.7 8.0 %collective-permute-start.11 = (bf16[384,1408]{1,0:T(8,128)(2,1)S(1)}, bf16[384,1408]{1,0:T(8,128)(2,1)S(1)}, u32[]{:S(2)}, u32[]{:S(2)}) collective-permute-start(bf16[384,1408]{1,0:T(8,128)(2,1)S(1)} %collective-permute-done.5.refs_0_), channel_id=1, source_target_pairs={{0,1},{1,0},{2,3},{3,2},{4,5},{5,4},{6,7},{7,6},{8,9},{9,8},{10,11... | collective-permute-start | bytes 3244040 | tf_op jit(solution)/shard_map/ppermute | solution.py:265
  114.3 32.0 %collective-permute-start.18 = (bf16[2048,256]{1,0:T(8,128)(2,1)S(1)}, bf16[2048,256]{1,0:T(8,128)(2,1)S(1)}, u32[]{:S(2)}, u32[]{:S(2)}) collective-permute-start(bf16[2048,256]{1,0:T(8,128)(2,1)S(1)} %slice.15), channel_id=1, source_target_pairs={{0,16},{16,0},{1,17},{17,1},{2,18},{18,2},{3,19},{19,3},{4,20},{20... | collective-permute-start | bytes 3145736 | tf_op jit(solution)/shard_map/ppermute | solution.py:262
  114.9 4.5 %collective-permute-start.12 = (bf16[384,640]{1,0:T(8,128)(2,1)S(1)}, bf16[384,640]{1,0:T(8,128)(2,1)S(1)}, u32[]{:S(2)}, u32[]{:S(2)}) collective-permute-start(bf16[384,640]{1,0:T(8,128)(2,1)S(1)} %collective-permute-done.6.refs_2_), channel_id=1, source_target_pairs={{0,1},{1,0},{2,3},{3,2},{4,5},{5,4},{6,7},{7,6},{8,9},{9,8},{10,11... | collective-permute-start | bytes 1474568 | tf_op jit(solution)/shard_map/ppermute | solution.py:265
  114.9 14.1 %collective-permute-start.13 = (bf16[512,256]{1,0:T(8,128)(2,1)S(1)}, bf16[512,256]{1,0:T(8,128)(2,1)S(1)}, u32[]{:S(2)}, u32[]{:S(2)}) collective-permute-start(bf16[512,256]{1,0:T(8,128)(2,1)S(1)} %copy-done.10), channel_id=1, source_target_pairs={{0,2},{2,0},{4,6},{6,4},{8,10},{10,8},{12,14},{14,12},{1,3},{3,1},... | collective-permute-start | bytes 786440 | tf_op jit(solution)/shard_map/ppermute | solution.py:259
  119.3 26.9 %collective-permute-start.16 = (bf16[512,256]{1,0:T(8,128)(2,1)S(1)}, bf16[512,256]{1,0:T(8,128)(2,1)S(1)}, u32[]{:S(2)}, u32[]{:S(2)}) collective-permute-start(bf16[512,256]{1,0:T(8,128)(2,1)S(1)} %copy-done.10), channel_id=1, source_target_pairs={{0,10},{2,8},{4,14},{6,12},{8,2},{10,0},{12,6},{14,4},{1,11},{3,9}... | collective-permute-start | bytes 786440 | tf_op jit(solution)/shard_map/ppermute | solution.py:259
  121.7 24.5 %collective-permute-start.15 = (bf16[512,256]{1,0:T(8,128)(2,1)S(1)}, bf16[512,256]{1,0:T(8,128)(2,1)S(1)}, u32[]{:S(2)}, u32[]{:S(2)}) collective-permute-start(bf16[512,256]{1,0:T(8,128)(2,1)S(1)} %copy-done.8), channel_id=1, source_target_pairs={{0,6},{2,4},{4,2},{6,0},{8,14},{10,12},{12,10},{14,8},{1,7},{3,5},... | collective-permute-start | bytes 786440 | tf_op jit(solution)/shard_map/ppermute | solution.py:259
  123.1 23.1 %collective-permute-start.17 = (bf16[512,256]{1,0:T(8,128)(2,1)S(1)}, bf16[512,256]{1,0:T(8,128)(2,1)S(1)}, u32[]{:S(2)}, u32[]{:S(2)}) collective-permute-start(bf16[512,256]{1,0:T(8,128)(2,1)S(1)} %copy-done.8), channel_id=1, source_target_pairs={{0,14},{2,12},{4,10},{6,8},{8,6},{10,4},{12,2},{14,0},{1,15},{3,13... | collective-permute-start | bytes 786440 | tf_op jit(solution)/shard_map/ppermute | solution.py:259
  129.0 17.3 %collective-permute-start.14 = (bf16[512,256]{1,0:T(8,128)(2,1)S(1)}, bf16[512,256]{1,0:T(8,128)(2,1)S(1)}, u32[]{:S(2)}, u32[]{:S(2)}) collective-permute-start(bf16[512,256]{1,0:T(8,128)(2,1)S(1)} %copy-done.12), channel_id=1, source_target_pairs={{0,4},{2,6},{4,0},{6,2},{8,12},{10,14},{12,8},{14,10},{1,5},{3,7},... | collective-permute-start | bytes 786440 | tf_op jit(solution)/shard_map/ppermute | solution.py:259
  150.6 9.6 %collective-permute-start.20 = (f32[128,128]{1,0:T(8,128)S(1)}, f32[128,128]{1,0:T(8,128)S(1)}, u32[]{:S(2)}, u32[]{:S(2)}) collective-permute-start(f32[128,128]{1,0:T(8,128)S(1)} %get-tuple-element.128), channel_id=1, source_target_pairs={{0,8},{2,10},{4,12},{6,14},{1,9},{3,11},{5,13},{7,15},{16,24},{18,... | collective-permute-start | bytes 196616 | tf_op jit(solution)/shard_map/ppermute | solution.py:239
  154.4 5.8 %collective-permute-start.19 = (f32[128,128]{1,0:T(8,128)S(1)}, f32[128,128]{1,0:T(8,128)S(1)}, u32[]{:S(2)}, u32[]{:S(2)}) collective-permute-start(f32[128,128]{1,0:T(8,128)S(1)} %get-tuple-element.118), channel_id=1, source_target_pairs={{0,8},{2,10},{4,12},{6,14},{1,9},{3,11},{5,13},{7,15},{16,24},{18,... | collective-permute-start | bytes 196616 | tf_op jit(solution)/shard_map/ppermute | solution.py:239
  162.2 8.8 %collective-permute-start.21 = (bf16[384,256]{1,0:T(8,128)(2,1)S(1)}, bf16[384,256]{1,0:T(8,128)(2,1)S(1)}, u32[]{:S(2)}, u32[]{:S(2)}) collective-permute-start(bf16[384,256]{1,0:T(8,128)(2,1)S(1)} %get-tuple-element.134), channel_id=1, source_target_pairs={{0,2},{2,0},{4,6},{6,4},{8,10},{10,8},{12,14},{14,12},{1,3},{3,1},... | collective-permute-start | bytes 589832 | tf_op jit(solution)/shard_map/ppermute | solution.py:259
  163.9 7.7 %collective-permute-start.22 = (bf16[384,256]{1,0:T(8,128)(2,1)S(1)}, bf16[384,256]{1,0:T(8,128)(2,1)S(1)}, u32[]{:S(2)}, u32[]{:S(2)}) collective-permute-start(bf16[384,256]{1,0:T(8,128)(2,1)S(1)} %get-tuple-element.135), channel_id=1, source_target_pairs={{0,4},{2,6},{4,0},{6,2},{8,12},{10,14},{12,8},{14,10},{1,5},{3,7},... | collective-permute-start | bytes 589832 | tf_op jit(solution)/shard_map/ppermute | solution.py:259
  163.9 9.6 %collective-permute-start.23 = (bf16[384,256]{1,0:T(8,128)(2,1)S(1)}, bf16[384,256]{1,0:T(8,128)(2,1)S(1)}, u32[]{:S(2)}, u32[]{:S(2)}) collective-permute-start(bf16[384,256]{1,0:T(8,128)(2,1)S(1)} %get-tuple-element.136), channel_id=1, source_target_pairs={{0,6},{2,4},{4,2},{6,0},{8,14},{10,12},{12,10},{14,8},{1,7},{3,5},... | collective-permute-start | bytes 589832 | tf_op jit(solution)/shard_map/ppermute | solution.py:259
  173.5 2.8 %collective-permute-start.24 = (bf16[384,256]{1,0:T(8,128)(2,1)S(1)}, bf16[384,256]{1,0:T(8,128)(2,1)S(1)}, u32[]{:S(2)}, u32[]{:S(2)}) collective-permute-start(bf16[384,256]{1,0:T(8,128)(2,1)S(1)} %attend.2.refs_0_), channel_id=1, source_target_pairs={{0,1},{1,0},{2,3},{3,2},{4,5},{5,4},{6,7},{7,6},{8,9},{9,8},{10,11... | collective-permute-start | bytes 589832 | tf_op jit(solution)/shard_map/ppermute | solution.py:265
  173.5 2.8 %collective-permute-start.25 = (bf16[384,256]{1,0:T(8,128)(2,1)S(1)}, bf16[384,256]{1,0:T(8,128)(2,1)S(1)}, u32[]{:S(2)}, u32[]{:S(2)}) collective-permute-start(bf16[384,256]{1,0:T(8,128)(2,1)S(1)} %collective-permute-done.21.refs_1_), channel_id=1, source_target_pairs={{0,1},{1,0},{2,3},{3,2},{4,5},{5,4},{6,7},{7,6},{8,9},{9,8},{10,11... | collective-permute-start | bytes 589832 | tf_op jit(solution)/shard_map/ppermute | solution.py:265
  174.0 2.3 %collective-permute-start.26 = (bf16[384,256]{1,0:T(8,128)(2,1)S(1)}, bf16[384,256]{1,0:T(8,128)(2,1)S(1)}, u32[]{:S(2)}, u32[]{:S(2)}) collective-permute-start(bf16[384,256]{1,0:T(8,128)(2,1)S(1)} %collective-permute-done.22.refs_2_), channel_id=1, source_target_pairs={{0,1},{1,0},{2,3},{3,2},{4,5},{5,4},{6,7},{7,6},{8,9},{9,8},{10,11... | collective-permute-start | bytes 589832 | tf_op jit(solution)/shard_map/ppermute | solution.py:265
  174.0 2.4 %collective-permute-start.27 = (bf16[384,256]{1,0:T(8,128)(2,1)S(1)}, bf16[384,256]{1,0:T(8,128)(2,1)S(1)}, u32[]{:S(2)}, u32[]{:S(2)}) collective-permute-start(bf16[384,256]{1,0:T(8,128)(2,1)S(1)} %collective-permute-done.23.refs_3_), channel_id=1, source_target_pairs={{0,1},{1,0},{2,3},{3,2},{4,5},{5,4},{6,7},{7,6},{8,9},{9,8},{10,11... | collective-permute-start | bytes 589832 | tf_op jit(solution)/shard_map/ppermute | solution.py:265
  (10 other events, 37.1 us)

commit v9 on v8

--- a/solution.py
+++ b/solution.py
@@ -145,29 +145,82 @@
     return call(kernel, "project", shapes, [VMEM] * len(args), [VMEM] * 4, LIMIT, flops, 2 * MIB)(*args)
 
 
-def queries(place, streams, pieces):
-    _, rows, width = streams[0].shape
-    count = len(pieces)
-    depth = pieces[0].shape[0]
-
-    def kernel(place_ref, *refs):
-        sources, ins = refs[: len(streams)], refs[len(streams) : len(streams) + count]
-        out, w_held = refs[-2:]
-        for m, piece in enumerate(ins):
-            row = pl.multiple_of(jnp.bitwise_xor(place_ref[3], m) * depth, depth)
-            w_held[pl.ds(row, depth), :] = piece[...]
+def flat_blocks(streams):
+    return [(stream, r) for stream in streams for r in range(stream.shape[0])]
+
+
+def weighted(place_ref, source, r, refs, parts, base):
+    total = base
+    for ref, (weight, start) in zip(refs, parts):
+        depth = weight.shape[0]
+        if isinstance(start, tuple):
+            lanes = pl.ds(pl.multiple_of(jnp.bitwise_xor(place_ref[3], start[0]) * depth, HDIM), depth)
+        else:
+            lanes = slice(start, start + depth)
+        term = dot(source[r, :, lanes], ref[...])
+        total = term if total is None else total + term
+    return total
+
+
+def run_blocks(kernel, name, place, streams, parts, base, out_shape):
+    rows, width = streams[0].shape[1:]
+    count = len(streams)
+    args = [*streams, *[weight for weight, _ in parts], *([] if base is None else [base])]
+
+    def body(place_ref, *refs):
+        weights = refs[count : count + len(parts)]
+        base_ref = None if base is None else refs[len(args) - 1]
+
+        def sums():
+            for i, (source, r) in enumerate(flat_blocks(refs[:count])):
+                yield i, weighted(place_ref, source, r, weights, parts, None if base is None else base_ref[i])
+
+        kernel(place_ref, sums, *refs[len(args) :])
+
+    flops = 4 * SUB * rows * sum(weight.shape[0] for weight, _ in parts) * HDIM
+    specs = [SMEM] + [VMEM] * len(args)
+    outs = [VMEM] * len(out_shape) if isinstance(out_shape, list) else VMEM
+    return call(body, name, out_shape, specs, outs, LIMIT, flops, 2 * MIB)(place, *args)
+
+
+def begin(place, streams, parts):
+    def kernel(place_ref, sums, out):
+        for i, total in sums():
+            out[i] = total
+
+    shape = pltpu.VMEM((SUB, streams[0].shape[1], 2 * HDIM), F32)
+    return run_blocks(kernel, "begin", place, streams, parts, None, shape)
+
+
+def keys_values(place, streams, parts, base):
+    rows = streams[0].shape[1]
+
+    def kernel(place_ref, sums, key_ref, value_ref, state_ref, total_ref):
+        for i, both in sums():
+            key_ref[i] = silu(both[:, :HDIM]).astype(BF16)
+            value_ref[i] = both[:, HDIM:].astype(BF16)
+        added = jnp.zeros((HDIM, HDIM), F32)
+        for i in range(SUB):
+            state = dot(key_ref[i], value_ref[i], ((0,), (0,)))
+            state_ref[i] = state
+            added = added + state
+        total_ref[...] = added
+
+    shape = jax.ShapeDtypeStruct((SUB, rows, HDIM), BF16)
+    shapes = [shape, shape, jax.ShapeDtypeStruct((SUB, HDIM, HDIM), F32), jax.ShapeDtypeStruct((HDIM, HDIM), F32)]
+    return run_blocks(kernel, "keys_values", place, streams, parts, base, shapes)
+
+
+def queries(place, streams, parts, base):
+    def kernel(place_ref, sums, out):
         swap = place_ref[1] == 1
-        blocks = [(source, r) for source in sources for r in range(source.shape[0])]
-        for i, (source, r) in enumerate(blocks):
-            both = silu(dot(source[r], w_held[...])).astype(BF16)
+        for i, total in sums():
+            both = silu(total).astype(BF16)
             out[i, :, :HDIM] = jnp.where(swap, both[:, HDIM:], both[:, :HDIM])
             out[i, :, HDIM:] = jnp.where(swap, both[:, :HDIM], both[:, HDIM:])
 
-    shape = jax.ShapeDtypeStruct((SUB, rows, 2 * HDIM), BF16)
-    flops = 4 * SUB * rows * width * HDIM
-    held = pltpu.VMEM((width, 2 * HDIM), BF16)
-    specs = [SMEM] + [VMEM] * (len(streams) + count)
-    return call(kernel, "queries", shape, specs, VMEM, LIMIT, flops, 2 * MIB, [held])(place, *streams, *pieces)
+    shape = jax.ShapeDtypeStruct((SUB, streams[0].shape[1], 2 * HDIM), BF16)
+    return run_blocks(kernel, "queries", place, streams, parts, base, shape)
 
 
 def attend(place, blocks, query, heads):
@@ -268,10 +321,8 @@
         return lax.all_to_all(packed, "ctx", 0, 0, tiled=True)
 
     def gather_queries(sent):
-        block = ctx % SUB
-        ordered = [lax.dynamic_index_in_dim(jnp.stack(sent), block ^ j, keepdims=False) for j in range(SUB)]
-        whole = spread(jnp.concatenate(ordered * groups, axis=0)).reshape(n_ctx, -1, 2 * HDIM)
-        return [lax.dynamic_index_in_dim(whole, ctx ^ m, keepdims=False) for m in range(n_ctx)]
+        ordered = [lax.dynamic_index_in_dim(jnp.stack(sent), (ctx % SUB) ^ j, keepdims=False) for j in range(SUB)]
+        return spread(jnp.concatenate(ordered * groups, axis=0))
 
     cut = half * 11 // 16 // HDIM * HDIM
     pieced = n_ctx == 2 * SUB
@@ -297,30 +348,35 @@
     left = xor(across[:, :cut], 1)
     right = xor(beside[:, cut:], 2)
     fetch(q_sent, 4, 6)
-    left, right, arrived, kv_upper, kv_mine, across, q_sent = ob(
-        (left, right, arrived, kv_upper, kv_mine, across, q_sent)
-    )
-    kv_lower = other_part(kv_mine[middle:])
-    fetch(q_sent, 5, 7, 3, 2, 1)
     near = [(tokens, 0, 0, 0), (far_tokens, 0, 0, 1), (beside, 1, 0, 0), (far_beside, 1, 0, 1)]
     near += [(across, 2, 0, 0), (other_core(across), 2, 0, 1)]
     near = stage(place, near, SUB - 1, rows, 2 * half)
-    corner = []
-    for array, column in ((left, 0), (right, cut)):
-        corner += [(array, 0, column, 0), (other_core(array), 0, column, 1)]
+    first = project(near, kv_mine)
+    left, right, arrived, kv_upper, kv_mine, q_sent, first = ob(
+        (left, right, arrived, kv_upper, kv_mine, q_sent, first)
+    )
+    kv_lower = other_part(kv_mine[middle:])
+    fetch(q_sent, 5, 7)
+    far_left, far_right = other_core(left), other_core(right)
+    far_left, q_sent = ob((far_left, q_sent))
+    fetch(q_sent, 3, 2, 1)
+    corner = [(left, 0, 0, 0), (far_left, 0, 0, 1), (right, 0, cut, 0), (far_right, 0, cut, 1)]
     corner = stage(place, corner, 1, rows, 2 * half)
 
-    def head(parts):
-        return [part[:3] for part in parts], exclusive_prefix(parts[-1][3], groups)
-
-    first = project(near, kv_mine)
+    streams = [near, corner]
     last = project(corner, kv_mine, first[3])
-    arrived, kv_lower, last = ob((arrived, kv_lower, last))
-    q_pieces = [arrived[m] for m in range(n_ctx)] if pieced else gather_queries(q_sent)
-    kv_other = [kv_upper, kv_lower]
-    second = project(near, kv_other)
-    heads = [head([first, last]), head([second, project(corner, kv_other, second[3])])]
-    query = queries(place, [near, corner], q_pieces)
+    carried = exclusive_prefix(last[3], groups)
+    kv_base = begin(place, streams, [(kv_upper, 0)])
+    if pieced:
+        early = (0, 4, 6)
+        q_base = begin(place, streams, [(arrived[m], (m,)) for m in early])
+        arrived, kv_lower, carried, kv_base, q_base = ob((arrived, kv_lower, carried, kv_base, q_base))
+        q_parts = [(arrived[m], (m,)) for m in range(n_ctx) if m not in early]
+    else:
+        q_base, q_parts = None, [(gather_queries(q_sent), 0)]
+    second = keys_values(place, streams, [(kv_lower, middle)], kv_base)
+    heads = [([first[:3], last[:3]], carried), ([second[:3]], exclusive_prefix(second[3], groups))]
+    query = queries(place, streams, q_parts, q_base)
     away = attend(place, (3, 1, 2), query, heads)
     home = attend(place, (0,), query, heads)
     normed = [home[0], xor(away[1], 1), xor(away[2], 2), xor(away[0], 3)]

time: 180 us -> 180 us (level)
  waiting for transfers between devices: 103 us -> 94.2 us
  starting transfers between devices: 36.3 us -> 43.2 us
    ppermute x2, starting transfers between devices: 5.29 us -> 14.1 us  [shift(): return lax.ppermute(v, 'ctx', pairs)]
    pallas_call x1 -> x4, Pallas kernels: 4.31 us -> 9.99 us  [run_blocks(): call(body, name, out_shape, specs, outs, LIMIT, flops, 2 * MIB)]
    ppermute x14, waiting for transfers between devices: 98.6 us -> 94.1 us  [xor(): return lax.ppermute(value, 'ctx', [(i, i ^ step) for i in range(n_ctx)])]
    pallas_call x4 -> x2, Pallas kernels: 8.51 us -> 4.25 us  [project(): call(kernel, 'project', shapes, [VMEM] * len(args), [VMEM] * 4, LIMIT, fl...]
    ppermute x10, waiting for transfers between devices: 3.93 us -> 0.03 us  [other_core(): return lax.ppermute(value, 'head', [(0, 1), (1, 0)])]
  transfers between devices with their start and end apart: 29 -> 29, of which waited for: 8 -> 6; matrix products, arithmetic and copies ran while one was open for 1% -> 2% of each run, Pallas kernels for 12% -> 14%
where the time goes in v9:
time: 180 us; the launch traced here: 179 us
  waiting for transfers between devices  94.2 us (52%)
  starting transfers between devices  43.2 us (24%)
  Pallas kernels  31.9 us (18%)
  local copies, waits for them, and re-layouts  9.7 us (5%)
    ppermute x14, waiting for transfers between devices, xor(): return lax.ppermute(value, 'ctx', [(i, i ^ step) for i in range(n_ctx)])  94.1 us
    ppermute x14, starting transfers between devices, xor(): return lax.ppermute(value, 'ctx', [(i, i ^ step) for i in range(n_ctx)])  18.3 us
    ppermute x2, starting transfers between devices, shift(): return lax.ppermute(v, 'ctx', pairs)  14.1 us
    pallas_call x4, Pallas kernels, run_blocks(): call(body, name, out_shape, specs, outs, LIMIT, flops, 2 * MIB)  9.99 us
    unnamed x26, local copies, waits for them, and re-layouts  7.05 us
    all_to_all x1, starting transfers between devices, spread(): return lax.all_to_all(packed, 'ctx', 0, 0, tiled=True)  6.93 us
    pallas_call x2, Pallas kernels, add_features(): call(kernel, 'add_features', shape, [VMEM] * len(args), VMEM, LIMIT, flop...  4.74 us
    pallas_call x2, Pallas kernels, project(): call(kernel, 'project', shapes, [VMEM] * len(args), [VMEM] * 4, LIMIT, fl...  4.25 us
  transfers between devices with their start and end apart: 29, of which 6 were waited for; matrix products, arithmetic and copies ran while one was open for 2% of the time, Pallas kernels for 14%

profile of v9, /device:TPU:0, one launch (start us, length us, event | category | flops | bytes accessed | tf_op | source)
XLA Modules:
  0.0 179.4 jit_solution(4949238596915122880)
XLA Ops:
  0.5 1.2 copy-done.4
  3.8 1.3 copy-done
  5.1 6.9 %all-to-all-start = ((bf16[8,512,256]{2,1,0:T(8,128)(2,1)}), bf16[8,512,256]{2,1,0:T(8,128)(2,1)S(1)}, u32[]{:S(2)}, u32[]{:S(2)}) async-start(bf16[8,512,256]{2,1,0:T(8,128)(2,1)} %bitcast.10), calls=%async_computation | async-start | bytes 4194304 | tf_op jit(solution)/shard_map/all_to_all | solution.py:321
  12.1 2.0 %collective-permute-start = (bf16[384,2048]{1,0:T(8,128)(2,1)}, bf16[384,2048]{1,0:T(8,128)(2,1)}, u32[]{:S(2)}, u32[]{:S(2)}) collective-permute-start(bf16[384,2048]{1,0:T(8,128)(2,1)} %refs_0_.1), channel_id=1, source_target_pairs={{0,2},{2,0},{4,6},{6,4},{8,10},{10,8},{12,14},{14,12},{1,3},{3,1},... | collective-permute-start | bytes 4718600 | tf_op jit(solution)/shard_map/ppermute | solution.py:312
  14.1 1.5 collective-permute-start.3
  15.5 55.8 %collective-permute-done.refs_2_ = bf16[384,2048]{1,0:T(8,128)(2,1)} collective-permute-done((bf16[384,2048]{1,0:T(8,128)(2,1)}, bf16[384,2048]{1,0:T(8,128)(2,1)}, u32[]{:S(2)}, u32[]{:S(2)}) %collective-permute-start) | collective-permute-done | bytes 1572896 | tf_op jit(solution)/shard_map/ppermute | solution.py:312
  75.3 7.3 %collective-permute-done.3.refs_4_ = bf16[384,2048]{1,0:T(8,128)(2,1)} collective-permute-done((bf16[384,2048]{1,0:T(8,128)(2,1)}, bf16[384,2048]{1,0:T(8,128)(2,1)}, u32[]{:S(2)}, u32[]{:S(2)}) %collective-permute-start.3) | collective-permute-done | bytes 1572896 | tf_op jit(solution)/shard_map/ppermute | solution.py:312
  82.7 1.4 slice.12
  84.1 1.5 collective-permute-start.6
  85.7 1.6 collective-permute-start.10
  88.4 1.6 collective-permute-start.7
  90.0 1.4 collective-permute-start.8
  91.4 1.5 collective-permute-start.9
  92.9 3.3 %stage.2.stream_ref.refs_0_ = bf16[3,384,4096]{2,1,0:T(8,128)(2,1)S(1)} custom-call(s32[4]{0:T(128)S(1)} %pad_add_fusion.place_ref, bf16[384,2048]{1,0:T(8,128)(2,1)S(1)} %copy-done.1, bf16[384,2048]{1,0:T(8,128)(2,1)S(1)} %copy-done.3, bf16[384,2048]{1,0:T(8,128)(2,1)} %collective-permute-done.refs_2_, bf16[384,2048]{1,0:T(8,128)(2,1)} %collective-permute-done.4.refs_3_, ...), custom_call_target="tpu_custom_call" | custom-call | bytes 18874368 | tf_op jit(solution)/shard_map/stage/pallas_call | solution.py:117
  96.2 3.0 %project.2 = (bf16[3,384,128]{2,1,0:T(8,128)(2,1)S(1)}, bf16[3,384,128]{2,1,0:T(8,128)(2,1)S(1)}, f32[3,128,128]{2,1,0:T(8,128)S(1)}, f32[128,128]{1,0:T(8,128)S(1)}) custom-call(bf16[3,384,4096]{2,1,0:T(8,128)(2,1)S(1)} %stage.2.stream_ref.refs_0_, bf16[4096,256]{1,0:T(8,128)(2,1)S(1)} %bitcast.7), custom_call_target="tpu_custom_call" | custom-call | flops 2415919104 | bytes 2097152 | tf_op jit(solution)/shard_map/project/pallas_call | solution.py:145
  99.2 8.1 %collective-permute-done.8.refs_3_ = bf16[512,256]{1,0:T(8,128)(2,1)S(1)} collective-permute-done((bf16[512,256]{1,0:T(8,128)(2,1)S(1)}, bf16[512,256]{1,0:T(8,128)(2,1)S(1)}, u32[]{:S(2)}, u32[]{:S(2)}) %collective-permute-start.8) | collective-permute-done | bytes 262176 | tf_op jit(solution)/shard_map/ppermute | solution.py:312
  107.3 7.5 %collective-permute-done.9.refs_4_ = bf16[512,256]{1,0:T(8,128)(2,1)S(1)} collective-permute-done((bf16[512,256]{1,0:T(8,128)(2,1)S(1)}, bf16[512,256]{1,0:T(8,128)(2,1)S(1)}, u32[]{:S(2)}, u32[]{:S(2)}) %collective-permute-start.9) | collective-permute-done | bytes 262176 | tf_op jit(solution)/shard_map/ppermute | solution.py:312
  115.8 2.4 %collective-permute-start.16 = (bf16[512,256]{1,0:T(8,128)(2,1)S(1)}, bf16[512,256]{1,0:T(8,128)(2,1)S(1)}, u32[]{:S(2)}, u32[]{:S(2)}) collective-permute-start(bf16[512,256]{1,0:T(8,128)(2,1)S(1)} %copy-done.12), channel_id=1, source_target_pairs={{0,10},{2,8},{4,14},{6,12},{8,2},{10,0},{12,6},{14,4},{1,11},{3,9}... | collective-permute-start | bytes 786440 | tf_op jit(solution)/shard_map/ppermute | solution.py:312
  118.2 2.3 %collective-permute-start.17 = (bf16[512,256]{1,0:T(8,128)(2,1)S(1)}, bf16[512,256]{1,0:T(8,128)(2,1)S(1)}, u32[]{:S(2)}, u32[]{:S(2)}) collective-permute-start(bf16[512,256]{1,0:T(8,128)(2,1)S(1)} %copy-done.8), channel_id=1, source_target_pairs={{0,14},{2,12},{4,10},{6,8},{8,6},{10,4},{12,2},{14,0},{1,15},{3,13... | collective-permute-start | bytes 786440 | tf_op jit(solution)/shard_map/ppermute | solution.py:312
  122.0 1.3 project.3
  123.3 14.7 %collective-permute-done.16.refs_5_ = bf16[512,256]{1,0:T(8,128)(2,1)S(1)} collective-permute-done((bf16[512,256]{1,0:T(8,128)(2,1)S(1)}, bf16[512,256]{1,0:T(8,128)(2,1)S(1)}, u32[]{:S(2)}, u32[]{:S(2)}) %collective-permute-start.16) | collective-permute-done | bytes 262176 | tf_op jit(solution)/shard_map/ppermute | solution.py:312
  138.0 2.3 %begin.2.refs_3_ = f32[4,384,256]{2,1,0:T(8,128)S(1)} custom-call(s32[4]{0:T(128)S(1)} %pad_add_fusion.place_ref, bf16[3,384,4096]{2,1,0:T(8,128)(2,1)S(1)} %stage.2.stream_ref.refs_0_, bf16[1,384,4096]{2,1,0:T(8,128)(2,1)S(1)} %stage.3.stream_ref.refs_1_, bf16[2048,256]{1,0:T(8,128)(2,1)S(1)} %collective-permute-done.10.refs_2_), custom_call_target="tpu_custom_call" | custom-call | flops 1610612736 | bytes 2097152 | tf_op jit(solution)/shard_map/begin/pallas_call | solution.py:183
  140.3 8.8 %collective-permute-start.19 = (f32[128,128]{1,0:T(8,128)S(1)}, f32[128,128]{1,0:T(8,128)S(1)}, u32[]{:S(2)}, u32[]{:S(2)}) collective-permute-start(f32[128,128]{1,0:T(8,128)S(1)} %get-tuple-element.106), channel_id=1, source_target_pairs={{0,8},{2,10},{4,12},{6,14},{1,9},{3,11},{5,13},{7,15},{16,24},{18,... | collective-permute-start | bytes 196616 | tf_op jit(solution)/shard_map/ppermute | solution.py:292
  149.2 1.9 %begin.3.refs_7_ = f32[4,384,256]{2,1,0:T(8,128)S(1)} custom-call(s32[4]{0:T(128)S(1)} %pad_add_fusion.place_ref, bf16[3,384,4096]{2,1,0:T(8,128)(2,1)S(1)} %stage.2.stream_ref.refs_0_, bf16[1,384,4096]{2,1,0:T(8,128)(2,1)S(1)} %stage.3.stream_ref.refs_1_, bf16[512,256]{1,0:T(8,128)(2,1)S(1)} %get-tuple-element.98.refs_2_, ...), custom_call_target="tpu_custom_call" | custom-call | flops 1207959552 | bytes 2097152 | tf_op jit(solution)/shard_map/begin/pallas_call | solution.py:183
  151.2 2.7 %keys_values.1 = (bf16[4,384,128]{2,1,0:T(8,128)(2,1)S(1)}, bf16[4,384,128]{2,1,0:T(8,128)(2,1)S(1)}, f32[4,128,128]{2,1,0:T(8,128)S(1)}, f32[128,128]{1,0:T(8,128)S(1)}) custom-call(s32[4]{0:T(128)S(1)} %pad_add_fusion.place_ref, bf16[3,384,4096]{2,1,0:T(8,128)(2,1)S(1)} %stage.2.stream_ref.refs_0_, bf16[1,384,4096]{2,1,0:T(8,128)(2,1)S(1)} %stage.3.stream_ref.refs_1_, ...), custom_call_target="tpu_custom_call" | custom-call | flops 1610612736 | bytes 2097152 | tf_op jit(solution)/shard_map/keys_values/pallas_call | solution.py:183
  153.9 5.3 %collective-permute-start.20 = (f32[128,128]{1,0:T(8,128)S(1)}, f32[128,128]{1,0:T(8,128)S(1)}, u32[]{:S(2)}, u32[]{:S(2)}) collective-permute-start(f32[128,128]{1,0:T(8,128)S(1)} %get-tuple-element.126), channel_id=1, source_target_pairs={{0,8},{2,10},{4,12},{6,14},{1,9},{3,11},{5,13},{7,15},{16,24},{18,... | collective-permute-start | bytes 196616 | tf_op jit(solution)/shard_map/ppermute | solution.py:292
  159.1 3.0 %queries.1.query_ref = bf16[4,384,256]{2,1,0:T(8,128)(2,1)S(1)} custom-call(s32[4]{0:T(128)S(1)} %pad_add_fusion.place_ref, bf16[3,384,4096]{2,1,0:T(8,128)(2,1)S(1)} %stage.2.stream_ref.refs_0_, bf16[1,384,4096]{2,1,0:T(8,128)(2,1)S(1)} %stage.3.stream_ref.refs_1_, bf16[512,256]{1,0:T(8,128)(2,1)S(1)} %collective-permute-done.13.refs_2_, ...), custom_call_target="tpu_custom_call" | custom-call | flops 2013265920 | bytes 2097152 | tf_op jit(solution)/shard_map/queries/pallas_call | solution.py:183
  162.2 2.0 %attend.3 = (bf16[384,256]{1,0:T(8,128)(2,1)S(1)}, bf16[384,256]{1,0:T(8,128)(2,1)S(1)}, bf16[384,256]{1,0:T(8,128)(2,1)S(1)}) custom-call(s32[4]{0:T(128)S(1)} %pad_add_fusion.place_ref, bf16[4,384,256]{2,1,0:T(8,128)(2,1)S(1)} %queries.1.query_ref, bf16[3,384,128]{2,1,0:T(8,128)(2,1)S(1)} %get-tuple-element.114.refs_0_, ...), custom_call_target="tpu_custom_call" | custom-call | flops 528482304 | bytes 2097152 | tf_op jit(solution)/shard_map/attend/pallas_call | solution.py:265
  164.4 3.4 %collective-permute-start.23 = (bf16[384,256]{1,0:T(8,128)(2,1)S(1)}, bf16[384,256]{1,0:T(8,128)(2,1)S(1)}, u32[]{:S(2)}, u32[]{:S(2)}) collective-permute-start(bf16[384,256]{1,0:T(8,128)(2,1)S(1)} %get-tuple-element.134), channel_id=1, source_target_pairs={{0,6},{2,4},{4,2},{6,0},{8,14},{10,12},{12,10},{14,8},{1,7},{3,5},... | collective-permute-start | bytes 589832 | tf_op jit(solution)/shard_map/ppermute | solution.py:312
  168.9 4.0 %stage_rows.1 = (bf16[4,256,2048]{2,1,0:T(8,128)(2,1)S(1)}, bf16[4,256,2048]{2,1,0:T(8,128)(2,1)S(1)}) custom-call(s32[4]{0:T(128)S(1)} %pad_add_fusion.place_ref, bf16[1024,4096]{1,0:T(8,128)(2,1)} %out_ref.1, bf16[1024,4096]{1,0:T(8,128)(2,1)} %collective-permute-done.2.far_ref), custom_call_target="tpu_custom_call" | custom-call | bytes 16777216 | tf_op jit(solution)/shard_map/stage_rows/pallas_call | solution.py:89
  174.7 1.8 %add_features.2.refs_5_ = f32[384,2048]{1,0:T(8,128)S(1)} custom-call(bf16[384,256]{1,0:T(8,128)(2,1)S(1)} %attend.2.refs_0_, bf16[384,256]{1,0:T(8,128)(2,1)S(1)} %collective-permute-done.21.refs_1_, bf16[384,256]{1,0:T(8,128)(2,1)S(1)} %collective-permute-done.22.refs_2_, bf16[384,256]{1,0:T(8,128)(2,1)S(1)} %collective-permute-done.23.refs_3_, ...), custom_call_target="tpu_custom_call" | custom-call | flops 1610612736 | bytes 8388608 | tf_op jit(solution)/shard_map/add_features/pallas_call | solution.py:286
  176.5 2.9 %add_features.3 = bf16[384,2048]{1,0:T(8,128)(2,1)} custom-call(bf16[384,256]{1,0:T(8,128)(2,1)S(1)} %collective-permute-done.24.refs_0_, bf16[384,256]{1,0:T(8,128)(2,1)S(1)} %collective-permute-done.25.refs_1_, bf16[384,256]{1,0:T(8,128)(2,1)S(1)} %collective-permute-done.26.refs_2_, bf16[384,256]{1,0:T(8,128)(2,1)S(1)} %collective-permute-done.27.refs_3_, ...), custom_call_target="tpu_custom_call" | custom-call | flops 1610612736 | bytes 8388608 | tf_op jit(solution)/shard_map/add_features/pallas_call | solution.py:286
  (72 shorter events, 13.2 us)
Async XLA Ops:
  0.0 72.5 %collective-permute-start.2 = (bf16[1024,4096]{1,0:T(8,128)(2,1)}, bf16[1024,4096]{1,0:T(8,128)(2,1)}, u32[]{:S(2)}, u32[]{:S(2)}) collective-permute-start(bf16[1024,4096]{1,0:T(8,128)(2,1)} %out_ref.1), channel_id=1, source_target_pairs={{0,1},{1,0},{2,3},{3,2},{4,5},{5,4},{6,7},{7,6},{8,9},{9,8},{10,11... | collective-permute-start | bytes 25165832 | tf_op jit(solution)/shard_map/ppermute | solution.py:318
  5.1 67.4 %copy-start.6 = (bf16[512,1024]{1,0:T(8,128)(2,1)S(1)}, bf16[512,1024]{1,0:T(8,128)(2,1)}, u32[]{:S(2)}) copy-start(bf16[512,1024]{1,0:T(8,128)(2,1)} %query_ref) | copy-start | bytes 3145732
  5.1 77.5 %all-to-all-start = ((bf16[8,512,256]{2,1,0:T(8,128)(2,1)}), bf16[8,512,256]{2,1,0:T(8,128)(2,1)S(1)}, u32[]{:S(2)}, u32[]{:S(2)}) async-start(bf16[8,512,256]{2,1,0:T(8,128)(2,1)} %bitcast.10), calls=%async_computation | async-start | bytes 4194304 | tf_op jit(solution)/shard_map/all_to_all | solution.py:321
  12.1 59.3 %collective-permute-start = (bf16[384,2048]{1,0:T(8,128)(2,1)}, bf16[384,2048]{1,0:T(8,128)(2,1)}, u32[]{:S(2)}, u32[]{:S(2)}) collective-permute-start(bf16[384,2048]{1,0:T(8,128)(2,1)} %refs_0_.1), channel_id=1, source_target_pairs={{0,2},{2,0},{4,6},{6,4},{8,10},{10,8},{12,14},{14,12},{1,3},{3,1},... | collective-permute-start | bytes 4718600 | tf_op jit(solution)/shard_map/ppermute | solution.py:312
  14.1 57.3 %collective-permute-start.1 = (bf16[384,2048]{1,0:T(8,128)(2,1)}, bf16[384,2048]{1,0:T(8,128)(2,1)S(1)}, u32[]{:S(2)}, u32[]{:S(2)}) collective-permute-start(bf16[384,2048]{1,0:T(8,128)(2,1)} %refs_0_.1), channel_id=1, source_target_pairs={{0,1},{1,0},{2,3},{3,2},{4,5},{5,4},{6,7},{7,6},{8,9},{9,8},{10,11... | collective-permute-start | bytes 4718600 | tf_op jit(solution)/shard_map/ppermute | solution.py:318
  14.1 68.6 %collective-permute-start.3 = (bf16[384,2048]{1,0:T(8,128)(2,1)}, bf16[384,2048]{1,0:T(8,128)(2,1)}, u32[]{:S(2)}, u32[]{:S(2)}) collective-permute-start(bf16[384,2048]{1,0:T(8,128)(2,1)} %refs_0_.1), channel_id=1, source_target_pairs={{0,4},{2,6},{4,0},{6,2},{8,12},{10,14},{12,8},{14,10},{1,5},{3,7},... | collective-permute-start | bytes 4718600 | tf_op jit(solution)/shard_map/ppermute | solution.py:312
  72.5 10.1 %collective-permute-start.4 = (bf16[384,2048]{1,0:T(8,128)(2,1)}, bf16[384,2048]{1,0:T(8,128)(2,1)}, u32[]{:S(2)}, u32[]{:S(2)}) collective-permute-start(bf16[384,2048]{1,0:T(8,128)(2,1)} %collective-permute-done.refs_2_), channel_id=1, source_target_pairs={{0,1},{1,0},{2,3},{3,2},{4,5},{5,4},{6,7},{7,6},{8,9},{9,8},{10,11... | collective-permute-start | bytes 4718600 | tf_op jit(solution)/shard_map/ppermute | solution.py:318
  82.7 8.7 %collective-permute-start.5 = (bf16[384,2048]{1,0:T(8,128)(2,1)}, bf16[384,2048]{1,0:T(8,128)(2,1)S(1)}, u32[]{:S(2)}, u32[]{:S(2)}) collective-permute-start(bf16[384,2048]{1,0:T(8,128)(2,1)} %collective-permute-done.3.refs_4_), channel_id=1, source_target_pairs={{0,1},{1,0},{2,3},{3,2},{4,5},{5,4},{6,7},{7,6},{8,9},{9,8},{10,11... | collective-permute-start | bytes 4718600 | tf_op jit(solution)/shard_map/ppermute | solution.py:318
  84.1 30.7 %collective-permute-start.6 = (bf16[384,1408]{1,0:T(8,128)(2,1)S(1)}, bf16[384,1408]{1,0:T(8,128)(2,1)S(1)}, u32[]{:S(2)}, u32[]{:S(2)}) collective-permute-start(bf16[384,1408]{1,0:T(8,128)(2,1)S(1)} %slice.12), channel_id=1, source_target_pairs={{0,2},{2,0},{4,6},{6,4},{8,10},{10,8},{12,14},{14,12},{1,3},{3,1},... | collective-permute-start | bytes 3244040 | tf_op jit(solution)/shard_map/ppermute | solution.py:312
  85.7 29.1 %collective-permute-start.10 = (bf16[2048,256]{1,0:T(8,128)(2,1)S(1)}, bf16[2048,256]{1,0:T(8,128)(2,1)S(1)}, u32[]{:S(2)}, u32[]{:S(2)}) collective-permute-start(bf16[2048,256]{1,0:T(8,128)(2,1)S(1)} %slice.14), channel_id=1, source_target_pairs={{0,16},{16,0},{1,17},{17,1},{2,18},{18,2},{3,19},{19,3},{4,20},{20... | collective-permute-start | bytes 3145736 | tf_op jit(solution)/shard_map/ppermute | solution.py:315
  88.4 26.4 %collective-permute-start.7 = (bf16[384,640]{1,0:T(8,128)(2,1)S(1)}, bf16[384,640]{1,0:T(8,128)(2,1)S(1)}, u32[]{:S(2)}, u32[]{:S(2)}) collective-permute-start(bf16[384,640]{1,0:T(8,128)(2,1)S(1)} %slice.13), channel_id=1, source_target_pairs={{0,4},{2,6},{4,0},{6,2},{8,12},{10,14},{12,8},{14,10},{1,5},{3,7},... | collective-permute-start | bytes 1474568 | tf_op jit(solution)/shard_map/ppermute | solution.py:312
  90.0 17.3 %collective-permute-start.8 = (bf16[512,256]{1,0:T(8,128)(2,1)S(1)}, bf16[512,256]{1,0:T(8,128)(2,1)S(1)}, u32[]{:S(2)}, u32[]{:S(2)}) collective-permute-start(bf16[512,256]{1,0:T(8,128)(2,1)S(1)} %get-tuple-element.98.refs_2_), channel_id=1, source_target_pairs={{0,8},{2,10},{4,12},{6,14},{8,0},{10,2},{12,4},{14,6},{1,9},{3,11}... | collective-permute-start | bytes 786440 | tf_op jit(solution)/shard_map/ppermute | solution.py:312
  91.4 23.4 %collective-permute-start.9 = (bf16[512,256]{1,0:T(8,128)(2,1)S(1)}, bf16[512,256]{1,0:T(8,128)(2,1)S(1)}, u32[]{:S(2)}, u32[]{:S(2)}) collective-permute-start(bf16[512,256]{1,0:T(8,128)(2,1)S(1)} %copy-done.10), channel_id=1, source_target_pairs={{0,12},{2,14},{4,8},{6,10},{8,4},{10,6},{12,0},{14,2},{1,13},{3,15... | collective-permute-start | bytes 786440 | tf_op jit(solution)/shard_map/ppermute | solution.py:312
  99.2 16.6 %copy-start.12 = (bf16[512,256]{1,0:T(8,128)(2,1)S(1)}, bf16[512,256]{1,0:T(8,128)(2,1)}, u32[]{:S(2)}) copy-start(bf16[512,256]{1,0:T(8,128)(2,1)} %copy-done.11) | copy-start | bytes 786436
  99.2 19.0 %copy-start.8 = (bf16[512,256]{1,0:T(8,128)(2,1)S(1)}, bf16[512,256]{1,0:T(8,128)(2,1)}, u32[]{:S(2)}) copy-start(bf16[512,256]{1,0:T(8,128)(2,1)} %copy-done.7) | copy-start | bytes 786436
  114.8 5.6 %collective-permute-start.11 = (bf16[384,1408]{1,0:T(8,128)(2,1)S(1)}, bf16[384,1408]{1,0:T(8,128)(2,1)S(1)}, u32[]{:S(2)}, u32[]{:S(2)}) collective-permute-start(bf16[384,1408]{1,0:T(8,128)(2,1)S(1)} %collective-permute-done.6.refs_0_), channel_id=1, source_target_pairs={{0,1},{1,0},{2,3},{3,2},{4,5},{5,4},{6,7},{7,6},{8,9},{9,8},{10,11... | collective-permute-start | bytes 3244040 | tf_op jit(solution)/shard_map/ppermute | solution.py:318
  115.0 36.1 %collective-permute-start.18 = (bf16[2048,256]{1,0:T(8,128)(2,1)S(1)}, bf16[2048,256]{1,0:T(8,128)(2,1)S(1)}, u32[]{:S(2)}, u32[]{:S(2)}) collective-permute-start(bf16[2048,256]{1,0:T(8,128)(2,1)S(1)} %slice.15), channel_id=1, source_target_pairs={{0,16},{16,0},{1,17},{17,1},{2,18},{18,2},{3,19},{19,3},{4,20},{20... | collective-permute-start | bytes 3145736 | tf_op jit(solution)/shard_map/ppermute | solution.py:315
  115.5 5.5 %collective-permute-start.12 = (bf16[384,640]{1,0:T(8,128)(2,1)S(1)}, bf16[384,640]{1,0:T(8,128)(2,1)S(1)}, u32[]{:S(2)}, u32[]{:S(2)}) collective-permute-start(bf16[384,640]{1,0:T(8,128)(2,1)S(1)} %collective-permute-done.7.refs_2_), channel_id=1, source_target_pairs={{0,1},{1,0},{2,3},{3,2},{4,5},{5,4},{6,7},{7,6},{8,9},{9,8},{10,11... | collective-permute-start | bytes 1474568 | tf_op jit(solution)/shard_map/ppermute | solution.py:318
  115.8 22.2 %collective-permute-start.16 = (bf16[512,256]{1,0:T(8,128)(2,1)S(1)}, bf16[512,256]{1,0:T(8,128)(2,1)S(1)}, u32[]{:S(2)}, u32[]{:S(2)}) collective-permute-start(bf16[512,256]{1,0:T(8,128)(2,1)S(1)} %copy-done.12), channel_id=1, source_target_pairs={{0,10},{2,8},{4,14},{6,12},{8,2},{10,0},{12,6},{14,4},{1,11},{3,9}... | collective-permute-start | bytes 786440 | tf_op jit(solution)/shard_map/ppermute | solution.py:312
  118.2 22.2 %collective-permute-start.17 = (bf16[512,256]{1,0:T(8,128)(2,1)S(1)}, bf16[512,256]{1,0:T(8,128)(2,1)S(1)}, u32[]{:S(2)}, u32[]{:S(2)}) collective-permute-start(bf16[512,256]{1,0:T(8,128)(2,1)S(1)} %copy-done.8), channel_id=1, source_target_pairs={{0,14},{2,12},{4,10},{6,8},{8,6},{10,4},{12,2},{14,0},{1,15},{3,13... | collective-permute-start | bytes 786440 | tf_op jit(solution)/shard_map/ppermute | solution.py:312
  120.5 30.7 %collective-permute-start.13 = (bf16[512,256]{1,0:T(8,128)(2,1)S(1)}, bf16[512,256]{1,0:T(8,128)(2,1)S(1)}, u32[]{:S(2)}, u32[]{:S(2)}) collective-permute-start(bf16[512,256]{1,0:T(8,128)(2,1)S(1)} %copy-done.12), channel_id=1, source_target_pairs={{0,2},{2,0},{4,6},{6,4},{8,10},{10,8},{12,14},{14,12},{1,3},{3,1},... | collective-permute-start | bytes 786440 | tf_op jit(solution)/shard_map/ppermute | solution.py:312
  121.0 30.1 %collective-permute-start.14 = (bf16[512,256]{1,0:T(8,128)(2,1)S(1)}, bf16[512,256]{1,0:T(8,128)(2,1)S(1)}, u32[]{:S(2)}, u32[]{:S(2)}) collective-permute-start(bf16[512,256]{1,0:T(8,128)(2,1)S(1)} %copy-done.10), channel_id=1, source_target_pairs={{0,4},{2,6},{4,0},{6,2},{8,12},{10,14},{12,8},{14,10},{1,5},{3,7},... | collective-permute-start | bytes 786440 | tf_op jit(solution)/shard_map/ppermute | solution.py:312
  138.0 13.2 %collective-permute-start.15 = (bf16[512,256]{1,0:T(8,128)(2,1)S(1)}, bf16[512,256]{1,0:T(8,128)(2,1)S(1)}, u32[]{:S(2)}, u32[]{:S(2)}) collective-permute-start(bf16[512,256]{1,0:T(8,128)(2,1)S(1)} %copy-done.8), channel_id=1, source_target_pairs={{0,6},{2,4},{4,2},{6,0},{8,14},{10,12},{12,10},{14,8},{1,7},{3,5},... | collective-permute-start | bytes 786440 | tf_op jit(solution)/shard_map/ppermute | solution.py:312
  140.3 10.8 %collective-permute-start.19 = (f32[128,128]{1,0:T(8,128)S(1)}, f32[128,128]{1,0:T(8,128)S(1)}, u32[]{:S(2)}, u32[]{:S(2)}) collective-permute-start(f32[128,128]{1,0:T(8,128)S(1)} %get-tuple-element.106), channel_id=1, source_target_pairs={{0,8},{2,10},{4,12},{6,14},{1,9},{3,11},{5,13},{7,15},{16,24},{18,... | collective-permute-start | bytes 196616 | tf_op jit(solution)/shard_map/ppermute | solution.py:292
  153.9 8.3 %collective-permute-start.20 = (f32[128,128]{1,0:T(8,128)S(1)}, f32[128,128]{1,0:T(8,128)S(1)}, u32[]{:S(2)}, u32[]{:S(2)}) collective-permute-start(f32[128,128]{1,0:T(8,128)S(1)} %get-tuple-element.126), channel_id=1, source_target_pairs={{0,8},{2,10},{4,12},{6,14},{1,9},{3,11},{5,13},{7,15},{16,24},{18,... | collective-permute-start | bytes 196616 | tf_op jit(solution)/shard_map/ppermute | solution.py:292
  164.2 8.8 %collective-permute-start.21 = (bf16[384,256]{1,0:T(8,128)(2,1)S(1)}, bf16[384,256]{1,0:T(8,128)(2,1)S(1)}, u32[]{:S(2)}, u32[]{:S(2)}) collective-permute-start(bf16[384,256]{1,0:T(8,128)(2,1)S(1)} %get-tuple-element.132), channel_id=1, source_target_pairs={{0,2},{2,0},{4,6},{6,4},{8,10},{10,8},{12,14},{14,12},{1,3},{3,1},... | collective-permute-start | bytes 589832 | tf_op jit(solution)/shard_map/ppermute | solution.py:312
  164.3 8.7 %collective-permute-start.22 = (bf16[384,256]{1,0:T(8,128)(2,1)S(1)}, bf16[384,256]{1,0:T(8,128)(2,1)S(1)}, u32[]{:S(2)}, u32[]{:S(2)}) collective-permute-start(bf16[384,256]{1,0:T(8,128)(2,1)S(1)} %get-tuple-element.133), channel_id=1, source_target_pairs={{0,4},{2,6},{4,0},{6,2},{8,12},{10,14},{12,8},{14,10},{1,5},{3,7},... | collective-permute-start | bytes 589832 | tf_op jit(solution)/shard_map/ppermute | solution.py:312
  164.4 9.3 %collective-permute-start.23 = (bf16[384,256]{1,0:T(8,128)(2,1)S(1)}, bf16[384,256]{1,0:T(8,128)(2,1)S(1)}, u32[]{:S(2)}, u32[]{:S(2)}) collective-permute-start(bf16[384,256]{1,0:T(8,128)(2,1)S(1)} %get-tuple-element.134), channel_id=1, source_target_pairs={{0,6},{2,4},{4,2},{6,0},{8,14},{10,12},{12,10},{14,8},{1,7},{3,5},... | collective-permute-start | bytes 589832 | tf_op jit(solution)/shard_map/ppermute | solution.py:312
  173.6 2.8 %collective-permute-start.24 = (bf16[384,256]{1,0:T(8,128)(2,1)S(1)}, bf16[384,256]{1,0:T(8,128)(2,1)S(1)}, u32[]{:S(2)}, u32[]{:S(2)}) collective-permute-start(bf16[384,256]{1,0:T(8,128)(2,1)S(1)} %attend.2.refs_0_), channel_id=1, source_target_pairs={{0,1},{1,0},{2,3},{3,2},{4,5},{5,4},{6,7},{7,6},{8,9},{9,8},{10,11... | collective-permute-start | bytes 589832 | tf_op jit(solution)/shard_map/ppermute | solution.py:318
  173.6 2.8 %collective-permute-start.25 = (bf16[384,256]{1,0:T(8,128)(2,1)S(1)}, bf16[384,256]{1,0:T(8,128)(2,1)S(1)}, u32[]{:S(2)}, u32[]{:S(2)}) collective-permute-start(bf16[384,256]{1,0:T(8,128)(2,1)S(1)} %collective-permute-done.21.refs_1_), channel_id=1, source_target_pairs={{0,1},{1,0},{2,3},{3,2},{4,5},{5,4},{6,7},{7,6},{8,9},{9,8},{10,11... | collective-permute-start | bytes 589832 | tf_op jit(solution)/shard_map/ppermute | solution.py:318
  174.2 2.3 %collective-permute-start.26 = (bf16[384,256]{1,0:T(8,128)(2,1)S(1)}, bf16[384,256]{1,0:T(8,128)(2,1)S(1)}, u32[]{:S(2)}, u32[]{:S(2)}) collective-permute-start(bf16[384,256]{1,0:T(8,128)(2,1)S(1)} %collective-permute-done.22.refs_2_), channel_id=1, source_target_pairs={{0,1},{1,0},{2,3},{3,2},{4,5},{5,4},{6,7},{7,6},{8,9},{9,8},{10,11... | collective-permute-start | bytes 589832 | tf_op jit(solution)/shard_map/ppermute | solution.py:318
  174.2 2.3 %collective-permute-start.27 = (bf16[384,256]{1,0:T(8,128)(2,1)S(1)}, bf16[384,256]{1,0:T(8,128)(2,1)S(1)}, u32[]{:S(2)}, u32[]{:S(2)}) collective-permute-start(bf16[384,256]{1,0:T(8,128)(2,1)S(1)} %collective-permute-done.23.refs_3_), channel_id=1, source_target_pairs={{0,1},{1,0},{2,3},{3,2},{4,5},{5,4},{6,7},{7,6},{8,9},{9,8},{10,11... | collective-permute-start | bytes 589832 | tf_op jit(solution)/shard_map/ppermute | solution.py:318
  (10 other events, 33.3 us)

commit v10 on v9

--- a/solution.py
+++ b/solution.py
@@ -162,20 +162,22 @@
     return total
 
 
-def run_blocks(kernel, name, place, streams, parts, base, out_shape):
+def run_blocks(kernel, name, place, streams, parts, base, out_shape, more=()):
     rows, width = streams[0].shape[1:]
     count = len(streams)
     args = [*streams, *[weight for weight, _ in parts], *([] if base is None else [base])]
+    given = len(args)
+    args += more
 
     def body(place_ref, *refs):
         weights = refs[count : count + len(parts)]
-        base_ref = None if base is None else refs[len(args) - 1]
+        base_ref = None if base is None else refs[given - 1]
 
         def sums():
             for i, (source, r) in enumerate(flat_blocks(refs[:count])):
                 yield i, weighted(place_ref, source, r, weights, parts, None if base is None else base_ref[i])
 
-        kernel(place_ref, sums, *refs[len(args) :])
+        kernel(place_ref, sums, *refs[given:])
 
     flops = 4 * SUB * rows * sum(weight.shape[0] for weight, _ in parts) * HDIM
     specs = [SMEM] + [VMEM] * len(args)
@@ -192,10 +194,10 @@
     return run_blocks(kernel, "begin", place, streams, parts, None, shape)
 
 
-def keys_values(place, streams, parts, base):
+def keys_values(place, streams, parts, base, total):
     rows = streams[0].shape[1]
 
-    def kernel(place_ref, sums, key_ref, value_ref, state_ref, total_ref):
+    def kernel(place_ref, sums, given_ref, key_ref, value_ref, state_ref, total_ref):
         for i, both in sums():
             key_ref[i] = silu(both[:, :HDIM]).astype(BF16)
             value_ref[i] = both[:, HDIM:].astype(BF16)
@@ -204,11 +206,12 @@
             state = dot(key_ref[i], value_ref[i], ((0,), (0,)))
             state_ref[i] = state
             added = added + state
-        total_ref[...] = added
+        total_ref[0] = given_ref[...]
+        total_ref[1] = added
 
     shape = jax.ShapeDtypeStruct((SUB, rows, HDIM), BF16)
-    shapes = [shape, shape, jax.ShapeDtypeStruct((SUB, HDIM, HDIM), F32), jax.ShapeDtypeStruct((HDIM, HDIM), F32)]
-    return run_blocks(kernel, "keys_values", place, streams, parts, base, shapes)
+    shapes = [shape, shape] + [jax.ShapeDtypeStruct((n, HDIM, HDIM), F32) for n in (SUB, 2)]
+    return run_blocks(kernel, "keys_values", place, streams, parts, base, shapes, [total])
 
 
 def queries(place, streams, parts, base):
@@ -223,17 +226,17 @@
     return run_blocks(kernel, "queries", place, streams, parts, base, shape)
 
 
-def attend(place, blocks, query, heads):
+def attend(place, blocks, query, heads, carried):
     rows = query.shape[1]
     count = len(blocks)
     flat, where = [], []
-    for parts, carried in heads:
+    for parts in heads:
         index = []
         for part in parts:
             index += [(len(flat), r) for r in range(part[0].shape[0])]
             flat += part
-        where.append((index, len(flat)))
-        flat.append(carried)
+        where.append(index)
+    flat.append(carried)
 
     def kernel(place_ref, query_ref, *refs):
         ins, outs = refs[: len(flat)], refs[len(flat) :]
@@ -242,8 +245,8 @@
         )
         block = place_ref[0]
         for i, r in enumerate(blocks):
-            for h, (index, carried) in enumerate(where):
-                earlier = ins[carried][...]
+            for h, index in enumerate(where):
+                earlier = ins[-1][h]
                 for other in range(SUB):
                     if other != r:
                         is_before = jnp.bitwise_xor(block, other) < jnp.bitwise_xor(block, r)
@@ -341,8 +344,9 @@
         if pieced:
             arrived.update({m: xor(sent[m % SUB], m) for m in steps})
 
-    across, kv_mine, beside, far_beside, q_sent = ob((across, kv_mine, beside, far_beside, q_sent))
     arrived = {0: q_sent[0]}
+    fetch(q_sent, 1)
+    across, kv_mine, beside, far_beside, q_sent, arrived = ob((across, kv_mine, beside, far_beside, q_sent, arrived))
     middle = kv_mine.shape[0] // 2
     kv_upper = other_part(kv_mine[:middle])
     left = xor(across[:, :cut], 1)
@@ -359,26 +363,26 @@
     fetch(q_sent, 5, 7)
     far_left, far_right = other_core(left), other_core(right)
     far_left, q_sent = ob((far_left, q_sent))
-    fetch(q_sent, 3, 2, 1)
+    fetch(q_sent, 3, 2)
     corner = [(left, 0, 0, 0), (far_left, 0, 0, 1), (right, 0, cut, 0), (far_right, 0, cut, 1)]
     corner = stage(place, corner, 1, rows, 2 * half)
 
     streams = [near, corner]
     last = project(corner, kv_mine, first[3])
-    carried = exclusive_prefix(last[3], groups)
     kv_base = begin(place, streams, [(kv_upper, 0)])
     if pieced:
-        early = (0, 4, 6)
+        early = (0, 1, 4, 6)
         q_base = begin(place, streams, [(arrived[m], (m,)) for m in early])
-        arrived, kv_lower, carried, kv_base, q_base = ob((arrived, kv_lower, carried, kv_base, q_base))
+        arrived, kv_lower, kv_base, q_base = ob((arrived, kv_lower, kv_base, q_base))
         q_parts = [(arrived[m], (m,)) for m in range(n_ctx) if m not in early]
     else:
         q_base, q_parts = None, [(gather_queries(q_sent), 0)]
-    second = keys_values(place, streams, [(kv_lower, middle)], kv_base)
-    heads = [([first[:3], last[:3]], carried), ([second[:3]], exclusive_prefix(second[3], groups))]
+    *second, totals = keys_values(place, streams, [(kv_lower, middle)], kv_base, last[3])
+    carried = exclusive_prefix(totals, groups)
+    heads = [[first[:3], last[:3]], [second]]
     query = queries(place, streams, q_parts, q_base)
-    away = attend(place, (3, 1, 2), query, heads)
-    home = attend(place, (0,), query, heads)
+    away = attend(place, (3, 1, 2), query, heads, carried)
+    home = attend(place, (0,), query, heads, carried)
     normed = [home[0], xor(away[1], 1), xor(away[2], 2), xor(away[0], 3)]
     home_0, w_far = lax.optimization_barrier((home[0], w_far))
     out_keep, out_far = stage_rows(place, w_out, w_far)

time: 180 us -> 177 us (0.983)
  starting transfers between devices: 43.2 us -> 35.9 us
  waiting for transfers between devices: 94.2 us -> 99.2 us
    ppermute x2 -> x1, starting transfers between devices: 14.1 us -> 6.8 us  [shift(): return lax.ppermute(v, 'ctx', pairs)]
    ppermute x2, waiting for transfers between devices: 0.01 us -> 2.68 us  [other_part(): return lax.ppermute(value, 'groups', [(0, 1), (1, 0)])]
    ppermute x14, waiting for transfers between devices: 94.1 us -> 96.5 us  [xor(): return lax.ppermute(value, 'ctx', [(i, i ^ step) for i in range(n_ctx)])]
    unnamed x26 -> x22, local copies, waits for them, and re-layouts: 7.05 us -> 6.36 us
  transfers between devices with their start and end apart: 29 -> 28, of which waited for: 6 -> 9; matrix products, arithmetic and copies ran while one was open for 2% -> 2% of each run, Pallas kernels for 14% -> 14%
where the time goes in v10:
time: 177 us
  waiting for transfers between devices  99.2 us (56%)
  starting transfers between devices  35.9 us (20%)
  Pallas kernels  32.6 us (18%)
  local copies, waits for them, and re-layouts  9.01 us (5%)
    ppermute x14, waiting for transfers between devices, xor(): return lax.ppermute(value, 'ctx', [(i, i ^ step) for i in range(n_ctx)])  96.5 us
    ppermute x14, starting transfers between devices, xor(): return lax.ppermute(value, 'ctx', [(i, i ^ step) for i in range(n_ctx)])  18.1 us
    pallas_call x4, Pallas kernels, run_blocks(): call(body, name, out_shape, specs, outs, LIMIT, flops, 2 * MIB)  9.97 us
    all_to_all x1, starting transfers between devices, spread(): return lax.all_to_all(packed, 'ctx', 0, 0, tiled=True)  6.93 us
    ppermute x1, starting transfers between devices, shift(): return lax.ppermute(v, 'ctx', pairs)  6.8 us
    unnamed x22, local copies, waits for them, and re-layouts  6.36 us
    pallas_call x2, Pallas kernels, add_features(): call(kernel, 'add_features', shape, [VMEM] * len(args), VMEM, LIMIT, flop...  4.74 us
    pallas_call x2, Pallas kernels, project(): call(kernel, 'project', shapes, [VMEM] * len(args), [VMEM] * 4, LIMIT, fl...  4.25 us
  transfers between devices with their start and end apart: 28, of which 9 were waited for; matrix products, arithmetic and copies ran while one was open for 2% of the time, Pallas kernels for 14%

profile of v10, /device:TPU:0, one launch (start us, length us, event | category | flops | bytes accessed | tf_op | source)
XLA Modules:
  0.0 177.0 jit_solution(15517908080136467844)
XLA Ops:
  3.8 1.3 copy-done
  5.1 6.9 %all-to-all-start = ((bf16[8,512,256]{2,1,0:T(8,128)(2,1)}), bf16[8,512,256]{2,1,0:T(8,128)(2,1)S(1)}, u32[]{:S(2)}, u32[]{:S(2)}) async-start(bf16[8,512,256]{2,1,0:T(8,128)(2,1)} %bitcast.10), calls=%async_computation | async-start | bytes 4194304 | tf_op jit(solution)/shard_map/all_to_all | solution.py:324
  12.1 2.0 %collective-permute-start = (bf16[384,2048]{1,0:T(8,128)(2,1)}, bf16[384,2048]{1,0:T(8,128)(2,1)}, u32[]{:S(2)}, u32[]{:S(2)}) collective-permute-start(bf16[384,2048]{1,0:T(8,128)(2,1)} %refs_0_.1), channel_id=1, source_target_pairs={{0,2},{2,0},{4,6},{6,4},{8,10},{10,8},{12,14},{14,12},{1,3},{3,1},... | collective-permute-start | bytes 4718600 | tf_op jit(solution)/shard_map/ppermute | solution.py:315
  14.1 1.5 collective-permute-start.3
  15.6 55.8 %collective-permute-done.refs_2_ = bf16[384,2048]{1,0:T(8,128)(2,1)} collective-permute-done((bf16[384,2048]{1,0:T(8,128)(2,1)}, bf16[384,2048]{1,0:T(8,128)(2,1)}, u32[]{:S(2)}, u32[]{:S(2)}) %collective-permute-start) | collective-permute-done | bytes 1572896 | tf_op jit(solution)/shard_map/ppermute | solution.py:315
  72.5 1.4 pack_queries.1
  75.6 7.0 %collective-permute-done.3.refs_4_ = bf16[384,2048]{1,0:T(8,128)(2,1)} collective-permute-done((bf16[384,2048]{1,0:T(8,128)(2,1)}, bf16[384,2048]{1,0:T(8,128)(2,1)}, u32[]{:S(2)}, u32[]{:S(2)}) %collective-permute-start.3) | collective-permute-done | bytes 1572896 | tf_op jit(solution)/shard_map/ppermute | solution.py:315
  82.7 1.6 collective-permute-done.5.refs_3_
  84.3 1.4 slice.12
  86.2 1.6 collective-permute-start.11
  88.8 1.8 %collective-permute-start.8 = (bf16[384,640]{1,0:T(8,128)(2,1)S(1)}, bf16[384,640]{1,0:T(8,128)(2,1)S(1)}, u32[]{:S(2)}, u32[]{:S(2)}) collective-permute-start(bf16[384,640]{1,0:T(8,128)(2,1)S(1)} %slice.13), channel_id=1, source_target_pairs={{0,4},{2,6},{4,0},{6,2},{8,12},{10,14},{12,8},{14,10},{1,5},{3,7},... | collective-permute-start | bytes 1474568 | tf_op jit(solution)/shard_map/ppermute | solution.py:315
  90.6 2.4 %collective-permute-start.10 = (bf16[512,256]{1,0:T(8,128)(2,1)S(1)}, bf16[512,256]{1,0:T(8,128)(2,1)S(1)}, u32[]{:S(2)}, u32[]{:S(2)}) collective-permute-start(bf16[512,256]{1,0:T(8,128)(2,1)S(1)} %copy-done.10), channel_id=1, source_target_pairs={{0,12},{2,14},{4,8},{6,10},{8,4},{10,6},{12,0},{14,2},{1,13},{3,15... | collective-permute-start | bytes 786440 | tf_op jit(solution)/shard_map/ppermute | solution.py:315
  93.0 3.3 %stage.2.stream_ref.refs_0_ = bf16[3,384,4096]{2,1,0:T(8,128)(2,1)S(1)} custom-call(s32[4]{0:T(128)S(1)} %pad_add_fusion.place_ref, bf16[384,2048]{1,0:T(8,128)(2,1)S(1)} %copy-done.1, bf16[384,2048]{1,0:T(8,128)(2,1)S(1)} %copy-done.3, bf16[384,2048]{1,0:T(8,128)(2,1)} %collective-permute-done.refs_2_, bf16[384,2048]{1,0:T(8,128)(2,1)} %collective-permute-done.4.refs_3_, ...), custom_call_target="tpu_custom_call" | custom-call | bytes 18874368 | tf_op jit(solution)/shard_map/stage/pallas_call | solution.py:117
  96.4 3.0 %project.2 = (bf16[3,384,128]{2,1,0:T(8,128)(2,1)S(1)}, bf16[3,384,128]{2,1,0:T(8,128)(2,1)S(1)}, f32[3,128,128]{2,1,0:T(8,128)S(1)}, f32[128,128]{1,0:T(8,128)S(1)}) custom-call(bf16[3,384,4096]{2,1,0:T(8,128)(2,1)S(1)} %stage.2.stream_ref.refs_0_, bf16[4096,256]{1,0:T(8,128)(2,1)S(1)} %bitcast.7), custom_call_target="tpu_custom_call" | custom-call | flops 2415919104 | bytes 2097152 | tf_op jit(solution)/shard_map/project/pallas_call | solution.py:145
  99.3 11.4 %collective-permute-done.10.refs_5_ = bf16[512,256]{1,0:T(8,128)(2,1)S(1)} collective-permute-done((bf16[512,256]{1,0:T(8,128)(2,1)S(1)}, bf16[512,256]{1,0:T(8,128)(2,1)S(1)}, u32[]{:S(2)}, u32[]{:S(2)}) %collective-permute-start.10) | collective-permute-done | bytes 262176 | tf_op jit(solution)/shard_map/ppermute | solution.py:315
  110.8 5.0 %collective-permute-done.9.refs_4_ = bf16[512,256]{1,0:T(8,128)(2,1)S(1)} collective-permute-done((bf16[512,256]{1,0:T(8,128)(2,1)S(1)}, bf16[512,256]{1,0:T(8,128)(2,1)S(1)}, u32[]{:S(2)}, u32[]{:S(2)}) %collective-permute-start.9) | collective-permute-done | bytes 262176 | tf_op jit(solution)/shard_map/ppermute | solution.py:315
  117.8 2.7 %collective-permute-start.17 = (bf16[512,256]{1,0:T(8,128)(2,1)S(1)}, bf16[512,256]{1,0:T(8,128)(2,1)S(1)}, u32[]{:S(2)}, u32[]{:S(2)}) collective-permute-start(bf16[512,256]{1,0:T(8,128)(2,1)S(1)} %copy-done.8), channel_id=1, source_target_pairs={{0,14},{2,12},{4,10},{6,8},{8,6},{10,4},{12,2},{14,0},{1,15},{3,13... | collective-permute-start | bytes 786440 | tf_op jit(solution)/shard_map/ppermute | solution.py:315
  121.2 1.9 %collective-permute-start.15 = (bf16[512,256]{1,0:T(8,128)(2,1)S(1)}, bf16[512,256]{1,0:T(8,128)(2,1)S(1)}, u32[]{:S(2)}, u32[]{:S(2)}) collective-permute-start(bf16[512,256]{1,0:T(8,128)(2,1)S(1)} %copy-done.8), channel_id=1, source_target_pairs={{0,6},{2,4},{4,2},{6,0},{8,14},{10,12},{12,10},{14,8},{1,7},{3,5},... | collective-permute-start | bytes 786440 | tf_op jit(solution)/shard_map/ppermute | solution.py:315
  124.0 2.3 %begin.2.refs_3_ = f32[4,384,256]{2,1,0:T(8,128)S(1)} custom-call(s32[4]{0:T(128)S(1)} %pad_add_fusion.place_ref, bf16[3,384,4096]{2,1,0:T(8,128)(2,1)S(1)} %stage.2.stream_ref.refs_0_, bf16[1,384,4096]{2,1,0:T(8,128)(2,1)S(1)} %stage.3.refs_1_.stream_ref, bf16[2048,256]{1,0:T(8,128)(2,1)S(1)} %collective-permute-done.11.refs_2_), custom_call_target="tpu_custom_call" | custom-call | flops 1610612736 | bytes 2097152 | tf_op jit(solution)/shard_map/begin/pallas_call | solution.py:185
  127.6 2.3 %begin.3.refs_6_ = f32[4,384,256]{2,1,0:T(8,128)S(1)} custom-call(s32[4]{0:T(128)S(1)} %pad_add_fusion.place_ref, bf16[3,384,4096]{2,1,0:T(8,128)(2,1)S(1)} %stage.2.stream_ref.refs_0_, bf16[1,384,4096]{2,1,0:T(8,128)(2,1)S(1)} %stage.3.refs_1_.stream_ref, bf16[512,256]{1,0:T(8,128)(2,1)S(1)} %get-tuple-element.100.refs_2_, ...), custom_call_target="tpu_custom_call" | custom-call | flops 1610612736 | bytes 2097152 | tf_op jit(solution)/shard_map/begin/pallas_call | solution.py:185
  130.0 8.9 %collective-permute-done.16.refs_4_ = bf16[512,256]{1,0:T(8,128)(2,1)S(1)} collective-permute-done((bf16[512,256]{1,0:T(8,128)(2,1)}, bf16[512,256]{1,0:T(8,128)(2,1)S(1)}, u32[]{:S(2)}, u32[]{:S(2)}) %collective-permute-start.16) | collective-permute-done | bytes 262176 | tf_op jit(solution)/shard_map/ppermute | solution.py:315
  138.9 2.7 %collective-permute-done.18.refs_2_ = bf16[2048,256]{1,0:T(8,128)(2,1)S(1)} collective-permute-done((bf16[2048,256]{1,0:T(8,128)(2,1)S(1)}, bf16[2048,256]{1,0:T(8,128)(2,1)S(1)}, u32[]{:S(2)}, u32[]{:S(2)}) %collective-permute-start.18) | collective-permute-done | bytes 1048608 | tf_op jit(solution)/shard_map/ppermute | solution.py:318
  141.6 4.0 %collective-permute-done.15.refs_3_ = bf16[512,256]{1,0:T(8,128)(2,1)S(1)} collective-permute-done((bf16[512,256]{1,0:T(8,128)(2,1)S(1)}, bf16[512,256]{1,0:T(8,128)(2,1)S(1)}, u32[]{:S(2)}, u32[]{:S(2)}) %collective-permute-start.15) | collective-permute-done | bytes 262176 | tf_op jit(solution)/shard_map/ppermute | solution.py:315
  145.6 2.7 %keys_values.1 = (bf16[4,384,128]{2,1,0:T(8,128)(2,1)S(1)}, bf16[4,384,128]{2,1,0:T(8,128)(2,1)S(1)}, f32[4,128,128]{2,1,0:T(8,128)S(1)}, f32[2,128,128]{2,1,0:T(8,128)S(1)}) custom-call(s32[4]{0:T(128)S(1)} %pad_add_fusion.place_ref, bf16[3,384,4096]{2,1,0:T(8,128)(2,1)S(1)} %stage.2.stream_ref.refs_0_, bf16[1,384,4096]{2,1,0:T(8,128)(2,1)S(1)} %stage.3.refs_1_.stream_ref, ...), custom_call_target="tpu_custom_call" | custom-call | flops 1610612736 | bytes 2097152 | tf_op jit(solution)/shard_map/keys_values/pallas_call | solution.py:185
  148.3 6.8 %collective-permute-start.19 = (f32[2,128,128]{2,1,0:T(8,128)S(1)}, f32[2,128,128]{2,1,0:T(8,128)S(1)}, u32[]{:S(2)}, u32[]{:S(2)}) collective-permute-start(f32[2,128,128]{2,1,0:T(8,128)S(1)} %get-tuple-element.126), channel_id=1, source_target_pairs={{0,8},{2,10},{4,12},{6,14},{1,9},{3,11},{5,13},{7,15},{16,24},{18,... | collective-permute-start | bytes 393224 | tf_op jit(solution)/shard_map/ppermute | solution.py:295
  155.1 2.6 %queries.1.query_ref = bf16[4,384,256]{2,1,0:T(8,128)(2,1)S(1)} custom-call(s32[4]{0:T(128)S(1)} %pad_add_fusion.place_ref, bf16[3,384,4096]{2,1,0:T(8,128)(2,1)S(1)} %stage.2.stream_ref.refs_0_, bf16[1,384,4096]{2,1,0:T(8,128)(2,1)S(1)} %stage.3.refs_1_.stream_ref, bf16[512,256]{1,0:T(8,128)(2,1)S(1)} %collective-permute-done.14.refs_2_, ...), custom_call_target="tpu_custom_call" | custom-call | flops 1610612736 | bytes 2097152 | tf_op jit(solution)/shard_map/queries/pallas_call | solution.py:185
  157.7 2.0 %attend.3 = (bf16[384,256]{1,0:T(8,128)(2,1)S(1)}, bf16[384,256]{1,0:T(8,128)(2,1)S(1)}, bf16[384,256]{1,0:T(8,128)(2,1)S(1)}) custom-call(s32[4]{0:T(128)S(1)} %pad_add_fusion.place_ref, bf16[4,384,256]{2,1,0:T(8,128)(2,1)S(1)} %queries.1.query_ref, bf16[3,384,128]{2,1,0:T(8,128)(2,1)S(1)} %get-tuple-element.113.refs_0_, ...), custom_call_target="tpu_custom_call" | custom-call | flops 528482304 | bytes 2097152 | tf_op jit(solution)/shard_map/attend/pallas_call | solution.py:268
  160.6 1.9 %collective-permute-start.21 = (bf16[384,256]{1,0:T(8,128)(2,1)S(1)}, bf16[384,256]{1,0:T(8,128)(2,1)S(1)}, u32[]{:S(2)}, u32[]{:S(2)}) collective-permute-start(bf16[384,256]{1,0:T(8,128)(2,1)S(1)} %get-tuple-element.133), channel_id=1, source_target_pairs={{0,4},{2,6},{4,0},{6,2},{8,12},{10,14},{12,8},{14,10},{1,5},{3,7},... | collective-permute-start | bytes 589832 | tf_op jit(solution)/shard_map/ppermute | solution.py:315
  164.4 4.0 %stage_rows.1 = (bf16[4,256,2048]{2,1,0:T(8,128)(2,1)S(1)}, bf16[4,256,2048]{2,1,0:T(8,128)(2,1)S(1)}) custom-call(s32[4]{0:T(128)S(1)} %pad_add_fusion.place_ref, bf16[1024,4096]{1,0:T(8,128)(2,1)} %out_ref.1, bf16[1024,4096]{1,0:T(8,128)(2,1)} %collective-permute-done.2.far_ref), custom_call_target="tpu_custom_call" | custom-call | bytes 16777216 | tf_op jit(solution)/shard_map/stage_rows/pallas_call | solution.py:89
  168.5 2.7 %collective-permute-done.22.refs_3_ = bf16[384,256]{1,0:T(8,128)(2,1)S(1)} collective-permute-done((bf16[384,256]{1,0:T(8,128)(2,1)S(1)}, bf16[384,256]{1,0:T(8,128)(2,1)S(1)}, u32[]{:S(2)}, u32[]{:S(2)}) %collective-permute-start.22) | collective-permute-done | bytes 196640 | tf_op jit(solution)/shard_map/ppermute | solution.py:315
  172.2 1.8 %add_features.2.refs_5_ = f32[384,2048]{1,0:T(8,128)S(1)} custom-call(bf16[384,256]{1,0:T(8,128)(2,1)S(1)} %attend.2.refs_0_, bf16[384,256]{1,0:T(8,128)(2,1)S(1)} %collective-permute-done.20.refs_1_, bf16[384,256]{1,0:T(8,128)(2,1)S(1)} %collective-permute-done.21.refs_2_, bf16[384,256]{1,0:T(8,128)(2,1)S(1)} %collective-permute-done.22.refs_3_, ...), custom_call_target="tpu_custom_call" | custom-call | flops 1610612736 | bytes 8388608 | tf_op jit(solution)/shard_map/add_features/pallas_call | solution.py:289
  174.1 2.9 %add_features.3 = bf16[384,2048]{1,0:T(8,128)(2,1)} custom-call(bf16[384,256]{1,0:T(8,128)(2,1)S(1)} %collective-permute-done.23.refs_0_, bf16[384,256]{1,0:T(8,128)(2,1)S(1)} %collective-permute-done.24.refs_1_, bf16[384,256]{1,0:T(8,128)(2,1)S(1)} %collective-permute-done.25.refs_2_, bf16[384,256]{1,0:T(8,128)(2,1)S(1)} %collective-permute-done.26.refs_3_, ...), custom_call_target="tpu_custom_call" | custom-call | flops 1610612736 | bytes 8388608 | tf_op jit(solution)/shard_map/add_features/pallas_call | solution.py:289
  (66 shorter events, 17.0 us)
Async XLA Ops:
  0.0 72.5 %collective-permute-start.2 = (bf16[1024,4096]{1,0:T(8,128)(2,1)}, bf16[1024,4096]{1,0:T(8,128)(2,1)}, u32[]{:S(2)}, u32[]{:S(2)}) collective-permute-start(bf16[1024,4096]{1,0:T(8,128)(2,1)} %out_ref.1), channel_id=1, source_target_pairs={{0,1},{1,0},{2,3},{3,2},{4,5},{5,4},{6,7},{7,6},{8,9},{9,8},{10,11... | collective-permute-start | bytes 25165832 | tf_op jit(solution)/shard_map/ppermute | solution.py:321
  5.1 67.4 %copy-start.6 = (bf16[512,1024]{1,0:T(8,128)(2,1)S(1)}, bf16[512,1024]{1,0:T(8,128)(2,1)}, u32[]{:S(2)}) copy-start(bf16[512,1024]{1,0:T(8,128)(2,1)} %query_ref) | copy-start | bytes 3145732
  5.1 77.5 %all-to-all-start = ((bf16[8,512,256]{2,1,0:T(8,128)(2,1)}), bf16[8,512,256]{2,1,0:T(8,128)(2,1)S(1)}, u32[]{:S(2)}, u32[]{:S(2)}) async-start(bf16[8,512,256]{2,1,0:T(8,128)(2,1)} %bitcast.10), calls=%async_computation | async-start | bytes 4194304 | tf_op jit(solution)/shard_map/all_to_all | solution.py:324
  12.1 59.3 %collective-permute-start = (bf16[384,2048]{1,0:T(8,128)(2,1)}, bf16[384,2048]{1,0:T(8,128)(2,1)}, u32[]{:S(2)}, u32[]{:S(2)}) collective-permute-start(bf16[384,2048]{1,0:T(8,128)(2,1)} %refs_0_.1), channel_id=1, source_target_pairs={{0,2},{2,0},{4,6},{6,4},{8,10},{10,8},{12,14},{14,12},{1,3},{3,1},... | collective-permute-start | bytes 4718600 | tf_op jit(solution)/shard_map/ppermute | solution.py:315
  14.1 57.3 %collective-permute-start.1 = (bf16[384,2048]{1,0:T(8,128)(2,1)}, bf16[384,2048]{1,0:T(8,128)(2,1)S(1)}, u32[]{:S(2)}, u32[]{:S(2)}) collective-permute-start(bf16[384,2048]{1,0:T(8,128)(2,1)} %refs_0_.1), channel_id=1, source_target_pairs={{0,1},{1,0},{2,3},{3,2},{4,5},{5,4},{6,7},{7,6},{8,9},{9,8},{10,11... | collective-permute-start | bytes 4718600 | tf_op jit(solution)/shard_map/ppermute | solution.py:321
  14.1 68.6 %collective-permute-start.3 = (bf16[384,2048]{1,0:T(8,128)(2,1)}, bf16[384,2048]{1,0:T(8,128)(2,1)}, u32[]{:S(2)}, u32[]{:S(2)}) collective-permute-start(bf16[384,2048]{1,0:T(8,128)(2,1)} %refs_0_.1), channel_id=1, source_target_pairs={{0,4},{2,6},{4,0},{6,2},{8,12},{10,14},{12,8},{14,10},{1,5},{3,7},... | collective-permute-start | bytes 4718600 | tf_op jit(solution)/shard_map/ppermute | solution.py:315
  72.5 11.7 %collective-permute-start.4 = (bf16[384,2048]{1,0:T(8,128)(2,1)}, bf16[384,2048]{1,0:T(8,128)(2,1)}, u32[]{:S(2)}, u32[]{:S(2)}) collective-permute-start(bf16[384,2048]{1,0:T(8,128)(2,1)} %collective-permute-done.refs_2_), channel_id=1, source_target_pairs={{0,1},{1,0},{2,3},{3,2},{4,5},{5,4},{6,7},{7,6},{8,9},{9,8},{10,11... | collective-permute-start | bytes 4718600 | tf_op jit(solution)/shard_map/ppermute | solution.py:321
  75.3 8.9 %collective-permute-start.5 = (bf16[512,256]{1,0:T(8,128)(2,1)}, bf16[512,256]{1,0:T(8,128)(2,1)S(1)}, u32[]{:S(2)}, u32[]{:S(2)}) collective-permute-start(bf16[512,256]{1,0:T(8,128)(2,1)} %get-tuple-element.95), channel_id=1, source_target_pairs={{0,2},{2,0},{4,6},{6,4},{8,10},{10,8},{12,14},{14,12},{1,3},{3,1},... | collective-permute-start | bytes 786440 | tf_op jit(solution)/shard_map/ppermute | solution.py:315
  84.3 8.7 %collective-permute-start.6 = (bf16[384,2048]{1,0:T(8,128)(2,1)}, bf16[384,2048]{1,0:T(8,128)(2,1)S(1)}, u32[]{:S(2)}, u32[]{:S(2)}) collective-permute-start(bf16[384,2048]{1,0:T(8,128)(2,1)} %collective-permute-done.3.refs_4_), channel_id=1, source_target_pairs={{0,1},{1,0},{2,3},{3,2},{4,5},{5,4},{6,7},{7,6},{8,9},{9,8},{10,11... | collective-permute-start | bytes 4718600 | tf_op jit(solution)/shard_map/ppermute | solution.py:321
  84.3 8.7 %copy-start.3 = (bf16[384,2048]{1,0:T(8,128)(2,1)S(1)}, bf16[384,2048]{1,0:T(8,128)(2,1)}, u32[]{:S(2)}) copy-start(bf16[384,2048]{1,0:T(8,128)(2,1)} %copy-done.2) | copy-start | bytes 4718596
  85.7 7.3 %copy-start.1 = (bf16[384,2048]{1,0:T(8,128)(2,1)S(1)}, bf16[384,2048]{1,0:T(8,128)(2,1)}, u32[]{:S(2)}) copy-start(bf16[384,2048]{1,0:T(8,128)(2,1)} %refs_0_.1) | copy-start | bytes 4718596
  85.7 30.0 %collective-permute-start.7 = (bf16[384,1408]{1,0:T(8,128)(2,1)S(1)}, bf16[384,1408]{1,0:T(8,128)(2,1)S(1)}, u32[]{:S(2)}, u32[]{:S(2)}) collective-permute-start(bf16[384,1408]{1,0:T(8,128)(2,1)S(1)} %slice.12), channel_id=1, source_target_pairs={{0,2},{2,0},{4,6},{6,4},{8,10},{10,8},{12,14},{14,12},{1,3},{3,1},... | collective-permute-start | bytes 3244040 | tf_op jit(solution)/shard_map/ppermute | solution.py:315
  86.2 29.6 %collective-permute-start.11 = (bf16[2048,256]{1,0:T(8,128)(2,1)S(1)}, bf16[2048,256]{1,0:T(8,128)(2,1)S(1)}, u32[]{:S(2)}, u32[]{:S(2)}) collective-permute-start(bf16[2048,256]{1,0:T(8,128)(2,1)S(1)} %slice.14), channel_id=1, source_target_pairs={{0,16},{16,0},{1,17},{17,1},{2,18},{18,2},{3,19},{19,3},{4,20},{20... | collective-permute-start | bytes 3145736 | tf_op jit(solution)/shard_map/ppermute | solution.py:318
  88.8 26.9 %collective-permute-start.8 = (bf16[384,640]{1,0:T(8,128)(2,1)S(1)}, bf16[384,640]{1,0:T(8,128)(2,1)S(1)}, u32[]{:S(2)}, u32[]{:S(2)}) collective-permute-start(bf16[384,640]{1,0:T(8,128)(2,1)S(1)} %slice.13), channel_id=1, source_target_pairs={{0,4},{2,6},{4,0},{6,2},{8,12},{10,14},{12,8},{14,10},{1,5},{3,7},... | collective-permute-start | bytes 1474568 | tf_op jit(solution)/shard_map/ppermute | solution.py:315
  90.6 20.1 %collective-permute-start.10 = (bf16[512,256]{1,0:T(8,128)(2,1)S(1)}, bf16[512,256]{1,0:T(8,128)(2,1)S(1)}, u32[]{:S(2)}, u32[]{:S(2)}) collective-permute-start(bf16[512,256]{1,0:T(8,128)(2,1)S(1)} %copy-done.10), channel_id=1, source_target_pairs={{0,12},{2,14},{4,8},{6,10},{8,4},{10,6},{12,0},{14,2},{1,13},{3,15... | collective-permute-start | bytes 786440 | tf_op jit(solution)/shard_map/ppermute | solution.py:315
  93.0 22.8 %collective-permute-start.9 = (bf16[512,256]{1,0:T(8,128)(2,1)S(1)}, bf16[512,256]{1,0:T(8,128)(2,1)S(1)}, u32[]{:S(2)}, u32[]{:S(2)}) collective-permute-start(bf16[512,256]{1,0:T(8,128)(2,1)S(1)} %get-tuple-element.100.refs_2_), channel_id=1, source_target_pairs={{0,8},{2,10},{4,12},{6,14},{8,0},{10,2},{12,4},{14,6},{1,9},{3,11}... | collective-permute-start | bytes 786440 | tf_op jit(solution)/shard_map/ppermute | solution.py:315
  99.3 18.5 %copy-start.8 = (bf16[512,256]{1,0:T(8,128)(2,1)S(1)}, bf16[512,256]{1,0:T(8,128)(2,1)}, u32[]{:S(2)}) copy-start(bf16[512,256]{1,0:T(8,128)(2,1)} %copy-done.7) | copy-start | bytes 786436
  115.8 4.8 %collective-permute-start.12 = (bf16[384,1408]{1,0:T(8,128)(2,1)S(1)}, bf16[384,1408]{1,0:T(8,128)(2,1)S(1)}, u32[]{:S(2)}, u32[]{:S(2)}) collective-permute-start(bf16[384,1408]{1,0:T(8,128)(2,1)S(1)} %collective-permute-done.7.refs_0_), channel_id=1, source_target_pairs={{0,1},{1,0},{2,3},{3,2},{4,5},{5,4},{6,7},{7,6},{8,9},{9,8},{10,11... | collective-permute-start | bytes 3244040 | tf_op jit(solution)/shard_map/ppermute | solution.py:321
  115.9 25.6 %collective-permute-start.18 = (bf16[2048,256]{1,0:T(8,128)(2,1)S(1)}, bf16[2048,256]{1,0:T(8,128)(2,1)S(1)}, u32[]{:S(2)}, u32[]{:S(2)}) collective-permute-start(bf16[2048,256]{1,0:T(8,128)(2,1)S(1)} %slice.15), channel_id=1, source_target_pairs={{0,16},{16,0},{1,17},{17,1},{2,18},{18,2},{3,19},{19,3},{4,20},{20... | collective-permute-start | bytes 3145736 | tf_op jit(solution)/shard_map/ppermute | solution.py:318
  116.6 4.6 %collective-permute-start.13 = (bf16[384,640]{1,0:T(8,128)(2,1)S(1)}, bf16[384,640]{1,0:T(8,128)(2,1)S(1)}, u32[]{:S(2)}, u32[]{:S(2)}) collective-permute-start(bf16[384,640]{1,0:T(8,128)(2,1)S(1)} %collective-permute-done.8.refs_2_), channel_id=1, source_target_pairs={{0,1},{1,0},{2,3},{3,2},{4,5},{5,4},{6,7},{7,6},{8,9},{9,8},{10,11... | collective-permute-start | bytes 1474568 | tf_op jit(solution)/shard_map/ppermute | solution.py:321
  116.8 22.1 %collective-permute-start.16 = (bf16[512,256]{1,0:T(8,128)(2,1)}, bf16[512,256]{1,0:T(8,128)(2,1)S(1)}, u32[]{:S(2)}, u32[]{:S(2)}) collective-permute-start(bf16[512,256]{1,0:T(8,128)(2,1)} %get-tuple-element.95), channel_id=1, source_target_pairs={{0,10},{2,8},{4,14},{6,12},{8,2},{10,0},{12,6},{14,4},{1,11},{3,9}... | collective-permute-start | bytes 786440 | tf_op jit(solution)/shard_map/ppermute | solution.py:315
  117.8 21.1 %collective-permute-start.17 = (bf16[512,256]{1,0:T(8,128)(2,1)S(1)}, bf16[512,256]{1,0:T(8,128)(2,1)S(1)}, u32[]{:S(2)}, u32[]{:S(2)}) collective-permute-start(bf16[512,256]{1,0:T(8,128)(2,1)S(1)} %copy-done.8), channel_id=1, source_target_pairs={{0,14},{2,12},{4,10},{6,8},{8,6},{10,4},{12,2},{14,0},{1,15},{3,13... | collective-permute-start | bytes 786440 | tf_op jit(solution)/shard_map/ppermute | solution.py:315
  120.5 21.0 %collective-permute-start.14 = (bf16[512,256]{1,0:T(8,128)(2,1)S(1)}, bf16[512,256]{1,0:T(8,128)(2,1)S(1)}, u32[]{:S(2)}, u32[]{:S(2)}) collective-permute-start(bf16[512,256]{1,0:T(8,128)(2,1)S(1)} %copy-done.10), channel_id=1, source_target_pairs={{0,4},{2,6},{4,0},{6,2},{8,12},{10,14},{12,8},{14,10},{1,5},{3,7},... | collective-permute-start | bytes 786440 | tf_op jit(solution)/shard_map/ppermute | solution.py:315
  121.2 24.4 %collective-permute-start.15 = (bf16[512,256]{1,0:T(8,128)(2,1)S(1)}, bf16[512,256]{1,0:T(8,128)(2,1)S(1)}, u32[]{:S(2)}, u32[]{:S(2)}) collective-permute-start(bf16[512,256]{1,0:T(8,128)(2,1)S(1)} %copy-done.8), channel_id=1, source_target_pairs={{0,6},{2,4},{4,2},{6,0},{8,14},{10,12},{12,10},{14,8},{1,7},{3,5},... | collective-permute-start | bytes 786440 | tf_op jit(solution)/shard_map/ppermute | solution.py:315
  148.3 9.4 %collective-permute-start.19 = (f32[2,128,128]{2,1,0:T(8,128)S(1)}, f32[2,128,128]{2,1,0:T(8,128)S(1)}, u32[]{:S(2)}, u32[]{:S(2)}) collective-permute-start(f32[2,128,128]{2,1,0:T(8,128)S(1)} %get-tuple-element.126), channel_id=1, source_target_pairs={{0,8},{2,10},{4,12},{6,14},{1,9},{3,11},{5,13},{7,15},{16,24},{18,... | collective-permute-start | bytes 393224 | tf_op jit(solution)/shard_map/ppermute | solution.py:295
  159.7 8.8 %collective-permute-start.20 = (bf16[384,256]{1,0:T(8,128)(2,1)S(1)}, bf16[384,256]{1,0:T(8,128)(2,1)S(1)}, u32[]{:S(2)}, u32[]{:S(2)}) collective-permute-start(bf16[384,256]{1,0:T(8,128)(2,1)S(1)} %get-tuple-element.132), channel_id=1, source_target_pairs={{0,2},{2,0},{4,6},{6,4},{8,10},{10,8},{12,14},{14,12},{1,3},{3,1},... | collective-permute-start | bytes 589832 | tf_op jit(solution)/shard_map/ppermute | solution.py:315
  160.6 7.9 %collective-permute-start.21 = (bf16[384,256]{1,0:T(8,128)(2,1)S(1)}, bf16[384,256]{1,0:T(8,128)(2,1)S(1)}, u32[]{:S(2)}, u32[]{:S(2)}) collective-permute-start(bf16[384,256]{1,0:T(8,128)(2,1)S(1)} %get-tuple-element.133), channel_id=1, source_target_pairs={{0,4},{2,6},{4,0},{6,2},{8,12},{10,14},{12,8},{14,10},{1,5},{3,7},... | collective-permute-start | bytes 589832 | tf_op jit(solution)/shard_map/ppermute | solution.py:315
  162.4 8.8 %collective-permute-start.22 = (bf16[384,256]{1,0:T(8,128)(2,1)S(1)}, bf16[384,256]{1,0:T(8,128)(2,1)S(1)}, u32[]{:S(2)}, u32[]{:S(2)}) collective-permute-start(bf16[384,256]{1,0:T(8,128)(2,1)S(1)} %get-tuple-element.134), channel_id=1, source_target_pairs={{0,6},{2,4},{4,2},{6,0},{8,14},{10,12},{12,10},{14,8},{1,7},{3,5},... | collective-permute-start | bytes 589832 | tf_op jit(solution)/shard_map/ppermute | solution.py:315
  171.2 2.8 %collective-permute-start.23 = (bf16[384,256]{1,0:T(8,128)(2,1)S(1)}, bf16[384,256]{1,0:T(8,128)(2,1)S(1)}, u32[]{:S(2)}, u32[]{:S(2)}) collective-permute-start(bf16[384,256]{1,0:T(8,128)(2,1)S(1)} %attend.2.refs_0_), channel_id=1, source_target_pairs={{0,1},{1,0},{2,3},{3,2},{4,5},{5,4},{6,7},{7,6},{8,9},{9,8},{10,11... | collective-permute-start | bytes 589832 | tf_op jit(solution)/shard_map/ppermute | solution.py:321
  171.2 2.8 %collective-permute-start.24 = (bf16[384,256]{1,0:T(8,128)(2,1)S(1)}, bf16[384,256]{1,0:T(8,128)(2,1)S(1)}, u32[]{:S(2)}, u32[]{:S(2)}) collective-permute-start(bf16[384,256]{1,0:T(8,128)(2,1)S(1)} %collective-permute-done.20.refs_1_), channel_id=1, source_target_pairs={{0,1},{1,0},{2,3},{3,2},{4,5},{5,4},{6,7},{7,6},{8,9},{9,8},{10,11... | collective-permute-start | bytes 589832 | tf_op jit(solution)/shard_map/ppermute | solution.py:321
  171.7 2.3 %collective-permute-start.25 = (bf16[384,256]{1,0:T(8,128)(2,1)S(1)}, bf16[384,256]{1,0:T(8,128)(2,1)S(1)}, u32[]{:S(2)}, u32[]{:S(2)}) collective-permute-start(bf16[384,256]{1,0:T(8,128)(2,1)S(1)} %collective-permute-done.21.refs_2_), channel_id=1, source_target_pairs={{0,1},{1,0},{2,3},{3,2},{4,5},{5,4},{6,7},{7,6},{8,9},{9,8},{10,11... | collective-permute-start | bytes 589832 | tf_op jit(solution)/shard_map/ppermute | solution.py:321
  171.7 2.4 %collective-permute-start.26 = (bf16[384,256]{1,0:T(8,128)(2,1)S(1)}, bf16[384,256]{1,0:T(8,128)(2,1)S(1)}, u32[]{:S(2)}, u32[]{:S(2)}) collective-permute-start(bf16[384,256]{1,0:T(8,128)(2,1)S(1)} %collective-permute-done.22.refs_3_), channel_id=1, source_target_pairs={{0,1},{1,0},{2,3},{3,2},{4,5},{5,4},{6,7},{7,6},{8,9},{9,8},{10,11... | collective-permute-start | bytes 589832 | tf_op jit(solution)/shard_map/ppermute | solution.py:321
  (7 other events, 11.3 us)

commit v11 on v10

--- a/solution.py
+++ b/solution.py
@@ -345,22 +345,18 @@
             arrived.update({m: xor(sent[m % SUB], m) for m in steps})
 
     arrived = {0: q_sent[0]}
-    fetch(q_sent, 1)
+    fetch(q_sent, 4, 1)
     across, kv_mine, beside, far_beside, q_sent, arrived = ob((across, kv_mine, beside, far_beside, q_sent, arrived))
-    middle = kv_mine.shape[0] // 2
-    kv_upper = other_part(kv_mine[:middle])
+    kv_other = other_part(kv_mine)
     left = xor(across[:, :cut], 1)
     right = xor(beside[:, cut:], 2)
-    fetch(q_sent, 4, 6)
+    fetch(q_sent, 6, 5)
     near = [(tokens, 0, 0, 0), (far_tokens, 0, 0, 1), (beside, 1, 0, 0), (far_beside, 1, 0, 1)]
     near += [(across, 2, 0, 0), (other_core(across), 2, 0, 1)]
     near = stage(place, near, SUB - 1, rows, 2 * half)
     first = project(near, kv_mine)
-    left, right, arrived, kv_upper, kv_mine, q_sent, first = ob(
-        (left, right, arrived, kv_upper, kv_mine, q_sent, first)
-    )
-    kv_lower = other_part(kv_mine[middle:])
-    fetch(q_sent, 5, 7)
+    left, right, arrived, q_sent, first = ob((left, right, arrived, q_sent, first))
+    fetch(q_sent, 7)
     far_left, far_right = other_core(left), other_core(right)
     far_left, q_sent = ob((far_left, q_sent))
     fetch(q_sent, 3, 2)
@@ -369,15 +365,14 @@
 
     streams = [near, corner]
     last = project(corner, kv_mine, first[3])
-    kv_base = begin(place, streams, [(kv_upper, 0)])
     if pieced:
-        early = (0, 1, 4, 6)
+        early = (0, 1, 4, 5, 6)
         q_base = begin(place, streams, [(arrived[m], (m,)) for m in early])
-        arrived, kv_lower, kv_base, q_base = ob((arrived, kv_lower, kv_base, q_base))
+        arrived, kv_other, q_base = ob((arrived, kv_other, q_base))
         q_parts = [(arrived[m], (m,)) for m in range(n_ctx) if m not in early]
     else:
         q_base, q_parts = None, [(gather_queries(q_sent), 0)]
-    *second, totals = keys_values(place, streams, [(kv_lower, middle)], kv_base, last[3])
+    *second, totals = keys_values(place, streams, [(kv_other, 0)], None, last[3])
     carried = exclusive_prefix(totals, groups)
     heads = [[first[:3], last[:3]], [second]]
     query = queries(place, streams, q_parts, q_base)

time: 177 us -> 179 us (1.011)
  starting transfers between devices: 35.9 us -> 37.9 us
    ppermute x14, starting transfers between devices: 18.1 us -> 24.4 us  [xor(): return lax.ppermute(value, 'ctx', [(i, i ^ step) for i in range(n_ctx)])]
    ppermute x1, starting transfers between devices: 6.8 us -> 2.97 us  [shift(): return lax.ppermute(v, 'ctx', pairs)]
    ppermute x2 -> x1, waiting for transfers between devices: 2.68 us -> 5.14 us  [other_part(): return lax.ppermute(value, 'groups', [(0, 1), (1, 0)])]
    pallas_call x4 -> x3, Pallas kernels: 9.97 us -> 9.21 us  [run_blocks(): call(body, name, out_shape, specs, outs, LIMIT, flops, 2 * MIB)]
  transfers between devices with their start and end apart: 28 -> 27, of which waited for: 9 -> 12; matrix products, arithmetic and copies ran while one was open for 2% -> 1% of each run, Pallas kernels for 14% -> 13%
where the time goes in v11:
time: 179 us
  waiting for transfers between devices  100 us (56%)
  starting transfers between devices  37.9 us (21%)
  Pallas kernels  31.8 us (18%)
  local copies, waits for them, and re-layouts  8.93 us (5%)
    ppermute x14, waiting for transfers between devices, xor(): return lax.ppermute(value, 'ctx', [(i, i ^ step) for i in range(n_ctx)])  94.7 us
    ppermute x14, starting transfers between devices, xor(): return lax.ppermute(value, 'ctx', [(i, i ^ step) for i in range(n_ctx)])  24.4 us
    pallas_call x3, Pallas kernels, run_blocks(): call(body, name, out_shape, specs, outs, LIMIT, flops, 2 * MIB)  9.21 us
    all_to_all x1, starting transfers between devices, spread(): return lax.all_to_all(packed, 'ctx', 0, 0, tiled=True)  6.93 us
    unnamed x22, local copies, waits for them, and re-layouts  6.39 us
    ppermute x1, waiting for transfers between devices, other_part(): return lax.ppermute(value, 'groups', [(0, 1), (1, 0)])  5.14 us
    pallas_call x2, Pallas kernels, add_features(): call(kernel, 'add_features', shape, [VMEM] * len(args), VMEM, LIMIT, flop...  4.74 us
    pallas_call x2, Pallas kernels, project(): call(kernel, 'project', shapes, [VMEM] * len(args), [VMEM] * 4, LIMIT, fl...  4.26 us
  transfers between devices with their start and end apart: 27, of which 12 were waited for; matrix products, arithmetic and copies ran while one was open for 1% of the time, Pallas kernels for 13%

profile of v11, /device:TPU:0, one launch (start us, length us, event | category | flops | bytes accessed | tf_op | source)
XLA Modules:
  0.0 178.9 jit_solution(8597707799844535226)
XLA Ops:
  5.1 6.9 %all-to-all-start = ((bf16[8,512,256]{2,1,0:T(8,128)(2,1)}), bf16[8,512,256]{2,1,0:T(8,128)(2,1)S(1)}, u32[]{:S(2)}, u32[]{:S(2)}) async-start(bf16[8,512,256]{2,1,0:T(8,128)(2,1)} %bitcast.9), calls=%async_computation | async-start | bytes 4194304 | tf_op jit(solution)/shard_map/all_to_all | solution.py:324
  12.1 2.0 %collective-permute-start = (bf16[384,2048]{1,0:T(8,128)(2,1)}, bf16[384,2048]{1,0:T(8,128)(2,1)}, u32[]{:S(2)}, u32[]{:S(2)}) collective-permute-start(bf16[384,2048]{1,0:T(8,128)(2,1)} %refs_0_.1), channel_id=1, source_target_pairs={{0,2},{2,0},{4,6},{6,4},{8,10},{10,8},{12,14},{14,12},{1,3},{3,1},... | collective-permute-start | bytes 4718600 | tf_op jit(solution)/shard_map/ppermute | solution.py:315
  14.1 1.5 collective-permute-start.3
  15.6 55.8 %collective-permute-done.refs_2_ = bf16[384,2048]{1,0:T(8,128)(2,1)} collective-permute-done((bf16[384,2048]{1,0:T(8,128)(2,1)}, bf16[384,2048]{1,0:T(8,128)(2,1)}, u32[]{:S(2)}, u32[]{:S(2)}) %collective-permute-start) | collective-permute-done | bytes 1572896 | tf_op jit(solution)/shard_map/ppermute | solution.py:315
  72.5 1.4 pack_queries.1
  75.7 2.6 %collective-permute-start.6 = (bf16[512,256]{1,0:T(8,128)(2,1)S(1)}, bf16[512,256]{1,0:T(8,128)(2,1)S(1)}, u32[]{:S(2)}, u32[]{:S(2)}) collective-permute-start(bf16[512,256]{1,0:T(8,128)(2,1)S(1)} %get-tuple-element.95.refs_2_), channel_id=1, source_target_pairs={{0,8},{2,10},{4,12},{6,14},{8,0},{10,2},{12,4},{14,6},{1,9},{3,11}... | collective-permute-start | bytes 786440 | tf_op jit(solution)/shard_map/ppermute | solution.py:315
  78.3 9.5 %collective-permute-done.3.refs_4_ = bf16[384,2048]{1,0:T(8,128)(2,1)} collective-permute-done((bf16[384,2048]{1,0:T(8,128)(2,1)}, bf16[384,2048]{1,0:T(8,128)(2,1)}, u32[]{:S(2)}, u32[]{:S(2)}) %collective-permute-start.3) | collective-permute-done | bytes 1572896 | tf_op jit(solution)/shard_map/ppermute | solution.py:315
  87.8 2.8 %collective-permute-done.6.refs_4_ = bf16[512,256]{1,0:T(8,128)(2,1)S(1)} collective-permute-done((bf16[512,256]{1,0:T(8,128)(2,1)S(1)}, bf16[512,256]{1,0:T(8,128)(2,1)S(1)}, u32[]{:S(2)}, u32[]{:S(2)}) %collective-permute-start.6) | collective-permute-done | bytes 262176 | tf_op jit(solution)/shard_map/ppermute | solution.py:315
  90.8 1.5 slice.6
  92.2 1.8 %collective-permute-start.8 = (bf16[384,1408]{1,0:T(8,128)(2,1)S(1)}, bf16[384,1408]{1,0:T(8,128)(2,1)S(1)}, u32[]{:S(2)}, u32[]{:S(2)}) collective-permute-start(bf16[384,1408]{1,0:T(8,128)(2,1)S(1)} %slice.6), channel_id=1, source_target_pairs={{0,2},{2,0},{4,6},{6,4},{8,10},{10,8},{12,14},{14,12},{1,3},{3,1},... | collective-permute-start | bytes 3244040 | tf_op jit(solution)/shard_map/ppermute | solution.py:315
  94.0 1.5 collective-permute-start.17
  97.1 3.2 %collective-permute-start.10 = (bf16[512,256]{1,0:T(8,128)(2,1)}, bf16[512,256]{1,0:T(8,128)(2,1)S(1)}, u32[]{:S(2)}, u32[]{:S(2)}) collective-permute-start(bf16[512,256]{1,0:T(8,128)(2,1)} %get-tuple-element.82), channel_id=1, source_target_pairs={{0,10},{2,8},{4,14},{6,12},{8,2},{10,0},{12,6},{14,4},{1,11},{3,9}... | collective-permute-start | bytes 786440 | tf_op jit(solution)/shard_map/ppermute | solution.py:315
  100.8 3.3 %stage.2.stream_ref.refs_0_ = bf16[3,384,4096]{2,1,0:T(8,128)(2,1)S(1)} custom-call(s32[4]{0:T(128)S(1)} %pad_add_fusion.place_ref, bf16[384,2048]{1,0:T(8,128)(2,1)S(1)} %copy-done.1, bf16[384,2048]{1,0:T(8,128)(2,1)S(1)} %copy-done.3, bf16[384,2048]{1,0:T(8,128)(2,1)} %collective-permute-done.refs_2_, bf16[384,2048]{1,0:T(8,128)(2,1)} %collective-permute-done.4.refs_3_, ...), custom_call_target="tpu_custom_call" | custom-call | bytes 18874368 | tf_op jit(solution)/shard_map/stage/pallas_call | solution.py:117
  104.2 3.0 %project.2 = (bf16[3,384,128]{2,1,0:T(8,128)(2,1)S(1)}, bf16[3,384,128]{2,1,0:T(8,128)(2,1)S(1)}, f32[3,128,128]{2,1,0:T(8,128)S(1)}, f32[128,128]{1,0:T(8,128)S(1)}) custom-call(bf16[3,384,4096]{2,1,0:T(8,128)(2,1)S(1)} %stage.2.stream_ref.refs_0_, bf16[4096,256]{1,0:T(8,128)(2,1)S(1)} %bitcast.7), custom_call_target="tpu_custom_call" | custom-call | flops 2415919104 | bytes 2097152 | tf_op jit(solution)/shard_map/project/pallas_call | solution.py:145
  107.1 7.3 %collective-permute-done.10.refs_5_ = bf16[512,256]{1,0:T(8,128)(2,1)S(1)} collective-permute-done((bf16[512,256]{1,0:T(8,128)(2,1)}, bf16[512,256]{1,0:T(8,128)(2,1)S(1)}, u32[]{:S(2)}, u32[]{:S(2)}) %collective-permute-start.10) | collective-permute-done | bytes 262176 | tf_op jit(solution)/shard_map/ppermute | solution.py:315
  114.5 8.0 %collective-permute-done.11.refs_6_ = bf16[512,256]{1,0:T(8,128)(2,1)S(1)} collective-permute-done((bf16[512,256]{1,0:T(8,128)(2,1)}, bf16[512,256]{1,0:T(8,128)(2,1)S(1)}, u32[]{:S(2)}, u32[]{:S(2)}) %collective-permute-start.11) | collective-permute-done | bytes 262176 | tf_op jit(solution)/shard_map/ppermute | solution.py:315
  122.5 1.6 collective-permute-done.8.refs_0_
  124.5 4.4 %collective-permute-start.16 = (bf16[512,256]{1,0:T(8,128)(2,1)S(1)}, bf16[512,256]{1,0:T(8,128)(2,1)S(1)}, u32[]{:S(2)}, u32[]{:S(2)}) collective-permute-start(bf16[512,256]{1,0:T(8,128)(2,1)S(1)} %copy-done.8), channel_id=1, source_target_pairs={{0,14},{2,12},{4,10},{6,8},{8,6},{10,4},{12,2},{14,0},{1,15},{3,13... | collective-permute-start | bytes 786440 | tf_op jit(solution)/shard_map/ppermute | solution.py:315
  129.0 1.7 collective-permute-start.15
  133.0 2.7 %begin.1.refs_5_ = f32[4,384,256]{2,1,0:T(8,128)S(1)} custom-call(s32[4]{0:T(128)S(1)} %pad_add_fusion.place_ref, bf16[3,384,4096]{2,1,0:T(8,128)(2,1)S(1)} %stage.2.stream_ref.refs_0_, bf16[1,384,4096]{2,1,0:T(8,128)(2,1)S(1)} %stage.3.refs_1_.stream_ref, bf16[512,256]{1,0:T(8,128)(2,1)S(1)} %get-tuple-element.95.refs_2_, ...), custom_call_target="tpu_custom_call" | custom-call | flops 2013265920 | bytes 2097152 | tf_op jit(solution)/shard_map/begin/pallas_call | solution.py:185
  136.5 5.1 %collective-permute-done.17.refs_2_ = bf16[4096,256]{1,0:T(8,128)(2,1)S(1)} collective-permute-done((bf16[4096,256]{1,0:T(8,128)(2,1)S(1)}, bf16[4096,256]{1,0:T(8,128)(2,1)S(1)}, u32[]{:S(2)}, u32[]{:S(2)}) %collective-permute-start.17) | collective-permute-done | bytes 2097184 | tf_op jit(solution)/shard_map/ppermute | solution.py:318
  141.6 5.2 %collective-permute-done.15.refs_3_ = bf16[512,256]{1,0:T(8,128)(2,1)S(1)} collective-permute-done((bf16[512,256]{1,0:T(8,128)(2,1)S(1)}, bf16[512,256]{1,0:T(8,128)(2,1)S(1)}, u32[]{:S(2)}, u32[]{:S(2)}) %collective-permute-start.15) | collective-permute-done | bytes 262176 | tf_op jit(solution)/shard_map/ppermute | solution.py:315
  146.8 4.3 %keys_values.1 = (bf16[4,384,128]{2,1,0:T(8,128)(2,1)S(1)}, bf16[4,384,128]{2,1,0:T(8,128)(2,1)S(1)}, f32[4,128,128]{2,1,0:T(8,128)S(1)}, f32[2,128,128]{2,1,0:T(8,128)S(1)}) custom-call(s32[4]{0:T(128)S(1)} %pad_add_fusion.place_ref, bf16[3,384,4096]{2,1,0:T(8,128)(2,1)S(1)} %stage.2.stream_ref.refs_0_, bf16[1,384,4096]{2,1,0:T(8,128)(2,1)S(1)} %stage.3.refs_1_.stream_ref, ...), custom_call_target="tpu_custom_call" | custom-call | flops 3221225472 | bytes 2097152 | tf_op jit(solution)/shard_map/keys_values/pallas_call | solution.py:185
  151.0 3.0 %collective-permute-start.18 = (f32[2,128,128]{2,1,0:T(8,128)S(1)}, f32[2,128,128]{2,1,0:T(8,128)S(1)}, u32[]{:S(2)}, u32[]{:S(2)}) collective-permute-start(f32[2,128,128]{2,1,0:T(8,128)S(1)} %get-tuple-element.118), channel_id=1, source_target_pairs={{0,8},{2,10},{4,12},{6,14},{1,9},{3,11},{5,13},{7,15},{16,24},{18,... | collective-permute-start | bytes 393224 | tf_op jit(solution)/shard_map/ppermute | solution.py:295
  154.0 2.2 %queries.1.query_ref = bf16[4,384,256]{2,1,0:T(8,128)(2,1)S(1)} custom-call(s32[4]{0:T(128)S(1)} %pad_add_fusion.place_ref, bf16[3,384,4096]{2,1,0:T(8,128)(2,1)S(1)} %stage.2.stream_ref.refs_0_, bf16[1,384,4096]{2,1,0:T(8,128)(2,1)S(1)} %stage.3.refs_1_.stream_ref, bf16[512,256]{1,0:T(8,128)(2,1)S(1)} %collective-permute-done.14.refs_2_, ...), custom_call_target="tpu_custom_call" | custom-call | flops 1207959552 | bytes 2097152 | tf_op jit(solution)/shard_map/queries/pallas_call | solution.py:185
  156.3 2.0 %attend.3 = (bf16[384,256]{1,0:T(8,128)(2,1)S(1)}, bf16[384,256]{1,0:T(8,128)(2,1)S(1)}, bf16[384,256]{1,0:T(8,128)(2,1)S(1)}) custom-call(s32[4]{0:T(128)S(1)} %pad_add_fusion.place_ref, bf16[4,384,256]{2,1,0:T(8,128)(2,1)S(1)} %queries.1.query_ref, bf16[3,384,128]{2,1,0:T(8,128)(2,1)S(1)} %get-tuple-element.106.refs_0_, ...), custom_call_target="tpu_custom_call" | custom-call | flops 528482304 | bytes 2097152 | tf_op jit(solution)/shard_map/attend/pallas_call | solution.py:268
  158.3 1.6 collective-permute-start.19
  159.9 4.2 %collective-permute-start.20 = (bf16[384,256]{1,0:T(8,128)(2,1)S(1)}, bf16[384,256]{1,0:T(8,128)(2,1)S(1)}, u32[]{:S(2)}, u32[]{:S(2)}) collective-permute-start(bf16[384,256]{1,0:T(8,128)(2,1)S(1)} %get-tuple-element.125), channel_id=1, source_target_pairs={{0,4},{2,6},{4,0},{6,2},{8,12},{10,14},{12,8},{14,10},{1,5},{3,7},... | collective-permute-start | bytes 589832 | tf_op jit(solution)/shard_map/ppermute | solution.py:315
  165.3 4.0 %stage_rows.1 = (bf16[4,256,2048]{2,1,0:T(8,128)(2,1)S(1)}, bf16[4,256,2048]{2,1,0:T(8,128)(2,1)S(1)}) custom-call(s32[4]{0:T(128)S(1)} %pad_add_fusion.place_ref, bf16[1024,4096]{1,0:T(8,128)(2,1)} %out_ref.1, bf16[1024,4096]{1,0:T(8,128)(2,1)} %collective-permute-done.2.far_ref), custom_call_target="tpu_custom_call" | custom-call | bytes 16777216 | tf_op jit(solution)/shard_map/stage_rows/pallas_call | solution.py:89
  169.9 3.3 %collective-permute-done.21.refs_3_ = bf16[384,256]{1,0:T(8,128)(2,1)S(1)} collective-permute-done((bf16[384,256]{1,0:T(8,128)(2,1)S(1)}, bf16[384,256]{1,0:T(8,128)(2,1)S(1)}, u32[]{:S(2)}, u32[]{:S(2)}) %collective-permute-start.21) | collective-permute-done | bytes 196640 | tf_op jit(solution)/shard_map/ppermute | solution.py:315
  174.1 1.8 %add_features.2.refs_5_ = f32[384,2048]{1,0:T(8,128)S(1)} custom-call(bf16[384,256]{1,0:T(8,128)(2,1)S(1)} %attend.2.refs_0_, bf16[384,256]{1,0:T(8,128)(2,1)S(1)} %collective-permute-done.19.refs_1_, bf16[384,256]{1,0:T(8,128)(2,1)S(1)} %collective-permute-done.20.refs_2_, bf16[384,256]{1,0:T(8,128)(2,1)S(1)} %collective-permute-done.21.refs_3_, ...), custom_call_target="tpu_custom_call" | custom-call | flops 1610612736 | bytes 8388608 | tf_op jit(solution)/shard_map/add_features/pallas_call | solution.py:289
  176.0 2.9 %add_features.3 = bf16[384,2048]{1,0:T(8,128)(2,1)} custom-call(bf16[384,256]{1,0:T(8,128)(2,1)S(1)} %collective-permute-done.22.refs_0_, bf16[384,256]{1,0:T(8,128)(2,1)S(1)} %collective-permute-done.23.refs_1_, bf16[384,256]{1,0:T(8,128)(2,1)S(1)} %collective-permute-done.24.refs_2_, bf16[384,256]{1,0:T(8,128)(2,1)S(1)} %collective-permute-done.25.refs_3_, ...), custom_call_target="tpu_custom_call" | custom-call | flops 1610612736 | bytes 8388608 | tf_op jit(solution)/shard_map/add_features/pallas_call | solution.py:289
  (61 shorter events, 16.5 us)
Async XLA Ops:
  0.0 72.5 %collective-permute-start.2 = (bf16[1024,4096]{1,0:T(8,128)(2,1)}, bf16[1024,4096]{1,0:T(8,128)(2,1)}, u32[]{:S(2)}, u32[]{:S(2)}) collective-permute-start(bf16[1024,4096]{1,0:T(8,128)(2,1)} %out_ref.1), channel_id=1, source_target_pairs={{0,1},{1,0},{2,3},{3,2},{4,5},{5,4},{6,7},{7,6},{8,9},{9,8},{10,11... | collective-permute-start | bytes 25165832 | tf_op jit(solution)/shard_map/ppermute | solution.py:321
  5.1 67.4 %copy-start.6 = (bf16[512,1024]{1,0:T(8,128)(2,1)S(1)}, bf16[512,1024]{1,0:T(8,128)(2,1)}, u32[]{:S(2)}) copy-start(bf16[512,1024]{1,0:T(8,128)(2,1)} %query_ref) | copy-start | bytes 3145732
  5.1 82.7 %all-to-all-start = ((bf16[8,512,256]{2,1,0:T(8,128)(2,1)}), bf16[8,512,256]{2,1,0:T(8,128)(2,1)S(1)}, u32[]{:S(2)}, u32[]{:S(2)}) async-start(bf16[8,512,256]{2,1,0:T(8,128)(2,1)} %bitcast.9), calls=%async_computation | async-start | bytes 4194304 | tf_op jit(solution)/shard_map/all_to_all | solution.py:324
  12.1 59.3 %collective-permute-start = (bf16[384,2048]{1,0:T(8,128)(2,1)}, bf16[384,2048]{1,0:T(8,128)(2,1)}, u32[]{:S(2)}, u32[]{:S(2)}) collective-permute-start(bf16[384,2048]{1,0:T(8,128)(2,1)} %refs_0_.1), channel_id=1, source_target_pairs={{0,2},{2,0},{4,6},{6,4},{8,10},{10,8},{12,14},{14,12},{1,3},{3,1},... | collective-permute-start | bytes 4718600 | tf_op jit(solution)/shard_map/ppermute | solution.py:315
  14.1 57.3 %collective-permute-start.1 = (bf16[384,2048]{1,0:T(8,128)(2,1)}, bf16[384,2048]{1,0:T(8,128)(2,1)S(1)}, u32[]{:S(2)}, u32[]{:S(2)}) collective-permute-start(bf16[384,2048]{1,0:T(8,128)(2,1)} %refs_0_.1), channel_id=1, source_target_pairs={{0,1},{1,0},{2,3},{3,2},{4,5},{5,4},{6,7},{7,6},{8,9},{9,8},{10,11... | collective-permute-start | bytes 4718600 | tf_op jit(solution)/shard_map/ppermute | solution.py:321
  14.1 73.7 %collective-permute-start.3 = (bf16[384,2048]{1,0:T(8,128)(2,1)}, bf16[384,2048]{1,0:T(8,128)(2,1)}, u32[]{:S(2)}, u32[]{:S(2)}) collective-permute-start(bf16[384,2048]{1,0:T(8,128)(2,1)} %refs_0_.1), channel_id=1, source_target_pairs={{0,4},{2,6},{4,0},{6,2},{8,12},{10,14},{12,8},{14,10},{1,5},{3,7},... | collective-permute-start | bytes 4718600 | tf_op jit(solution)/shard_map/ppermute | solution.py:315
  72.5 18.1 %collective-permute-start.4 = (bf16[384,2048]{1,0:T(8,128)(2,1)}, bf16[384,2048]{1,0:T(8,128)(2,1)}, u32[]{:S(2)}, u32[]{:S(2)}) collective-permute-start(bf16[384,2048]{1,0:T(8,128)(2,1)} %collective-permute-done.refs_2_), channel_id=1, source_target_pairs={{0,1},{1,0},{2,3},{3,2},{4,5},{5,4},{6,7},{7,6},{8,9},{9,8},{10,11... | collective-permute-start | bytes 4718600 | tf_op jit(solution)/shard_map/ppermute | solution.py:321
  75.4 12.5 %collective-permute-start.5 = (bf16[512,256]{1,0:T(8,128)(2,1)}, bf16[512,256]{1,0:T(8,128)(2,1)S(1)}, u32[]{:S(2)}, u32[]{:S(2)}) collective-permute-start(bf16[512,256]{1,0:T(8,128)(2,1)} %get-tuple-element.82), channel_id=1, source_target_pairs={{0,2},{2,0},{4,6},{6,4},{8,10},{10,8},{12,14},{14,12},{1,3},{3,1},... | collective-permute-start | bytes 786440 | tf_op jit(solution)/shard_map/ppermute | solution.py:315
  75.7 15.0 %collective-permute-start.6 = (bf16[512,256]{1,0:T(8,128)(2,1)S(1)}, bf16[512,256]{1,0:T(8,128)(2,1)S(1)}, u32[]{:S(2)}, u32[]{:S(2)}) collective-permute-start(bf16[512,256]{1,0:T(8,128)(2,1)S(1)} %get-tuple-element.95.refs_2_), channel_id=1, source_target_pairs={{0,8},{2,10},{4,12},{6,14},{8,0},{10,2},{12,4},{14,6},{1,9},{3,11}... | collective-permute-start | bytes 786440 | tf_op jit(solution)/shard_map/ppermute | solution.py:315
  90.7 10.1 %copy-start.1 = (bf16[384,2048]{1,0:T(8,128)(2,1)S(1)}, bf16[384,2048]{1,0:T(8,128)(2,1)}, u32[]{:S(2)}) copy-start(bf16[384,2048]{1,0:T(8,128)(2,1)} %refs_0_.1) | copy-start | bytes 4718596
  90.7 10.1 %copy-start.3 = (bf16[384,2048]{1,0:T(8,128)(2,1)S(1)}, bf16[384,2048]{1,0:T(8,128)(2,1)}, u32[]{:S(2)}) copy-start(bf16[384,2048]{1,0:T(8,128)(2,1)} %copy-done.2) | copy-start | bytes 4718596
  90.7 9.6 %collective-permute-start.7 = (bf16[384,2048]{1,0:T(8,128)(2,1)}, bf16[384,2048]{1,0:T(8,128)(2,1)S(1)}, u32[]{:S(2)}, u32[]{:S(2)}) collective-permute-start(bf16[384,2048]{1,0:T(8,128)(2,1)} %collective-permute-done.3.refs_4_), channel_id=1, source_target_pairs={{0,1},{1,0},{2,3},{3,2},{4,5},{5,4},{6,7},{7,6},{8,9},{9,8},{10,11... | collective-permute-start | bytes 4718600 | tf_op jit(solution)/shard_map/ppermute | solution.py:321
  92.2 31.8 %collective-permute-start.8 = (bf16[384,1408]{1,0:T(8,128)(2,1)S(1)}, bf16[384,1408]{1,0:T(8,128)(2,1)S(1)}, u32[]{:S(2)}, u32[]{:S(2)}) collective-permute-start(bf16[384,1408]{1,0:T(8,128)(2,1)S(1)} %slice.6), channel_id=1, source_target_pairs={{0,2},{2,0},{4,6},{6,4},{8,10},{10,8},{12,14},{14,12},{1,3},{3,1},... | collective-permute-start | bytes 3244040 | tf_op jit(solution)/shard_map/ppermute | solution.py:315
  94.0 47.6 %collective-permute-start.17 = (bf16[4096,256]{1,0:T(8,128)(2,1)S(1)}, bf16[4096,256]{1,0:T(8,128)(2,1)S(1)}, u32[]{:S(2)}, u32[]{:S(2)}) collective-permute-start(bf16[4096,256]{1,0:T(8,128)(2,1)S(1)} %bitcast.6), channel_id=1, source_target_pairs={{0,16},{16,0},{1,17},{17,1},{2,18},{18,2},{3,19},{19,3},{4,20},{20... | collective-permute-start | bytes 6291464 | tf_op jit(solution)/shard_map/ppermute | solution.py:318
  96.6 25.8 %collective-permute-start.9 = (bf16[384,640]{1,0:T(8,128)(2,1)S(1)}, bf16[384,640]{1,0:T(8,128)(2,1)S(1)}, u32[]{:S(2)}, u32[]{:S(2)}) collective-permute-start(bf16[384,640]{1,0:T(8,128)(2,1)S(1)} %slice.7), channel_id=1, source_target_pairs={{0,4},{2,6},{4,0},{6,2},{8,12},{10,14},{12,8},{14,10},{1,5},{3,7},... | collective-permute-start | bytes 1474568 | tf_op jit(solution)/shard_map/ppermute | solution.py:315
  97.1 17.4 %collective-permute-start.10 = (bf16[512,256]{1,0:T(8,128)(2,1)}, bf16[512,256]{1,0:T(8,128)(2,1)S(1)}, u32[]{:S(2)}, u32[]{:S(2)}) collective-permute-start(bf16[512,256]{1,0:T(8,128)(2,1)} %get-tuple-element.82), channel_id=1, source_target_pairs={{0,10},{2,8},{4,14},{6,12},{8,2},{10,0},{12,6},{14,4},{1,11},{3,9}... | collective-permute-start | bytes 786440 | tf_op jit(solution)/shard_map/ppermute | solution.py:315
  100.2 22.2 %collective-permute-start.11 = (bf16[512,256]{1,0:T(8,128)(2,1)}, bf16[512,256]{1,0:T(8,128)(2,1)S(1)}, u32[]{:S(2)}, u32[]{:S(2)}) collective-permute-start(bf16[512,256]{1,0:T(8,128)(2,1)} %copy-done.9), channel_id=1, source_target_pairs={{0,12},{2,14},{4,8},{6,10},{8,4},{10,6},{12,0},{14,2},{1,13},{3,15... | collective-permute-start | bytes 786440 | tf_op jit(solution)/shard_map/ppermute | solution.py:315
  104.1 20.4 %copy-start.8 = (bf16[512,256]{1,0:T(8,128)(2,1)S(1)}, bf16[512,256]{1,0:T(8,128)(2,1)}, u32[]{:S(2)}) copy-start(bf16[512,256]{1,0:T(8,128)(2,1)} %copy-done.7) | copy-start | bytes 786436
  104.1 24.8 %copy-start.10 = (bf16[512,256]{1,0:T(8,128)(2,1)S(1)}, bf16[512,256]{1,0:T(8,128)(2,1)}, u32[]{:S(2)}) copy-start(bf16[512,256]{1,0:T(8,128)(2,1)} %copy-done.9) | copy-start | bytes 786436
  124.0 5.0 %collective-permute-start.12 = (bf16[384,1408]{1,0:T(8,128)(2,1)S(1)}, bf16[384,1408]{1,0:T(8,128)(2,1)S(1)}, u32[]{:S(2)}, u32[]{:S(2)}) collective-permute-start(bf16[384,1408]{1,0:T(8,128)(2,1)S(1)} %collective-permute-done.8.refs_0_), channel_id=1, source_target_pairs={{0,1},{1,0},{2,3},{3,2},{4,5},{5,4},{6,7},{7,6},{8,9},{9,8},{10,11... | collective-permute-start | bytes 3244040 | tf_op jit(solution)/shard_map/ppermute | solution.py:321
  124.0 6.7 %collective-permute-start.13 = (bf16[384,640]{1,0:T(8,128)(2,1)S(1)}, bf16[384,640]{1,0:T(8,128)(2,1)S(1)}, u32[]{:S(2)}, u32[]{:S(2)}) collective-permute-start(bf16[384,640]{1,0:T(8,128)(2,1)S(1)} %collective-permute-done.9.refs_2_), channel_id=1, source_target_pairs={{0,1},{1,0},{2,3},{3,2},{4,5},{5,4},{6,7},{7,6},{8,9},{9,8},{10,11... | collective-permute-start | bytes 1474568 | tf_op jit(solution)/shard_map/ppermute | solution.py:321
  124.5 12.0 %collective-permute-start.16 = (bf16[512,256]{1,0:T(8,128)(2,1)S(1)}, bf16[512,256]{1,0:T(8,128)(2,1)S(1)}, u32[]{:S(2)}, u32[]{:S(2)}) collective-permute-start(bf16[512,256]{1,0:T(8,128)(2,1)S(1)} %copy-done.8), channel_id=1, source_target_pairs={{0,14},{2,12},{4,10},{6,8},{8,6},{10,4},{12,2},{14,0},{1,15},{3,13... | collective-permute-start | bytes 786440 | tf_op jit(solution)/shard_map/ppermute | solution.py:315
  129.0 12.7 %collective-permute-start.14 = (bf16[512,256]{1,0:T(8,128)(2,1)S(1)}, bf16[512,256]{1,0:T(8,128)(2,1)S(1)}, u32[]{:S(2)}, u32[]{:S(2)}) collective-permute-start(bf16[512,256]{1,0:T(8,128)(2,1)S(1)} %copy-done.10), channel_id=1, source_target_pairs={{0,4},{2,6},{4,0},{6,2},{8,12},{10,14},{12,8},{14,10},{1,5},{3,7},... | collective-permute-start | bytes 786440 | tf_op jit(solution)/shard_map/ppermute | solution.py:315
  129.0 17.8 %collective-permute-start.15 = (bf16[512,256]{1,0:T(8,128)(2,1)S(1)}, bf16[512,256]{1,0:T(8,128)(2,1)S(1)}, u32[]{:S(2)}, u32[]{:S(2)}) collective-permute-start(bf16[512,256]{1,0:T(8,128)(2,1)S(1)} %copy-done.8), channel_id=1, source_target_pairs={{0,6},{2,4},{4,2},{6,0},{8,14},{10,12},{12,10},{14,8},{1,7},{3,5},... | collective-permute-start | bytes 786440 | tf_op jit(solution)/shard_map/ppermute | solution.py:315
  151.0 5.3 %collective-permute-start.18 = (f32[2,128,128]{2,1,0:T(8,128)S(1)}, f32[2,128,128]{2,1,0:T(8,128)S(1)}, u32[]{:S(2)}, u32[]{:S(2)}) collective-permute-start(f32[2,128,128]{2,1,0:T(8,128)S(1)} %get-tuple-element.118), channel_id=1, source_target_pairs={{0,8},{2,10},{4,12},{6,14},{1,9},{3,11},{5,13},{7,15},{16,24},{18,... | collective-permute-start | bytes 393224 | tf_op jit(solution)/shard_map/ppermute | solution.py:295
  158.3 11.0 %collective-permute-start.19 = (bf16[384,256]{1,0:T(8,128)(2,1)S(1)}, bf16[384,256]{1,0:T(8,128)(2,1)S(1)}, u32[]{:S(2)}, u32[]{:S(2)}) collective-permute-start(bf16[384,256]{1,0:T(8,128)(2,1)S(1)} %get-tuple-element.124), channel_id=1, source_target_pairs={{0,2},{2,0},{4,6},{6,4},{8,10},{10,8},{12,14},{14,12},{1,3},{3,1},... | collective-permute-start | bytes 589832 | tf_op jit(solution)/shard_map/ppermute | solution.py:315
  159.9 10.0 %collective-permute-start.20 = (bf16[384,256]{1,0:T(8,128)(2,1)S(1)}, bf16[384,256]{1,0:T(8,128)(2,1)S(1)}, u32[]{:S(2)}, u32[]{:S(2)}) collective-permute-start(bf16[384,256]{1,0:T(8,128)(2,1)S(1)} %get-tuple-element.125), channel_id=1, source_target_pairs={{0,4},{2,6},{4,0},{6,2},{8,12},{10,14},{12,8},{14,10},{1,5},{3,7},... | collective-permute-start | bytes 589832 | tf_op jit(solution)/shard_map/ppermute | solution.py:315
  164.1 9.0 %collective-permute-start.21 = (bf16[384,256]{1,0:T(8,128)(2,1)S(1)}, bf16[384,256]{1,0:T(8,128)(2,1)S(1)}, u32[]{:S(2)}, u32[]{:S(2)}) collective-permute-start(bf16[384,256]{1,0:T(8,128)(2,1)S(1)} %get-tuple-element.126), channel_id=1, source_target_pairs={{0,6},{2,4},{4,2},{6,0},{8,14},{10,12},{12,10},{14,8},{1,7},{3,5},... | collective-permute-start | bytes 589832 | tf_op jit(solution)/shard_map/ppermute | solution.py:315
  173.1 2.8 %collective-permute-start.22 = (bf16[384,256]{1,0:T(8,128)(2,1)S(1)}, bf16[384,256]{1,0:T(8,128)(2,1)S(1)}, u32[]{:S(2)}, u32[]{:S(2)}) collective-permute-start(bf16[384,256]{1,0:T(8,128)(2,1)S(1)} %attend.2.refs_0_), channel_id=1, source_target_pairs={{0,1},{1,0},{2,3},{3,2},{4,5},{5,4},{6,7},{7,6},{8,9},{9,8},{10,11... | collective-permute-start | bytes 589832 | tf_op jit(solution)/shard_map/ppermute | solution.py:321
  173.1 2.8 %collective-permute-start.23 = (bf16[384,256]{1,0:T(8,128)(2,1)S(1)}, bf16[384,256]{1,0:T(8,128)(2,1)S(1)}, u32[]{:S(2)}, u32[]{:S(2)}) collective-permute-start(bf16[384,256]{1,0:T(8,128)(2,1)S(1)} %collective-permute-done.19.refs_1_), channel_id=1, source_target_pairs={{0,1},{1,0},{2,3},{3,2},{4,5},{5,4},{6,7},{7,6},{8,9},{9,8},{10,11... | collective-permute-start | bytes 589832 | tf_op jit(solution)/shard_map/ppermute | solution.py:321
  173.6 2.3 %collective-permute-start.24 = (bf16[384,256]{1,0:T(8,128)(2,1)S(1)}, bf16[384,256]{1,0:T(8,128)(2,1)S(1)}, u32[]{:S(2)}, u32[]{:S(2)}) collective-permute-start(bf16[384,256]{1,0:T(8,128)(2,1)S(1)} %collective-permute-done.20.refs_2_), channel_id=1, source_target_pairs={{0,1},{1,0},{2,3},{3,2},{4,5},{5,4},{6,7},{7,6},{8,9},{9,8},{10,11... | collective-permute-start | bytes 589832 | tf_op jit(solution)/shard_map/ppermute | solution.py:321
  173.6 2.3 %collective-permute-start.25 = (bf16[384,256]{1,0:T(8,128)(2,1)S(1)}, bf16[384,256]{1,0:T(8,128)(2,1)S(1)}, u32[]{:S(2)}, u32[]{:S(2)}) collective-permute-start(bf16[384,256]{1,0:T(8,128)(2,1)S(1)} %collective-permute-done.21.refs_3_), channel_id=1, source_target_pairs={{0,1},{1,0},{2,3},{3,2},{4,5},{5,4},{6,7},{7,6},{8,9},{9,8},{10,11... | collective-permute-start | bytes 589832 | tf_op jit(solution)/shard_map/ppermute | solution.py:321
  (6 other events, 6.4 us)

commit v12 on v10

--- a/solution.py
+++ b/solution.py
@@ -40,18 +40,24 @@
 def pack_keys_values(place, w_key, w_value, count):
     depth = w_key.shape[0]
 
-    def kernel(place_ref, key_ref, value_ref, out):
-        for j in range(SUB):
-            start = pl.multiple_of((2 * j + place_ref[1]) * HDIM, HDIM)
-            key = key_ref[:, pl.ds(start, HDIM)]
-            value = value_ref[:, pl.ds(start, HDIM)]
-            for i in range(j, count, SUB):
-                out[i * depth : (i + 1) * depth, :HDIM] = key
-                out[i * depth : (i + 1) * depth, HDIM:] = value
+    def kernel(place_ref, key_ref, value_ref, out, sems):
+        copies = []
+        for i in range(count):
+            start = pl.multiple_of((2 * (i % SUB) + place_ref[1]) * HDIM, HDIM)
+            for h, ref in enumerate((key_ref, value_ref)):
+                target = out.at[pl.ds(i * depth, depth), pl.ds(h * HDIM, HDIM)]
+                copies.append(pltpu.make_async_copy(ref.at[:, pl.ds(start, HDIM)], target, sems.at[2 * i + h]))
+        for copy in copies:
+            copy.start()
+        for copy in copies:
+            copy.wait()
 
     shape = jax.ShapeDtypeStruct((count * depth, 2 * HDIM), BF16)
     moved = count * depth * 2 * HDIM * 4
-    return call(kernel, "pack_keys_values", shape, [SMEM, VMEM, VMEM], VMEM, LIMIT, 0, moved)(place, w_key, w_value)
+    sems = pltpu.SemaphoreType.DMA((2 * count,))
+    return call(kernel, "pack_keys_values", shape, [SMEM, ANY, ANY], ANY, 56, 0, moved, [sems])(
+        place, w_key, w_value
+    )
 
 
 def pack_queries(place, w_query):
@@ -346,11 +352,14 @@
 
     arrived = {0: q_sent[0]}
     fetch(q_sent, 1)
-    across, kv_mine, beside, far_beside, q_sent, arrived = ob((across, kv_mine, beside, far_beside, q_sent, arrived))
+    beside_cut = beside[:, cut:]
+    across, kv_mine, beside, far_beside, q_sent, arrived, beside_cut = ob(
+        (across, kv_mine, beside, far_beside, q_sent, arrived, beside_cut)
+    )
     middle = kv_mine.shape[0] // 2
     kv_upper = other_part(kv_mine[:middle])
     left = xor(across[:, :cut], 1)
-    right = xor(beside[:, cut:], 2)
+    right = xor(beside_cut, 2)
     fetch(q_sent, 4, 6)
     near = [(tokens, 0, 0, 0), (far_tokens, 0, 0, 1), (beside, 1, 0, 0), (far_beside, 1, 0, 1)]
     near += [(across, 2, 0, 0), (other_core(across), 2, 0, 1)]
@@ -381,10 +390,9 @@
     carried = exclusive_prefix(totals, groups)
     heads = [[first[:3], last[:3]], [second]]
     query = queries(place, streams, q_parts, q_base)
-    away = attend(place, (3, 1, 2), query, heads, carried)
-    home = attend(place, (0,), query, heads, carried)
-    normed = [home[0], xor(away[1], 1), xor(away[2], 2), xor(away[0], 3)]
-    home_0, w_far = lax.optimization_barrier((home[0], w_far))
+    normed = [attend(place, (r,), query, heads, carried)[0] for r in (3, 1, 2, 0)]
+    normed = [normed[3], xor(normed[1], 1), xor(normed[2], 2), xor(normed[0], 3)]
+    home_0, w_far = lax.optimization_barrier((normed[0], w_far))
     out_keep, out_far = stage_rows(place, w_out, w_far)
     out_keep, out_far, *normed = lax.optimization_barrier((out_keep, out_far, home_0, *normed[1:]))
     partial = add_features(normed, out_keep)

time: 177 us -> 237 us (1.34)
  Pallas kernels: 32.6 us -> 98.8 us
  local copies, waits for them, and re-layouts: 9.01 us -> 5.23 us
  waiting for transfers between devices: 99.2 us -> 95.9 us
    pallas_call x1, Pallas kernels: 0.82 us -> 65.4 us  [pack_keys_values(): call(kernel, 'pack_keys_values', shape, [SMEM, ANY, ANY], ANY, 56, 0, mov...]
    unnamed x22 -> x18, local copies, waits for them, and re-layouts: 6.36 us -> 2.58 us
    ppermute x14, waiting for transfers between devices: 96.5 us -> 93.1 us  [xor(): return lax.ppermute(value, 'ctx', [(i, i ^ step) for i in range(n_ctx)])]
  transfers between devices with their start and end apart: 28 -> 28, of which waited for: 9 -> 9; matrix products, arithmetic and copies ran while one was open for 2% -> 1% of each run, Pallas kernels for 14% -> 39%
where the time goes in v12:
time: 237 us
  Pallas kernels  98.8 us (42%)
  waiting for transfers between devices  95.9 us (40%)
  starting transfers between devices  36.1 us (15%)
  local copies, waits for them, and re-layouts  5.23 us (2%)
    ppermute x14, waiting for transfers between devices, xor(): return lax.ppermute(value, 'ctx', [(i, i ^ step) for i in range(n_ctx)])  93.1 us
    pallas_call x1, Pallas kernels, pack_keys_values(): call(kernel, 'pack_keys_values', shape, [SMEM, ANY, ANY], ANY, 56, 0, mov...  65.4 us
    ppermute x14, starting transfers between devices, xor(): return lax.ppermute(value, 'ctx', [(i, i ^ step) for i in range(n_ctx)])  18.3 us
    pallas_call x4, Pallas kernels, run_blocks(): call(body, name, out_shape, specs, outs, LIMIT, flops, 2 * MIB)  9.98 us
    ppermute x1, starting transfers between devices, shift(): return lax.ppermute(v, 'ctx', pairs)  6.97 us
    all_to_all x1, starting transfers between devices, spread(): return lax.all_to_all(packed, 'ctx', 0, 0, tiled=True)  6.95 us
  transfers between devices with their start and end apart: 28, of which 9 were waited for; matrix products, arithmetic and copies ran while one was open for 1% of the time, Pallas kernels for 39%

profile of v12, /device:TPU:0, one launch (start us, length us, event | category | flops | bytes accessed | tf_op | source)
XLA Modules:
  0.0 236.9 jit_solution(6877116538824200888)
XLA Ops:
  1.0 65.4 %pack_keys_values.1 = bf16[4096,256]{1,0:T(8,128)(2,1)} custom-call(s32[4]{0:T(128)} %pad_add_fusion.place_ref, bf16[512,1024]{1,0:T(8,128)(2,1)} %key_ref.1, bf16[512,1024]{1,0:T(8,128)(2,1)} %value_ref.1), custom_call_target="tpu_custom_call" | custom-call | bytes 4194304 | tf_op jit(solution)/shard_map/pack_keys_values/pallas_call | solution.py:58
  66.5 6.9 %all-to-all-start = ((bf16[8,512,256]{2,1,0:T(8,128)(2,1)}), bf16[8,512,256]{2,1,0:T(8,128)(2,1)S(1)}, u32[]{:S(2)}, u32[]{:S(2)}) async-start(bf16[8,512,256]{2,1,0:T(8,128)(2,1)} %bitcast.10), calls=%async_computation | async-start | bytes 4194304 | tf_op jit(solution)/shard_map/all_to_all | solution.py:330
  73.4 2.0 collective-permute-start
  75.5 1.5 collective-permute-start.3
  76.9 55.8 %collective-permute-done.refs_2_ = bf16[384,2048]{1,0:T(8,128)(2,1)} collective-permute-done((bf16[384,2048]{1,0:T(8,128)(2,1)}, bf16[384,2048]{1,0:T(8,128)(2,1)}, u32[]{:S(2)}, u32[]{:S(2)}) %collective-permute-start) | collective-permute-done | bytes 1572896 | tf_op jit(solution)/shard_map/ppermute | solution.py:321
  133.9 1.4 pack_queries.1
  138.1 5.9 %collective-permute-done.3.refs_4_ = bf16[384,2048]{1,0:T(8,128)(2,1)} collective-permute-done((bf16[384,2048]{1,0:T(8,128)(2,1)}, bf16[384,2048]{1,0:T(8,128)(2,1)}, u32[]{:S(2)}, u32[]{:S(2)}) %collective-permute-start.3) | collective-permute-done | bytes 1572896 | tf_op jit(solution)/shard_map/ppermute | solution.py:321
  144.0 1.6 collective-permute-done.5.refs_3_
  145.6 1.4 slice.13
  147.5 1.6 collective-permute-start.11
  149.1 1.7 collective-permute-start.8
  150.9 2.4 collective-permute-start.10
  153.2 3.3 %stage.2.stream_ref.refs_0_ = bf16[3,384,4096]{2,1,0:T(8,128)(2,1)S(1)} custom-call(s32[4]{0:T(128)S(1)} %copy-done.4, bf16[384,2048]{1,0:T(8,128)(2,1)S(1)} %copy-done, bf16[384,2048]{1,0:T(8,128)(2,1)S(1)} %copy-done.2, bf16[384,2048]{1,0:T(8,128)(2,1)} %collective-permute-done.refs_2_, bf16[384,2048]{1,0:T(8,128)(2,1)} %collective-permute-done.4.refs_3_, ...), custom_call_target="tpu_custom_call" | custom-call | bytes 18874368 | tf_op jit(solution)/shard_map/stage/pallas_call | solution.py:123
  156.6 3.0 %project.2 = (bf16[3,384,128]{2,1,0:T(8,128)(2,1)S(1)}, bf16[3,384,128]{2,1,0:T(8,128)(2,1)S(1)}, f32[3,128,128]{2,1,0:T(8,128)S(1)}, f32[128,128]{1,0:T(8,128)S(1)}) custom-call(bf16[3,384,4096]{2,1,0:T(8,128)(2,1)S(1)} %stage.2.stream_ref.refs_0_, bf16[4096,256]{1,0:T(8,128)(2,1)S(1)} %bitcast.7), custom_call_target="tpu_custom_call" | custom-call | flops 2415919104 | bytes 2097152 | tf_op jit(solution)/shard_map/project/pallas_call | solution.py:151
  159.6 11.4 %collective-permute-done.10.refs_5_ = bf16[512,256]{1,0:T(8,128)(2,1)S(1)} collective-permute-done((bf16[512,256]{1,0:T(8,128)(2,1)S(1)}, bf16[512,256]{1,0:T(8,128)(2,1)S(1)}, u32[]{:S(2)}, u32[]{:S(2)}) %collective-permute-start.10) | collective-permute-done | bytes 262176 | tf_op jit(solution)/shard_map/ppermute | solution.py:321
  171.0 5.0 %collective-permute-done.9.refs_4_ = bf16[512,256]{1,0:T(8,128)(2,1)S(1)} collective-permute-done((bf16[512,256]{1,0:T(8,128)(2,1)S(1)}, bf16[512,256]{1,0:T(8,128)(2,1)S(1)}, u32[]{:S(2)}, u32[]{:S(2)}) %collective-permute-start.9) | collective-permute-done | bytes 262176 | tf_op jit(solution)/shard_map/ppermute | solution.py:321
  176.9 1.4 collective-permute-start.16
  178.3 2.4 %collective-permute-start.17 = (bf16[512,256]{1,0:T(8,128)(2,1)S(1)}, bf16[512,256]{1,0:T(8,128)(2,1)S(1)}, u32[]{:S(2)}, u32[]{:S(2)}) collective-permute-start(bf16[512,256]{1,0:T(8,128)(2,1)S(1)} %copy-done.6), channel_id=1, source_target_pairs={{0,14},{2,12},{4,10},{6,8},{8,6},{10,4},{12,2},{14,0},{1,15},{3,13... | collective-permute-start | bytes 786440 | tf_op jit(solution)/shard_map/ppermute | solution.py:321
  181.4 1.9 collective-permute-start.15
  184.2 2.3 begin.2.refs_3_
  186.6 1.3 project.3
  187.9 2.3 begin.3.refs_6_
  190.2 8.9 %collective-permute-done.16.refs_4_ = bf16[512,256]{1,0:T(8,128)(2,1)S(1)} collective-permute-done((bf16[512,256]{1,0:T(8,128)(2,1)}, bf16[512,256]{1,0:T(8,128)(2,1)S(1)}, u32[]{:S(2)}, u32[]{:S(2)}) %collective-permute-start.16) | collective-permute-done | bytes 262176 | tf_op jit(solution)/shard_map/ppermute | solution.py:321
  199.1 2.7 %collective-permute-done.18.refs_2_ = bf16[2048,256]{1,0:T(8,128)(2,1)S(1)} collective-permute-done((bf16[2048,256]{1,0:T(8,128)(2,1)S(1)}, bf16[2048,256]{1,0:T(8,128)(2,1)S(1)}, u32[]{:S(2)}, u32[]{:S(2)}) %collective-permute-start.18) | collective-permute-done | bytes 1048608 | tf_op jit(solution)/shard_map/ppermute | solution.py:324
  201.8 3.9 %collective-permute-done.15.refs_3_ = bf16[512,256]{1,0:T(8,128)(2,1)S(1)} collective-permute-done((bf16[512,256]{1,0:T(8,128)(2,1)S(1)}, bf16[512,256]{1,0:T(8,128)(2,1)S(1)}, u32[]{:S(2)}, u32[]{:S(2)}) %collective-permute-start.15) | collective-permute-done | bytes 262176 | tf_op jit(solution)/shard_map/ppermute | solution.py:321
  205.7 2.7 %keys_values.1 = (bf16[4,384,128]{2,1,0:T(8,128)(2,1)S(1)}, bf16[4,384,128]{2,1,0:T(8,128)(2,1)S(1)}, f32[4,128,128]{2,1,0:T(8,128)S(1)}, f32[2,128,128]{2,1,0:T(8,128)S(1)}) custom-call(s32[4]{0:T(128)S(1)} %copy-done.4, bf16[3,384,4096]{2,1,0:T(8,128)(2,1)S(1)} %stage.2.stream_ref.refs_0_, bf16[1,384,4096]{2,1,0:T(8,128)(2,1)S(1)} %stage.3.refs_1_.stream_ref, ...), custom_call_target="tpu_custom_call" | custom-call | flops 1610612736 | bytes 2097152 | tf_op jit(solution)/shard_map/keys_values/pallas_call | solution.py:191
  208.4 7.0 %collective-permute-start.19 = (f32[2,128,128]{2,1,0:T(8,128)S(1)}, f32[2,128,128]{2,1,0:T(8,128)S(1)}, u32[]{:S(2)}, u32[]{:S(2)}) collective-permute-start(f32[2,128,128]{2,1,0:T(8,128)S(1)} %get-tuple-element.125), channel_id=1, source_target_pairs={{0,8},{2,10},{4,12},{6,14},{1,9},{3,11},{5,13},{7,15},{16,24},{18,... | collective-permute-start | bytes 393224 | tf_op jit(solution)/shard_map/ppermute | solution.py:301
  215.4 2.6 %queries.1.query_ref = bf16[4,384,256]{2,1,0:T(8,128)(2,1)S(1)} custom-call(s32[4]{0:T(128)S(1)} %copy-done.4, bf16[3,384,4096]{2,1,0:T(8,128)(2,1)S(1)} %stage.2.stream_ref.refs_0_, bf16[1,384,4096]{2,1,0:T(8,128)(2,1)S(1)} %stage.3.refs_1_.stream_ref, bf16[512,256]{1,0:T(8,128)(2,1)S(1)} %collective-permute-done.14.refs_2_, ...), custom_call_target="tpu_custom_call" | custom-call | flops 1610612736 | bytes 2097152 | tf_op jit(solution)/shard_map/queries/pallas_call | solution.py:191
  219.3 2.2 collective-permute-start.22
  226.5 4.0 %stage_rows.1 = (bf16[4,256,2048]{2,1,0:T(8,128)(2,1)S(1)}, bf16[4,256,2048]{2,1,0:T(8,128)(2,1)S(1)}) custom-call(s32[4]{0:T(128)S(1)} %copy-done.4, bf16[1024,4096]{1,0:T(8,128)(2,1)} %out_ref.1, bf16[1024,4096]{1,0:T(8,128)(2,1)} %collective-permute-done.2.far_ref), custom_call_target="tpu_custom_call" | custom-call | bytes 16777216 | tf_op jit(solution)/shard_map/stage_rows/pallas_call | solution.py:95
  232.1 1.8 add_features.2.refs_5_
  233.9 2.9 %add_features.3 = bf16[384,2048]{1,0:T(8,128)(2,1)} custom-call(bf16[384,256]{1,0:T(8,128)(2,1)S(1)} %collective-permute-done.23.refs_0_, bf16[384,256]{1,0:T(8,128)(2,1)S(1)} %collective-permute-done.24.refs_1_, bf16[384,256]{1,0:T(8,128)(2,1)S(1)} %collective-permute-done.25.refs_2_, bf16[384,256]{1,0:T(8,128)(2,1)S(1)} %collective-permute-done.26.refs_3_, ...), custom_call_target="tpu_custom_call" | custom-call | flops 1610612736 | bytes 8388608 | tf_op jit(solution)/shard_map/add_features/pallas_call | solution.py:295
  (64 shorter events, 15.7 us)
Async XLA Ops:
  0.0 133.9 %collective-permute-start.2 = (bf16[1024,4096]{1,0:T(8,128)(2,1)}, bf16[1024,4096]{1,0:T(8,128)(2,1)}, u32[]{:S(2)}, u32[]{:S(2)}) collective-permute-start(bf16[1024,4096]{1,0:T(8,128)(2,1)} %out_ref.1), channel_id=1, source_target_pairs={{0,1},{1,0},{2,3},{3,2},{4,5},{5,4},{6,7},{7,6},{8,9},{9,8},{10,11... | collective-permute-start | bytes 25165832 | tf_op jit(solution)/shard_map/ppermute | solution.py:327
  66.5 67.4 %copy-start.3 = (bf16[512,1024]{1,0:T(8,128)(2,1)S(1)}, bf16[512,1024]{1,0:T(8,128)(2,1)}, u32[]{:S(2)}) copy-start(bf16[512,1024]{1,0:T(8,128)(2,1)} %query_ref) | copy-start | bytes 3145732
  66.5 67.4 %copy-start.4 = (s32[4]{0:T(128)S(1)}, s32[4]{0:T(128)}, u32[]{:S(2)}) copy-start(s32[4]{0:T(128)} %pad_add_fusion.place_ref) | copy-start | bytes 52
  66.5 77.5 %all-to-all-start = ((bf16[8,512,256]{2,1,0:T(8,128)(2,1)}), bf16[8,512,256]{2,1,0:T(8,128)(2,1)S(1)}, u32[]{:S(2)}, u32[]{:S(2)}) async-start(bf16[8,512,256]{2,1,0:T(8,128)(2,1)} %bitcast.10), calls=%async_computation | async-start | bytes 4194304 | tf_op jit(solution)/shard_map/all_to_all | solution.py:330
  73.4 59.3 %collective-permute-start = (bf16[384,2048]{1,0:T(8,128)(2,1)}, bf16[384,2048]{1,0:T(8,128)(2,1)}, u32[]{:S(2)}, u32[]{:S(2)}) collective-permute-start(bf16[384,2048]{1,0:T(8,128)(2,1)} %refs_0_.1), channel_id=1, source_target_pairs={{0,2},{2,0},{4,6},{6,4},{8,10},{10,8},{12,14},{14,12},{1,3},{3,1},... | collective-permute-start | bytes 4718600 | tf_op jit(solution)/shard_map/ppermute | solution.py:321
  75.5 57.3 %collective-permute-start.1 = (bf16[384,2048]{1,0:T(8,128)(2,1)}, bf16[384,2048]{1,0:T(8,128)(2,1)S(1)}, u32[]{:S(2)}, u32[]{:S(2)}) collective-permute-start(bf16[384,2048]{1,0:T(8,128)(2,1)} %refs_0_.1), channel_id=1, source_target_pairs={{0,1},{1,0},{2,3},{3,2},{4,5},{5,4},{6,7},{7,6},{8,9},{9,8},{10,11... | collective-permute-start | bytes 4718600 | tf_op jit(solution)/shard_map/ppermute | solution.py:327
  75.5 68.6 %collective-permute-start.3 = (bf16[384,2048]{1,0:T(8,128)(2,1)}, bf16[384,2048]{1,0:T(8,128)(2,1)}, u32[]{:S(2)}, u32[]{:S(2)}) collective-permute-start(bf16[384,2048]{1,0:T(8,128)(2,1)} %refs_0_.1), channel_id=1, source_target_pairs={{0,4},{2,6},{4,0},{6,2},{8,12},{10,14},{12,8},{14,10},{1,5},{3,7},... | collective-permute-start | bytes 4718600 | tf_op jit(solution)/shard_map/ppermute | solution.py:321
  133.9 11.8 %collective-permute-start.4 = (bf16[384,2048]{1,0:T(8,128)(2,1)}, bf16[384,2048]{1,0:T(8,128)(2,1)}, u32[]{:S(2)}, u32[]{:S(2)}) collective-permute-start(bf16[384,2048]{1,0:T(8,128)(2,1)} %collective-permute-done.refs_2_), channel_id=1, source_target_pairs={{0,1},{1,0},{2,3},{3,2},{4,5},{5,4},{6,7},{7,6},{8,9},{9,8},{10,11... | collective-permute-start | bytes 4718600 | tf_op jit(solution)/shard_map/ppermute | solution.py:327
  136.7 8.9 %collective-permute-start.5 = (bf16[512,256]{1,0:T(8,128)(2,1)}, bf16[512,256]{1,0:T(8,128)(2,1)S(1)}, u32[]{:S(2)}, u32[]{:S(2)}) collective-permute-start(bf16[512,256]{1,0:T(8,128)(2,1)} %get-tuple-element.94), channel_id=1, source_target_pairs={{0,2},{2,0},{4,6},{6,4},{8,10},{10,8},{12,14},{14,12},{1,3},{3,1},... | collective-permute-start | bytes 786440 | tf_op jit(solution)/shard_map/ppermute | solution.py:321
  145.6 7.6 %collective-permute-start.6 = (bf16[384,2048]{1,0:T(8,128)(2,1)}, bf16[384,2048]{1,0:T(8,128)(2,1)S(1)}, u32[]{:S(2)}, u32[]{:S(2)}) collective-permute-start(bf16[384,2048]{1,0:T(8,128)(2,1)} %collective-permute-done.3.refs_4_), channel_id=1, source_target_pairs={{0,1},{1,0},{2,3},{3,2},{4,5},{5,4},{6,7},{7,6},{8,9},{9,8},{10,11... | collective-permute-start | bytes 4718600 | tf_op jit(solution)/shard_map/ppermute | solution.py:327
  145.6 7.6 %copy-start.2 = (bf16[384,2048]{1,0:T(8,128)(2,1)S(1)}, bf16[384,2048]{1,0:T(8,128)(2,1)}, u32[]{:S(2)}) copy-start(bf16[384,2048]{1,0:T(8,128)(2,1)} %copy-done.1) | copy-start | bytes 4718596
  147.1 28.9 %collective-permute-start.7 = (bf16[384,1408]{1,0:T(8,128)(2,1)S(1)}, bf16[384,1408]{1,0:T(8,128)(2,1)S(1)}, u32[]{:S(2)}, u32[]{:S(2)}) collective-permute-start(bf16[384,1408]{1,0:T(8,128)(2,1)S(1)} %slice.13), channel_id=1, source_target_pairs={{0,2},{2,0},{4,6},{6,4},{8,10},{10,8},{12,14},{14,12},{1,3},{3,1},... | collective-permute-start | bytes 3244040 | tf_op jit(solution)/shard_map/ppermute | solution.py:321
  147.5 28.5 %collective-permute-start.11 = (bf16[2048,256]{1,0:T(8,128)(2,1)S(1)}, bf16[2048,256]{1,0:T(8,128)(2,1)S(1)}, u32[]{:S(2)}, u32[]{:S(2)}) collective-permute-start(bf16[2048,256]{1,0:T(8,128)(2,1)S(1)} %slice.14), channel_id=1, source_target_pairs={{0,16},{16,0},{1,17},{17,1},{2,18},{18,2},{3,19},{19,3},{4,20},{20... | collective-permute-start | bytes 3145736 | tf_op jit(solution)/shard_map/ppermute | solution.py:324
  149.1 26.9 %collective-permute-start.8 = (bf16[384,640]{1,0:T(8,128)(2,1)S(1)}, bf16[384,640]{1,0:T(8,128)(2,1)S(1)}, u32[]{:S(2)}, u32[]{:S(2)}) collective-permute-start(bf16[384,640]{1,0:T(8,128)(2,1)S(1)} %slice.12), channel_id=1, source_target_pairs={{0,4},{2,6},{4,0},{6,2},{8,12},{10,14},{12,8},{14,10},{1,5},{3,7},... | collective-permute-start | bytes 1474568 | tf_op jit(solution)/shard_map/ppermute | solution.py:321
  150.9 20.1 %collective-permute-start.10 = (bf16[512,256]{1,0:T(8,128)(2,1)S(1)}, bf16[512,256]{1,0:T(8,128)(2,1)S(1)}, u32[]{:S(2)}, u32[]{:S(2)}) collective-permute-start(bf16[512,256]{1,0:T(8,128)(2,1)S(1)} %copy-done.8), channel_id=1, source_target_pairs={{0,12},{2,14},{4,8},{6,10},{8,4},{10,6},{12,0},{14,2},{1,13},{3,15... | collective-permute-start | bytes 786440 | tf_op jit(solution)/shard_map/ppermute | solution.py:321
  153.2 22.8 %collective-permute-start.9 = (bf16[512,256]{1,0:T(8,128)(2,1)S(1)}, bf16[512,256]{1,0:T(8,128)(2,1)S(1)}, u32[]{:S(2)}, u32[]{:S(2)}) collective-permute-start(bf16[512,256]{1,0:T(8,128)(2,1)S(1)} %get-tuple-element.99.refs_2_), channel_id=1, source_target_pairs={{0,8},{2,10},{4,12},{6,14},{8,0},{10,2},{12,4},{14,6},{1,9},{3,11}... | collective-permute-start | bytes 786440 | tf_op jit(solution)/shard_map/ppermute | solution.py:321
  159.6 18.8 %copy-start.6 = (bf16[512,256]{1,0:T(8,128)(2,1)S(1)}, bf16[512,256]{1,0:T(8,128)(2,1)}, u32[]{:S(2)}) copy-start(bf16[512,256]{1,0:T(8,128)(2,1)} %copy-done.5) | copy-start | bytes 786436
  176.0 4.8 %collective-permute-start.12 = (bf16[384,1408]{1,0:T(8,128)(2,1)S(1)}, bf16[384,1408]{1,0:T(8,128)(2,1)S(1)}, u32[]{:S(2)}, u32[]{:S(2)}) collective-permute-start(bf16[384,1408]{1,0:T(8,128)(2,1)S(1)} %collective-permute-done.7.refs_0_), channel_id=1, source_target_pairs={{0,1},{1,0},{2,3},{3,2},{4,5},{5,4},{6,7},{7,6},{8,9},{9,8},{10,11... | collective-permute-start | bytes 3244040 | tf_op jit(solution)/shard_map/ppermute | solution.py:327
  176.2 25.6 %collective-permute-start.18 = (bf16[2048,256]{1,0:T(8,128)(2,1)S(1)}, bf16[2048,256]{1,0:T(8,128)(2,1)S(1)}, u32[]{:S(2)}, u32[]{:S(2)}) collective-permute-start(bf16[2048,256]{1,0:T(8,128)(2,1)S(1)} %slice.15), channel_id=1, source_target_pairs={{0,16},{16,0},{1,17},{17,1},{2,18},{18,2},{3,19},{19,3},{4,20},{20... | collective-permute-start | bytes 3145736 | tf_op jit(solution)/shard_map/ppermute | solution.py:324
  176.7 4.7 %collective-permute-start.13 = (bf16[384,640]{1,0:T(8,128)(2,1)S(1)}, bf16[384,640]{1,0:T(8,128)(2,1)S(1)}, u32[]{:S(2)}, u32[]{:S(2)}) collective-permute-start(bf16[384,640]{1,0:T(8,128)(2,1)S(1)} %collective-permute-done.8.refs_2_), channel_id=1, source_target_pairs={{0,1},{1,0},{2,3},{3,2},{4,5},{5,4},{6,7},{7,6},{8,9},{9,8},{10,11... | collective-permute-start | bytes 1474568 | tf_op jit(solution)/shard_map/ppermute | solution.py:327
  176.9 22.1 %collective-permute-start.16 = (bf16[512,256]{1,0:T(8,128)(2,1)}, bf16[512,256]{1,0:T(8,128)(2,1)S(1)}, u32[]{:S(2)}, u32[]{:S(2)}) collective-permute-start(bf16[512,256]{1,0:T(8,128)(2,1)} %get-tuple-element.94), channel_id=1, source_target_pairs={{0,10},{2,8},{4,14},{6,12},{8,2},{10,0},{12,6},{14,4},{1,11},{3,9}... | collective-permute-start | bytes 786440 | tf_op jit(solution)/shard_map/ppermute | solution.py:321
  178.3 20.7 %collective-permute-start.17 = (bf16[512,256]{1,0:T(8,128)(2,1)S(1)}, bf16[512,256]{1,0:T(8,128)(2,1)S(1)}, u32[]{:S(2)}, u32[]{:S(2)}) collective-permute-start(bf16[512,256]{1,0:T(8,128)(2,1)S(1)} %copy-done.6), channel_id=1, source_target_pairs={{0,14},{2,12},{4,10},{6,8},{8,6},{10,4},{12,2},{14,0},{1,15},{3,13... | collective-permute-start | bytes 786440 | tf_op jit(solution)/shard_map/ppermute | solution.py:321
  180.8 21.0 %collective-permute-start.14 = (bf16[512,256]{1,0:T(8,128)(2,1)S(1)}, bf16[512,256]{1,0:T(8,128)(2,1)S(1)}, u32[]{:S(2)}, u32[]{:S(2)}) collective-permute-start(bf16[512,256]{1,0:T(8,128)(2,1)S(1)} %copy-done.8), channel_id=1, source_target_pairs={{0,4},{2,6},{4,0},{6,2},{8,12},{10,14},{12,8},{14,10},{1,5},{3,7},... | collective-permute-start | bytes 786440 | tf_op jit(solution)/shard_map/ppermute | solution.py:321
  181.4 24.3 %collective-permute-start.15 = (bf16[512,256]{1,0:T(8,128)(2,1)S(1)}, bf16[512,256]{1,0:T(8,128)(2,1)S(1)}, u32[]{:S(2)}, u32[]{:S(2)}) collective-permute-start(bf16[512,256]{1,0:T(8,128)(2,1)S(1)} %copy-done.6), channel_id=1, source_target_pairs={{0,6},{2,4},{4,2},{6,0},{8,14},{10,12},{12,10},{14,8},{1,7},{3,5},... | collective-permute-start | bytes 786440 | tf_op jit(solution)/shard_map/ppermute | solution.py:321
  208.4 9.6 %collective-permute-start.19 = (f32[2,128,128]{2,1,0:T(8,128)S(1)}, f32[2,128,128]{2,1,0:T(8,128)S(1)}, u32[]{:S(2)}, u32[]{:S(2)}) collective-permute-start(f32[2,128,128]{2,1,0:T(8,128)S(1)} %get-tuple-element.125), channel_id=1, source_target_pairs={{0,8},{2,10},{4,12},{6,14},{1,9},{3,11},{5,13},{7,15},{16,24},{18,... | collective-permute-start | bytes 393224 | tf_op jit(solution)/shard_map/ppermute | solution.py:301
  219.3 11.3 %collective-permute-start.22 = (bf16[384,256]{1,0:T(8,128)(2,1)S(1)}, bf16[384,256]{1,0:T(8,128)(2,1)S(1)}, u32[]{:S(2)}, u32[]{:S(2)}) collective-permute-start(bf16[384,256]{1,0:T(8,128)(2,1)S(1)} %attend.7), channel_id=1, source_target_pairs={{0,6},{2,4},{4,2},{6,0},{8,14},{10,12},{12,10},{14,8},{1,7},{3,5},... | collective-permute-start | bytes 589832 | tf_op jit(solution)/shard_map/ppermute | solution.py:321
  222.6 7.9 %collective-permute-start.21 = (bf16[384,256]{1,0:T(8,128)(2,1)S(1)}, bf16[384,256]{1,0:T(8,128)(2,1)S(1)}, u32[]{:S(2)}, u32[]{:S(2)}) collective-permute-start(bf16[384,256]{1,0:T(8,128)(2,1)S(1)} %attend.6), channel_id=1, source_target_pairs={{0,4},{2,6},{4,0},{6,2},{8,12},{10,14},{12,8},{14,10},{1,5},{3,7},... | collective-permute-start | bytes 589832 | tf_op jit(solution)/shard_map/ppermute | solution.py:321
  224.1 7.0 %collective-permute-start.20 = (bf16[384,256]{1,0:T(8,128)(2,1)S(1)}, bf16[384,256]{1,0:T(8,128)(2,1)S(1)}, u32[]{:S(2)}, u32[]{:S(2)}) collective-permute-start(bf16[384,256]{1,0:T(8,128)(2,1)S(1)} %attend.5), channel_id=1, source_target_pairs={{0,2},{2,0},{4,6},{6,4},{8,10},{10,8},{12,14},{14,12},{1,3},{3,1},... | collective-permute-start | bytes 589832 | tf_op jit(solution)/shard_map/ppermute | solution.py:321
  231.1 2.8 %collective-permute-start.23 = (bf16[384,256]{1,0:T(8,128)(2,1)S(1)}, bf16[384,256]{1,0:T(8,128)(2,1)S(1)}, u32[]{:S(2)}, u32[]{:S(2)}) collective-permute-start(bf16[384,256]{1,0:T(8,128)(2,1)S(1)} %attend.4.refs_0_), channel_id=1, source_target_pairs={{0,1},{1,0},{2,3},{3,2},{4,5},{5,4},{6,7},{7,6},{8,9},{9,8},{10,11... | collective-permute-start | bytes 589832 | tf_op jit(solution)/shard_map/ppermute | solution.py:327
  231.1 2.8 %collective-permute-start.24 = (bf16[384,256]{1,0:T(8,128)(2,1)S(1)}, bf16[384,256]{1,0:T(8,128)(2,1)S(1)}, u32[]{:S(2)}, u32[]{:S(2)}) collective-permute-start(bf16[384,256]{1,0:T(8,128)(2,1)S(1)} %collective-permute-done.20.refs_1_), channel_id=1, source_target_pairs={{0,1},{1,0},{2,3},{3,2},{4,5},{5,4},{6,7},{7,6},{8,9},{9,8},{10,11... | collective-permute-start | bytes 589832 | tf_op jit(solution)/shard_map/ppermute | solution.py:327
  231.6 2.3 collective-permute-start.25
  231.6 2.3 collective-permute-start.26
  (5 other events, 12.5 us)

commit v13 on v10

--- a/solution.py
+++ b/solution.py
@@ -346,11 +346,14 @@
 
     arrived = {0: q_sent[0]}
     fetch(q_sent, 1)
-    across, kv_mine, beside, far_beside, q_sent, arrived = ob((across, kv_mine, beside, far_beside, q_sent, arrived))
+    beside_cut = beside[:, cut:]
+    across, kv_mine, beside, far_beside, q_sent, arrived, beside_cut = ob(
+        (across, kv_mine, beside, far_beside, q_sent, arrived, beside_cut)
+    )
     middle = kv_mine.shape[0] // 2
     kv_upper = other_part(kv_mine[:middle])
     left = xor(across[:, :cut], 1)
-    right = xor(beside[:, cut:], 2)
+    right = xor(beside_cut, 2)
     fetch(q_sent, 4, 6)
     near = [(tokens, 0, 0, 0), (far_tokens, 0, 0, 1), (beside, 1, 0, 0), (far_beside, 1, 0, 1)]
     near += [(across, 2, 0, 0), (other_core(across), 2, 0, 1)]
@@ -381,10 +384,9 @@
     carried = exclusive_prefix(totals, groups)
     heads = [[first[:3], last[:3]], [second]]
     query = queries(place, streams, q_parts, q_base)
-    away = attend(place, (3, 1, 2), query, heads, carried)
-    home = attend(place, (0,), query, heads, carried)
-    normed = [home[0], xor(away[1], 1), xor(away[2], 2), xor(away[0], 3)]
-    home_0, w_far = lax.optimization_barrier((home[0], w_far))
+    normed = [attend(place, (r,), query, heads, carried)[0] for r in (3, 1, 2, 0)]
+    normed = [normed[3], xor(normed[1], 1), xor(normed[2], 2), xor(normed[0], 3)]
+    home_0, w_far = lax.optimization_barrier((normed[0], w_far))
     out_keep, out_far = stage_rows(place, w_out, w_far)
     out_keep, out_far, *normed = lax.optimization_barrier((out_keep, out_far, home_0, *normed[1:]))
     partial = add_features(normed, out_keep)

time: 177 us -> 176 us (level)
  waiting for transfers between devices: 99.2 us -> 95.1 us
    ppermute x14, waiting for transfers between devices: 96.5 us -> 92.4 us  [xor(): return lax.ppermute(value, 'ctx', [(i, i ^ step) for i in range(n_ctx)])]
    pallas_call x2 -> x4, Pallas kernels: 3.16 us -> 4.74 us  [attend(): call(kernel, 'attend', shapes, specs, [VMEM] * count, LIMIT, flops, 2 * MIB)]
  transfers between devices with their start and end apart: 28 -> 28, of which waited for: 9 -> 9; matrix products, arithmetic and copies ran while one was open for 2% -> 2% of each run, Pallas kernels for 14% -> 16%
where the time goes in v13:
time: 176 us
  waiting for transfers between devices  95.1 us (54%)
  starting transfers between devices  36.1 us (21%)
  Pallas kernels  34.2 us (19%)
  local copies, waits for them, and re-layouts  9.81 us (6%)
    ppermute x14, waiting for transfers between devices, xor(): return lax.ppermute(value, 'ctx', [(i, i ^ step) for i in range(n_ctx)])  92.4 us
    ppermute x14, starting transfers between devices, xor(): return lax.ppermute(value, 'ctx', [(i, i ^ step) for i in range(n_ctx)])  18.5 us
    pallas_call x4, Pallas kernels, run_blocks(): call(body, name, out_shape, specs, outs, LIMIT, flops, 2 * MIB)  9.99 us
    all_to_all x1, starting transfers between devices, spread(): return lax.all_to_all(packed, 'ctx', 0, 0, tiled=True)  6.93 us
    ppermute x1, starting transfers between devices, shift(): return lax.ppermute(v, 'ctx', pairs)  6.76 us
    unnamed x22, local copies, waits for them, and re-layouts  6.36 us
    pallas_call x2, Pallas kernels, add_features(): call(kernel, 'add_features', shape, [VMEM] * len(args), VMEM, LIMIT, flop...  4.74 us
    pallas_call x4, Pallas kernels, attend(): call(kernel, 'attend', shapes, specs, [VMEM] * count, LIMIT, flops, 2 * MIB)  4.74 us
  transfers between devices with their start and end apart: 28, of which 9 were waited for; matrix products, arithmetic and copies ran while one was open for 2% of the time, Pallas kernels for 16%

profile of v13, /device:TPU:0, one launch (start us, length us, event | category | flops | bytes accessed | tf_op | source)
XLA Modules:
  0.0 175.6 jit_solution(6995734841402245016)
XLA Ops:
  3.8 1.3 copy-done
  5.1 6.9 %all-to-all-start = ((bf16[8,512,256]{2,1,0:T(8,128)(2,1)}), bf16[8,512,256]{2,1,0:T(8,128)(2,1)S(1)}, u32[]{:S(2)}, u32[]{:S(2)}) async-start(bf16[8,512,256]{2,1,0:T(8,128)(2,1)} %bitcast.10), calls=%async_computation | async-start | bytes 4194304 | tf_op jit(solution)/shard_map/all_to_all | solution.py:324
  12.1 2.0 %collective-permute-start = (bf16[384,2048]{1,0:T(8,128)(2,1)}, bf16[384,2048]{1,0:T(8,128)(2,1)}, u32[]{:S(2)}, u32[]{:S(2)}) collective-permute-start(bf16[384,2048]{1,0:T(8,128)(2,1)} %refs_0_.1), channel_id=1, source_target_pairs={{0,2},{2,0},{4,6},{6,4},{8,10},{10,8},{12,14},{14,12},{1,3},{3,1},... | collective-permute-start | bytes 4718600 | tf_op jit(solution)/shard_map/ppermute | solution.py:315
  14.1 1.5 collective-permute-start.3
  15.6 55.8 %collective-permute-done.refs_2_ = bf16[384,2048]{1,0:T(8,128)(2,1)} collective-permute-done((bf16[384,2048]{1,0:T(8,128)(2,1)}, bf16[384,2048]{1,0:T(8,128)(2,1)}, u32[]{:S(2)}, u32[]{:S(2)}) %collective-permute-start) | collective-permute-done | bytes 1572896 | tf_op jit(solution)/shard_map/ppermute | solution.py:315
  72.5 1.4 pack_queries.1
  75.6 1.9 %slice.12 = bf16[384,640]{1,0:T(8,128)(2,1)} slice(bf16[384,2048]{1,0:T(8,128)(2,1)} %collective-permute-done.refs_2_), slice={[0:384], [1408:2048]} | slice | bytes 983040 | tf_op jit(solution)/shard_map/slice | solution.py:349
  77.5 5.2 %collective-permute-done.3.refs_4_ = bf16[384,2048]{1,0:T(8,128)(2,1)} collective-permute-done((bf16[384,2048]{1,0:T(8,128)(2,1)}, bf16[384,2048]{1,0:T(8,128)(2,1)}, u32[]{:S(2)}, u32[]{:S(2)}) %collective-permute-start.3) | collective-permute-done | bytes 1572896 | tf_op jit(solution)/shard_map/ppermute | solution.py:315
  82.7 1.6 collective-permute-done.5.refs_3_
  84.3 1.4 slice.13
  86.2 1.6 collective-permute-start.11
  87.8 1.7 collective-permute-start.8
  89.5 2.4 %collective-permute-start.10 = (bf16[512,256]{1,0:T(8,128)(2,1)S(1)}, bf16[512,256]{1,0:T(8,128)(2,1)S(1)}, u32[]{:S(2)}, u32[]{:S(2)}) collective-permute-start(bf16[512,256]{1,0:T(8,128)(2,1)S(1)} %copy-done.10), channel_id=1, source_target_pairs={{0,12},{2,14},{4,8},{6,10},{8,4},{10,6},{12,0},{14,2},{1,13},{3,15... | collective-permute-start | bytes 786440 | tf_op jit(solution)/shard_map/ppermute | solution.py:315
  91.9 3.3 %stage.2.stream_ref.refs_0_ = bf16[3,384,4096]{2,1,0:T(8,128)(2,1)S(1)} custom-call(s32[4]{0:T(128)S(1)} %pad_add_fusion.place_ref, bf16[384,2048]{1,0:T(8,128)(2,1)S(1)} %copy-done.1, bf16[384,2048]{1,0:T(8,128)(2,1)S(1)} %copy-done.3, bf16[384,2048]{1,0:T(8,128)(2,1)} %collective-permute-done.refs_2_, bf16[384,2048]{1,0:T(8,128)(2,1)} %collective-permute-done.4.refs_3_, ...), custom_call_target="tpu_custom_call" | custom-call | bytes 18874368 | tf_op jit(solution)/shard_map/stage/pallas_call | solution.py:117
  95.2 3.0 %project.2 = (bf16[3,384,128]{2,1,0:T(8,128)(2,1)S(1)}, bf16[3,384,128]{2,1,0:T(8,128)(2,1)S(1)}, f32[3,128,128]{2,1,0:T(8,128)S(1)}, f32[128,128]{1,0:T(8,128)S(1)}) custom-call(bf16[3,384,4096]{2,1,0:T(8,128)(2,1)S(1)} %stage.2.stream_ref.refs_0_, bf16[4096,256]{1,0:T(8,128)(2,1)S(1)} %bitcast.7), custom_call_target="tpu_custom_call" | custom-call | flops 2415919104 | bytes 2097152 | tf_op jit(solution)/shard_map/project/pallas_call | solution.py:145
  98.2 11.7 %collective-permute-done.10.refs_5_ = bf16[512,256]{1,0:T(8,128)(2,1)S(1)} collective-permute-done((bf16[512,256]{1,0:T(8,128)(2,1)S(1)}, bf16[512,256]{1,0:T(8,128)(2,1)S(1)}, u32[]{:S(2)}, u32[]{:S(2)}) %collective-permute-start.10) | collective-permute-done | bytes 262176 | tf_op jit(solution)/shard_map/ppermute | solution.py:315
  109.9 4.8 %collective-permute-done.9.refs_4_ = bf16[512,256]{1,0:T(8,128)(2,1)S(1)} collective-permute-done((bf16[512,256]{1,0:T(8,128)(2,1)S(1)}, bf16[512,256]{1,0:T(8,128)(2,1)S(1)}, u32[]{:S(2)}, u32[]{:S(2)}) %collective-permute-start.9) | collective-permute-done | bytes 262176 | tf_op jit(solution)/shard_map/ppermute | solution.py:315
  115.6 1.4 collective-permute-start.16
  117.0 2.4 %collective-permute-start.17 = (bf16[512,256]{1,0:T(8,128)(2,1)S(1)}, bf16[512,256]{1,0:T(8,128)(2,1)S(1)}, u32[]{:S(2)}, u32[]{:S(2)}) collective-permute-start(bf16[512,256]{1,0:T(8,128)(2,1)S(1)} %copy-done.8), channel_id=1, source_target_pairs={{0,14},{2,12},{4,10},{6,8},{8,6},{10,4},{12,2},{14,0},{1,15},{3,13... | collective-permute-start | bytes 786440 | tf_op jit(solution)/shard_map/ppermute | solution.py:315
  120.0 2.1 %collective-permute-start.15 = (bf16[512,256]{1,0:T(8,128)(2,1)S(1)}, bf16[512,256]{1,0:T(8,128)(2,1)S(1)}, u32[]{:S(2)}, u32[]{:S(2)}) collective-permute-start(bf16[512,256]{1,0:T(8,128)(2,1)S(1)} %copy-done.8), channel_id=1, source_target_pairs={{0,6},{2,4},{4,2},{6,0},{8,14},{10,12},{12,10},{14,8},{1,7},{3,5},... | collective-permute-start | bytes 786440 | tf_op jit(solution)/shard_map/ppermute | solution.py:315
  123.1 2.3 %begin.2.refs_3_ = f32[4,384,256]{2,1,0:T(8,128)S(1)} custom-call(s32[4]{0:T(128)S(1)} %pad_add_fusion.place_ref, bf16[3,384,4096]{2,1,0:T(8,128)(2,1)S(1)} %stage.2.stream_ref.refs_0_, bf16[1,384,4096]{2,1,0:T(8,128)(2,1)S(1)} %stage.3.refs_1_.stream_ref, bf16[2048,256]{1,0:T(8,128)(2,1)S(1)} %collective-permute-done.11.refs_2_), custom_call_target="tpu_custom_call" | custom-call | flops 1610612736 | bytes 2097152 | tf_op jit(solution)/shard_map/begin/pallas_call | solution.py:185
  126.7 2.3 %begin.3.refs_6_ = f32[4,384,256]{2,1,0:T(8,128)S(1)} custom-call(s32[4]{0:T(128)S(1)} %pad_add_fusion.place_ref, bf16[3,384,4096]{2,1,0:T(8,128)(2,1)S(1)} %stage.2.stream_ref.refs_0_, bf16[1,384,4096]{2,1,0:T(8,128)(2,1)S(1)} %stage.3.refs_1_.stream_ref, bf16[512,256]{1,0:T(8,128)(2,1)S(1)} %get-tuple-element.99.refs_2_, ...), custom_call_target="tpu_custom_call" | custom-call | flops 1610612736 | bytes 2097152 | tf_op jit(solution)/shard_map/begin/pallas_call | solution.py:185
  129.1 8.6 %collective-permute-done.16.refs_4_ = bf16[512,256]{1,0:T(8,128)(2,1)S(1)} collective-permute-done((bf16[512,256]{1,0:T(8,128)(2,1)}, bf16[512,256]{1,0:T(8,128)(2,1)S(1)}, u32[]{:S(2)}, u32[]{:S(2)}) %collective-permute-start.16) | collective-permute-done | bytes 262176 | tf_op jit(solution)/shard_map/ppermute | solution.py:315
  137.7 2.7 %collective-permute-done.18.refs_2_ = bf16[2048,256]{1,0:T(8,128)(2,1)S(1)} collective-permute-done((bf16[2048,256]{1,0:T(8,128)(2,1)S(1)}, bf16[2048,256]{1,0:T(8,128)(2,1)S(1)}, u32[]{:S(2)}, u32[]{:S(2)}) %collective-permute-start.18) | collective-permute-done | bytes 1048608 | tf_op jit(solution)/shard_map/ppermute | solution.py:318
  140.4 4.1 %collective-permute-done.15.refs_3_ = bf16[512,256]{1,0:T(8,128)(2,1)S(1)} collective-permute-done((bf16[512,256]{1,0:T(8,128)(2,1)S(1)}, bf16[512,256]{1,0:T(8,128)(2,1)S(1)}, u32[]{:S(2)}, u32[]{:S(2)}) %collective-permute-start.15) | collective-permute-done | bytes 262176 | tf_op jit(solution)/shard_map/ppermute | solution.py:315
  144.6 2.7 %keys_values.1 = (bf16[4,384,128]{2,1,0:T(8,128)(2,1)S(1)}, bf16[4,384,128]{2,1,0:T(8,128)(2,1)S(1)}, f32[4,128,128]{2,1,0:T(8,128)S(1)}, f32[2,128,128]{2,1,0:T(8,128)S(1)}) custom-call(s32[4]{0:T(128)S(1)} %pad_add_fusion.place_ref, bf16[3,384,4096]{2,1,0:T(8,128)(2,1)S(1)} %stage.2.stream_ref.refs_0_, bf16[1,384,4096]{2,1,0:T(8,128)(2,1)S(1)} %stage.3.refs_1_.stream_ref, ...), custom_call_target="tpu_custom_call" | custom-call | flops 1610612736 | bytes 2097152 | tf_op jit(solution)/shard_map/keys_values/pallas_call | solution.py:185
  147.3 6.8 %collective-permute-start.19 = (f32[2,128,128]{2,1,0:T(8,128)S(1)}, f32[2,128,128]{2,1,0:T(8,128)S(1)}, u32[]{:S(2)}, u32[]{:S(2)}) collective-permute-start(f32[2,128,128]{2,1,0:T(8,128)S(1)} %get-tuple-element.125), channel_id=1, source_target_pairs={{0,8},{2,10},{4,12},{6,14},{1,9},{3,11},{5,13},{7,15},{16,24},{18,... | collective-permute-start | bytes 393224 | tf_op jit(solution)/shard_map/ppermute | solution.py:295
  154.0 2.6 %queries.1.query_ref = bf16[4,384,256]{2,1,0:T(8,128)(2,1)S(1)} custom-call(s32[4]{0:T(128)S(1)} %pad_add_fusion.place_ref, bf16[3,384,4096]{2,1,0:T(8,128)(2,1)S(1)} %stage.2.stream_ref.refs_0_, bf16[1,384,4096]{2,1,0:T(8,128)(2,1)S(1)} %stage.3.refs_1_.stream_ref, bf16[512,256]{1,0:T(8,128)(2,1)S(1)} %collective-permute-done.14.refs_2_, ...), custom_call_target="tpu_custom_call" | custom-call | flops 1610612736 | bytes 2097152 | tf_op jit(solution)/shard_map/queries/pallas_call | solution.py:185
  157.9 2.3 %collective-permute-start.22 = (bf16[384,256]{1,0:T(8,128)(2,1)S(1)}, bf16[384,256]{1,0:T(8,128)(2,1)S(1)}, u32[]{:S(2)}, u32[]{:S(2)}) collective-permute-start(bf16[384,256]{1,0:T(8,128)(2,1)S(1)} %attend.7), channel_id=1, source_target_pairs={{0,6},{2,4},{4,2},{6,0},{8,14},{10,12},{12,10},{14,8},{1,7},{3,5},... | collective-permute-start | bytes 589832 | tf_op jit(solution)/shard_map/ppermute | solution.py:315
  165.1 4.0 %stage_rows.1 = (bf16[4,256,2048]{2,1,0:T(8,128)(2,1)S(1)}, bf16[4,256,2048]{2,1,0:T(8,128)(2,1)S(1)}) custom-call(s32[4]{0:T(128)S(1)} %pad_add_fusion.place_ref, bf16[1024,4096]{1,0:T(8,128)(2,1)} %out_ref.1, bf16[1024,4096]{1,0:T(8,128)(2,1)} %collective-permute-done.2.far_ref), custom_call_target="tpu_custom_call" | custom-call | bytes 16777216 | tf_op jit(solution)/shard_map/stage_rows/pallas_call | solution.py:89
  170.8 1.8 %add_features.2.refs_5_ = f32[384,2048]{1,0:T(8,128)S(1)} custom-call(bf16[384,256]{1,0:T(8,128)(2,1)S(1)} %attend.4.refs_0_, bf16[384,256]{1,0:T(8,128)(2,1)S(1)} %collective-permute-done.20.refs_1_, bf16[384,256]{1,0:T(8,128)(2,1)S(1)} %collective-permute-done.21.refs_2_, bf16[384,256]{1,0:T(8,128)(2,1)S(1)} %collective-permute-done.22.refs_3_, ...), custom_call_target="tpu_custom_call" | custom-call | flops 1610612736 | bytes 8388608 | tf_op jit(solution)/shard_map/add_features/pallas_call | solution.py:289
  172.6 2.9 %add_features.3 = bf16[384,2048]{1,0:T(8,128)(2,1)} custom-call(bf16[384,256]{1,0:T(8,128)(2,1)S(1)} %collective-permute-done.23.refs_0_, bf16[384,256]{1,0:T(8,128)(2,1)S(1)} %collective-permute-done.24.refs_1_, bf16[384,256]{1,0:T(8,128)(2,1)S(1)} %collective-permute-done.25.refs_2_, bf16[384,256]{1,0:T(8,128)(2,1)S(1)} %collective-permute-done.26.refs_3_, ...), custom_call_target="tpu_custom_call" | custom-call | flops 1610612736 | bytes 8388608 | tf_op jit(solution)/shard_map/add_features/pallas_call | solution.py:289
  (68 shorter events, 18.6 us)
Async XLA Ops:
  0.0 72.5 %collective-permute-start.2 = (bf16[1024,4096]{1,0:T(8,128)(2,1)}, bf16[1024,4096]{1,0:T(8,128)(2,1)}, u32[]{:S(2)}, u32[]{:S(2)}) collective-permute-start(bf16[1024,4096]{1,0:T(8,128)(2,1)} %out_ref.1), channel_id=1, source_target_pairs={{0,1},{1,0},{2,3},{3,2},{4,5},{5,4},{6,7},{7,6},{8,9},{9,8},{10,11... | collective-permute-start | bytes 25165832 | tf_op jit(solution)/shard_map/ppermute | solution.py:321
  5.1 67.4 %copy-start.6 = (bf16[512,1024]{1,0:T(8,128)(2,1)S(1)}, bf16[512,1024]{1,0:T(8,128)(2,1)}, u32[]{:S(2)}) copy-start(bf16[512,1024]{1,0:T(8,128)(2,1)} %query_ref) | copy-start | bytes 3145732
  5.1 77.5 %all-to-all-start = ((bf16[8,512,256]{2,1,0:T(8,128)(2,1)}), bf16[8,512,256]{2,1,0:T(8,128)(2,1)S(1)}, u32[]{:S(2)}, u32[]{:S(2)}) async-start(bf16[8,512,256]{2,1,0:T(8,128)(2,1)} %bitcast.10), calls=%async_computation | async-start | bytes 4194304 | tf_op jit(solution)/shard_map/all_to_all | solution.py:324
  12.1 59.3 %collective-permute-start = (bf16[384,2048]{1,0:T(8,128)(2,1)}, bf16[384,2048]{1,0:T(8,128)(2,1)}, u32[]{:S(2)}, u32[]{:S(2)}) collective-permute-start(bf16[384,2048]{1,0:T(8,128)(2,1)} %refs_0_.1), channel_id=1, source_target_pairs={{0,2},{2,0},{4,6},{6,4},{8,10},{10,8},{12,14},{14,12},{1,3},{3,1},... | collective-permute-start | bytes 4718600 | tf_op jit(solution)/shard_map/ppermute | solution.py:315
  14.1 57.3 %collective-permute-start.1 = (bf16[384,2048]{1,0:T(8,128)(2,1)}, bf16[384,2048]{1,0:T(8,128)(2,1)S(1)}, u32[]{:S(2)}, u32[]{:S(2)}) collective-permute-start(bf16[384,2048]{1,0:T(8,128)(2,1)} %refs_0_.1), channel_id=1, source_target_pairs={{0,1},{1,0},{2,3},{3,2},{4,5},{5,4},{6,7},{7,6},{8,9},{9,8},{10,11... | collective-permute-start | bytes 4718600 | tf_op jit(solution)/shard_map/ppermute | solution.py:321
  14.1 68.6 %collective-permute-start.3 = (bf16[384,2048]{1,0:T(8,128)(2,1)}, bf16[384,2048]{1,0:T(8,128)(2,1)}, u32[]{:S(2)}, u32[]{:S(2)}) collective-permute-start(bf16[384,2048]{1,0:T(8,128)(2,1)} %refs_0_.1), channel_id=1, source_target_pairs={{0,4},{2,6},{4,0},{6,2},{8,12},{10,14},{12,8},{14,10},{1,5},{3,7},... | collective-permute-start | bytes 4718600 | tf_op jit(solution)/shard_map/ppermute | solution.py:315
  72.5 11.7 %collective-permute-start.4 = (bf16[384,2048]{1,0:T(8,128)(2,1)}, bf16[384,2048]{1,0:T(8,128)(2,1)}, u32[]{:S(2)}, u32[]{:S(2)}) collective-permute-start(bf16[384,2048]{1,0:T(8,128)(2,1)} %collective-permute-done.refs_2_), channel_id=1, source_target_pairs={{0,1},{1,0},{2,3},{3,2},{4,5},{5,4},{6,7},{7,6},{8,9},{9,8},{10,11... | collective-permute-start | bytes 4718600 | tf_op jit(solution)/shard_map/ppermute | solution.py:321
  75.3 8.9 %collective-permute-start.5 = (bf16[512,256]{1,0:T(8,128)(2,1)}, bf16[512,256]{1,0:T(8,128)(2,1)S(1)}, u32[]{:S(2)}, u32[]{:S(2)}) collective-permute-start(bf16[512,256]{1,0:T(8,128)(2,1)} %get-tuple-element.94), channel_id=1, source_target_pairs={{0,2},{2,0},{4,6},{6,4},{8,10},{10,8},{12,14},{14,12},{1,3},{3,1},... | collective-permute-start | bytes 786440 | tf_op jit(solution)/shard_map/ppermute | solution.py:315
  84.3 7.6 %collective-permute-start.6 = (bf16[384,2048]{1,0:T(8,128)(2,1)}, bf16[384,2048]{1,0:T(8,128)(2,1)S(1)}, u32[]{:S(2)}, u32[]{:S(2)}) collective-permute-start(bf16[384,2048]{1,0:T(8,128)(2,1)} %collective-permute-done.3.refs_4_), channel_id=1, source_target_pairs={{0,1},{1,0},{2,3},{3,2},{4,5},{5,4},{6,7},{7,6},{8,9},{9,8},{10,11... | collective-permute-start | bytes 4718600 | tf_op jit(solution)/shard_map/ppermute | solution.py:321
  84.3 7.6 %copy-start.3 = (bf16[384,2048]{1,0:T(8,128)(2,1)S(1)}, bf16[384,2048]{1,0:T(8,128)(2,1)}, u32[]{:S(2)}) copy-start(bf16[384,2048]{1,0:T(8,128)(2,1)} %copy-done.2) | copy-start | bytes 4718596
  85.7 6.1 %copy-start.1 = (bf16[384,2048]{1,0:T(8,128)(2,1)S(1)}, bf16[384,2048]{1,0:T(8,128)(2,1)}, u32[]{:S(2)}) copy-start(bf16[384,2048]{1,0:T(8,128)(2,1)} %refs_0_.1) | copy-start | bytes 4718596
  85.7 28.9 %collective-permute-start.7 = (bf16[384,1408]{1,0:T(8,128)(2,1)S(1)}, bf16[384,1408]{1,0:T(8,128)(2,1)S(1)}, u32[]{:S(2)}, u32[]{:S(2)}) collective-permute-start(bf16[384,1408]{1,0:T(8,128)(2,1)S(1)} %slice.13), channel_id=1, source_target_pairs={{0,2},{2,0},{4,6},{6,4},{8,10},{10,8},{12,14},{14,12},{1,3},{3,1},... | collective-permute-start | bytes 3244040 | tf_op jit(solution)/shard_map/ppermute | solution.py:315
  86.2 28.5 %collective-permute-start.11 = (bf16[2048,256]{1,0:T(8,128)(2,1)S(1)}, bf16[2048,256]{1,0:T(8,128)(2,1)S(1)}, u32[]{:S(2)}, u32[]{:S(2)}) collective-permute-start(bf16[2048,256]{1,0:T(8,128)(2,1)S(1)} %slice.14), channel_id=1, source_target_pairs={{0,16},{16,0},{1,17},{17,1},{2,18},{18,2},{3,19},{19,3},{4,20},{20... | collective-permute-start | bytes 3145736 | tf_op jit(solution)/shard_map/ppermute | solution.py:318
  87.8 26.9 %collective-permute-start.8 = (bf16[384,640]{1,0:T(8,128)(2,1)}, bf16[384,640]{1,0:T(8,128)(2,1)S(1)}, u32[]{:S(2)}, u32[]{:S(2)}) collective-permute-start(bf16[384,640]{1,0:T(8,128)(2,1)} %slice.12), channel_id=1, source_target_pairs={{0,4},{2,6},{4,0},{6,2},{8,12},{10,14},{12,8},{14,10},{1,5},{3,7},... | collective-permute-start | bytes 1474568 | tf_op jit(solution)/shard_map/ppermute | solution.py:315
  89.5 20.4 %collective-permute-start.10 = (bf16[512,256]{1,0:T(8,128)(2,1)S(1)}, bf16[512,256]{1,0:T(8,128)(2,1)S(1)}, u32[]{:S(2)}, u32[]{:S(2)}) collective-permute-start(bf16[512,256]{1,0:T(8,128)(2,1)S(1)} %copy-done.10), channel_id=1, source_target_pairs={{0,12},{2,14},{4,8},{6,10},{8,4},{10,6},{12,0},{14,2},{1,13},{3,15... | collective-permute-start | bytes 786440 | tf_op jit(solution)/shard_map/ppermute | solution.py:315
  91.9 22.8 %collective-permute-start.9 = (bf16[512,256]{1,0:T(8,128)(2,1)S(1)}, bf16[512,256]{1,0:T(8,128)(2,1)S(1)}, u32[]{:S(2)}, u32[]{:S(2)}) collective-permute-start(bf16[512,256]{1,0:T(8,128)(2,1)S(1)} %get-tuple-element.99.refs_2_), channel_id=1, source_target_pairs={{0,8},{2,10},{4,12},{6,14},{8,0},{10,2},{12,4},{14,6},{1,9},{3,11}... | collective-permute-start | bytes 786440 | tf_op jit(solution)/shard_map/ppermute | solution.py:315
  98.2 18.8 %copy-start.8 = (bf16[512,256]{1,0:T(8,128)(2,1)S(1)}, bf16[512,256]{1,0:T(8,128)(2,1)}, u32[]{:S(2)}) copy-start(bf16[512,256]{1,0:T(8,128)(2,1)} %copy-done.7) | copy-start | bytes 786436
  114.6 4.8 %collective-permute-start.12 = (bf16[384,1408]{1,0:T(8,128)(2,1)S(1)}, bf16[384,1408]{1,0:T(8,128)(2,1)S(1)}, u32[]{:S(2)}, u32[]{:S(2)}) collective-permute-start(bf16[384,1408]{1,0:T(8,128)(2,1)S(1)} %collective-permute-done.7.refs_0_), channel_id=1, source_target_pairs={{0,1},{1,0},{2,3},{3,2},{4,5},{5,4},{6,7},{7,6},{8,9},{9,8},{10,11... | collective-permute-start | bytes 3244040 | tf_op jit(solution)/shard_map/ppermute | solution.py:321
  114.8 25.6 %collective-permute-start.18 = (bf16[2048,256]{1,0:T(8,128)(2,1)S(1)}, bf16[2048,256]{1,0:T(8,128)(2,1)S(1)}, u32[]{:S(2)}, u32[]{:S(2)}) collective-permute-start(bf16[2048,256]{1,0:T(8,128)(2,1)S(1)} %slice.15), channel_id=1, source_target_pairs={{0,16},{16,0},{1,17},{17,1},{2,18},{18,2},{3,19},{19,3},{4,20},{20... | collective-permute-start | bytes 3145736 | tf_op jit(solution)/shard_map/ppermute | solution.py:318
  115.4 4.7 %collective-permute-start.13 = (bf16[384,640]{1,0:T(8,128)(2,1)S(1)}, bf16[384,640]{1,0:T(8,128)(2,1)S(1)}, u32[]{:S(2)}, u32[]{:S(2)}) collective-permute-start(bf16[384,640]{1,0:T(8,128)(2,1)S(1)} %collective-permute-done.8.refs_2_), channel_id=1, source_target_pairs={{0,1},{1,0},{2,3},{3,2},{4,5},{5,4},{6,7},{7,6},{8,9},{9,8},{10,11... | collective-permute-start | bytes 1474568 | tf_op jit(solution)/shard_map/ppermute | solution.py:321
  115.6 22.1 %collective-permute-start.16 = (bf16[512,256]{1,0:T(8,128)(2,1)}, bf16[512,256]{1,0:T(8,128)(2,1)S(1)}, u32[]{:S(2)}, u32[]{:S(2)}) collective-permute-start(bf16[512,256]{1,0:T(8,128)(2,1)} %get-tuple-element.94), channel_id=1, source_target_pairs={{0,10},{2,8},{4,14},{6,12},{8,2},{10,0},{12,6},{14,4},{1,11},{3,9}... | collective-permute-start | bytes 786440 | tf_op jit(solution)/shard_map/ppermute | solution.py:315
  117.0 20.7 %collective-permute-start.17 = (bf16[512,256]{1,0:T(8,128)(2,1)S(1)}, bf16[512,256]{1,0:T(8,128)(2,1)S(1)}, u32[]{:S(2)}, u32[]{:S(2)}) collective-permute-start(bf16[512,256]{1,0:T(8,128)(2,1)S(1)} %copy-done.8), channel_id=1, source_target_pairs={{0,14},{2,12},{4,10},{6,8},{8,6},{10,4},{12,2},{14,0},{1,15},{3,13... | collective-permute-start | bytes 786440 | tf_op jit(solution)/shard_map/ppermute | solution.py:315
  119.4 21.0 %collective-permute-start.14 = (bf16[512,256]{1,0:T(8,128)(2,1)S(1)}, bf16[512,256]{1,0:T(8,128)(2,1)S(1)}, u32[]{:S(2)}, u32[]{:S(2)}) collective-permute-start(bf16[512,256]{1,0:T(8,128)(2,1)S(1)} %copy-done.10), channel_id=1, source_target_pairs={{0,4},{2,6},{4,0},{6,2},{8,12},{10,14},{12,8},{14,10},{1,5},{3,7},... | collective-permute-start | bytes 786440 | tf_op jit(solution)/shard_map/ppermute | solution.py:315
  120.0 24.5 %collective-permute-start.15 = (bf16[512,256]{1,0:T(8,128)(2,1)S(1)}, bf16[512,256]{1,0:T(8,128)(2,1)S(1)}, u32[]{:S(2)}, u32[]{:S(2)}) collective-permute-start(bf16[512,256]{1,0:T(8,128)(2,1)S(1)} %copy-done.8), channel_id=1, source_target_pairs={{0,6},{2,4},{4,2},{6,0},{8,14},{10,12},{12,10},{14,8},{1,7},{3,5},... | collective-permute-start | bytes 786440 | tf_op jit(solution)/shard_map/ppermute | solution.py:315
  147.3 9.4 %collective-permute-start.19 = (f32[2,128,128]{2,1,0:T(8,128)S(1)}, f32[2,128,128]{2,1,0:T(8,128)S(1)}, u32[]{:S(2)}, u32[]{:S(2)}) collective-permute-start(f32[2,128,128]{2,1,0:T(8,128)S(1)} %get-tuple-element.125), channel_id=1, source_target_pairs={{0,8},{2,10},{4,12},{6,14},{1,9},{3,11},{5,13},{7,15},{16,24},{18,... | collective-permute-start | bytes 393224 | tf_op jit(solution)/shard_map/ppermute | solution.py:295
  157.9 11.3 %collective-permute-start.22 = (bf16[384,256]{1,0:T(8,128)(2,1)S(1)}, bf16[384,256]{1,0:T(8,128)(2,1)S(1)}, u32[]{:S(2)}, u32[]{:S(2)}) collective-permute-start(bf16[384,256]{1,0:T(8,128)(2,1)S(1)} %attend.7), channel_id=1, source_target_pairs={{0,6},{2,4},{4,2},{6,0},{8,14},{10,12},{12,10},{14,8},{1,7},{3,5},... | collective-permute-start | bytes 589832 | tf_op jit(solution)/shard_map/ppermute | solution.py:315
  161.4 7.8 %collective-permute-start.21 = (bf16[384,256]{1,0:T(8,128)(2,1)S(1)}, bf16[384,256]{1,0:T(8,128)(2,1)S(1)}, u32[]{:S(2)}, u32[]{:S(2)}) collective-permute-start(bf16[384,256]{1,0:T(8,128)(2,1)S(1)} %attend.6), channel_id=1, source_target_pairs={{0,4},{2,6},{4,0},{6,2},{8,12},{10,14},{12,8},{14,10},{1,5},{3,7},... | collective-permute-start | bytes 589832 | tf_op jit(solution)/shard_map/ppermute | solution.py:315
  162.8 6.9 %collective-permute-start.20 = (bf16[384,256]{1,0:T(8,128)(2,1)S(1)}, bf16[384,256]{1,0:T(8,128)(2,1)S(1)}, u32[]{:S(2)}, u32[]{:S(2)}) collective-permute-start(bf16[384,256]{1,0:T(8,128)(2,1)S(1)} %attend.5), channel_id=1, source_target_pairs={{0,2},{2,0},{4,6},{6,4},{8,10},{10,8},{12,14},{14,12},{1,3},{3,1},... | collective-permute-start | bytes 589832 | tf_op jit(solution)/shard_map/ppermute | solution.py:315
  169.7 2.8 %collective-permute-start.23 = (bf16[384,256]{1,0:T(8,128)(2,1)S(1)}, bf16[384,256]{1,0:T(8,128)(2,1)S(1)}, u32[]{:S(2)}, u32[]{:S(2)}) collective-permute-start(bf16[384,256]{1,0:T(8,128)(2,1)S(1)} %attend.4.refs_0_), channel_id=1, source_target_pairs={{0,1},{1,0},{2,3},{3,2},{4,5},{5,4},{6,7},{7,6},{8,9},{9,8},{10,11... | collective-permute-start | bytes 589832 | tf_op jit(solution)/shard_map/ppermute | solution.py:321
  169.7 2.8 %collective-permute-start.24 = (bf16[384,256]{1,0:T(8,128)(2,1)S(1)}, bf16[384,256]{1,0:T(8,128)(2,1)S(1)}, u32[]{:S(2)}, u32[]{:S(2)}) collective-permute-start(bf16[384,256]{1,0:T(8,128)(2,1)S(1)} %collective-permute-done.20.refs_1_), channel_id=1, source_target_pairs={{0,1},{1,0},{2,3},{3,2},{4,5},{5,4},{6,7},{7,6},{8,9},{9,8},{10,11... | collective-permute-start | bytes 589832 | tf_op jit(solution)/shard_map/ppermute | solution.py:321
  170.3 2.3 %collective-permute-start.25 = (bf16[384,256]{1,0:T(8,128)(2,1)S(1)}, bf16[384,256]{1,0:T(8,128)(2,1)S(1)}, u32[]{:S(2)}, u32[]{:S(2)}) collective-permute-start(bf16[384,256]{1,0:T(8,128)(2,1)S(1)} %collective-permute-done.21.refs_2_), channel_id=1, source_target_pairs={{0,1},{1,0},{2,3},{3,2},{4,5},{5,4},{6,7},{7,6},{8,9},{9,8},{10,11... | collective-permute-start | bytes 589832 | tf_op jit(solution)/shard_map/ppermute | solution.py:321
  170.3 2.4 %collective-permute-start.26 = (bf16[384,256]{1,0:T(8,128)(2,1)S(1)}, bf16[384,256]{1,0:T(8,128)(2,1)S(1)}, u32[]{:S(2)}, u32[]{:S(2)}) collective-permute-start(bf16[384,256]{1,0:T(8,128)(2,1)S(1)} %collective-permute-done.22.refs_3_), channel_id=1, source_target_pairs={{0,1},{1,0},{2,3},{3,2},{4,5},{5,4},{6,7},{7,6},{8,9},{9,8},{10,11... | collective-permute-start | bytes 589832 | tf_op jit(solution)/shard_map/ppermute | solution.py:321
  (7 other events, 10.1 us)

commit v14 on v13

--- a/solution.py
+++ b/solution.py
@@ -185,13 +185,13 @@
     return call(body, name, out_shape, specs, outs, LIMIT, flops, 2 * MIB)(place, *args)
 
 
-def begin(place, streams, parts):
+def begin(place, streams, parts, base=None):
     def kernel(place_ref, sums, out):
         for i, total in sums():
             out[i] = total
 
     shape = pltpu.VMEM((SUB, streams[0].shape[1], 2 * HDIM), F32)
-    return run_blocks(kernel, "begin", place, streams, parts, None, shape)
+    return run_blocks(kernel, "begin", place, streams, parts, base, shape)
 
 
 def keys_values(place, streams, parts, base, total):
@@ -376,8 +376,10 @@
     if pieced:
         early = (0, 1, 4, 6)
         q_base = begin(place, streams, [(arrived[m], (m,)) for m in early])
+        latest = arrived.pop(7)
         arrived, kv_lower, kv_base, q_base = ob((arrived, kv_lower, kv_base, q_base))
-        q_parts = [(arrived[m], (m,)) for m in range(n_ctx) if m not in early]
+        q_base = begin(place, streams, [(arrived[m], (m,)) for m in sorted(arrived) if m not in early], q_base)
+        q_parts = [(latest, (7,))]
     else:
         q_base, q_parts = None, [(gather_queries(q_sent), 0)]
     *second, totals = keys_values(place, streams, [(kv_lower, middle)], kv_base, last[3])

time: 176 us -> 176 us (level)
    pallas_call x4 -> x5, Pallas kernels: 9.99 us -> 10.7 us  [run_blocks(): call(body, name, out_shape, specs, outs, LIMIT, flops, 2 * MIB)]
  transfers between devices with their start and end apart: 28 -> 28, of which waited for: 9 -> 8; matrix products, arithmetic and copies ran while one was open for 2% -> 2% of each run, Pallas kernels for 16% -> 17%
where the time goes in v14:
time: 176 us
  waiting for transfers between devices  94.6 us (54%)
  starting transfers between devices  36.1 us (21%)
  Pallas kernels  34.9 us (20%)
  local copies, waits for them, and re-layouts  9.81 us (6%)
    ppermute x14, waiting for transfers between devices, xor(): return lax.ppermute(value, 'ctx', [(i, i ^ step) for i in range(n_ctx)])  91.8 us
    ppermute x14, starting transfers between devices, xor(): return lax.ppermute(value, 'ctx', [(i, i ^ step) for i in range(n_ctx)])  18.5 us
    pallas_call x5, Pallas kernels, run_blocks(): call(body, name, out_shape, specs, outs, LIMIT, flops, 2 * MIB)  10.7 us
    all_to_all x1, starting transfers between devices, spread(): return lax.all_to_all(packed, 'ctx', 0, 0, tiled=True)  6.93 us
    ppermute x1, starting transfers between devices, shift(): return lax.ppermute(v, 'ctx', pairs)  6.76 us
    unnamed x22, local copies, waits for them, and re-layouts  6.36 us
    pallas_call x4, Pallas kernels, attend(): call(kernel, 'attend', shapes, specs, [VMEM] * count, LIMIT, flops, 2 * MIB)  4.74 us
    pallas_call x2, Pallas kernels, add_features(): call(kernel, 'add_features', shape, [VMEM] * len(args), VMEM, LIMIT, flop...  4.74 us
  transfers between devices with their start and end apart: 28, of which 8 were waited for; matrix products, arithmetic and copies ran while one was open for 2% of the time, Pallas kernels for 17%

profile of v14, /device:TPU:0, one launch (start us, length us, event | category | flops | bytes accessed | tf_op | source)
XLA Modules:
  0.0 175.8 jit_solution(6209673874140430847)
XLA Ops:
  5.1 6.9 %all-to-all-start = ((bf16[8,512,256]{2,1,0:T(8,128)(2,1)}), bf16[8,512,256]{2,1,0:T(8,128)(2,1)S(1)}, u32[]{:S(2)}, u32[]{:S(2)}) async-start(bf16[8,512,256]{2,1,0:T(8,128)(2,1)} %bitcast.10), calls=%async_computation | async-start | bytes 4194304 | tf_op jit(solution)/shard_map/all_to_all | solution.py:324
  12.1 2.0 %collective-permute-start = (bf16[384,2048]{1,0:T(8,128)(2,1)}, bf16[384,2048]{1,0:T(8,128)(2,1)}, u32[]{:S(2)}, u32[]{:S(2)}) collective-permute-start(bf16[384,2048]{1,0:T(8,128)(2,1)} %refs_0_.1), channel_id=1, source_target_pairs={{0,2},{2,0},{4,6},{6,4},{8,10},{10,8},{12,14},{14,12},{1,3},{3,1},... | collective-permute-start | bytes 4718600 | tf_op jit(solution)/shard_map/ppermute | solution.py:315
  14.1 1.5 collective-permute-start.3
  15.6 55.8 %collective-permute-done.refs_2_ = bf16[384,2048]{1,0:T(8,128)(2,1)} collective-permute-done((bf16[384,2048]{1,0:T(8,128)(2,1)}, bf16[384,2048]{1,0:T(8,128)(2,1)}, u32[]{:S(2)}, u32[]{:S(2)}) %collective-permute-start) | collective-permute-done | bytes 1572896 | tf_op jit(solution)/shard_map/ppermute | solution.py:315
  72.5 1.4 pack_queries.1
  75.6 1.9 %slice.12 = bf16[384,640]{1,0:T(8,128)(2,1)} slice(bf16[384,2048]{1,0:T(8,128)(2,1)} %collective-permute-done.refs_2_), slice={[0:384], [1408:2048]} | slice | bytes 983040 | tf_op jit(solution)/shard_map/slice | solution.py:349
  77.5 5.2 %collective-permute-done.3.refs_4_ = bf16[384,2048]{1,0:T(8,128)(2,1)} collective-permute-done((bf16[384,2048]{1,0:T(8,128)(2,1)}, bf16[384,2048]{1,0:T(8,128)(2,1)}, u32[]{:S(2)}, u32[]{:S(2)}) %collective-permute-start.3) | collective-permute-done | bytes 1572896 | tf_op jit(solution)/shard_map/ppermute | solution.py:315
  82.7 1.6 collective-permute-done.5.refs_3_
  84.3 1.4 slice.13
  86.2 1.6 collective-permute-start.11
  87.8 1.7 collective-permute-start.8
  89.5 2.4 %collective-permute-start.10 = (bf16[512,256]{1,0:T(8,128)(2,1)S(1)}, bf16[512,256]{1,0:T(8,128)(2,1)S(1)}, u32[]{:S(2)}, u32[]{:S(2)}) collective-permute-start(bf16[512,256]{1,0:T(8,128)(2,1)S(1)} %copy-done.10), channel_id=1, source_target_pairs={{0,12},{2,14},{4,8},{6,10},{8,4},{10,6},{12,0},{14,2},{1,13},{3,15... | collective-permute-start | bytes 786440 | tf_op jit(solution)/shard_map/ppermute | solution.py:315
  91.9 3.3 %stage.2.stream_ref.refs_0_ = bf16[3,384,4096]{2,1,0:T(8,128)(2,1)S(1)} custom-call(s32[4]{0:T(128)S(1)} %pad_add_fusion.place_ref, bf16[384,2048]{1,0:T(8,128)(2,1)S(1)} %copy-done.1, bf16[384,2048]{1,0:T(8,128)(2,1)S(1)} %copy-done.3, bf16[384,2048]{1,0:T(8,128)(2,1)} %collective-permute-done.refs_2_, bf16[384,2048]{1,0:T(8,128)(2,1)} %collective-permute-done.4.refs_3_, ...), custom_call_target="tpu_custom_call" | custom-call | bytes 18874368 | tf_op jit(solution)/shard_map/stage/pallas_call | solution.py:117
  95.2 3.0 %project.2 = (bf16[3,384,128]{2,1,0:T(8,128)(2,1)S(1)}, bf16[3,384,128]{2,1,0:T(8,128)(2,1)S(1)}, f32[3,128,128]{2,1,0:T(8,128)S(1)}, f32[128,128]{1,0:T(8,128)S(1)}) custom-call(bf16[3,384,4096]{2,1,0:T(8,128)(2,1)S(1)} %stage.2.stream_ref.refs_0_, bf16[4096,256]{1,0:T(8,128)(2,1)S(1)} %bitcast.7), custom_call_target="tpu_custom_call" | custom-call | flops 2415919104 | bytes 2097152 | tf_op jit(solution)/shard_map/project/pallas_call | solution.py:145
  98.2 11.7 %collective-permute-done.10.refs_5_ = bf16[512,256]{1,0:T(8,128)(2,1)S(1)} collective-permute-done((bf16[512,256]{1,0:T(8,128)(2,1)S(1)}, bf16[512,256]{1,0:T(8,128)(2,1)S(1)}, u32[]{:S(2)}, u32[]{:S(2)}) %collective-permute-start.10) | collective-permute-done | bytes 262176 | tf_op jit(solution)/shard_map/ppermute | solution.py:315
  109.9 4.8 %collective-permute-done.9.refs_4_ = bf16[512,256]{1,0:T(8,128)(2,1)S(1)} collective-permute-done((bf16[512,256]{1,0:T(8,128)(2,1)S(1)}, bf16[512,256]{1,0:T(8,128)(2,1)S(1)}, u32[]{:S(2)}, u32[]{:S(2)}) %collective-permute-start.9) | collective-permute-done | bytes 262176 | tf_op jit(solution)/shard_map/ppermute | solution.py:315
  115.6 1.4 collective-permute-start.17
  117.0 2.4 %collective-permute-start.14 = (bf16[512,256]{1,0:T(8,128)(2,1)S(1)}, bf16[512,256]{1,0:T(8,128)(2,1)S(1)}, u32[]{:S(2)}, u32[]{:S(2)}) collective-permute-start(bf16[512,256]{1,0:T(8,128)(2,1)S(1)} %copy-done.8), channel_id=1, source_target_pairs={{0,14},{2,12},{4,10},{6,8},{8,6},{10,4},{12,2},{14,0},{1,15},{3,13... | collective-permute-start | bytes 786440 | tf_op jit(solution)/shard_map/ppermute | solution.py:315
  120.0 2.1 %collective-permute-start.16 = (bf16[512,256]{1,0:T(8,128)(2,1)S(1)}, bf16[512,256]{1,0:T(8,128)(2,1)S(1)}, u32[]{:S(2)}, u32[]{:S(2)}) collective-permute-start(bf16[512,256]{1,0:T(8,128)(2,1)S(1)} %copy-done.8), channel_id=1, source_target_pairs={{0,6},{2,4},{4,2},{6,0},{8,14},{10,12},{12,10},{14,8},{1,7},{3,5},... | collective-permute-start | bytes 786440 | tf_op jit(solution)/shard_map/ppermute | solution.py:315
  123.1 2.3 %begin.3.refs_3_ = f32[4,384,256]{2,1,0:T(8,128)S(1)} custom-call(s32[4]{0:T(128)S(1)} %pad_add_fusion.place_ref, bf16[3,384,4096]{2,1,0:T(8,128)(2,1)S(1)} %stage.2.stream_ref.refs_0_, bf16[1,384,4096]{2,1,0:T(8,128)(2,1)S(1)} %stage.3.refs_1_.stream_ref, bf16[2048,256]{1,0:T(8,128)(2,1)S(1)} %collective-permute-done.11.refs_2_), custom_call_target="tpu_custom_call" | custom-call | flops 1610612736 | bytes 2097152 | tf_op jit(solution)/shard_map/begin/pallas_call | solution.py:185
  126.7 2.3 %begin.4.refs_5_ = f32[4,384,256]{2,1,0:T(8,128)S(1)} custom-call(s32[4]{0:T(128)S(1)} %pad_add_fusion.place_ref, bf16[3,384,4096]{2,1,0:T(8,128)(2,1)S(1)} %stage.2.stream_ref.refs_0_, bf16[1,384,4096]{2,1,0:T(8,128)(2,1)S(1)} %stage.3.refs_1_.stream_ref, bf16[512,256]{1,0:T(8,128)(2,1)S(1)} %get-tuple-element.98.refs_2_, ...), custom_call_target="tpu_custom_call" | custom-call | flops 1610612736 | bytes 2097152 | tf_op jit(solution)/shard_map/begin/pallas_call | solution.py:185
  129.0 8.6 %collective-permute-done.17.refs_4_ = bf16[512,256]{1,0:T(8,128)(2,1)S(1)} collective-permute-done((bf16[512,256]{1,0:T(8,128)(2,1)}, bf16[512,256]{1,0:T(8,128)(2,1)S(1)}, u32[]{:S(2)}, u32[]{:S(2)}) %collective-permute-start.17) | collective-permute-done | bytes 262176 | tf_op jit(solution)/shard_map/ppermute | solution.py:315
  137.7 2.7 %collective-permute-done.18.refs_2_ = bf16[2048,256]{1,0:T(8,128)(2,1)S(1)} collective-permute-done((bf16[2048,256]{1,0:T(8,128)(2,1)S(1)}, bf16[2048,256]{1,0:T(8,128)(2,1)S(1)}, u32[]{:S(2)}, u32[]{:S(2)}) %collective-permute-start.18) | collective-permute-done | bytes 1048608 | tf_op jit(solution)/shard_map/ppermute | solution.py:318
  140.4 4.1 %collective-permute-done.16.refs_3_ = bf16[512,256]{1,0:T(8,128)(2,1)S(1)} collective-permute-done((bf16[512,256]{1,0:T(8,128)(2,1)S(1)}, bf16[512,256]{1,0:T(8,128)(2,1)S(1)}, u32[]{:S(2)}, u32[]{:S(2)}) %collective-permute-start.16) | collective-permute-done | bytes 262176 | tf_op jit(solution)/shard_map/ppermute | solution.py:315
  144.6 2.7 %keys_values.1 = (bf16[4,384,128]{2,1,0:T(8,128)(2,1)S(1)}, bf16[4,384,128]{2,1,0:T(8,128)(2,1)S(1)}, f32[4,128,128]{2,1,0:T(8,128)S(1)}, f32[2,128,128]{2,1,0:T(8,128)S(1)}) custom-call(s32[4]{0:T(128)S(1)} %pad_add_fusion.place_ref, bf16[3,384,4096]{2,1,0:T(8,128)(2,1)S(1)} %stage.2.stream_ref.refs_0_, bf16[1,384,4096]{2,1,0:T(8,128)(2,1)S(1)} %stage.3.refs_1_.stream_ref, ...), custom_call_target="tpu_custom_call" | custom-call | flops 1610612736 | bytes 2097152 | tf_op jit(solution)/shard_map/keys_values/pallas_call | solution.py:185
  147.3 6.8 %collective-permute-start.19 = (f32[2,128,128]{2,1,0:T(8,128)S(1)}, f32[2,128,128]{2,1,0:T(8,128)S(1)}, u32[]{:S(2)}, u32[]{:S(2)}) collective-permute-start(f32[2,128,128]{2,1,0:T(8,128)S(1)} %get-tuple-element.123), channel_id=1, source_target_pairs={{0,8},{2,10},{4,12},{6,14},{1,9},{3,11},{5,13},{7,15},{16,24},{18,... | collective-permute-start | bytes 393224 | tf_op jit(solution)/shard_map/ppermute | solution.py:295
  154.0 1.9 %begin.5.refs_3_ = f32[4,384,256]{2,1,0:T(8,128)S(1)} custom-call(s32[4]{0:T(128)S(1)} %pad_add_fusion.place_ref, bf16[3,384,4096]{2,1,0:T(8,128)(2,1)S(1)} %stage.2.stream_ref.refs_0_, bf16[1,384,4096]{2,1,0:T(8,128)(2,1)S(1)} %stage.3.refs_1_.stream_ref, bf16[512,256]{1,0:T(8,128)(2,1)S(1)} %collective-permute-done.15.refs_2_, ...), custom_call_target="tpu_custom_call" | custom-call | flops 1207959552 | bytes 2097152 | tf_op jit(solution)/shard_map/begin/pallas_call | solution.py:185
  156.0 1.4 queries.1.query_ref
  159.9 2.4 %collective-permute-start.21 = (bf16[384,256]{1,0:T(8,128)(2,1)S(1)}, bf16[384,256]{1,0:T(8,128)(2,1)S(1)}, u32[]{:S(2)}, u32[]{:S(2)}) collective-permute-start(bf16[384,256]{1,0:T(8,128)(2,1)S(1)} %attend.6), channel_id=1, source_target_pairs={{0,4},{2,6},{4,0},{6,2},{8,12},{10,14},{12,8},{14,10},{1,5},{3,7},... | collective-permute-start | bytes 589832 | tf_op jit(solution)/shard_map/ppermute | solution.py:315
  165.9 4.0 %stage_rows.1 = (bf16[4,256,2048]{2,1,0:T(8,128)(2,1)S(1)}, bf16[4,256,2048]{2,1,0:T(8,128)(2,1)S(1)}) custom-call(s32[4]{0:T(128)S(1)} %pad_add_fusion.place_ref, bf16[1024,4096]{1,0:T(8,128)(2,1)} %out_ref.1, bf16[1024,4096]{1,0:T(8,128)(2,1)} %collective-permute-done.2.far_ref), custom_call_target="tpu_custom_call" | custom-call | bytes 16777216 | tf_op jit(solution)/shard_map/stage_rows/pallas_call | solution.py:89
  171.0 1.8 %add_features.2.refs_5_ = f32[384,2048]{1,0:T(8,128)S(1)} custom-call(bf16[384,256]{1,0:T(8,128)(2,1)S(1)} %attend.4.refs_0_, bf16[384,256]{1,0:T(8,128)(2,1)S(1)} %collective-permute-done.20.refs_1_, bf16[384,256]{1,0:T(8,128)(2,1)S(1)} %collective-permute-done.21.refs_2_, bf16[384,256]{1,0:T(8,128)(2,1)S(1)} %collective-permute-done.22.refs_3_, ...), custom_call_target="tpu_custom_call" | custom-call | flops 1610612736 | bytes 8388608 | tf_op jit(solution)/shard_map/add_features/pallas_call | solution.py:289
  172.9 2.9 %add_features.3 = bf16[384,2048]{1,0:T(8,128)(2,1)} custom-call(bf16[384,256]{1,0:T(8,128)(2,1)S(1)} %collective-permute-done.23.refs_0_, bf16[384,256]{1,0:T(8,128)(2,1)S(1)} %collective-permute-done.24.refs_1_, bf16[384,256]{1,0:T(8,128)(2,1)S(1)} %collective-permute-done.25.refs_2_, bf16[384,256]{1,0:T(8,128)(2,1)S(1)} %collective-permute-done.26.refs_3_, ...), custom_call_target="tpu_custom_call" | custom-call | flops 1610612736 | bytes 8388608 | tf_op jit(solution)/shard_map/add_features/pallas_call | solution.py:289
  (69 shorter events, 19.3 us)
Async XLA Ops:
  0.0 72.5 %collective-permute-start.2 = (bf16[1024,4096]{1,0:T(8,128)(2,1)}, bf16[1024,4096]{1,0:T(8,128)(2,1)}, u32[]{:S(2)}, u32[]{:S(2)}) collective-permute-start(bf16[1024,4096]{1,0:T(8,128)(2,1)} %out_ref.1), channel_id=1, source_target_pairs={{0,1},{1,0},{2,3},{3,2},{4,5},{5,4},{6,7},{7,6},{8,9},{9,8},{10,11... | collective-permute-start | bytes 25165832 | tf_op jit(solution)/shard_map/ppermute | solution.py:321
  5.1 67.4 %copy-start.6 = (bf16[512,1024]{1,0:T(8,128)(2,1)S(1)}, bf16[512,1024]{1,0:T(8,128)(2,1)}, u32[]{:S(2)}) copy-start(bf16[512,1024]{1,0:T(8,128)(2,1)} %query_ref) | copy-start | bytes 3145732
  5.1 77.5 %all-to-all-start = ((bf16[8,512,256]{2,1,0:T(8,128)(2,1)}), bf16[8,512,256]{2,1,0:T(8,128)(2,1)S(1)}, u32[]{:S(2)}, u32[]{:S(2)}) async-start(bf16[8,512,256]{2,1,0:T(8,128)(2,1)} %bitcast.10), calls=%async_computation | async-start | bytes 4194304 | tf_op jit(solution)/shard_map/all_to_all | solution.py:324
  12.1 59.3 %collective-permute-start = (bf16[384,2048]{1,0:T(8,128)(2,1)}, bf16[384,2048]{1,0:T(8,128)(2,1)}, u32[]{:S(2)}, u32[]{:S(2)}) collective-permute-start(bf16[384,2048]{1,0:T(8,128)(2,1)} %refs_0_.1), channel_id=1, source_target_pairs={{0,2},{2,0},{4,6},{6,4},{8,10},{10,8},{12,14},{14,12},{1,3},{3,1},... | collective-permute-start | bytes 4718600 | tf_op jit(solution)/shard_map/ppermute | solution.py:315
  14.1 57.3 %collective-permute-start.1 = (bf16[384,2048]{1,0:T(8,128)(2,1)}, bf16[384,2048]{1,0:T(8,128)(2,1)S(1)}, u32[]{:S(2)}, u32[]{:S(2)}) collective-permute-start(bf16[384,2048]{1,0:T(8,128)(2,1)} %refs_0_.1), channel_id=1, source_target_pairs={{0,1},{1,0},{2,3},{3,2},{4,5},{5,4},{6,7},{7,6},{8,9},{9,8},{10,11... | collective-permute-start | bytes 4718600 | tf_op jit(solution)/shard_map/ppermute | solution.py:321
  14.1 68.6 %collective-permute-start.3 = (bf16[384,2048]{1,0:T(8,128)(2,1)}, bf16[384,2048]{1,0:T(8,128)(2,1)}, u32[]{:S(2)}, u32[]{:S(2)}) collective-permute-start(bf16[384,2048]{1,0:T(8,128)(2,1)} %refs_0_.1), channel_id=1, source_target_pairs={{0,4},{2,6},{4,0},{6,2},{8,12},{10,14},{12,8},{14,10},{1,5},{3,7},... | collective-permute-start | bytes 4718600 | tf_op jit(solution)/shard_map/ppermute | solution.py:315
  72.5 11.7 %collective-permute-start.4 = (bf16[384,2048]{1,0:T(8,128)(2,1)}, bf16[384,2048]{1,0:T(8,128)(2,1)}, u32[]{:S(2)}, u32[]{:S(2)}) collective-permute-start(bf16[384,2048]{1,0:T(8,128)(2,1)} %collective-permute-done.refs_2_), channel_id=1, source_target_pairs={{0,1},{1,0},{2,3},{3,2},{4,5},{5,4},{6,7},{7,6},{8,9},{9,8},{10,11... | collective-permute-start | bytes 4718600 | tf_op jit(solution)/shard_map/ppermute | solution.py:321
  75.3 8.9 %collective-permute-start.5 = (bf16[512,256]{1,0:T(8,128)(2,1)}, bf16[512,256]{1,0:T(8,128)(2,1)S(1)}, u32[]{:S(2)}, u32[]{:S(2)}) collective-permute-start(bf16[512,256]{1,0:T(8,128)(2,1)} %get-tuple-element.93), channel_id=1, source_target_pairs={{0,2},{2,0},{4,6},{6,4},{8,10},{10,8},{12,14},{14,12},{1,3},{3,1},... | collective-permute-start | bytes 786440 | tf_op jit(solution)/shard_map/ppermute | solution.py:315
  84.3 7.6 %collective-permute-start.6 = (bf16[384,2048]{1,0:T(8,128)(2,1)}, bf16[384,2048]{1,0:T(8,128)(2,1)S(1)}, u32[]{:S(2)}, u32[]{:S(2)}) collective-permute-start(bf16[384,2048]{1,0:T(8,128)(2,1)} %collective-permute-done.3.refs_4_), channel_id=1, source_target_pairs={{0,1},{1,0},{2,3},{3,2},{4,5},{5,4},{6,7},{7,6},{8,9},{9,8},{10,11... | collective-permute-start | bytes 4718600 | tf_op jit(solution)/shard_map/ppermute | solution.py:321
  84.3 7.6 %copy-start.3 = (bf16[384,2048]{1,0:T(8,128)(2,1)S(1)}, bf16[384,2048]{1,0:T(8,128)(2,1)}, u32[]{:S(2)}) copy-start(bf16[384,2048]{1,0:T(8,128)(2,1)} %copy-done.2) | copy-start | bytes 4718596
  85.7 6.1 %copy-start.1 = (bf16[384,2048]{1,0:T(8,128)(2,1)S(1)}, bf16[384,2048]{1,0:T(8,128)(2,1)}, u32[]{:S(2)}) copy-start(bf16[384,2048]{1,0:T(8,128)(2,1)} %refs_0_.1) | copy-start | bytes 4718596
  85.7 28.9 %collective-permute-start.7 = (bf16[384,1408]{1,0:T(8,128)(2,1)S(1)}, bf16[384,1408]{1,0:T(8,128)(2,1)S(1)}, u32[]{:S(2)}, u32[]{:S(2)}) collective-permute-start(bf16[384,1408]{1,0:T(8,128)(2,1)S(1)} %slice.13), channel_id=1, source_target_pairs={{0,2},{2,0},{4,6},{6,4},{8,10},{10,8},{12,14},{14,12},{1,3},{3,1},... | collective-permute-start | bytes 3244040 | tf_op jit(solution)/shard_map/ppermute | solution.py:315
  86.2 28.5 %collective-permute-start.11 = (bf16[2048,256]{1,0:T(8,128)(2,1)S(1)}, bf16[2048,256]{1,0:T(8,128)(2,1)S(1)}, u32[]{:S(2)}, u32[]{:S(2)}) collective-permute-start(bf16[2048,256]{1,0:T(8,128)(2,1)S(1)} %slice.14), channel_id=1, source_target_pairs={{0,16},{16,0},{1,17},{17,1},{2,18},{18,2},{3,19},{19,3},{4,20},{20... | collective-permute-start | bytes 3145736 | tf_op jit(solution)/shard_map/ppermute | solution.py:318
  87.8 26.9 %collective-permute-start.8 = (bf16[384,640]{1,0:T(8,128)(2,1)}, bf16[384,640]{1,0:T(8,128)(2,1)S(1)}, u32[]{:S(2)}, u32[]{:S(2)}) collective-permute-start(bf16[384,640]{1,0:T(8,128)(2,1)} %slice.12), channel_id=1, source_target_pairs={{0,4},{2,6},{4,0},{6,2},{8,12},{10,14},{12,8},{14,10},{1,5},{3,7},... | collective-permute-start | bytes 1474568 | tf_op jit(solution)/shard_map/ppermute | solution.py:315
  89.5 20.4 %collective-permute-start.10 = (bf16[512,256]{1,0:T(8,128)(2,1)S(1)}, bf16[512,256]{1,0:T(8,128)(2,1)S(1)}, u32[]{:S(2)}, u32[]{:S(2)}) collective-permute-start(bf16[512,256]{1,0:T(8,128)(2,1)S(1)} %copy-done.10), channel_id=1, source_target_pairs={{0,12},{2,14},{4,8},{6,10},{8,4},{10,6},{12,0},{14,2},{1,13},{3,15... | collective-permute-start | bytes 786440 | tf_op jit(solution)/shard_map/ppermute | solution.py:315
  91.9 22.8 %collective-permute-start.9 = (bf16[512,256]{1,0:T(8,128)(2,1)S(1)}, bf16[512,256]{1,0:T(8,128)(2,1)S(1)}, u32[]{:S(2)}, u32[]{:S(2)}) collective-permute-start(bf16[512,256]{1,0:T(8,128)(2,1)S(1)} %get-tuple-element.98.refs_2_), channel_id=1, source_target_pairs={{0,8},{2,10},{4,12},{6,14},{8,0},{10,2},{12,4},{14,6},{1,9},{3,11}... | collective-permute-start | bytes 786440 | tf_op jit(solution)/shard_map/ppermute | solution.py:315
  98.2 18.8 %copy-start.8 = (bf16[512,256]{1,0:T(8,128)(2,1)S(1)}, bf16[512,256]{1,0:T(8,128)(2,1)}, u32[]{:S(2)}) copy-start(bf16[512,256]{1,0:T(8,128)(2,1)} %copy-done.7) | copy-start | bytes 786436
  114.6 4.8 %collective-permute-start.12 = (bf16[384,1408]{1,0:T(8,128)(2,1)S(1)}, bf16[384,1408]{1,0:T(8,128)(2,1)S(1)}, u32[]{:S(2)}, u32[]{:S(2)}) collective-permute-start(bf16[384,1408]{1,0:T(8,128)(2,1)S(1)} %collective-permute-done.7.refs_0_), channel_id=1, source_target_pairs={{0,1},{1,0},{2,3},{3,2},{4,5},{5,4},{6,7},{7,6},{8,9},{9,8},{10,11... | collective-permute-start | bytes 3244040 | tf_op jit(solution)/shard_map/ppermute | solution.py:321
  114.8 25.6 %collective-permute-start.18 = (bf16[2048,256]{1,0:T(8,128)(2,1)S(1)}, bf16[2048,256]{1,0:T(8,128)(2,1)S(1)}, u32[]{:S(2)}, u32[]{:S(2)}) collective-permute-start(bf16[2048,256]{1,0:T(8,128)(2,1)S(1)} %slice.15), channel_id=1, source_target_pairs={{0,16},{16,0},{1,17},{17,1},{2,18},{18,2},{3,19},{19,3},{4,20},{20... | collective-permute-start | bytes 3145736 | tf_op jit(solution)/shard_map/ppermute | solution.py:318
  115.4 4.7 %collective-permute-start.13 = (bf16[384,640]{1,0:T(8,128)(2,1)S(1)}, bf16[384,640]{1,0:T(8,128)(2,1)S(1)}, u32[]{:S(2)}, u32[]{:S(2)}) collective-permute-start(bf16[384,640]{1,0:T(8,128)(2,1)S(1)} %collective-permute-done.8.refs_2_), channel_id=1, source_target_pairs={{0,1},{1,0},{2,3},{3,2},{4,5},{5,4},{6,7},{7,6},{8,9},{9,8},{10,11... | collective-permute-start | bytes 1474568 | tf_op jit(solution)/shard_map/ppermute | solution.py:321
  115.6 22.1 %collective-permute-start.17 = (bf16[512,256]{1,0:T(8,128)(2,1)}, bf16[512,256]{1,0:T(8,128)(2,1)S(1)}, u32[]{:S(2)}, u32[]{:S(2)}) collective-permute-start(bf16[512,256]{1,0:T(8,128)(2,1)} %get-tuple-element.93), channel_id=1, source_target_pairs={{0,10},{2,8},{4,14},{6,12},{8,2},{10,0},{12,6},{14,4},{1,11},{3,9}... | collective-permute-start | bytes 786440 | tf_op jit(solution)/shard_map/ppermute | solution.py:315
  117.0 39.0 %collective-permute-start.14 = (bf16[512,256]{1,0:T(8,128)(2,1)S(1)}, bf16[512,256]{1,0:T(8,128)(2,1)S(1)}, u32[]{:S(2)}, u32[]{:S(2)}) collective-permute-start(bf16[512,256]{1,0:T(8,128)(2,1)S(1)} %copy-done.8), channel_id=1, source_target_pairs={{0,14},{2,12},{4,10},{6,8},{8,6},{10,4},{12,2},{14,0},{1,15},{3,13... | collective-permute-start | bytes 786440 | tf_op jit(solution)/shard_map/ppermute | solution.py:315
  119.4 21.0 %collective-permute-start.15 = (bf16[512,256]{1,0:T(8,128)(2,1)S(1)}, bf16[512,256]{1,0:T(8,128)(2,1)S(1)}, u32[]{:S(2)}, u32[]{:S(2)}) collective-permute-start(bf16[512,256]{1,0:T(8,128)(2,1)S(1)} %copy-done.10), channel_id=1, source_target_pairs={{0,4},{2,6},{4,0},{6,2},{8,12},{10,14},{12,8},{14,10},{1,5},{3,7},... | collective-permute-start | bytes 786440 | tf_op jit(solution)/shard_map/ppermute | solution.py:315
  120.0 24.5 %collective-permute-start.16 = (bf16[512,256]{1,0:T(8,128)(2,1)S(1)}, bf16[512,256]{1,0:T(8,128)(2,1)S(1)}, u32[]{:S(2)}, u32[]{:S(2)}) collective-permute-start(bf16[512,256]{1,0:T(8,128)(2,1)S(1)} %copy-done.8), channel_id=1, source_target_pairs={{0,6},{2,4},{4,2},{6,0},{8,14},{10,12},{12,10},{14,8},{1,7},{3,5},... | collective-permute-start | bytes 786440 | tf_op jit(solution)/shard_map/ppermute | solution.py:315
  147.3 10.1 %collective-permute-start.19 = (f32[2,128,128]{2,1,0:T(8,128)S(1)}, f32[2,128,128]{2,1,0:T(8,128)S(1)}, u32[]{:S(2)}, u32[]{:S(2)}) collective-permute-start(f32[2,128,128]{2,1,0:T(8,128)S(1)} %get-tuple-element.123), channel_id=1, source_target_pairs={{0,8},{2,10},{4,12},{6,14},{1,9},{3,11},{5,13},{7,15},{16,24},{18,... | collective-permute-start | bytes 393224 | tf_op jit(solution)/shard_map/ppermute | solution.py:295
  158.6 11.3 %collective-permute-start.22 = (bf16[384,256]{1,0:T(8,128)(2,1)S(1)}, bf16[384,256]{1,0:T(8,128)(2,1)S(1)}, u32[]{:S(2)}, u32[]{:S(2)}) collective-permute-start(bf16[384,256]{1,0:T(8,128)(2,1)S(1)} %attend.7), channel_id=1, source_target_pairs={{0,6},{2,4},{4,2},{6,0},{8,14},{10,12},{12,10},{14,8},{1,7},{3,5},... | collective-permute-start | bytes 589832 | tf_op jit(solution)/shard_map/ppermute | solution.py:315
  159.9 10.0 %collective-permute-start.21 = (bf16[384,256]{1,0:T(8,128)(2,1)S(1)}, bf16[384,256]{1,0:T(8,128)(2,1)S(1)}, u32[]{:S(2)}, u32[]{:S(2)}) collective-permute-start(bf16[384,256]{1,0:T(8,128)(2,1)S(1)} %attend.6), channel_id=1, source_target_pairs={{0,4},{2,6},{4,0},{6,2},{8,12},{10,14},{12,8},{14,10},{1,5},{3,7},... | collective-permute-start | bytes 589832 | tf_op jit(solution)/shard_map/ppermute | solution.py:315
  163.5 6.5 %collective-permute-start.20 = (bf16[384,256]{1,0:T(8,128)(2,1)S(1)}, bf16[384,256]{1,0:T(8,128)(2,1)S(1)}, u32[]{:S(2)}, u32[]{:S(2)}) collective-permute-start(bf16[384,256]{1,0:T(8,128)(2,1)S(1)} %attend.5), channel_id=1, source_target_pairs={{0,2},{2,0},{4,6},{6,4},{8,10},{10,8},{12,14},{14,12},{1,3},{3,1},... | collective-permute-start | bytes 589832 | tf_op jit(solution)/shard_map/ppermute | solution.py:315
  169.9 2.9 %collective-permute-start.23 = (bf16[384,256]{1,0:T(8,128)(2,1)S(1)}, bf16[384,256]{1,0:T(8,128)(2,1)S(1)}, u32[]{:S(2)}, u32[]{:S(2)}) collective-permute-start(bf16[384,256]{1,0:T(8,128)(2,1)S(1)} %attend.4.refs_0_), channel_id=1, source_target_pairs={{0,1},{1,0},{2,3},{3,2},{4,5},{5,4},{6,7},{7,6},{8,9},{9,8},{10,11... | collective-permute-start | bytes 589832 | tf_op jit(solution)/shard_map/ppermute | solution.py:321
  170.0 2.8 %collective-permute-start.24 = (bf16[384,256]{1,0:T(8,128)(2,1)S(1)}, bf16[384,256]{1,0:T(8,128)(2,1)S(1)}, u32[]{:S(2)}, u32[]{:S(2)}) collective-permute-start(bf16[384,256]{1,0:T(8,128)(2,1)S(1)} %collective-permute-done.20.refs_1_), channel_id=1, source_target_pairs={{0,1},{1,0},{2,3},{3,2},{4,5},{5,4},{6,7},{7,6},{8,9},{9,8},{10,11... | collective-permute-start | bytes 589832 | tf_op jit(solution)/shard_map/ppermute | solution.py:321
  170.5 2.3 %collective-permute-start.25 = (bf16[384,256]{1,0:T(8,128)(2,1)S(1)}, bf16[384,256]{1,0:T(8,128)(2,1)S(1)}, u32[]{:S(2)}, u32[]{:S(2)}) collective-permute-start(bf16[384,256]{1,0:T(8,128)(2,1)S(1)} %collective-permute-done.21.refs_2_), channel_id=1, source_target_pairs={{0,1},{1,0},{2,3},{3,2},{4,5},{5,4},{6,7},{7,6},{8,9},{9,8},{10,11... | collective-permute-start | bytes 589832 | tf_op jit(solution)/shard_map/ppermute | solution.py:321
  170.6 2.3 %collective-permute-start.26 = (bf16[384,256]{1,0:T(8,128)(2,1)S(1)}, bf16[384,256]{1,0:T(8,128)(2,1)S(1)}, u32[]{:S(2)}, u32[]{:S(2)}) collective-permute-start(bf16[384,256]{1,0:T(8,128)(2,1)S(1)} %collective-permute-done.22.refs_3_), channel_id=1, source_target_pairs={{0,1},{1,0},{2,3},{3,2},{4,5},{5,4},{6,7},{7,6},{8,9},{9,8},{10,11... | collective-permute-start | bytes 589832 | tf_op jit(solution)/shard_map/ppermute | solution.py:321
  (7 other events, 10.1 us)

commit v15 on v14

--- a/solution.py
+++ b/solution.py
@@ -376,10 +376,10 @@
     if pieced:
         early = (0, 1, 4, 6)
         q_base = begin(place, streams, [(arrived[m], (m,)) for m in early])
-        latest = arrived.pop(7)
+        latest = {m: arrived.pop(m) for m in (3, 7)}
         arrived, kv_lower, kv_base, q_base = ob((arrived, kv_lower, kv_base, q_base))
         q_base = begin(place, streams, [(arrived[m], (m,)) for m in sorted(arrived) if m not in early], q_base)
-        q_parts = [(latest, (7,))]
+        q_parts = [(piece, (m,)) for m, piece in latest.items()]
     else:
         q_base, q_parts = None, [(gather_queries(q_sent), 0)]
     *second, totals = keys_values(place, streams, [(kv_lower, middle)], kv_base, last[3])

time: 176 us -> 170 us (0.966)
  starting transfers between devices: 36.1 us -> 33.1 us
  waiting for transfers between devices: 94.6 us -> 91.6 us
    ppermute x1, starting transfers between devices: 6.76 us -> 2.48 us  [shift(): return lax.ppermute(v, 'ctx', pairs)]
    ppermute x14, waiting for transfers between devices: 91.8 us -> 88.8 us  [xor(): return lax.ppermute(value, 'ctx', [(i, i ^ step) for i in range(n_ctx)])]
  transfers between devices with their start and end apart: 28 -> 28, of which waited for: 8 -> 9; matrix products, arithmetic and copies ran while one was open for 2% -> 2% of each run, Pallas kernels for 17% -> 18%
where the time goes in v15:
time: 170 us
  waiting for transfers between devices  91.6 us (54%)
  Pallas kernels  34.9 us (21%)
  starting transfers between devices  33.1 us (19%)
  local copies, waits for them, and re-layouts  9.81 us (6%)
    ppermute x14, waiting for transfers between devices, xor(): return lax.ppermute(value, 'ctx', [(i, i ^ step) for i in range(n_ctx)])  88.8 us
    ppermute x14, starting transfers between devices, xor(): return lax.ppermute(value, 'ctx', [(i, i ^ step) for i in range(n_ctx)])  19.8 us
    pallas_call x5, Pallas kernels, run_blocks(): call(body, name, out_shape, specs, outs, LIMIT, flops, 2 * MIB)  10.7 us
    all_to_all x1, starting transfers between devices, spread(): return lax.all_to_all(packed, 'ctx', 0, 0, tiled=True)  6.93 us
    unnamed x22, local copies, waits for them, and re-layouts  6.36 us
    pallas_call x4, Pallas kernels, attend(): call(kernel, 'attend', shapes, specs, [VMEM] * count, LIMIT, flops, 2 * MIB)  4.75 us
    pallas_call x2, Pallas kernels, add_features(): call(kernel, 'add_features', shape, [VMEM] * len(args), VMEM, LIMIT, flop...  4.74 us
    pallas_call x2, Pallas kernels, project(): call(kernel, 'project', shapes, [VMEM] * len(args), [VMEM] * 4, LIMIT, fl...  4.25 us
  transfers between devices with their start and end apart: 28, of which 9 were waited for; matrix products, arithmetic and copies ran while one was open for 2% of the time, Pallas kernels for 18%

profile of v15, /device:TPU:0, one launch (start us, length us, event | category | flops | bytes accessed | tf_op | source)
XLA Modules:
  0.0 169.8 jit_solution(7048184464969530489)
XLA Ops:
  3.8 1.3 copy-done
  5.1 6.9 %all-to-all-start = ((bf16[8,512,256]{2,1,0:T(8,128)(2,1)}), bf16[8,512,256]{2,1,0:T(8,128)(2,1)S(1)}, u32[]{:S(2)}, u32[]{:S(2)}) async-start(bf16[8,512,256]{2,1,0:T(8,128)(2,1)} %bitcast.10), calls=%async_computation | async-start | bytes 4194304 | tf_op jit(solution)/shard_map/all_to_all | solution.py:324
  12.1 2.0 %collective-permute-start = (bf16[384,2048]{1,0:T(8,128)(2,1)}, bf16[384,2048]{1,0:T(8,128)(2,1)}, u32[]{:S(2)}, u32[]{:S(2)}) collective-permute-start(bf16[384,2048]{1,0:T(8,128)(2,1)} %refs_0_.1), channel_id=1, source_target_pairs={{0,2},{2,0},{4,6},{6,4},{8,10},{10,8},{12,14},{14,12},{1,3},{3,1},... | collective-permute-start | bytes 4718600 | tf_op jit(solution)/shard_map/ppermute | solution.py:315
  14.1 1.5 collective-permute-start.3
  15.6 55.8 %collective-permute-done.refs_2_ = bf16[384,2048]{1,0:T(8,128)(2,1)} collective-permute-done((bf16[384,2048]{1,0:T(8,128)(2,1)}, bf16[384,2048]{1,0:T(8,128)(2,1)}, u32[]{:S(2)}, u32[]{:S(2)}) %collective-permute-start) | collective-permute-done | bytes 1572896 | tf_op jit(solution)/shard_map/ppermute | solution.py:315
  72.5 1.4 pack_queries.1
  75.6 1.9 %slice.12 = bf16[384,640]{1,0:T(8,128)(2,1)} slice(bf16[384,2048]{1,0:T(8,128)(2,1)} %collective-permute-done.refs_2_), slice={[0:384], [1408:2048]} | slice | bytes 983040 | tf_op jit(solution)/shard_map/slice | solution.py:349
  77.5 5.2 %collective-permute-done.3.refs_4_ = bf16[384,2048]{1,0:T(8,128)(2,1)} collective-permute-done((bf16[384,2048]{1,0:T(8,128)(2,1)}, bf16[384,2048]{1,0:T(8,128)(2,1)}, u32[]{:S(2)}, u32[]{:S(2)}) %collective-permute-start.3) | collective-permute-done | bytes 1572896 | tf_op jit(solution)/shard_map/ppermute | solution.py:315
  82.7 1.6 collective-permute-done.5.refs_3_
  84.3 1.4 slice.13
  86.2 1.6 collective-permute-start.11
  87.8 1.7 %collective-permute-start.8 = (bf16[384,640]{1,0:T(8,128)(2,1)}, bf16[384,640]{1,0:T(8,128)(2,1)S(1)}, u32[]{:S(2)}, u32[]{:S(2)}) collective-permute-start(bf16[384,640]{1,0:T(8,128)(2,1)} %slice.12), channel_id=1, source_target_pairs={{0,4},{2,6},{4,0},{6,2},{8,12},{10,14},{12,8},{14,10},{1,5},{3,7},... | collective-permute-start | bytes 1474568 | tf_op jit(solution)/shard_map/ppermute | solution.py:315
  89.5 2.4 %collective-permute-start.10 = (bf16[512,256]{1,0:T(8,128)(2,1)S(1)}, bf16[512,256]{1,0:T(8,128)(2,1)S(1)}, u32[]{:S(2)}, u32[]{:S(2)}) collective-permute-start(bf16[512,256]{1,0:T(8,128)(2,1)S(1)} %copy-done.10), channel_id=1, source_target_pairs={{0,12},{2,14},{4,8},{6,10},{8,4},{10,6},{12,0},{14,2},{1,13},{3,15... | collective-permute-start | bytes 786440 | tf_op jit(solution)/shard_map/ppermute | solution.py:315
  91.9 3.3 %stage.2.stream_ref.refs_0_ = bf16[3,384,4096]{2,1,0:T(8,128)(2,1)S(1)} custom-call(s32[4]{0:T(128)S(1)} %pad_add_fusion.place_ref, bf16[384,2048]{1,0:T(8,128)(2,1)S(1)} %copy-done.1, bf16[384,2048]{1,0:T(8,128)(2,1)S(1)} %copy-done.3, bf16[384,2048]{1,0:T(8,128)(2,1)} %collective-permute-done.refs_2_, bf16[384,2048]{1,0:T(8,128)(2,1)} %collective-permute-done.4.refs_3_, ...), custom_call_target="tpu_custom_call" | custom-call | bytes 18874368 | tf_op jit(solution)/shard_map/stage/pallas_call | solution.py:117
  95.2 3.0 %project.2 = (bf16[3,384,128]{2,1,0:T(8,128)(2,1)S(1)}, bf16[3,384,128]{2,1,0:T(8,128)(2,1)S(1)}, f32[3,128,128]{2,1,0:T(8,128)S(1)}, f32[128,128]{1,0:T(8,128)S(1)}) custom-call(bf16[3,384,4096]{2,1,0:T(8,128)(2,1)S(1)} %stage.2.stream_ref.refs_0_, bf16[4096,256]{1,0:T(8,128)(2,1)S(1)} %bitcast.7), custom_call_target="tpu_custom_call" | custom-call | flops 2415919104 | bytes 2097152 | tf_op jit(solution)/shard_map/project/pallas_call | solution.py:145
  98.2 11.7 %collective-permute-done.10.refs_5_ = bf16[512,256]{1,0:T(8,128)(2,1)S(1)} collective-permute-done((bf16[512,256]{1,0:T(8,128)(2,1)S(1)}, bf16[512,256]{1,0:T(8,128)(2,1)S(1)}, u32[]{:S(2)}, u32[]{:S(2)}) %collective-permute-start.10) | collective-permute-done | bytes 262176 | tf_op jit(solution)/shard_map/ppermute | solution.py:315
  109.9 4.8 %collective-permute-done.9.refs_4_ = bf16[512,256]{1,0:T(8,128)(2,1)S(1)} collective-permute-done((bf16[512,256]{1,0:T(8,128)(2,1)S(1)}, bf16[512,256]{1,0:T(8,128)(2,1)S(1)}, u32[]{:S(2)}, u32[]{:S(2)}) %collective-permute-start.9) | collective-permute-done | bytes 262176 | tf_op jit(solution)/shard_map/ppermute | solution.py:315
  115.6 1.4 collective-permute-start.17
  117.0 2.4 %collective-permute-start.15 = (bf16[512,256]{1,0:T(8,128)(2,1)S(1)}, bf16[512,256]{1,0:T(8,128)(2,1)S(1)}, u32[]{:S(2)}, u32[]{:S(2)}) collective-permute-start(bf16[512,256]{1,0:T(8,128)(2,1)S(1)} %copy-done.8), channel_id=1, source_target_pairs={{0,14},{2,12},{4,10},{6,8},{8,6},{10,4},{12,2},{14,0},{1,15},{3,13... | collective-permute-start | bytes 786440 | tf_op jit(solution)/shard_map/ppermute | solution.py:315
  120.0 2.1 %collective-permute-start.14 = (bf16[512,256]{1,0:T(8,128)(2,1)S(1)}, bf16[512,256]{1,0:T(8,128)(2,1)S(1)}, u32[]{:S(2)}, u32[]{:S(2)}) collective-permute-start(bf16[512,256]{1,0:T(8,128)(2,1)S(1)} %copy-done.8), channel_id=1, source_target_pairs={{0,6},{2,4},{4,2},{6,0},{8,14},{10,12},{12,10},{14,8},{1,7},{3,5},... | collective-permute-start | bytes 786440 | tf_op jit(solution)/shard_map/ppermute | solution.py:315
  123.1 2.3 %begin.3.refs_3_ = f32[4,384,256]{2,1,0:T(8,128)S(1)} custom-call(s32[4]{0:T(128)S(1)} %pad_add_fusion.place_ref, bf16[3,384,4096]{2,1,0:T(8,128)(2,1)S(1)} %stage.2.stream_ref.refs_0_, bf16[1,384,4096]{2,1,0:T(8,128)(2,1)S(1)} %stage.3.refs_1_.stream_ref, bf16[2048,256]{1,0:T(8,128)(2,1)S(1)} %collective-permute-done.11.refs_2_), custom_call_target="tpu_custom_call" | custom-call | flops 1610612736 | bytes 2097152 | tf_op jit(solution)/shard_map/begin/pallas_call | solution.py:185
  125.4 2.3 %begin.4.refs_4_ = f32[4,384,256]{2,1,0:T(8,128)S(1)} custom-call(s32[4]{0:T(128)S(1)} %pad_add_fusion.place_ref, bf16[3,384,4096]{2,1,0:T(8,128)(2,1)S(1)} %stage.2.stream_ref.refs_0_, bf16[1,384,4096]{2,1,0:T(8,128)(2,1)S(1)} %stage.3.refs_1_.stream_ref, bf16[512,256]{1,0:T(8,128)(2,1)S(1)} %get-tuple-element.98.refs_2_, ...), custom_call_target="tpu_custom_call" | custom-call | flops 1610612736 | bytes 2097152 | tf_op jit(solution)/shard_map/begin/pallas_call | solution.py:185
  129.0 8.6 %collective-permute-done.17.refs_3_ = bf16[512,256]{1,0:T(8,128)(2,1)S(1)} collective-permute-done((bf16[512,256]{1,0:T(8,128)(2,1)}, bf16[512,256]{1,0:T(8,128)(2,1)S(1)}, u32[]{:S(2)}, u32[]{:S(2)}) %collective-permute-start.17) | collective-permute-done | bytes 262176 | tf_op jit(solution)/shard_map/ppermute | solution.py:315
  137.7 2.7 %collective-permute-done.18.refs_2_ = bf16[2048,256]{1,0:T(8,128)(2,1)S(1)} collective-permute-done((bf16[2048,256]{1,0:T(8,128)(2,1)S(1)}, bf16[2048,256]{1,0:T(8,128)(2,1)S(1)}, u32[]{:S(2)}, u32[]{:S(2)}) %collective-permute-start.18) | collective-permute-done | bytes 1048608 | tf_op jit(solution)/shard_map/ppermute | solution.py:318
  140.4 2.7 %keys_values.1 = (bf16[4,384,128]{2,1,0:T(8,128)(2,1)S(1)}, bf16[4,384,128]{2,1,0:T(8,128)(2,1)S(1)}, f32[4,128,128]{2,1,0:T(8,128)S(1)}, f32[2,128,128]{2,1,0:T(8,128)S(1)}) custom-call(s32[4]{0:T(128)S(1)} %pad_add_fusion.place_ref, bf16[3,384,4096]{2,1,0:T(8,128)(2,1)S(1)} %stage.2.stream_ref.refs_0_, bf16[1,384,4096]{2,1,0:T(8,128)(2,1)S(1)} %stage.3.refs_1_.stream_ref, ...), custom_call_target="tpu_custom_call" | custom-call | flops 1610612736 | bytes 2097152 | tf_op jit(solution)/shard_map/keys_values/pallas_call | solution.py:185
  143.1 2.5 %collective-permute-start.19 = (f32[2,128,128]{2,1,0:T(8,128)S(1)}, f32[2,128,128]{2,1,0:T(8,128)S(1)}, u32[]{:S(2)}, u32[]{:S(2)}) collective-permute-start(f32[2,128,128]{2,1,0:T(8,128)S(1)} %get-tuple-element.121), channel_id=1, source_target_pairs={{0,8},{2,10},{4,12},{6,14},{1,9},{3,11},{5,13},{7,15},{16,24},{18,... | collective-permute-start | bytes 393224 | tf_op jit(solution)/shard_map/ppermute | solution.py:295
  145.6 1.5 begin.5.refs_4_
  147.2 1.8 %queries.1.query_ref = bf16[4,384,256]{2,1,0:T(8,128)(2,1)S(1)} custom-call(s32[4]{0:T(128)S(1)} %pad_add_fusion.place_ref, bf16[3,384,4096]{2,1,0:T(8,128)(2,1)S(1)} %stage.2.stream_ref.refs_0_, bf16[1,384,4096]{2,1,0:T(8,128)(2,1)S(1)} %stage.3.refs_1_.stream_ref, bf16[512,256]{1,0:T(8,128)(2,1)S(1)} %collective-permute-done.14.refs_2_, ...), custom_call_target="tpu_custom_call" | custom-call | flops 805306368 | bytes 2097152 | tf_op jit(solution)/shard_map/queries/pallas_call | solution.py:185
  150.2 4.3 %collective-permute-start.22 = (bf16[384,256]{1,0:T(8,128)(2,1)S(1)}, bf16[384,256]{1,0:T(8,128)(2,1)S(1)}, u32[]{:S(2)}, u32[]{:S(2)}) collective-permute-start(bf16[384,256]{1,0:T(8,128)(2,1)S(1)} %attend.7), channel_id=1, source_target_pairs={{0,6},{2,4},{4,2},{6,0},{8,14},{10,12},{12,10},{14,8},{1,7},{3,5},... | collective-permute-start | bytes 589832 | tf_op jit(solution)/shard_map/ppermute | solution.py:315
  158.7 4.0 %stage_rows.1 = (bf16[4,256,2048]{2,1,0:T(8,128)(2,1)S(1)}, bf16[4,256,2048]{2,1,0:T(8,128)(2,1)S(1)}) custom-call(s32[4]{0:T(128)S(1)} %pad_add_fusion.place_ref, bf16[1024,4096]{1,0:T(8,128)(2,1)} %out_ref.1, bf16[1024,4096]{1,0:T(8,128)(2,1)} %collective-permute-done.2.far_ref), custom_call_target="tpu_custom_call" | custom-call | bytes 16777216 | tf_op jit(solution)/shard_map/stage_rows/pallas_call | solution.py:89
  165.0 1.8 %add_features.2.refs_5_ = f32[384,2048]{1,0:T(8,128)S(1)} custom-call(bf16[384,256]{1,0:T(8,128)(2,1)S(1)} %attend.4.refs_0_, bf16[384,256]{1,0:T(8,128)(2,1)S(1)} %collective-permute-done.20.refs_1_, bf16[384,256]{1,0:T(8,128)(2,1)S(1)} %collective-permute-done.21.refs_2_, bf16[384,256]{1,0:T(8,128)(2,1)S(1)} %collective-permute-done.22.refs_3_, ...), custom_call_target="tpu_custom_call" | custom-call | flops 1610612736 | bytes 8388608 | tf_op jit(solution)/shard_map/add_features/pallas_call | solution.py:289
  166.8 2.9 %add_features.3 = bf16[384,2048]{1,0:T(8,128)(2,1)} custom-call(bf16[384,256]{1,0:T(8,128)(2,1)S(1)} %collective-permute-done.23.refs_0_, bf16[384,256]{1,0:T(8,128)(2,1)S(1)} %collective-permute-done.24.refs_1_, bf16[384,256]{1,0:T(8,128)(2,1)S(1)} %collective-permute-done.25.refs_2_, bf16[384,256]{1,0:T(8,128)(2,1)S(1)} %collective-permute-done.26.refs_3_, ...), custom_call_target="tpu_custom_call" | custom-call | flops 1610612736 | bytes 8388608 | tf_op jit(solution)/shard_map/add_features/pallas_call | solution.py:289
  (69 shorter events, 18.5 us)
Async XLA Ops:
  0.0 72.5 %collective-permute-start.2 = (bf16[1024,4096]{1,0:T(8,128)(2,1)}, bf16[1024,4096]{1,0:T(8,128)(2,1)}, u32[]{:S(2)}, u32[]{:S(2)}) collective-permute-start(bf16[1024,4096]{1,0:T(8,128)(2,1)} %out_ref.1), channel_id=1, source_target_pairs={{0,1},{1,0},{2,3},{3,2},{4,5},{5,4},{6,7},{7,6},{8,9},{9,8},{10,11... | collective-permute-start | bytes 25165832 | tf_op jit(solution)/shard_map/ppermute | solution.py:321
  5.1 67.4 %copy-start.6 = (bf16[512,1024]{1,0:T(8,128)(2,1)S(1)}, bf16[512,1024]{1,0:T(8,128)(2,1)}, u32[]{:S(2)}) copy-start(bf16[512,1024]{1,0:T(8,128)(2,1)} %query_ref) | copy-start | bytes 3145732
  5.1 77.5 %all-to-all-start = ((bf16[8,512,256]{2,1,0:T(8,128)(2,1)}), bf16[8,512,256]{2,1,0:T(8,128)(2,1)S(1)}, u32[]{:S(2)}, u32[]{:S(2)}) async-start(bf16[8,512,256]{2,1,0:T(8,128)(2,1)} %bitcast.10), calls=%async_computation | async-start | bytes 4194304 | tf_op jit(solution)/shard_map/all_to_all | solution.py:324
  12.1 59.3 %collective-permute-start = (bf16[384,2048]{1,0:T(8,128)(2,1)}, bf16[384,2048]{1,0:T(8,128)(2,1)}, u32[]{:S(2)}, u32[]{:S(2)}) collective-permute-start(bf16[384,2048]{1,0:T(8,128)(2,1)} %refs_0_.1), channel_id=1, source_target_pairs={{0,2},{2,0},{4,6},{6,4},{8,10},{10,8},{12,14},{14,12},{1,3},{3,1},... | collective-permute-start | bytes 4718600 | tf_op jit(solution)/shard_map/ppermute | solution.py:315
  14.1 57.3 %collective-permute-start.1 = (bf16[384,2048]{1,0:T(8,128)(2,1)}, bf16[384,2048]{1,0:T(8,128)(2,1)S(1)}, u32[]{:S(2)}, u32[]{:S(2)}) collective-permute-start(bf16[384,2048]{1,0:T(8,128)(2,1)} %refs_0_.1), channel_id=1, source_target_pairs={{0,1},{1,0},{2,3},{3,2},{4,5},{5,4},{6,7},{7,6},{8,9},{9,8},{10,11... | collective-permute-start | bytes 4718600 | tf_op jit(solution)/shard_map/ppermute | solution.py:321
  14.1 68.6 %collective-permute-start.3 = (bf16[384,2048]{1,0:T(8,128)(2,1)}, bf16[384,2048]{1,0:T(8,128)(2,1)}, u32[]{:S(2)}, u32[]{:S(2)}) collective-permute-start(bf16[384,2048]{1,0:T(8,128)(2,1)} %refs_0_.1), channel_id=1, source_target_pairs={{0,4},{2,6},{4,0},{6,2},{8,12},{10,14},{12,8},{14,10},{1,5},{3,7},... | collective-permute-start | bytes 4718600 | tf_op jit(solution)/shard_map/ppermute | solution.py:315
  72.5 11.7 %collective-permute-start.4 = (bf16[384,2048]{1,0:T(8,128)(2,1)}, bf16[384,2048]{1,0:T(8,128)(2,1)}, u32[]{:S(2)}, u32[]{:S(2)}) collective-permute-start(bf16[384,2048]{1,0:T(8,128)(2,1)} %collective-permute-done.refs_2_), channel_id=1, source_target_pairs={{0,1},{1,0},{2,3},{3,2},{4,5},{5,4},{6,7},{7,6},{8,9},{9,8},{10,11... | collective-permute-start | bytes 4718600 | tf_op jit(solution)/shard_map/ppermute | solution.py:321
  75.3 8.9 %collective-permute-start.5 = (bf16[512,256]{1,0:T(8,128)(2,1)}, bf16[512,256]{1,0:T(8,128)(2,1)S(1)}, u32[]{:S(2)}, u32[]{:S(2)}) collective-permute-start(bf16[512,256]{1,0:T(8,128)(2,1)} %get-tuple-element.92), channel_id=1, source_target_pairs={{0,2},{2,0},{4,6},{6,4},{8,10},{10,8},{12,14},{14,12},{1,3},{3,1},... | collective-permute-start | bytes 786440 | tf_op jit(solution)/shard_map/ppermute | solution.py:315
  84.3 7.6 %collective-permute-start.6 = (bf16[384,2048]{1,0:T(8,128)(2,1)}, bf16[384,2048]{1,0:T(8,128)(2,1)S(1)}, u32[]{:S(2)}, u32[]{:S(2)}) collective-permute-start(bf16[384,2048]{1,0:T(8,128)(2,1)} %collective-permute-done.3.refs_4_), channel_id=1, source_target_pairs={{0,1},{1,0},{2,3},{3,2},{4,5},{5,4},{6,7},{7,6},{8,9},{9,8},{10,11... | collective-permute-start | bytes 4718600 | tf_op jit(solution)/shard_map/ppermute | solution.py:321
  84.3 7.6 %copy-start.3 = (bf16[384,2048]{1,0:T(8,128)(2,1)S(1)}, bf16[384,2048]{1,0:T(8,128)(2,1)}, u32[]{:S(2)}) copy-start(bf16[384,2048]{1,0:T(8,128)(2,1)} %copy-done.2) | copy-start | bytes 4718596
  85.7 6.1 %copy-start.1 = (bf16[384,2048]{1,0:T(8,128)(2,1)S(1)}, bf16[384,2048]{1,0:T(8,128)(2,1)}, u32[]{:S(2)}) copy-start(bf16[384,2048]{1,0:T(8,128)(2,1)} %refs_0_.1) | copy-start | bytes 4718596
  85.7 28.9 %collective-permute-start.7 = (bf16[384,1408]{1,0:T(8,128)(2,1)S(1)}, bf16[384,1408]{1,0:T(8,128)(2,1)S(1)}, u32[]{:S(2)}, u32[]{:S(2)}) collective-permute-start(bf16[384,1408]{1,0:T(8,128)(2,1)S(1)} %slice.13), channel_id=1, source_target_pairs={{0,2},{2,0},{4,6},{6,4},{8,10},{10,8},{12,14},{14,12},{1,3},{3,1},... | collective-permute-start | bytes 3244040 | tf_op jit(solution)/shard_map/ppermute | solution.py:315
  86.2 28.5 %collective-permute-start.11 = (bf16[2048,256]{1,0:T(8,128)(2,1)S(1)}, bf16[2048,256]{1,0:T(8,128)(2,1)S(1)}, u32[]{:S(2)}, u32[]{:S(2)}) collective-permute-start(bf16[2048,256]{1,0:T(8,128)(2,1)S(1)} %slice.14), channel_id=1, source_target_pairs={{0,16},{16,0},{1,17},{17,1},{2,18},{18,2},{3,19},{19,3},{4,20},{20... | collective-permute-start | bytes 3145736 | tf_op jit(solution)/shard_map/ppermute | solution.py:318
  87.8 26.9 %collective-permute-start.8 = (bf16[384,640]{1,0:T(8,128)(2,1)}, bf16[384,640]{1,0:T(8,128)(2,1)S(1)}, u32[]{:S(2)}, u32[]{:S(2)}) collective-permute-start(bf16[384,640]{1,0:T(8,128)(2,1)} %slice.12), channel_id=1, source_target_pairs={{0,4},{2,6},{4,0},{6,2},{8,12},{10,14},{12,8},{14,10},{1,5},{3,7},... | collective-permute-start | bytes 1474568 | tf_op jit(solution)/shard_map/ppermute | solution.py:315
  89.5 20.4 %collective-permute-start.10 = (bf16[512,256]{1,0:T(8,128)(2,1)S(1)}, bf16[512,256]{1,0:T(8,128)(2,1)S(1)}, u32[]{:S(2)}, u32[]{:S(2)}) collective-permute-start(bf16[512,256]{1,0:T(8,128)(2,1)S(1)} %copy-done.10), channel_id=1, source_target_pairs={{0,12},{2,14},{4,8},{6,10},{8,4},{10,6},{12,0},{14,2},{1,13},{3,15... | collective-permute-start | bytes 786440 | tf_op jit(solution)/shard_map/ppermute | solution.py:315
  91.9 22.8 %collective-permute-start.9 = (bf16[512,256]{1,0:T(8,128)(2,1)S(1)}, bf16[512,256]{1,0:T(8,128)(2,1)S(1)}, u32[]{:S(2)}, u32[]{:S(2)}) collective-permute-start(bf16[512,256]{1,0:T(8,128)(2,1)S(1)} %get-tuple-element.98.refs_2_), channel_id=1, source_target_pairs={{0,8},{2,10},{4,12},{6,14},{8,0},{10,2},{12,4},{14,6},{1,9},{3,11}... | collective-permute-start | bytes 786440 | tf_op jit(solution)/shard_map/ppermute | solution.py:315
  98.2 18.8 %copy-start.8 = (bf16[512,256]{1,0:T(8,128)(2,1)S(1)}, bf16[512,256]{1,0:T(8,128)(2,1)}, u32[]{:S(2)}) copy-start(bf16[512,256]{1,0:T(8,128)(2,1)} %copy-done.7) | copy-start | bytes 786436
  114.6 4.8 %collective-permute-start.12 = (bf16[384,1408]{1,0:T(8,128)(2,1)S(1)}, bf16[384,1408]{1,0:T(8,128)(2,1)S(1)}, u32[]{:S(2)}, u32[]{:S(2)}) collective-permute-start(bf16[384,1408]{1,0:T(8,128)(2,1)S(1)} %collective-permute-done.7.refs_0_), channel_id=1, source_target_pairs={{0,1},{1,0},{2,3},{3,2},{4,5},{5,4},{6,7},{7,6},{8,9},{9,8},{10,11... | collective-permute-start | bytes 3244040 | tf_op jit(solution)/shard_map/ppermute | solution.py:321
  114.8 25.6 %collective-permute-start.18 = (bf16[2048,256]{1,0:T(8,128)(2,1)S(1)}, bf16[2048,256]{1,0:T(8,128)(2,1)S(1)}, u32[]{:S(2)}, u32[]{:S(2)}) collective-permute-start(bf16[2048,256]{1,0:T(8,128)(2,1)S(1)} %slice.15), channel_id=1, source_target_pairs={{0,16},{16,0},{1,17},{17,1},{2,18},{18,2},{3,19},{19,3},{4,20},{20... | collective-permute-start | bytes 3145736 | tf_op jit(solution)/shard_map/ppermute | solution.py:318
  115.4 4.7 %collective-permute-start.13 = (bf16[384,640]{1,0:T(8,128)(2,1)S(1)}, bf16[384,640]{1,0:T(8,128)(2,1)S(1)}, u32[]{:S(2)}, u32[]{:S(2)}) collective-permute-start(bf16[384,640]{1,0:T(8,128)(2,1)S(1)} %collective-permute-done.8.refs_2_), channel_id=1, source_target_pairs={{0,1},{1,0},{2,3},{3,2},{4,5},{5,4},{6,7},{7,6},{8,9},{9,8},{10,11... | collective-permute-start | bytes 1474568 | tf_op jit(solution)/shard_map/ppermute | solution.py:321
  115.6 22.1 %collective-permute-start.17 = (bf16[512,256]{1,0:T(8,128)(2,1)}, bf16[512,256]{1,0:T(8,128)(2,1)S(1)}, u32[]{:S(2)}, u32[]{:S(2)}) collective-permute-start(bf16[512,256]{1,0:T(8,128)(2,1)} %get-tuple-element.92), channel_id=1, source_target_pairs={{0,10},{2,8},{4,14},{6,12},{8,2},{10,0},{12,6},{14,4},{1,11},{3,9}... | collective-permute-start | bytes 786440 | tf_op jit(solution)/shard_map/ppermute | solution.py:315
  117.0 30.2 %collective-permute-start.15 = (bf16[512,256]{1,0:T(8,128)(2,1)S(1)}, bf16[512,256]{1,0:T(8,128)(2,1)S(1)}, u32[]{:S(2)}, u32[]{:S(2)}) collective-permute-start(bf16[512,256]{1,0:T(8,128)(2,1)S(1)} %copy-done.8), channel_id=1, source_target_pairs={{0,14},{2,12},{4,10},{6,8},{8,6},{10,4},{12,2},{14,0},{1,15},{3,13... | collective-permute-start | bytes 786440 | tf_op jit(solution)/shard_map/ppermute | solution.py:315
  119.4 21.0 %collective-permute-start.16 = (bf16[512,256]{1,0:T(8,128)(2,1)S(1)}, bf16[512,256]{1,0:T(8,128)(2,1)S(1)}, u32[]{:S(2)}, u32[]{:S(2)}) collective-permute-start(bf16[512,256]{1,0:T(8,128)(2,1)S(1)} %copy-done.10), channel_id=1, source_target_pairs={{0,4},{2,6},{4,0},{6,2},{8,12},{10,14},{12,8},{14,10},{1,5},{3,7},... | collective-permute-start | bytes 786440 | tf_op jit(solution)/shard_map/ppermute | solution.py:315
  120.0 27.1 %collective-permute-start.14 = (bf16[512,256]{1,0:T(8,128)(2,1)S(1)}, bf16[512,256]{1,0:T(8,128)(2,1)S(1)}, u32[]{:S(2)}, u32[]{:S(2)}) collective-permute-start(bf16[512,256]{1,0:T(8,128)(2,1)S(1)} %copy-done.8), channel_id=1, source_target_pairs={{0,6},{2,4},{4,2},{6,0},{8,14},{10,12},{12,10},{14,8},{1,7},{3,5},... | collective-permute-start | bytes 786440 | tf_op jit(solution)/shard_map/ppermute | solution.py:315
  143.1 5.9 %collective-permute-start.19 = (f32[2,128,128]{2,1,0:T(8,128)S(1)}, f32[2,128,128]{2,1,0:T(8,128)S(1)}, u32[]{:S(2)}, u32[]{:S(2)}) collective-permute-start(f32[2,128,128]{2,1,0:T(8,128)S(1)} %get-tuple-element.121), channel_id=1, source_target_pairs={{0,8},{2,10},{4,12},{6,14},{1,9},{3,11},{5,13},{7,15},{16,24},{18,... | collective-permute-start | bytes 393224 | tf_op jit(solution)/shard_map/ppermute | solution.py:295
  150.2 12.6 %collective-permute-start.22 = (bf16[384,256]{1,0:T(8,128)(2,1)S(1)}, bf16[384,256]{1,0:T(8,128)(2,1)S(1)}, u32[]{:S(2)}, u32[]{:S(2)}) collective-permute-start(bf16[384,256]{1,0:T(8,128)(2,1)S(1)} %attend.7), channel_id=1, source_target_pairs={{0,6},{2,4},{4,2},{6,0},{8,14},{10,12},{12,10},{14,8},{1,7},{3,5},... | collective-permute-start | bytes 589832 | tf_op jit(solution)/shard_map/ppermute | solution.py:315
  155.6 7.4 %collective-permute-start.21 = (bf16[384,256]{1,0:T(8,128)(2,1)S(1)}, bf16[384,256]{1,0:T(8,128)(2,1)S(1)}, u32[]{:S(2)}, u32[]{:S(2)}) collective-permute-start(bf16[384,256]{1,0:T(8,128)(2,1)S(1)} %attend.6), channel_id=1, source_target_pairs={{0,4},{2,6},{4,0},{6,2},{8,12},{10,14},{12,8},{14,10},{1,5},{3,7},... | collective-permute-start | bytes 589832 | tf_op jit(solution)/shard_map/ppermute | solution.py:315
  156.9 7.0 %collective-permute-start.20 = (bf16[384,256]{1,0:T(8,128)(2,1)S(1)}, bf16[384,256]{1,0:T(8,128)(2,1)S(1)}, u32[]{:S(2)}, u32[]{:S(2)}) collective-permute-start(bf16[384,256]{1,0:T(8,128)(2,1)S(1)} %attend.5), channel_id=1, source_target_pairs={{0,2},{2,0},{4,6},{6,4},{8,10},{10,8},{12,14},{14,12},{1,3},{3,1},... | collective-permute-start | bytes 589832 | tf_op jit(solution)/shard_map/ppermute | solution.py:315
  163.9 2.8 %collective-permute-start.23 = (bf16[384,256]{1,0:T(8,128)(2,1)S(1)}, bf16[384,256]{1,0:T(8,128)(2,1)S(1)}, u32[]{:S(2)}, u32[]{:S(2)}) collective-permute-start(bf16[384,256]{1,0:T(8,128)(2,1)S(1)} %attend.4.refs_0_), channel_id=1, source_target_pairs={{0,1},{1,0},{2,3},{3,2},{4,5},{5,4},{6,7},{7,6},{8,9},{9,8},{10,11... | collective-permute-start | bytes 589832 | tf_op jit(solution)/shard_map/ppermute | solution.py:321
  163.9 2.8 %collective-permute-start.24 = (bf16[384,256]{1,0:T(8,128)(2,1)S(1)}, bf16[384,256]{1,0:T(8,128)(2,1)S(1)}, u32[]{:S(2)}, u32[]{:S(2)}) collective-permute-start(bf16[384,256]{1,0:T(8,128)(2,1)S(1)} %collective-permute-done.20.refs_1_), channel_id=1, source_target_pairs={{0,1},{1,0},{2,3},{3,2},{4,5},{5,4},{6,7},{7,6},{8,9},{9,8},{10,11... | collective-permute-start | bytes 589832 | tf_op jit(solution)/shard_map/ppermute | solution.py:321
  164.5 2.3 %collective-permute-start.25 = (bf16[384,256]{1,0:T(8,128)(2,1)S(1)}, bf16[384,256]{1,0:T(8,128)(2,1)S(1)}, u32[]{:S(2)}, u32[]{:S(2)}) collective-permute-start(bf16[384,256]{1,0:T(8,128)(2,1)S(1)} %collective-permute-done.21.refs_2_), channel_id=1, source_target_pairs={{0,1},{1,0},{2,3},{3,2},{4,5},{5,4},{6,7},{7,6},{8,9},{9,8},{10,11... | collective-permute-start | bytes 589832 | tf_op jit(solution)/shard_map/ppermute | solution.py:321
  164.5 2.4 %collective-permute-start.26 = (bf16[384,256]{1,0:T(8,128)(2,1)S(1)}, bf16[384,256]{1,0:T(8,128)(2,1)S(1)}, u32[]{:S(2)}, u32[]{:S(2)}) collective-permute-start(bf16[384,256]{1,0:T(8,128)(2,1)S(1)} %collective-permute-done.22.refs_3_), channel_id=1, source_target_pairs={{0,1},{1,0},{2,3},{3,2},{4,5},{5,4},{6,7},{7,6},{8,9},{9,8},{10,11... | collective-permute-start | bytes 589832 | tf_op jit(solution)/shard_map/ppermute | solution.py:321
  (7 other events, 10.1 us)

commit v16 on v15

--- a/solution.py
+++ b/solution.py
@@ -377,8 +377,8 @@
         early = (0, 1, 4, 6)
         q_base = begin(place, streams, [(arrived[m], (m,)) for m in early])
         latest = {m: arrived.pop(m) for m in (3, 7)}
+        q_base = begin(place, streams, [(arrived[m], (m,)) for m in sorted(arrived) if m not in early], q_base)
         arrived, kv_lower, kv_base, q_base = ob((arrived, kv_lower, kv_base, q_base))
-        q_base = begin(place, streams, [(arrived[m], (m,)) for m in sorted(arrived) if m not in early], q_base)
         q_parts = [(piece, (m,)) for m, piece in latest.items()]
     else:
         q_base, q_parts = None, [(gather_queries(q_sent), 0)]

time: 170 us -> 170 us (level)
    ppermute x2, waiting for transfers between devices: 2.73 us -> 0.01 us  [other_part(): return lax.ppermute(value, 'groups', [(0, 1), (1, 0)])]
    ppermute x14, waiting for transfers between devices: 88.8 us -> 90.8 us  [xor(): return lax.ppermute(value, 'ctx', [(i, i ^ step) for i in range(n_ctx)])]
  transfers between devices with their start and end apart: 28 -> 28, of which waited for: 9 -> 10; matrix products, arithmetic and copies ran while one was open for 2% -> 2% of each run, Pallas kernels for 18% -> 18%
where the time goes in v16:
time: 170 us
  waiting for transfers between devices  91.3 us (54%)
  Pallas kernels  34.9 us (21%)
  starting transfers between devices  33.4 us (20%)
  local copies, waits for them, and re-layouts  9.81 us (6%)
    ppermute x14, waiting for transfers between devices, xor(): return lax.ppermute(value, 'ctx', [(i, i ^ step) for i in range(n_ctx)])  90.8 us
    ppermute x14, starting transfers between devices, xor(): return lax.ppermute(value, 'ctx', [(i, i ^ step) for i in range(n_ctx)])  20.6 us
    pallas_call x5, Pallas kernels, run_blocks(): call(body, name, out_shape, specs, outs, LIMIT, flops, 2 * MIB)  10.7 us
    all_to_all x1, starting transfers between devices, spread(): return lax.all_to_all(packed, 'ctx', 0, 0, tiled=True)  6.93 us
    unnamed x22, local copies, waits for them, and re-layouts  6.36 us
    pallas_call x2, Pallas kernels, add_features(): call(kernel, 'add_features', shape, [VMEM] * len(args), VMEM, LIMIT, flop...  4.74 us
    pallas_call x4, Pallas kernels, attend(): call(kernel, 'attend', shapes, specs, [VMEM] * count, LIMIT, flops, 2 * MIB)  4.73 us
    pallas_call x2, Pallas kernels, project(): call(kernel, 'project', shapes, [VMEM] * len(args), [VMEM] * 4, LIMIT, fl...  4.25 us
  transfers between devices with their start and end apart: 28, of which 10 were waited for; matrix products, arithmetic and copies ran while one was open for 2% of the time, Pallas kernels for 18%

profile of v16, /device:TPU:0, one launch (start us, length us, event | category | flops | bytes accessed | tf_op | source)
XLA Modules:
  0.0 169.7 jit_solution(2530419396697481298)
XLA Ops:
  3.8 1.3 copy-done
  5.1 6.9 %all-to-all-start = ((bf16[8,512,256]{2,1,0:T(8,128)(2,1)}), bf16[8,512,256]{2,1,0:T(8,128)(2,1)S(1)}, u32[]{:S(2)}, u32[]{:S(2)}) async-start(bf16[8,512,256]{2,1,0:T(8,128)(2,1)} %bitcast.10), calls=%async_computation | async-start | bytes 4194304 | tf_op jit(solution)/shard_map/all_to_all | solution.py:324
  12.1 2.0 %collective-permute-start = (bf16[384,2048]{1,0:T(8,128)(2,1)}, bf16[384,2048]{1,0:T(8,128)(2,1)}, u32[]{:S(2)}, u32[]{:S(2)}) collective-permute-start(bf16[384,2048]{1,0:T(8,128)(2,1)} %refs_0_.1), channel_id=1, source_target_pairs={{0,2},{2,0},{4,6},{6,4},{8,10},{10,8},{12,14},{14,12},{1,3},{3,1},... | collective-permute-start | bytes 4718600 | tf_op jit(solution)/shard_map/ppermute | solution.py:315
  14.1 1.5 collective-permute-start.3
  15.6 55.8 %collective-permute-done.refs_2_ = bf16[384,2048]{1,0:T(8,128)(2,1)} collective-permute-done((bf16[384,2048]{1,0:T(8,128)(2,1)}, bf16[384,2048]{1,0:T(8,128)(2,1)}, u32[]{:S(2)}, u32[]{:S(2)}) %collective-permute-start) | collective-permute-done | bytes 1572896 | tf_op jit(solution)/shard_map/ppermute | solution.py:315
  72.5 1.4 pack_queries.1
  75.6 1.9 %slice.12 = bf16[384,640]{1,0:T(8,128)(2,1)} slice(bf16[384,2048]{1,0:T(8,128)(2,1)} %collective-permute-done.refs_2_), slice={[0:384], [1408:2048]} | slice | bytes 983040 | tf_op jit(solution)/shard_map/slice | solution.py:349
  77.5 5.2 %collective-permute-done.3.refs_4_ = bf16[384,2048]{1,0:T(8,128)(2,1)} collective-permute-done((bf16[384,2048]{1,0:T(8,128)(2,1)}, bf16[384,2048]{1,0:T(8,128)(2,1)}, u32[]{:S(2)}, u32[]{:S(2)}) %collective-permute-start.3) | collective-permute-done | bytes 1572896 | tf_op jit(solution)/shard_map/ppermute | solution.py:315
  82.7 1.6 collective-permute-done.5.refs_3_
  84.3 1.4 slice.13
  86.2 1.6 collective-permute-start.11
  87.8 1.7 %collective-permute-start.8 = (bf16[384,640]{1,0:T(8,128)(2,1)}, bf16[384,640]{1,0:T(8,128)(2,1)S(1)}, u32[]{:S(2)}, u32[]{:S(2)}) collective-permute-start(bf16[384,640]{1,0:T(8,128)(2,1)} %slice.12), channel_id=1, source_target_pairs={{0,4},{2,6},{4,0},{6,2},{8,12},{10,14},{12,8},{14,10},{1,5},{3,7},... | collective-permute-start | bytes 1474568 | tf_op jit(solution)/shard_map/ppermute | solution.py:315
  89.5 2.4 %collective-permute-start.10 = (bf16[512,256]{1,0:T(8,128)(2,1)S(1)}, bf16[512,256]{1,0:T(8,128)(2,1)S(1)}, u32[]{:S(2)}, u32[]{:S(2)}) collective-permute-start(bf16[512,256]{1,0:T(8,128)(2,1)S(1)} %copy-done.10), channel_id=1, source_target_pairs={{0,12},{2,14},{4,8},{6,10},{8,4},{10,6},{12,0},{14,2},{1,13},{3,15... | collective-permute-start | bytes 786440 | tf_op jit(solution)/shard_map/ppermute | solution.py:315
  91.9 3.3 %stage.2.stream_ref.refs_0_ = bf16[3,384,4096]{2,1,0:T(8,128)(2,1)S(1)} custom-call(s32[4]{0:T(128)S(1)} %pad_add_fusion.place_ref, bf16[384,2048]{1,0:T(8,128)(2,1)S(1)} %copy-done.1, bf16[384,2048]{1,0:T(8,128)(2,1)S(1)} %copy-done.3, bf16[384,2048]{1,0:T(8,128)(2,1)} %collective-permute-done.refs_2_, bf16[384,2048]{1,0:T(8,128)(2,1)} %collective-permute-done.4.refs_3_, ...), custom_call_target="tpu_custom_call" | custom-call | bytes 18874368 | tf_op jit(solution)/shard_map/stage/pallas_call | solution.py:117
  95.2 3.0 %project.2 = (bf16[3,384,128]{2,1,0:T(8,128)(2,1)S(1)}, bf16[3,384,128]{2,1,0:T(8,128)(2,1)S(1)}, f32[3,128,128]{2,1,0:T(8,128)S(1)}, f32[128,128]{1,0:T(8,128)S(1)}) custom-call(bf16[3,384,4096]{2,1,0:T(8,128)(2,1)S(1)} %stage.2.stream_ref.refs_0_, bf16[4096,256]{1,0:T(8,128)(2,1)S(1)} %bitcast.7), custom_call_target="tpu_custom_call" | custom-call | flops 2415919104 | bytes 2097152 | tf_op jit(solution)/shard_map/project/pallas_call | solution.py:145
  98.2 11.7 %collective-permute-done.10.refs_5_ = bf16[512,256]{1,0:T(8,128)(2,1)S(1)} collective-permute-done((bf16[512,256]{1,0:T(8,128)(2,1)S(1)}, bf16[512,256]{1,0:T(8,128)(2,1)S(1)}, u32[]{:S(2)}, u32[]{:S(2)}) %collective-permute-start.10) | collective-permute-done | bytes 262176 | tf_op jit(solution)/shard_map/ppermute | solution.py:315
  109.9 4.8 %collective-permute-done.9.refs_4_ = bf16[512,256]{1,0:T(8,128)(2,1)S(1)} collective-permute-done((bf16[512,256]{1,0:T(8,128)(2,1)S(1)}, bf16[512,256]{1,0:T(8,128)(2,1)S(1)}, u32[]{:S(2)}, u32[]{:S(2)}) %collective-permute-start.9) | collective-permute-done | bytes 262176 | tf_op jit(solution)/shard_map/ppermute | solution.py:315
  115.6 1.4 collective-permute-start.17
  117.0 2.4 %collective-permute-start.15 = (bf16[512,256]{1,0:T(8,128)(2,1)S(1)}, bf16[512,256]{1,0:T(8,128)(2,1)S(1)}, u32[]{:S(2)}, u32[]{:S(2)}) collective-permute-start(bf16[512,256]{1,0:T(8,128)(2,1)S(1)} %copy-done.8), channel_id=1, source_target_pairs={{0,14},{2,12},{4,10},{6,8},{8,6},{10,4},{12,2},{14,0},{1,15},{3,13... | collective-permute-start | bytes 786440 | tf_op jit(solution)/shard_map/ppermute | solution.py:315
  120.0 2.1 %collective-permute-start.14 = (bf16[512,256]{1,0:T(8,128)(2,1)S(1)}, bf16[512,256]{1,0:T(8,128)(2,1)S(1)}, u32[]{:S(2)}, u32[]{:S(2)}) collective-permute-start(bf16[512,256]{1,0:T(8,128)(2,1)S(1)} %copy-done.8), channel_id=1, source_target_pairs={{0,6},{2,4},{4,2},{6,0},{8,14},{10,12},{12,10},{14,8},{1,7},{3,5},... | collective-permute-start | bytes 786440 | tf_op jit(solution)/shard_map/ppermute | solution.py:315
  123.1 2.3 %begin.3.refs_3_ = f32[4,384,256]{2,1,0:T(8,128)S(1)} custom-call(s32[4]{0:T(128)S(1)} %pad_add_fusion.place_ref, bf16[3,384,4096]{2,1,0:T(8,128)(2,1)S(1)} %stage.2.stream_ref.refs_0_, bf16[1,384,4096]{2,1,0:T(8,128)(2,1)S(1)} %stage.3.refs_1_.stream_ref, bf16[2048,256]{1,0:T(8,128)(2,1)S(1)} %collective-permute-done.11.refs_2_), custom_call_target="tpu_custom_call" | custom-call | flops 1610612736 | bytes 2097152 | tf_op jit(solution)/shard_map/begin/pallas_call | solution.py:185
  126.7 2.3 %begin.4.refs_4_ = f32[4,384,256]{2,1,0:T(8,128)S(1)} custom-call(s32[4]{0:T(128)S(1)} %pad_add_fusion.place_ref, bf16[3,384,4096]{2,1,0:T(8,128)(2,1)S(1)} %stage.2.stream_ref.refs_0_, bf16[1,384,4096]{2,1,0:T(8,128)(2,1)S(1)} %stage.3.refs_1_.stream_ref, bf16[512,256]{1,0:T(8,128)(2,1)S(1)} %get-tuple-element.96.refs_2_, ...), custom_call_target="tpu_custom_call" | custom-call | flops 1610612736 | bytes 2097152 | tf_op jit(solution)/shard_map/begin/pallas_call | solution.py:185
  129.0 8.6 %collective-permute-done.17.refs_3_ = bf16[512,256]{1,0:T(8,128)(2,1)S(1)} collective-permute-done((bf16[512,256]{1,0:T(8,128)(2,1)}, bf16[512,256]{1,0:T(8,128)(2,1)S(1)}, u32[]{:S(2)}, u32[]{:S(2)}) %collective-permute-start.17) | collective-permute-done | bytes 262176 | tf_op jit(solution)/shard_map/ppermute | solution.py:315
  137.7 2.0 %collective-permute-done.16.refs_2_ = bf16[512,256]{1,0:T(8,128)(2,1)S(1)} collective-permute-done((bf16[512,256]{1,0:T(8,128)(2,1)S(1)}, bf16[512,256]{1,0:T(8,128)(2,1)S(1)}, u32[]{:S(2)}, u32[]{:S(2)}) %collective-permute-start.16) | collective-permute-done | bytes 262176 | tf_op jit(solution)/shard_map/ppermute | solution.py:315
  139.7 1.5 begin.5.refs_4_
  141.2 2.7 %keys_values.1 = (bf16[4,384,128]{2,1,0:T(8,128)(2,1)S(1)}, bf16[4,384,128]{2,1,0:T(8,128)(2,1)S(1)}, f32[4,128,128]{2,1,0:T(8,128)S(1)}, f32[2,128,128]{2,1,0:T(8,128)S(1)}) custom-call(s32[4]{0:T(128)S(1)} %pad_add_fusion.place_ref, bf16[3,384,4096]{2,1,0:T(8,128)(2,1)S(1)} %stage.2.stream_ref.refs_0_, bf16[1,384,4096]{2,1,0:T(8,128)(2,1)S(1)} %stage.3.refs_1_.stream_ref, ...), custom_call_target="tpu_custom_call" | custom-call | flops 1610612736 | bytes 2097152 | tf_op jit(solution)/shard_map/keys_values/pallas_call | solution.py:185
  143.9 1.9 %collective-permute-start.19 = (f32[2,128,128]{2,1,0:T(8,128)S(1)}, f32[2,128,128]{2,1,0:T(8,128)S(1)}, u32[]{:S(2)}, u32[]{:S(2)}) collective-permute-start(f32[2,128,128]{2,1,0:T(8,128)S(1)} %get-tuple-element.117), channel_id=1, source_target_pairs={{0,8},{2,10},{4,12},{6,14},{1,9},{3,11},{5,13},{7,15},{16,24},{18,... | collective-permute-start | bytes 393224 | tf_op jit(solution)/shard_map/ppermute | solution.py:295
  145.8 1.8 %queries.1.query_ref = bf16[4,384,256]{2,1,0:T(8,128)(2,1)S(1)} custom-call(s32[4]{0:T(128)S(1)} %pad_add_fusion.place_ref, bf16[3,384,4096]{2,1,0:T(8,128)(2,1)S(1)} %stage.2.stream_ref.refs_0_, bf16[1,384,4096]{2,1,0:T(8,128)(2,1)S(1)} %stage.3.refs_1_.stream_ref, bf16[512,256]{1,0:T(8,128)(2,1)S(1)} %collective-permute-done.14.refs_2_, ...), custom_call_target="tpu_custom_call" | custom-call | flops 805306368 | bytes 2097152 | tf_op jit(solution)/shard_map/queries/pallas_call | solution.py:185
  149.3 5.1 %collective-permute-start.22 = (bf16[384,256]{1,0:T(8,128)(2,1)S(1)}, bf16[384,256]{1,0:T(8,128)(2,1)S(1)}, u32[]{:S(2)}, u32[]{:S(2)}) collective-permute-start(bf16[384,256]{1,0:T(8,128)(2,1)S(1)} %attend.7), channel_id=1, source_target_pairs={{0,6},{2,4},{4,2},{6,0},{8,14},{10,12},{12,10},{14,8},{1,7},{3,5},... | collective-permute-start | bytes 589832 | tf_op jit(solution)/shard_map/ppermute | solution.py:315
  158.7 4.0 %stage_rows.1 = (bf16[4,256,2048]{2,1,0:T(8,128)(2,1)S(1)}, bf16[4,256,2048]{2,1,0:T(8,128)(2,1)S(1)}) custom-call(s32[4]{0:T(128)S(1)} %pad_add_fusion.place_ref, bf16[1024,4096]{1,0:T(8,128)(2,1)} %out_ref.1, bf16[1024,4096]{1,0:T(8,128)(2,1)} %collective-permute-done.2.far_ref), custom_call_target="tpu_custom_call" | custom-call | bytes 16777216 | tf_op jit(solution)/shard_map/stage_rows/pallas_call | solution.py:89
  165.0 1.8 %add_features.2.refs_5_ = f32[384,2048]{1,0:T(8,128)S(1)} custom-call(bf16[384,256]{1,0:T(8,128)(2,1)S(1)} %attend.4.refs_0_, bf16[384,256]{1,0:T(8,128)(2,1)S(1)} %collective-permute-done.20.refs_1_, bf16[384,256]{1,0:T(8,128)(2,1)S(1)} %collective-permute-done.21.refs_2_, bf16[384,256]{1,0:T(8,128)(2,1)S(1)} %collective-permute-done.22.refs_3_, ...), custom_call_target="tpu_custom_call" | custom-call | flops 1610612736 | bytes 8388608 | tf_op jit(solution)/shard_map/add_features/pallas_call | solution.py:289
  166.8 2.9 %add_features.3 = bf16[384,2048]{1,0:T(8,128)(2,1)} custom-call(bf16[384,256]{1,0:T(8,128)(2,1)S(1)} %collective-permute-done.23.refs_0_, bf16[384,256]{1,0:T(8,128)(2,1)S(1)} %collective-permute-done.24.refs_1_, bf16[384,256]{1,0:T(8,128)(2,1)S(1)} %collective-permute-done.25.refs_2_, bf16[384,256]{1,0:T(8,128)(2,1)S(1)} %collective-permute-done.26.refs_3_, ...), custom_call_target="tpu_custom_call" | custom-call | flops 1610612736 | bytes 8388608 | tf_op jit(solution)/shard_map/add_features/pallas_call | solution.py:289
  (69 shorter events, 19.0 us)
Async XLA Ops:
  0.0 72.5 %collective-permute-start.2 = (bf16[1024,4096]{1,0:T(8,128)(2,1)}, bf16[1024,4096]{1,0:T(8,128)(2,1)}, u32[]{:S(2)}, u32[]{:S(2)}) collective-permute-start(bf16[1024,4096]{1,0:T(8,128)(2,1)} %out_ref.1), channel_id=1, source_target_pairs={{0,1},{1,0},{2,3},{3,2},{4,5},{5,4},{6,7},{7,6},{8,9},{9,8},{10,11... | collective-permute-start | bytes 25165832 | tf_op jit(solution)/shard_map/ppermute | solution.py:321
  5.1 67.4 %copy-start.6 = (bf16[512,1024]{1,0:T(8,128)(2,1)S(1)}, bf16[512,1024]{1,0:T(8,128)(2,1)}, u32[]{:S(2)}) copy-start(bf16[512,1024]{1,0:T(8,128)(2,1)} %query_ref) | copy-start | bytes 3145732
  5.1 77.5 %all-to-all-start = ((bf16[8,512,256]{2,1,0:T(8,128)(2,1)}), bf16[8,512,256]{2,1,0:T(8,128)(2,1)S(1)}, u32[]{:S(2)}, u32[]{:S(2)}) async-start(bf16[8,512,256]{2,1,0:T(8,128)(2,1)} %bitcast.10), calls=%async_computation | async-start | bytes 4194304 | tf_op jit(solution)/shard_map/all_to_all | solution.py:324
  12.1 59.3 %collective-permute-start = (bf16[384,2048]{1,0:T(8,128)(2,1)}, bf16[384,2048]{1,0:T(8,128)(2,1)}, u32[]{:S(2)}, u32[]{:S(2)}) collective-permute-start(bf16[384,2048]{1,0:T(8,128)(2,1)} %refs_0_.1), channel_id=1, source_target_pairs={{0,2},{2,0},{4,6},{6,4},{8,10},{10,8},{12,14},{14,12},{1,3},{3,1},... | collective-permute-start | bytes 4718600 | tf_op jit(solution)/shard_map/ppermute | solution.py:315
  14.1 57.3 %collective-permute-start.1 = (bf16[384,2048]{1,0:T(8,128)(2,1)}, bf16[384,2048]{1,0:T(8,128)(2,1)S(1)}, u32[]{:S(2)}, u32[]{:S(2)}) collective-permute-start(bf16[384,2048]{1,0:T(8,128)(2,1)} %refs_0_.1), channel_id=1, source_target_pairs={{0,1},{1,0},{2,3},{3,2},{4,5},{5,4},{6,7},{7,6},{8,9},{9,8},{10,11... | collective-permute-start | bytes 4718600 | tf_op jit(solution)/shard_map/ppermute | solution.py:321
  14.1 68.6 %collective-permute-start.3 = (bf16[384,2048]{1,0:T(8,128)(2,1)}, bf16[384,2048]{1,0:T(8,128)(2,1)}, u32[]{:S(2)}, u32[]{:S(2)}) collective-permute-start(bf16[384,2048]{1,0:T(8,128)(2,1)} %refs_0_.1), channel_id=1, source_target_pairs={{0,4},{2,6},{4,0},{6,2},{8,12},{10,14},{12,8},{14,10},{1,5},{3,7},... | collective-permute-start | bytes 4718600 | tf_op jit(solution)/shard_map/ppermute | solution.py:315
  72.5 11.7 %collective-permute-start.4 = (bf16[384,2048]{1,0:T(8,128)(2,1)}, bf16[384,2048]{1,0:T(8,128)(2,1)}, u32[]{:S(2)}, u32[]{:S(2)}) collective-permute-start(bf16[384,2048]{1,0:T(8,128)(2,1)} %collective-permute-done.refs_2_), channel_id=1, source_target_pairs={{0,1},{1,0},{2,3},{3,2},{4,5},{5,4},{6,7},{7,6},{8,9},{9,8},{10,11... | collective-permute-start | bytes 4718600 | tf_op jit(solution)/shard_map/ppermute | solution.py:321
  75.3 8.9 %collective-permute-start.5 = (bf16[512,256]{1,0:T(8,128)(2,1)}, bf16[512,256]{1,0:T(8,128)(2,1)S(1)}, u32[]{:S(2)}, u32[]{:S(2)}) collective-permute-start(bf16[512,256]{1,0:T(8,128)(2,1)} %get-tuple-element.90), channel_id=1, source_target_pairs={{0,2},{2,0},{4,6},{6,4},{8,10},{10,8},{12,14},{14,12},{1,3},{3,1},... | collective-permute-start | bytes 786440 | tf_op jit(solution)/shard_map/ppermute | solution.py:315
  84.3 7.6 %collective-permute-start.6 = (bf16[384,2048]{1,0:T(8,128)(2,1)}, bf16[384,2048]{1,0:T(8,128)(2,1)S(1)}, u32[]{:S(2)}, u32[]{:S(2)}) collective-permute-start(bf16[384,2048]{1,0:T(8,128)(2,1)} %collective-permute-done.3.refs_4_), channel_id=1, source_target_pairs={{0,1},{1,0},{2,3},{3,2},{4,5},{5,4},{6,7},{7,6},{8,9},{9,8},{10,11... | collective-permute-start | bytes 4718600 | tf_op jit(solution)/shard_map/ppermute | solution.py:321
  84.3 7.6 %copy-start.3 = (bf16[384,2048]{1,0:T(8,128)(2,1)S(1)}, bf16[384,2048]{1,0:T(8,128)(2,1)}, u32[]{:S(2)}) copy-start(bf16[384,2048]{1,0:T(8,128)(2,1)} %copy-done.2) | copy-start | bytes 4718596
  85.7 6.1 %copy-start.1 = (bf16[384,2048]{1,0:T(8,128)(2,1)S(1)}, bf16[384,2048]{1,0:T(8,128)(2,1)}, u32[]{:S(2)}) copy-start(bf16[384,2048]{1,0:T(8,128)(2,1)} %refs_0_.1) | copy-start | bytes 4718596
  85.7 28.9 %collective-permute-start.7 = (bf16[384,1408]{1,0:T(8,128)(2,1)S(1)}, bf16[384,1408]{1,0:T(8,128)(2,1)S(1)}, u32[]{:S(2)}, u32[]{:S(2)}) collective-permute-start(bf16[384,1408]{1,0:T(8,128)(2,1)S(1)} %slice.13), channel_id=1, source_target_pairs={{0,2},{2,0},{4,6},{6,4},{8,10},{10,8},{12,14},{14,12},{1,3},{3,1},... | collective-permute-start | bytes 3244040 | tf_op jit(solution)/shard_map/ppermute | solution.py:315
  86.2 28.5 %collective-permute-start.11 = (bf16[2048,256]{1,0:T(8,128)(2,1)S(1)}, bf16[2048,256]{1,0:T(8,128)(2,1)S(1)}, u32[]{:S(2)}, u32[]{:S(2)}) collective-permute-start(bf16[2048,256]{1,0:T(8,128)(2,1)S(1)} %slice.14), channel_id=1, source_target_pairs={{0,16},{16,0},{1,17},{17,1},{2,18},{18,2},{3,19},{19,3},{4,20},{20... | collective-permute-start | bytes 3145736 | tf_op jit(solution)/shard_map/ppermute | solution.py:318
  87.8 26.9 %collective-permute-start.8 = (bf16[384,640]{1,0:T(8,128)(2,1)}, bf16[384,640]{1,0:T(8,128)(2,1)S(1)}, u32[]{:S(2)}, u32[]{:S(2)}) collective-permute-start(bf16[384,640]{1,0:T(8,128)(2,1)} %slice.12), channel_id=1, source_target_pairs={{0,4},{2,6},{4,0},{6,2},{8,12},{10,14},{12,8},{14,10},{1,5},{3,7},... | collective-permute-start | bytes 1474568 | tf_op jit(solution)/shard_map/ppermute | solution.py:315
  89.5 20.4 %collective-permute-start.10 = (bf16[512,256]{1,0:T(8,128)(2,1)S(1)}, bf16[512,256]{1,0:T(8,128)(2,1)S(1)}, u32[]{:S(2)}, u32[]{:S(2)}) collective-permute-start(bf16[512,256]{1,0:T(8,128)(2,1)S(1)} %copy-done.10), channel_id=1, source_target_pairs={{0,12},{2,14},{4,8},{6,10},{8,4},{10,6},{12,0},{14,2},{1,13},{3,15... | collective-permute-start | bytes 786440 | tf_op jit(solution)/shard_map/ppermute | solution.py:315
  91.9 22.8 %collective-permute-start.9 = (bf16[512,256]{1,0:T(8,128)(2,1)S(1)}, bf16[512,256]{1,0:T(8,128)(2,1)S(1)}, u32[]{:S(2)}, u32[]{:S(2)}) collective-permute-start(bf16[512,256]{1,0:T(8,128)(2,1)S(1)} %get-tuple-element.96.refs_2_), channel_id=1, source_target_pairs={{0,8},{2,10},{4,12},{6,14},{8,0},{10,2},{12,4},{14,6},{1,9},{3,11}... | collective-permute-start | bytes 786440 | tf_op jit(solution)/shard_map/ppermute | solution.py:315
  98.2 18.8 %copy-start.8 = (bf16[512,256]{1,0:T(8,128)(2,1)S(1)}, bf16[512,256]{1,0:T(8,128)(2,1)}, u32[]{:S(2)}) copy-start(bf16[512,256]{1,0:T(8,128)(2,1)} %copy-done.7) | copy-start | bytes 786436
  114.6 4.8 %collective-permute-start.12 = (bf16[384,1408]{1,0:T(8,128)(2,1)S(1)}, bf16[384,1408]{1,0:T(8,128)(2,1)S(1)}, u32[]{:S(2)}, u32[]{:S(2)}) collective-permute-start(bf16[384,1408]{1,0:T(8,128)(2,1)S(1)} %collective-permute-done.7.refs_0_), channel_id=1, source_target_pairs={{0,1},{1,0},{2,3},{3,2},{4,5},{5,4},{6,7},{7,6},{8,9},{9,8},{10,11... | collective-permute-start | bytes 3244040 | tf_op jit(solution)/shard_map/ppermute | solution.py:321
  114.8 26.4 %collective-permute-start.18 = (bf16[2048,256]{1,0:T(8,128)(2,1)S(1)}, bf16[2048,256]{1,0:T(8,128)(2,1)S(1)}, u32[]{:S(2)}, u32[]{:S(2)}) collective-permute-start(bf16[2048,256]{1,0:T(8,128)(2,1)S(1)} %slice.15), channel_id=1, source_target_pairs={{0,16},{16,0},{1,17},{17,1},{2,18},{18,2},{3,19},{19,3},{4,20},{20... | collective-permute-start | bytes 3145736 | tf_op jit(solution)/shard_map/ppermute | solution.py:318
  115.4 4.7 %collective-permute-start.13 = (bf16[384,640]{1,0:T(8,128)(2,1)S(1)}, bf16[384,640]{1,0:T(8,128)(2,1)S(1)}, u32[]{:S(2)}, u32[]{:S(2)}) collective-permute-start(bf16[384,640]{1,0:T(8,128)(2,1)S(1)} %collective-permute-done.8.refs_2_), channel_id=1, source_target_pairs={{0,1},{1,0},{2,3},{3,2},{4,5},{5,4},{6,7},{7,6},{8,9},{9,8},{10,11... | collective-permute-start | bytes 1474568 | tf_op jit(solution)/shard_map/ppermute | solution.py:321
  115.6 22.1 %collective-permute-start.17 = (bf16[512,256]{1,0:T(8,128)(2,1)}, bf16[512,256]{1,0:T(8,128)(2,1)S(1)}, u32[]{:S(2)}, u32[]{:S(2)}) collective-permute-start(bf16[512,256]{1,0:T(8,128)(2,1)} %get-tuple-element.90), channel_id=1, source_target_pairs={{0,10},{2,8},{4,14},{6,12},{8,2},{10,0},{12,6},{14,4},{1,11},{3,9}... | collective-permute-start | bytes 786440 | tf_op jit(solution)/shard_map/ppermute | solution.py:315
  117.0 28.9 %collective-permute-start.15 = (bf16[512,256]{1,0:T(8,128)(2,1)S(1)}, bf16[512,256]{1,0:T(8,128)(2,1)S(1)}, u32[]{:S(2)}, u32[]{:S(2)}) collective-permute-start(bf16[512,256]{1,0:T(8,128)(2,1)S(1)} %copy-done.8), channel_id=1, source_target_pairs={{0,14},{2,12},{4,10},{6,8},{8,6},{10,4},{12,2},{14,0},{1,15},{3,13... | collective-permute-start | bytes 786440 | tf_op jit(solution)/shard_map/ppermute | solution.py:315
  119.4 20.3 %collective-permute-start.16 = (bf16[512,256]{1,0:T(8,128)(2,1)S(1)}, bf16[512,256]{1,0:T(8,128)(2,1)S(1)}, u32[]{:S(2)}, u32[]{:S(2)}) collective-permute-start(bf16[512,256]{1,0:T(8,128)(2,1)S(1)} %copy-done.10), channel_id=1, source_target_pairs={{0,4},{2,6},{4,0},{6,2},{8,12},{10,14},{12,8},{14,10},{1,5},{3,7},... | collective-permute-start | bytes 786440 | tf_op jit(solution)/shard_map/ppermute | solution.py:315
  120.0 25.8 %collective-permute-start.14 = (bf16[512,256]{1,0:T(8,128)(2,1)S(1)}, bf16[512,256]{1,0:T(8,128)(2,1)S(1)}, u32[]{:S(2)}, u32[]{:S(2)}) collective-permute-start(bf16[512,256]{1,0:T(8,128)(2,1)S(1)} %copy-done.8), channel_id=1, source_target_pairs={{0,6},{2,4},{4,2},{6,0},{8,14},{10,12},{12,10},{14,8},{1,7},{3,5},... | collective-permute-start | bytes 786440 | tf_op jit(solution)/shard_map/ppermute | solution.py:315
  143.9 4.2 %collective-permute-start.19 = (f32[2,128,128]{2,1,0:T(8,128)S(1)}, f32[2,128,128]{2,1,0:T(8,128)S(1)}, u32[]{:S(2)}, u32[]{:S(2)}) collective-permute-start(f32[2,128,128]{2,1,0:T(8,128)S(1)} %get-tuple-element.117), channel_id=1, source_target_pairs={{0,8},{2,10},{4,12},{6,14},{1,9},{3,11},{5,13},{7,15},{16,24},{18,... | collective-permute-start | bytes 393224 | tf_op jit(solution)/shard_map/ppermute | solution.py:295
  149.3 13.4 %collective-permute-start.22 = (bf16[384,256]{1,0:T(8,128)(2,1)S(1)}, bf16[384,256]{1,0:T(8,128)(2,1)S(1)}, u32[]{:S(2)}, u32[]{:S(2)}) collective-permute-start(bf16[384,256]{1,0:T(8,128)(2,1)S(1)} %attend.7), channel_id=1, source_target_pairs={{0,6},{2,4},{4,2},{6,0},{8,14},{10,12},{12,10},{14,8},{1,7},{3,5},... | collective-permute-start | bytes 589832 | tf_op jit(solution)/shard_map/ppermute | solution.py:315
  155.6 7.4 %collective-permute-start.21 = (bf16[384,256]{1,0:T(8,128)(2,1)S(1)}, bf16[384,256]{1,0:T(8,128)(2,1)S(1)}, u32[]{:S(2)}, u32[]{:S(2)}) collective-permute-start(bf16[384,256]{1,0:T(8,128)(2,1)S(1)} %attend.6), channel_id=1, source_target_pairs={{0,4},{2,6},{4,0},{6,2},{8,12},{10,14},{12,8},{14,10},{1,5},{3,7},... | collective-permute-start | bytes 589832 | tf_op jit(solution)/shard_map/ppermute | solution.py:315
  156.9 7.0 %collective-permute-start.20 = (bf16[384,256]{1,0:T(8,128)(2,1)S(1)}, bf16[384,256]{1,0:T(8,128)(2,1)S(1)}, u32[]{:S(2)}, u32[]{:S(2)}) collective-permute-start(bf16[384,256]{1,0:T(8,128)(2,1)S(1)} %attend.5), channel_id=1, source_target_pairs={{0,2},{2,0},{4,6},{6,4},{8,10},{10,8},{12,14},{14,12},{1,3},{3,1},... | collective-permute-start | bytes 589832 | tf_op jit(solution)/shard_map/ppermute | solution.py:315
  163.9 2.8 %collective-permute-start.23 = (bf16[384,256]{1,0:T(8,128)(2,1)S(1)}, bf16[384,256]{1,0:T(8,128)(2,1)S(1)}, u32[]{:S(2)}, u32[]{:S(2)}) collective-permute-start(bf16[384,256]{1,0:T(8,128)(2,1)S(1)} %attend.4.refs_0_), channel_id=1, source_target_pairs={{0,1},{1,0},{2,3},{3,2},{4,5},{5,4},{6,7},{7,6},{8,9},{9,8},{10,11... | collective-permute-start | bytes 589832 | tf_op jit(solution)/shard_map/ppermute | solution.py:321
  163.9 2.8 %collective-permute-start.24 = (bf16[384,256]{1,0:T(8,128)(2,1)S(1)}, bf16[384,256]{1,0:T(8,128)(2,1)S(1)}, u32[]{:S(2)}, u32[]{:S(2)}) collective-permute-start(bf16[384,256]{1,0:T(8,128)(2,1)S(1)} %collective-permute-done.20.refs_1_), channel_id=1, source_target_pairs={{0,1},{1,0},{2,3},{3,2},{4,5},{5,4},{6,7},{7,6},{8,9},{9,8},{10,11... | collective-permute-start | bytes 589832 | tf_op jit(solution)/shard_map/ppermute | solution.py:321
  164.4 2.3 %collective-permute-start.25 = (bf16[384,256]{1,0:T(8,128)(2,1)S(1)}, bf16[384,256]{1,0:T(8,128)(2,1)S(1)}, u32[]{:S(2)}, u32[]{:S(2)}) collective-permute-start(bf16[384,256]{1,0:T(8,128)(2,1)S(1)} %collective-permute-done.21.refs_2_), channel_id=1, source_target_pairs={{0,1},{1,0},{2,3},{3,2},{4,5},{5,4},{6,7},{7,6},{8,9},{9,8},{10,11... | collective-permute-start | bytes 589832 | tf_op jit(solution)/shard_map/ppermute | solution.py:321
  164.5 2.3 %collective-permute-start.26 = (bf16[384,256]{1,0:T(8,128)(2,1)S(1)}, bf16[384,256]{1,0:T(8,128)(2,1)S(1)}, u32[]{:S(2)}, u32[]{:S(2)}) collective-permute-start(bf16[384,256]{1,0:T(8,128)(2,1)S(1)} %collective-permute-done.22.refs_3_), channel_id=1, source_target_pairs={{0,1},{1,0},{2,3},{3,2},{4,5},{5,4},{6,7},{7,6},{8,9},{9,8},{10,11... | collective-permute-start | bytes 589832 | tf_op jit(solution)/shard_map/ppermute | solution.py:321
  (7 other events, 10.1 us)

commit v17 on v15

--- a/solution.py
+++ b/solution.py
@@ -386,7 +386,7 @@
     carried = exclusive_prefix(totals, groups)
     heads = [[first[:3], last[:3]], [second]]
     query = queries(place, streams, q_parts, q_base)
-    normed = [attend(place, (r,), query, heads, carried)[0] for r in (3, 1, 2, 0)]
+    normed = [n for blocks in ((3,), (1, 2), (0,)) for n in attend(place, blocks, query, heads, carried)]
     normed = [normed[3], xor(normed[1], 1), xor(normed[2], 2), xor(normed[0], 3)]
     home_0, w_far = lax.optimization_barrier((normed[0], w_far))
     out_keep, out_far = stage_rows(place, w_out, w_far)

time: 170 us -> 170 us (level)
    pallas_call x4 -> x3, Pallas kernels: 4.75 us -> 3.94 us  [attend(): call(kernel, 'attend', shapes, specs, [VMEM] * count, LIMIT, flops, 2 * MIB)]
  transfers between devices with their start and end apart: 28 -> 28, of which waited for: 9 -> 8; matrix products, arithmetic and copies ran while one was open for 2% -> 2% of each run, Pallas kernels for 18% -> 18%
where the time goes in v17:
time: 170 us
  waiting for transfers between devices  92.2 us (54%)
  Pallas kernels  34.1 us (20%)
  starting transfers between devices  33 us (19%)
  local copies, waits for them, and re-layouts  9.81 us (6%)
    ppermute x14, waiting for transfers between devices, xor(): return lax.ppermute(value, 'ctx', [(i, i ^ step) for i in range(n_ctx)])  89.5 us
    ppermute x14, starting transfers between devices, xor(): return lax.ppermute(value, 'ctx', [(i, i ^ step) for i in range(n_ctx)])  19.7 us
    pallas_call x5, Pallas kernels, run_blocks(): call(body, name, out_shape, specs, outs, LIMIT, flops, 2 * MIB)  10.7 us
    all_to_all x1, starting transfers between devices, spread(): return lax.all_to_all(packed, 'ctx', 0, 0, tiled=True)  6.93 us
    unnamed x22, local copies, waits for them, and re-layouts  6.34 us
    pallas_call x2, Pallas kernels, add_features(): call(kernel, 'add_features', shape, [VMEM] * len(args), VMEM, LIMIT, flop...  4.74 us
    pallas_call x2, Pallas kernels, project(): call(kernel, 'project', shapes, [VMEM] * len(args), [VMEM] * 4, LIMIT, fl...  4.25 us
    pallas_call x2, Pallas kernels, stage(): call(kernel, 'stage', shape, [SMEM] + [ANY] * count, VMEM, 20 if blocks >...  4.25 us
  transfers between devices with their start and end apart: 28, of which 8 were waited for; matrix products, arithmetic and copies ran while one was open for 2% of the time, Pallas kernels for 18%

profile of v17, /device:TPU:0, one launch (start us, length us, event | category | flops | bytes accessed | tf_op | source)
XLA Modules:
  0.0 169.5 jit_solution(11819458460283147647)
XLA Ops:
  5.1 6.9 %all-to-all-start = ((bf16[8,512,256]{2,1,0:T(8,128)(2,1)}), bf16[8,512,256]{2,1,0:T(8,128)(2,1)S(1)}, u32[]{:S(2)}, u32[]{:S(2)}) async-start(bf16[8,512,256]{2,1,0:T(8,128)(2,1)} %bitcast.10), calls=%async_computation | async-start | bytes 4194304 | tf_op jit(solution)/shard_map/all_to_all | solution.py:324
  12.1 2.0 %collective-permute-start = (bf16[384,2048]{1,0:T(8,128)(2,1)}, bf16[384,2048]{1,0:T(8,128)(2,1)}, u32[]{:S(2)}, u32[]{:S(2)}) collective-permute-start(bf16[384,2048]{1,0:T(8,128)(2,1)} %refs_0_.1), channel_id=1, source_target_pairs={{0,2},{2,0},{4,6},{6,4},{8,10},{10,8},{12,14},{14,12},{1,3},{3,1},... | collective-permute-start | bytes 4718600 | tf_op jit(solution)/shard_map/ppermute | solution.py:315
  14.1 1.5 collective-permute-start.3
  15.6 55.8 %collective-permute-done.refs_2_ = bf16[384,2048]{1,0:T(8,128)(2,1)} collective-permute-done((bf16[384,2048]{1,0:T(8,128)(2,1)}, bf16[384,2048]{1,0:T(8,128)(2,1)}, u32[]{:S(2)}, u32[]{:S(2)}) %collective-permute-start) | collective-permute-done | bytes 1572896 | tf_op jit(solution)/shard_map/ppermute | solution.py:315
  72.5 1.4 pack_queries.1
  75.6 1.9 %slice.12 = bf16[384,640]{1,0:T(8,128)(2,1)} slice(bf16[384,2048]{1,0:T(8,128)(2,1)} %collective-permute-done.refs_2_), slice={[0:384], [1408:2048]} | slice | bytes 983040 | tf_op jit(solution)/shard_map/slice | solution.py:349
  77.5 5.2 %collective-permute-done.3.refs_4_ = bf16[384,2048]{1,0:T(8,128)(2,1)} collective-permute-done((bf16[384,2048]{1,0:T(8,128)(2,1)}, bf16[384,2048]{1,0:T(8,128)(2,1)}, u32[]{:S(2)}, u32[]{:S(2)}) %collective-permute-start.3) | collective-permute-done | bytes 1572896 | tf_op jit(solution)/shard_map/ppermute | solution.py:315
  82.7 1.6 collective-permute-done.5.refs_3_
  84.3 1.4 slice.13
  86.2 1.6 collective-permute-start.11
  87.7 1.7 %collective-permute-start.8 = (bf16[384,640]{1,0:T(8,128)(2,1)}, bf16[384,640]{1,0:T(8,128)(2,1)S(1)}, u32[]{:S(2)}, u32[]{:S(2)}) collective-permute-start(bf16[384,640]{1,0:T(8,128)(2,1)} %slice.12), channel_id=1, source_target_pairs={{0,4},{2,6},{4,0},{6,2},{8,12},{10,14},{12,8},{14,10},{1,5},{3,7},... | collective-permute-start | bytes 1474568 | tf_op jit(solution)/shard_map/ppermute | solution.py:315
  89.5 2.4 %collective-permute-start.10 = (bf16[512,256]{1,0:T(8,128)(2,1)S(1)}, bf16[512,256]{1,0:T(8,128)(2,1)S(1)}, u32[]{:S(2)}, u32[]{:S(2)}) collective-permute-start(bf16[512,256]{1,0:T(8,128)(2,1)S(1)} %copy-done.10), channel_id=1, source_target_pairs={{0,12},{2,14},{4,8},{6,10},{8,4},{10,6},{12,0},{14,2},{1,13},{3,15... | collective-permute-start | bytes 786440 | tf_op jit(solution)/shard_map/ppermute | solution.py:315
  91.9 3.3 %stage.2.stream_ref.refs_0_ = bf16[3,384,4096]{2,1,0:T(8,128)(2,1)S(1)} custom-call(s32[4]{0:T(128)S(1)} %pad_add_fusion.place_ref, bf16[384,2048]{1,0:T(8,128)(2,1)S(1)} %copy-done.1, bf16[384,2048]{1,0:T(8,128)(2,1)S(1)} %copy-done.3, bf16[384,2048]{1,0:T(8,128)(2,1)} %collective-permute-done.refs_2_, bf16[384,2048]{1,0:T(8,128)(2,1)} %collective-permute-done.4.refs_3_, ...), custom_call_target="tpu_custom_call" | custom-call | bytes 18874368 | tf_op jit(solution)/shard_map/stage/pallas_call | solution.py:117
  95.2 3.0 %project.2 = (bf16[3,384,128]{2,1,0:T(8,128)(2,1)S(1)}, bf16[3,384,128]{2,1,0:T(8,128)(2,1)S(1)}, f32[3,128,128]{2,1,0:T(8,128)S(1)}, f32[128,128]{1,0:T(8,128)S(1)}) custom-call(bf16[3,384,4096]{2,1,0:T(8,128)(2,1)S(1)} %stage.2.stream_ref.refs_0_, bf16[4096,256]{1,0:T(8,128)(2,1)S(1)} %bitcast.7), custom_call_target="tpu_custom_call" | custom-call | flops 2415919104 | bytes 2097152 | tf_op jit(solution)/shard_map/project/pallas_call | solution.py:145
  98.2 11.6 %collective-permute-done.10.refs_5_ = bf16[512,256]{1,0:T(8,128)(2,1)S(1)} collective-permute-done((bf16[512,256]{1,0:T(8,128)(2,1)S(1)}, bf16[512,256]{1,0:T(8,128)(2,1)S(1)}, u32[]{:S(2)}, u32[]{:S(2)}) %collective-permute-start.10) | collective-permute-done | bytes 262176 | tf_op jit(solution)/shard_map/ppermute | solution.py:315
  109.8 4.8 %collective-permute-done.9.refs_4_ = bf16[512,256]{1,0:T(8,128)(2,1)S(1)} collective-permute-done((bf16[512,256]{1,0:T(8,128)(2,1)S(1)}, bf16[512,256]{1,0:T(8,128)(2,1)S(1)}, u32[]{:S(2)}, u32[]{:S(2)}) %collective-permute-start.9) | collective-permute-done | bytes 262176 | tf_op jit(solution)/shard_map/ppermute | solution.py:315
  116.9 2.4 %collective-permute-start.15 = (bf16[512,256]{1,0:T(8,128)(2,1)S(1)}, bf16[512,256]{1,0:T(8,128)(2,1)S(1)}, u32[]{:S(2)}, u32[]{:S(2)}) collective-permute-start(bf16[512,256]{1,0:T(8,128)(2,1)S(1)} %copy-done.8), channel_id=1, source_target_pairs={{0,14},{2,12},{4,10},{6,8},{8,6},{10,4},{12,2},{14,0},{1,15},{3,13... | collective-permute-start | bytes 786440 | tf_op jit(solution)/shard_map/ppermute | solution.py:315
  120.0 2.1 %collective-permute-start.14 = (bf16[512,256]{1,0:T(8,128)(2,1)S(1)}, bf16[512,256]{1,0:T(8,128)(2,1)S(1)}, u32[]{:S(2)}, u32[]{:S(2)}) collective-permute-start(bf16[512,256]{1,0:T(8,128)(2,1)S(1)} %copy-done.8), channel_id=1, source_target_pairs={{0,6},{2,4},{4,2},{6,0},{8,14},{10,12},{12,10},{14,8},{1,7},{3,5},... | collective-permute-start | bytes 786440 | tf_op jit(solution)/shard_map/ppermute | solution.py:315
  123.1 2.3 %begin.3.refs_3_ = f32[4,384,256]{2,1,0:T(8,128)S(1)} custom-call(s32[4]{0:T(128)S(1)} %pad_add_fusion.place_ref, bf16[3,384,4096]{2,1,0:T(8,128)(2,1)S(1)} %stage.2.stream_ref.refs_0_, bf16[1,384,4096]{2,1,0:T(8,128)(2,1)S(1)} %stage.3.refs_1_.stream_ref, bf16[2048,256]{1,0:T(8,128)(2,1)S(1)} %collective-permute-done.11.refs_2_), custom_call_target="tpu_custom_call" | custom-call | flops 1610612736 | bytes 2097152 | tf_op jit(solution)/shard_map/begin/pallas_call | solution.py:185
  125.4 2.3 %begin.4.refs_4_ = f32[4,384,256]{2,1,0:T(8,128)S(1)} custom-call(s32[4]{0:T(128)S(1)} %pad_add_fusion.place_ref, bf16[3,384,4096]{2,1,0:T(8,128)(2,1)S(1)} %stage.2.stream_ref.refs_0_, bf16[1,384,4096]{2,1,0:T(8,128)(2,1)S(1)} %stage.3.refs_1_.stream_ref, bf16[512,256]{1,0:T(8,128)(2,1)S(1)} %get-tuple-element.100.refs_2_, ...), custom_call_target="tpu_custom_call" | custom-call | flops 1610612736 | bytes 2097152 | tf_op jit(solution)/shard_map/begin/pallas_call | solution.py:185
  129.0 8.6 %collective-permute-done.17.refs_3_ = bf16[512,256]{1,0:T(8,128)(2,1)S(1)} collective-permute-done((bf16[512,256]{1,0:T(8,128)(2,1)}, bf16[512,256]{1,0:T(8,128)(2,1)S(1)}, u32[]{:S(2)}, u32[]{:S(2)}) %collective-permute-start.17) | collective-permute-done | bytes 262176 | tf_op jit(solution)/shard_map/ppermute | solution.py:315
  137.7 2.7 %collective-permute-done.18.refs_2_ = bf16[2048,256]{1,0:T(8,128)(2,1)S(1)} collective-permute-done((bf16[2048,256]{1,0:T(8,128)(2,1)S(1)}, bf16[2048,256]{1,0:T(8,128)(2,1)S(1)}, u32[]{:S(2)}, u32[]{:S(2)}) %collective-permute-start.18) | collective-permute-done | bytes 1048608 | tf_op jit(solution)/shard_map/ppermute | solution.py:318
  140.4 2.7 %keys_values.1 = (bf16[4,384,128]{2,1,0:T(8,128)(2,1)S(1)}, bf16[4,384,128]{2,1,0:T(8,128)(2,1)S(1)}, f32[4,128,128]{2,1,0:T(8,128)S(1)}, f32[2,128,128]{2,1,0:T(8,128)S(1)}) custom-call(s32[4]{0:T(128)S(1)} %pad_add_fusion.place_ref, bf16[3,384,4096]{2,1,0:T(8,128)(2,1)S(1)} %stage.2.stream_ref.refs_0_, bf16[1,384,4096]{2,1,0:T(8,128)(2,1)S(1)} %stage.3.refs_1_.stream_ref, ...), custom_call_target="tpu_custom_call" | custom-call | flops 1610612736 | bytes 2097152 | tf_op jit(solution)/shard_map/keys_values/pallas_call | solution.py:185
  143.1 2.5 %collective-permute-start.19 = (f32[2,128,128]{2,1,0:T(8,128)S(1)}, f32[2,128,128]{2,1,0:T(8,128)S(1)}, u32[]{:S(2)}, u32[]{:S(2)}) collective-permute-start(f32[2,128,128]{2,1,0:T(8,128)S(1)} %get-tuple-element.123), channel_id=1, source_target_pairs={{0,8},{2,10},{4,12},{6,14},{1,9},{3,11},{5,13},{7,15},{16,24},{18,... | collective-permute-start | bytes 393224 | tf_op jit(solution)/shard_map/ppermute | solution.py:295
  145.6 1.5 begin.5.refs_4_
  147.1 1.8 %queries.1.query_ref = bf16[4,384,256]{2,1,0:T(8,128)(2,1)S(1)} custom-call(s32[4]{0:T(128)S(1)} %pad_add_fusion.place_ref, bf16[3,384,4096]{2,1,0:T(8,128)(2,1)S(1)} %stage.2.stream_ref.refs_0_, bf16[1,384,4096]{2,1,0:T(8,128)(2,1)S(1)} %stage.3.refs_1_.stream_ref, bf16[512,256]{1,0:T(8,128)(2,1)S(1)} %collective-permute-done.14.refs_2_, ...), custom_call_target="tpu_custom_call" | custom-call | flops 805306368 | bytes 2097152 | tf_op jit(solution)/shard_map/queries/pallas_call | solution.py:185
  150.2 4.3 %collective-permute-start.22 = (bf16[384,256]{1,0:T(8,128)(2,1)S(1)}, bf16[384,256]{1,0:T(8,128)(2,1)S(1)}, u32[]{:S(2)}, u32[]{:S(2)}) collective-permute-start(bf16[384,256]{1,0:T(8,128)(2,1)S(1)} %attend.5), channel_id=1, source_target_pairs={{0,6},{2,4},{4,2},{6,0},{8,14},{10,12},{12,10},{14,8},{1,7},{3,5},... | collective-permute-start | bytes 589832 | tf_op jit(solution)/shard_map/ppermute | solution.py:315
  154.4 1.6 attend.4
  157.8 4.0 %stage_rows.1 = (bf16[4,256,2048]{2,1,0:T(8,128)(2,1)S(1)}, bf16[4,256,2048]{2,1,0:T(8,128)(2,1)S(1)}) custom-call(s32[4]{0:T(128)S(1)} %pad_add_fusion.place_ref, bf16[1024,4096]{1,0:T(8,128)(2,1)} %out_ref.1, bf16[1024,4096]{1,0:T(8,128)(2,1)} %collective-permute-done.2.far_ref), custom_call_target="tpu_custom_call" | custom-call | bytes 16777216 | tf_op jit(solution)/shard_map/stage_rows/pallas_call | solution.py:89
  161.9 1.8 %collective-permute-done.20.refs_1_ = bf16[384,256]{1,0:T(8,128)(2,1)S(1)} collective-permute-done((bf16[384,256]{1,0:T(8,128)(2,1)S(1)}, bf16[384,256]{1,0:T(8,128)(2,1)S(1)}, u32[]{:S(2)}, u32[]{:S(2)}) %collective-permute-start.20) | collective-permute-done | bytes 196640 | tf_op jit(solution)/shard_map/ppermute | solution.py:315
  164.7 1.8 %add_features.2.refs_5_ = f32[384,2048]{1,0:T(8,128)S(1)} custom-call(bf16[384,256]{1,0:T(8,128)(2,1)S(1)} %attend.3.refs_0_, bf16[384,256]{1,0:T(8,128)(2,1)S(1)} %collective-permute-done.20.refs_1_, bf16[384,256]{1,0:T(8,128)(2,1)S(1)} %collective-permute-done.21.refs_2_, bf16[384,256]{1,0:T(8,128)(2,1)S(1)} %collective-permute-done.22.refs_3_, ...), custom_call_target="tpu_custom_call" | custom-call | flops 1610612736 | bytes 8388608 | tf_op jit(solution)/shard_map/add_features/pallas_call | solution.py:289
  166.6 2.9 %add_features.3 = bf16[384,2048]{1,0:T(8,128)(2,1)} custom-call(bf16[384,256]{1,0:T(8,128)(2,1)S(1)} %collective-permute-done.23.refs_0_, bf16[384,256]{1,0:T(8,128)(2,1)S(1)} %collective-permute-done.24.refs_1_, bf16[384,256]{1,0:T(8,128)(2,1)S(1)} %collective-permute-done.25.refs_2_, bf16[384,256]{1,0:T(8,128)(2,1)S(1)} %collective-permute-done.26.refs_3_, ...), custom_call_target="tpu_custom_call" | custom-call | flops 1610612736 | bytes 8388608 | tf_op jit(solution)/shard_map/add_features/pallas_call | solution.py:289
  (68 shorter events, 17.6 us)
Async XLA Ops:
  0.0 72.5 %collective-permute-start.2 = (bf16[1024,4096]{1,0:T(8,128)(2,1)}, bf16[1024,4096]{1,0:T(8,128)(2,1)}, u32[]{:S(2)}, u32[]{:S(2)}) collective-permute-start(bf16[1024,4096]{1,0:T(8,128)(2,1)} %out_ref.1), channel_id=1, source_target_pairs={{0,1},{1,0},{2,3},{3,2},{4,5},{5,4},{6,7},{7,6},{8,9},{9,8},{10,11... | collective-permute-start | bytes 25165832 | tf_op jit(solution)/shard_map/ppermute | solution.py:321
  5.1 67.4 %copy-start.6 = (bf16[512,1024]{1,0:T(8,128)(2,1)S(1)}, bf16[512,1024]{1,0:T(8,128)(2,1)}, u32[]{:S(2)}) copy-start(bf16[512,1024]{1,0:T(8,128)(2,1)} %query_ref) | copy-start | bytes 3145732
  5.1 77.5 %all-to-all-start = ((bf16[8,512,256]{2,1,0:T(8,128)(2,1)}), bf16[8,512,256]{2,1,0:T(8,128)(2,1)S(1)}, u32[]{:S(2)}, u32[]{:S(2)}) async-start(bf16[8,512,256]{2,1,0:T(8,128)(2,1)} %bitcast.10), calls=%async_computation | async-start | bytes 4194304 | tf_op jit(solution)/shard_map/all_to_all | solution.py:324
  12.1 59.3 %collective-permute-start = (bf16[384,2048]{1,0:T(8,128)(2,1)}, bf16[384,2048]{1,0:T(8,128)(2,1)}, u32[]{:S(2)}, u32[]{:S(2)}) collective-permute-start(bf16[384,2048]{1,0:T(8,128)(2,1)} %refs_0_.1), channel_id=1, source_target_pairs={{0,2},{2,0},{4,6},{6,4},{8,10},{10,8},{12,14},{14,12},{1,3},{3,1},... | collective-permute-start | bytes 4718600 | tf_op jit(solution)/shard_map/ppermute | solution.py:315
  14.1 57.3 %collective-permute-start.1 = (bf16[384,2048]{1,0:T(8,128)(2,1)}, bf16[384,2048]{1,0:T(8,128)(2,1)S(1)}, u32[]{:S(2)}, u32[]{:S(2)}) collective-permute-start(bf16[384,2048]{1,0:T(8,128)(2,1)} %refs_0_.1), channel_id=1, source_target_pairs={{0,1},{1,0},{2,3},{3,2},{4,5},{5,4},{6,7},{7,6},{8,9},{9,8},{10,11... | collective-permute-start | bytes 4718600 | tf_op jit(solution)/shard_map/ppermute | solution.py:321
  14.1 68.6 %collective-permute-start.3 = (bf16[384,2048]{1,0:T(8,128)(2,1)}, bf16[384,2048]{1,0:T(8,128)(2,1)}, u32[]{:S(2)}, u32[]{:S(2)}) collective-permute-start(bf16[384,2048]{1,0:T(8,128)(2,1)} %refs_0_.1), channel_id=1, source_target_pairs={{0,4},{2,6},{4,0},{6,2},{8,12},{10,14},{12,8},{14,10},{1,5},{3,7},... | collective-permute-start | bytes 4718600 | tf_op jit(solution)/shard_map/ppermute | solution.py:315
  72.5 11.7 %collective-permute-start.4 = (bf16[384,2048]{1,0:T(8,128)(2,1)}, bf16[384,2048]{1,0:T(8,128)(2,1)}, u32[]{:S(2)}, u32[]{:S(2)}) collective-permute-start(bf16[384,2048]{1,0:T(8,128)(2,1)} %collective-permute-done.refs_2_), channel_id=1, source_target_pairs={{0,1},{1,0},{2,3},{3,2},{4,5},{5,4},{6,7},{7,6},{8,9},{9,8},{10,11... | collective-permute-start | bytes 4718600 | tf_op jit(solution)/shard_map/ppermute | solution.py:321
  75.3 8.9 %collective-permute-start.5 = (bf16[512,256]{1,0:T(8,128)(2,1)}, bf16[512,256]{1,0:T(8,128)(2,1)S(1)}, u32[]{:S(2)}, u32[]{:S(2)}) collective-permute-start(bf16[512,256]{1,0:T(8,128)(2,1)} %get-tuple-element.94), channel_id=1, source_target_pairs={{0,2},{2,0},{4,6},{6,4},{8,10},{10,8},{12,14},{14,12},{1,3},{3,1},... | collective-permute-start | bytes 786440 | tf_op jit(solution)/shard_map/ppermute | solution.py:315
  84.3 7.6 %collective-permute-start.6 = (bf16[384,2048]{1,0:T(8,128)(2,1)}, bf16[384,2048]{1,0:T(8,128)(2,1)S(1)}, u32[]{:S(2)}, u32[]{:S(2)}) collective-permute-start(bf16[384,2048]{1,0:T(8,128)(2,1)} %collective-permute-done.3.refs_4_), channel_id=1, source_target_pairs={{0,1},{1,0},{2,3},{3,2},{4,5},{5,4},{6,7},{7,6},{8,9},{9,8},{10,11... | collective-permute-start | bytes 4718600 | tf_op jit(solution)/shard_map/ppermute | solution.py:321
  84.3 7.6 %copy-start.3 = (bf16[384,2048]{1,0:T(8,128)(2,1)S(1)}, bf16[384,2048]{1,0:T(8,128)(2,1)}, u32[]{:S(2)}) copy-start(bf16[384,2048]{1,0:T(8,128)(2,1)} %copy-done.2) | copy-start | bytes 4718596
  85.7 6.1 %copy-start.1 = (bf16[384,2048]{1,0:T(8,128)(2,1)S(1)}, bf16[384,2048]{1,0:T(8,128)(2,1)}, u32[]{:S(2)}) copy-start(bf16[384,2048]{1,0:T(8,128)(2,1)} %refs_0_.1) | copy-start | bytes 4718596
  85.7 28.9 %collective-permute-start.7 = (bf16[384,1408]{1,0:T(8,128)(2,1)S(1)}, bf16[384,1408]{1,0:T(8,128)(2,1)S(1)}, u32[]{:S(2)}, u32[]{:S(2)}) collective-permute-start(bf16[384,1408]{1,0:T(8,128)(2,1)S(1)} %slice.13), channel_id=1, source_target_pairs={{0,2},{2,0},{4,6},{6,4},{8,10},{10,8},{12,14},{14,12},{1,3},{3,1},... | collective-permute-start | bytes 3244040 | tf_op jit(solution)/shard_map/ppermute | solution.py:315
  86.2 28.5 %collective-permute-start.11 = (bf16[2048,256]{1,0:T(8,128)(2,1)S(1)}, bf16[2048,256]{1,0:T(8,128)(2,1)S(1)}, u32[]{:S(2)}, u32[]{:S(2)}) collective-permute-start(bf16[2048,256]{1,0:T(8,128)(2,1)S(1)} %slice.14), channel_id=1, source_target_pairs={{0,16},{16,0},{1,17},{17,1},{2,18},{18,2},{3,19},{19,3},{4,20},{20... | collective-permute-start | bytes 3145736 | tf_op jit(solution)/shard_map/ppermute | solution.py:318
  87.7 26.9 %collective-permute-start.8 = (bf16[384,640]{1,0:T(8,128)(2,1)}, bf16[384,640]{1,0:T(8,128)(2,1)S(1)}, u32[]{:S(2)}, u32[]{:S(2)}) collective-permute-start(bf16[384,640]{1,0:T(8,128)(2,1)} %slice.12), channel_id=1, source_target_pairs={{0,4},{2,6},{4,0},{6,2},{8,12},{10,14},{12,8},{14,10},{1,5},{3,7},... | collective-permute-start | bytes 1474568 | tf_op jit(solution)/shard_map/ppermute | solution.py:315
  89.5 20.4 %collective-permute-start.10 = (bf16[512,256]{1,0:T(8,128)(2,1)S(1)}, bf16[512,256]{1,0:T(8,128)(2,1)S(1)}, u32[]{:S(2)}, u32[]{:S(2)}) collective-permute-start(bf16[512,256]{1,0:T(8,128)(2,1)S(1)} %copy-done.10), channel_id=1, source_target_pairs={{0,12},{2,14},{4,8},{6,10},{8,4},{10,6},{12,0},{14,2},{1,13},{3,15... | collective-permute-start | bytes 786440 | tf_op jit(solution)/shard_map/ppermute | solution.py:315
  91.8 22.8 %collective-permute-start.9 = (bf16[512,256]{1,0:T(8,128)(2,1)S(1)}, bf16[512,256]{1,0:T(8,128)(2,1)S(1)}, u32[]{:S(2)}, u32[]{:S(2)}) collective-permute-start(bf16[512,256]{1,0:T(8,128)(2,1)S(1)} %get-tuple-element.100.refs_2_), channel_id=1, source_target_pairs={{0,8},{2,10},{4,12},{6,14},{8,0},{10,2},{12,4},{14,6},{1,9},{3,11}... | collective-permute-start | bytes 786440 | tf_op jit(solution)/shard_map/ppermute | solution.py:315
  98.2 18.8 %copy-start.8 = (bf16[512,256]{1,0:T(8,128)(2,1)S(1)}, bf16[512,256]{1,0:T(8,128)(2,1)}, u32[]{:S(2)}) copy-start(bf16[512,256]{1,0:T(8,128)(2,1)} %copy-done.7) | copy-start | bytes 786436
  114.6 4.8 %collective-permute-start.12 = (bf16[384,1408]{1,0:T(8,128)(2,1)S(1)}, bf16[384,1408]{1,0:T(8,128)(2,1)S(1)}, u32[]{:S(2)}, u32[]{:S(2)}) collective-permute-start(bf16[384,1408]{1,0:T(8,128)(2,1)S(1)} %collective-permute-done.7.refs_0_), channel_id=1, source_target_pairs={{0,1},{1,0},{2,3},{3,2},{4,5},{5,4},{6,7},{7,6},{8,9},{9,8},{10,11... | collective-permute-start | bytes 3244040 | tf_op jit(solution)/shard_map/ppermute | solution.py:321
  114.8 25.6 %collective-permute-start.18 = (bf16[2048,256]{1,0:T(8,128)(2,1)S(1)}, bf16[2048,256]{1,0:T(8,128)(2,1)S(1)}, u32[]{:S(2)}, u32[]{:S(2)}) collective-permute-start(bf16[2048,256]{1,0:T(8,128)(2,1)S(1)} %slice.15), channel_id=1, source_target_pairs={{0,16},{16,0},{1,17},{17,1},{2,18},{18,2},{3,19},{19,3},{4,20},{20... | collective-permute-start | bytes 3145736 | tf_op jit(solution)/shard_map/ppermute | solution.py:318
  115.4 4.7 %collective-permute-start.13 = (bf16[384,640]{1,0:T(8,128)(2,1)S(1)}, bf16[384,640]{1,0:T(8,128)(2,1)S(1)}, u32[]{:S(2)}, u32[]{:S(2)}) collective-permute-start(bf16[384,640]{1,0:T(8,128)(2,1)S(1)} %collective-permute-done.8.refs_2_), channel_id=1, source_target_pairs={{0,1},{1,0},{2,3},{3,2},{4,5},{5,4},{6,7},{7,6},{8,9},{9,8},{10,11... | collective-permute-start | bytes 1474568 | tf_op jit(solution)/shard_map/ppermute | solution.py:321
  115.6 22.1 %collective-permute-start.17 = (bf16[512,256]{1,0:T(8,128)(2,1)}, bf16[512,256]{1,0:T(8,128)(2,1)S(1)}, u32[]{:S(2)}, u32[]{:S(2)}) collective-permute-start(bf16[512,256]{1,0:T(8,128)(2,1)} %get-tuple-element.94), channel_id=1, source_target_pairs={{0,10},{2,8},{4,14},{6,12},{8,2},{10,0},{12,6},{14,4},{1,11},{3,9}... | collective-permute-start | bytes 786440 | tf_op jit(solution)/shard_map/ppermute | solution.py:315
  116.9 30.2 %collective-permute-start.15 = (bf16[512,256]{1,0:T(8,128)(2,1)S(1)}, bf16[512,256]{1,0:T(8,128)(2,1)S(1)}, u32[]{:S(2)}, u32[]{:S(2)}) collective-permute-start(bf16[512,256]{1,0:T(8,128)(2,1)S(1)} %copy-done.8), channel_id=1, source_target_pairs={{0,14},{2,12},{4,10},{6,8},{8,6},{10,4},{12,2},{14,0},{1,15},{3,13... | collective-permute-start | bytes 786440 | tf_op jit(solution)/shard_map/ppermute | solution.py:315
  119.4 21.0 %collective-permute-start.16 = (bf16[512,256]{1,0:T(8,128)(2,1)S(1)}, bf16[512,256]{1,0:T(8,128)(2,1)S(1)}, u32[]{:S(2)}, u32[]{:S(2)}) collective-permute-start(bf16[512,256]{1,0:T(8,128)(2,1)S(1)} %copy-done.10), channel_id=1, source_target_pairs={{0,4},{2,6},{4,0},{6,2},{8,12},{10,14},{12,8},{14,10},{1,5},{3,7},... | collective-permute-start | bytes 786440 | tf_op jit(solution)/shard_map/ppermute | solution.py:315
  120.0 27.1 %collective-permute-start.14 = (bf16[512,256]{1,0:T(8,128)(2,1)S(1)}, bf16[512,256]{1,0:T(8,128)(2,1)S(1)}, u32[]{:S(2)}, u32[]{:S(2)}) collective-permute-start(bf16[512,256]{1,0:T(8,128)(2,1)S(1)} %copy-done.8), channel_id=1, source_target_pairs={{0,6},{2,4},{4,2},{6,0},{8,14},{10,12},{12,10},{14,8},{1,7},{3,5},... | collective-permute-start | bytes 786440 | tf_op jit(solution)/shard_map/ppermute | solution.py:315
  143.1 5.9 %collective-permute-start.19 = (f32[2,128,128]{2,1,0:T(8,128)S(1)}, f32[2,128,128]{2,1,0:T(8,128)S(1)}, u32[]{:S(2)}, u32[]{:S(2)}) collective-permute-start(f32[2,128,128]{2,1,0:T(8,128)S(1)} %get-tuple-element.123), channel_id=1, source_target_pairs={{0,8},{2,10},{4,12},{6,14},{1,9},{3,11},{5,13},{7,15},{16,24},{18,... | collective-permute-start | bytes 393224 | tf_op jit(solution)/shard_map/ppermute | solution.py:295
  150.2 11.7 %collective-permute-start.22 = (bf16[384,256]{1,0:T(8,128)(2,1)S(1)}, bf16[384,256]{1,0:T(8,128)(2,1)S(1)}, u32[]{:S(2)}, u32[]{:S(2)}) collective-permute-start(bf16[384,256]{1,0:T(8,128)(2,1)S(1)} %attend.5), channel_id=1, source_target_pairs={{0,6},{2,4},{4,2},{6,0},{8,14},{10,12},{12,10},{14,8},{1,7},{3,5},... | collective-permute-start | bytes 589832 | tf_op jit(solution)/shard_map/ppermute | solution.py:315
  156.0 7.7 %collective-permute-start.20 = (bf16[384,256]{1,0:T(8,128)(2,1)S(1)}, bf16[384,256]{1,0:T(8,128)(2,1)S(1)}, u32[]{:S(2)}, u32[]{:S(2)}) collective-permute-start(bf16[384,256]{1,0:T(8,128)(2,1)S(1)} %get-tuple-element.129), channel_id=1, source_target_pairs={{0,2},{2,0},{4,6},{6,4},{8,10},{10,8},{12,14},{14,12},{1,3},{3,1},... | collective-permute-start | bytes 589832 | tf_op jit(solution)/shard_map/ppermute | solution.py:315
  156.6 7.1 %collective-permute-start.21 = (bf16[384,256]{1,0:T(8,128)(2,1)S(1)}, bf16[384,256]{1,0:T(8,128)(2,1)S(1)}, u32[]{:S(2)}, u32[]{:S(2)}) collective-permute-start(bf16[384,256]{1,0:T(8,128)(2,1)S(1)} %get-tuple-element.130), channel_id=1, source_target_pairs={{0,4},{2,6},{4,0},{6,2},{8,12},{10,14},{12,8},{14,10},{1,5},{3,7},... | collective-permute-start | bytes 589832 | tf_op jit(solution)/shard_map/ppermute | solution.py:315
  163.7 2.8 %collective-permute-start.23 = (bf16[384,256]{1,0:T(8,128)(2,1)S(1)}, bf16[384,256]{1,0:T(8,128)(2,1)S(1)}, u32[]{:S(2)}, u32[]{:S(2)}) collective-permute-start(bf16[384,256]{1,0:T(8,128)(2,1)S(1)} %attend.3.refs_0_), channel_id=1, source_target_pairs={{0,1},{1,0},{2,3},{3,2},{4,5},{5,4},{6,7},{7,6},{8,9},{9,8},{10,11... | collective-permute-start | bytes 589832 | tf_op jit(solution)/shard_map/ppermute | solution.py:321
  163.7 2.8 %collective-permute-start.24 = (bf16[384,256]{1,0:T(8,128)(2,1)S(1)}, bf16[384,256]{1,0:T(8,128)(2,1)S(1)}, u32[]{:S(2)}, u32[]{:S(2)}) collective-permute-start(bf16[384,256]{1,0:T(8,128)(2,1)S(1)} %collective-permute-done.20.refs_1_), channel_id=1, source_target_pairs={{0,1},{1,0},{2,3},{3,2},{4,5},{5,4},{6,7},{7,6},{8,9},{9,8},{10,11... | collective-permute-start | bytes 589832 | tf_op jit(solution)/shard_map/ppermute | solution.py:321
  164.2 2.3 %collective-permute-start.25 = (bf16[384,256]{1,0:T(8,128)(2,1)S(1)}, bf16[384,256]{1,0:T(8,128)(2,1)S(1)}, u32[]{:S(2)}, u32[]{:S(2)}) collective-permute-start(bf16[384,256]{1,0:T(8,128)(2,1)S(1)} %collective-permute-done.21.refs_2_), channel_id=1, source_target_pairs={{0,1},{1,0},{2,3},{3,2},{4,5},{5,4},{6,7},{7,6},{8,9},{9,8},{10,11... | collective-permute-start | bytes 589832 | tf_op jit(solution)/shard_map/ppermute | solution.py:321
  164.2 2.3 %collective-permute-start.26 = (bf16[384,256]{1,0:T(8,128)(2,1)S(1)}, bf16[384,256]{1,0:T(8,128)(2,1)S(1)}, u32[]{:S(2)}, u32[]{:S(2)}) collective-permute-start(bf16[384,256]{1,0:T(8,128)(2,1)S(1)} %collective-permute-done.22.refs_3_), channel_id=1, source_target_pairs={{0,1},{1,0},{2,3},{3,2},{4,5},{5,4},{6,7},{7,6},{8,9},{9,8},{10,11... | collective-permute-start | bytes 589832 | tf_op jit(solution)/shard_map/ppermute | solution.py:321
  (7 other events, 10.1 us)

commit v18 on v17

--- a/solution.py
+++ b/solution.py
@@ -86,7 +86,7 @@
 
     shapes = [pltpu.VMEM((SUB, depth, half), BF16)] * 2
     sems = pltpu.SemaphoreType.DMA((2 * SUB,))
-    return call(kernel, "stage_rows", shapes, [SMEM, ANY, ANY], [VMEM] * 2, 40, 0, rows * width * 4, [sems])(
+    return call(kernel, "stage_rows", shapes, [SMEM, ANY, ANY], [VMEM] * 2, 28, 0, rows * width * 4, [sems])(
         place, w_out, w_far
     )
 
@@ -372,12 +372,14 @@
 
     streams = [near, corner]
     last = project(corner, kv_mine, first[3])
+    last, w_far = ob((last, w_far))
+    w_rows = stage_rows(place, w_out, w_far)
     kv_base = begin(place, streams, [(kv_upper, 0)])
     if pieced:
         early = (0, 1, 4, 6)
         q_base = begin(place, streams, [(arrived[m], (m,)) for m in early])
         latest = {m: arrived.pop(m) for m in (3, 7)}
-        arrived, kv_lower, kv_base, q_base = ob((arrived, kv_lower, kv_base, q_base))
+        arrived, kv_lower, kv_base, q_base, w_rows = ob((arrived, kv_lower, kv_base, q_base, w_rows))
         q_base = begin(place, streams, [(arrived[m], (m,)) for m in sorted(arrived) if m not in early], q_base)
         q_parts = [(piece, (m,)) for m, piece in latest.items()]
     else:
@@ -388,9 +390,7 @@
     query = queries(place, streams, q_parts, q_base)
     normed = [n for blocks in ((3,), (1, 2), (0,)) for n in attend(place, blocks, query, heads, carried)]
     normed = [normed[3], xor(normed[1], 1), xor(normed[2], 2), xor(normed[0], 3)]
-    home_0, w_far = lax.optimization_barrier((normed[0], w_far))
-    out_keep, out_far = stage_rows(place, w_out, w_far)
-    out_keep, out_far, *normed = lax.optimization_barrier((out_keep, out_far, home_0, *normed[1:]))
+    out_keep, out_far = w_rows
     partial = add_features(normed, out_keep)
     return add_features([other_core(n) for n in normed], out_far, partial)
 

time: 170 us -> 175 us (1.029)
  local copies, waits for them, and re-layouts: 9.81 us -> 12.8 us
    unnamed x22 -> x30, local copies, waits for them, and re-layouts: 6.34 us -> 9.2 us
    pallas_call x5, Pallas kernels: 10.7 us -> 12.5 us  [run_blocks(): call(body, name, out_shape, specs, outs, LIMIT, flops, 2 * MIB)]
  transfers between devices with their start and end apart: 28 -> 28, of which waited for: 8 -> 10; matrix products, arithmetic and copies ran while one was open for 2% -> 2% of each run, Pallas kernels for 18% -> 17%
where the time goes in v18:
time: 175 us; the launch traced here: 174 us
  waiting for transfers between devices  93.6 us (53%)
  Pallas kernels  35 us (20%)
  starting transfers between devices  32.5 us (19%)
  local copies, waits for them, and re-layouts  12.8 us (7%)
    ppermute x14, waiting for transfers between devices, xor(): return lax.ppermute(value, 'ctx', [(i, i ^ step) for i in range(n_ctx)])  90.8 us
    ppermute x14, starting transfers between devices, xor(): return lax.ppermute(value, 'ctx', [(i, i ^ step) for i in range(n_ctx)])  20.3 us
    pallas_call x5, Pallas kernels, run_blocks(): call(body, name, out_shape, specs, outs, LIMIT, flops, 2 * MIB)  12.5 us
    unnamed x30, local copies, waits for them, and re-layouts  9.2 us
    all_to_all x1, starting transfers between devices, spread(): return lax.all_to_all(packed, 'ctx', 0, 0, tiled=True)  6.93 us
    pallas_call x2, Pallas kernels, add_features(): call(kernel, 'add_features', shape, [VMEM] * len(args), VMEM, LIMIT, flop...  4.72 us
    pallas_call x2, Pallas kernels, stage(): call(kernel, 'stage', shape, [SMEM] + [ANY] * count, VMEM, 20 if blocks >...  4.24 us
    pallas_call x2, Pallas kernels, project(): call(kernel, 'project', shapes, [VMEM] * len(args), [VMEM] * 4, LIMIT, fl...  4.24 us
  transfers between devices with their start and end apart: 28, of which 10 were waited for; matrix products, arithmetic and copies ran while one was open for 2% of the time, Pallas kernels for 17%

profile of v18, /device:TPU:0, one launch (start us, length us, event | category | flops | bytes accessed | tf_op | source)
XLA Modules:
  0.0 174.4 jit_solution(4613729459773127391)
XLA Ops:
  5.1 6.9 %all-to-all-start = ((bf16[8,512,256]{2,1,0:T(8,128)(2,1)}), bf16[8,512,256]{2,1,0:T(8,128)(2,1)S(1)}, u32[]{:S(2)}, u32[]{:S(2)}) async-start(bf16[8,512,256]{2,1,0:T(8,128)(2,1)} %bitcast.12), calls=%async_computation | async-start | bytes 4194304 | tf_op jit(solution)/shard_map/all_to_all | solution.py:324
  12.3 1.8 %collective-permute-start = (bf16[384,2048]{1,0:T(8,128)(2,1)}, bf16[384,2048]{1,0:T(8,128)(2,1)}, u32[]{:S(2)}, u32[]{:S(2)}) collective-permute-start(bf16[384,2048]{1,0:T(8,128)(2,1)} %refs_0_.1), channel_id=1, source_target_pairs={{0,2},{2,0},{4,6},{6,4},{8,10},{10,8},{12,14},{14,12},{1,3},{3,1},... | collective-permute-start | bytes 4718600 | tf_op jit(solution)/shard_map/ppermute | solution.py:315
  16.8 54.5 %collective-permute-done.refs_2_ = bf16[384,2048]{1,0:T(8,128)(2,1)} collective-permute-done((bf16[384,2048]{1,0:T(8,128)(2,1)}, bf16[384,2048]{1,0:T(8,128)(2,1)}, u32[]{:S(2)}, u32[]{:S(2)}) %collective-permute-start) | collective-permute-done | bytes 1572896 | tf_op jit(solution)/shard_map/ppermute | solution.py:315
  71.4 1.5 pack_queries.1
  74.3 8.4 %collective-permute-done.3.refs_4_ = bf16[384,2048]{1,0:T(8,128)(2,1)} collective-permute-done((bf16[384,2048]{1,0:T(8,128)(2,1)}, bf16[384,2048]{1,0:T(8,128)(2,1)}, u32[]{:S(2)}, u32[]{:S(2)}) %collective-permute-start.3) | collective-permute-done | bytes 1572896 | tf_op jit(solution)/shard_map/ppermute | solution.py:315
  84.2 1.5 collective-permute-start.7
  85.8 1.6 collective-permute-start.11
  87.4 1.5 collective-permute-start.8
  91.8 3.3 %stage.2.stream_ref.refs_0_ = bf16[3,384,4096]{2,1,0:T(8,128)(2,1)S(1)} custom-call(s32[4]{0:T(128)S(1)} %pad_add_fusion.place_ref, bf16[384,2048]{1,0:T(8,128)(2,1)S(1)} %copy-done.7, bf16[384,2048]{1,0:T(8,128)(2,1)S(1)} %copy-done.9, bf16[384,2048]{1,0:T(8,128)(2,1)} %collective-permute-done.refs_2_, bf16[384,2048]{1,0:T(8,128)(2,1)} %collective-permute-done.4.refs_3_, ...), custom_call_target="tpu_custom_call" | custom-call | bytes 18874368 | tf_op jit(solution)/shard_map/stage/pallas_call | solution.py:117
  95.1 3.0 %project.2 = (bf16[3,384,128]{2,1,0:T(8,128)(2,1)S(1)}, bf16[3,384,128]{2,1,0:T(8,128)(2,1)S(1)}, f32[3,128,128]{2,1,0:T(8,128)S(1)}, f32[128,128]{1,0:T(8,128)S(1)}) custom-call(bf16[3,384,4096]{2,1,0:T(8,128)(2,1)S(1)} %stage.2.stream_ref.refs_0_, bf16[4096,256]{1,0:T(8,128)(2,1)S(1)} %bitcast.7), custom_call_target="tpu_custom_call" | custom-call | flops 2415919104 | bytes 2097152 | tf_op jit(solution)/shard_map/project/pallas_call | solution.py:145
  98.1 8.1 %collective-permute-done.9.refs_4_ = bf16[512,256]{1,0:T(8,128)(2,1)S(1)} collective-permute-done((bf16[512,256]{1,0:T(8,128)(2,1)S(1)}, bf16[512,256]{1,0:T(8,128)(2,1)S(1)}, u32[]{:S(2)}, u32[]{:S(2)}) %collective-permute-start.9) | collective-permute-done | bytes 262176 | tf_op jit(solution)/shard_map/ppermute | solution.py:315
  106.2 7.5 %collective-permute-done.10.refs_5_ = bf16[512,256]{1,0:T(8,128)(2,1)S(1)} collective-permute-done((bf16[512,256]{1,0:T(8,128)(2,1)}, bf16[512,256]{1,0:T(8,128)(2,1)S(1)}, u32[]{:S(2)}, u32[]{:S(2)}) %collective-permute-start.10) | collective-permute-done | bytes 262176 | tf_op jit(solution)/shard_map/ppermute | solution.py:315
  115.6 2.4 %collective-permute-start.17 = (bf16[512,256]{1,0:T(8,128)(2,1)}, bf16[512,256]{1,0:T(8,128)(2,1)}, u32[]{:S(2)}, u32[]{:S(2)}) collective-permute-start(bf16[512,256]{1,0:T(8,128)(2,1)} %get-tuple-element.93), channel_id=1, source_target_pairs={{0,10},{2,8},{4,14},{6,12},{8,2},{10,0},{12,6},{14,4},{1,11},{3,9}... | collective-permute-start | bytes 786440 | tf_op jit(solution)/shard_map/ppermute | solution.py:315
  118.0 2.3 %collective-permute-start.15 = (bf16[512,256]{1,0:T(8,128)(2,1)}, bf16[512,256]{1,0:T(8,128)(2,1)}, u32[]{:S(2)}, u32[]{:S(2)}) collective-permute-start(bf16[512,256]{1,0:T(8,128)(2,1)} %get-tuple-element.98), channel_id=1, source_target_pairs={{0,14},{2,12},{4,10},{6,8},{8,6},{10,4},{12,2},{14,0},{1,15},{3,13... | collective-permute-start | bytes 786440 | tf_op jit(solution)/shard_map/ppermute | solution.py:315
  120.3 2.0 %collective-permute-start.16 = (bf16[512,256]{1,0:T(8,128)(2,1)}, bf16[512,256]{1,0:T(8,128)(2,1)}, u32[]{:S(2)}, u32[]{:S(2)}) collective-permute-start(bf16[512,256]{1,0:T(8,128)(2,1)} %get-tuple-element.101), channel_id=1, source_target_pairs={{0,4},{2,6},{4,0},{6,2},{8,12},{10,14},{12,8},{14,10},{1,5},{3,7},... | collective-permute-start | bytes 786440 | tf_op jit(solution)/shard_map/ppermute | solution.py:315
  123.3 2.3 %begin.3.refs_3_ = f32[4,384,256]{2,1,0:T(8,128)S(1)} custom-call(s32[4]{0:T(128)S(1)} %pad_add_fusion.place_ref, bf16[3,384,4096]{2,1,0:T(8,128)(2,1)S(1)} %stage.2.stream_ref.refs_0_, bf16[1,384,4096]{2,1,0:T(8,128)(2,1)S(1)} %stage.3.refs_1_.stream_ref, bf16[2048,256]{1,0:T(8,128)(2,1)S(1)} %collective-permute-done.11.refs_2_), custom_call_target="tpu_custom_call" | custom-call | flops 1610612736 | bytes 2097152 | tf_op jit(solution)/shard_map/begin/pallas_call | solution.py:185
  126.9 2.3 %begin.4.refs_4_ = f32[4,384,256]{2,1,0:T(8,128)S(1)} custom-call(s32[4]{0:T(128)S(1)} %pad_add_fusion.place_ref, bf16[3,384,4096]{2,1,0:T(8,128)(2,1)S(1)} %stage.2.stream_ref.refs_0_, bf16[1,384,4096]{2,1,0:T(8,128)(2,1)S(1)} %stage.3.refs_1_.stream_ref, bf16[512,256]{1,0:T(8,128)(2,1)S(1)} %get-tuple-element.99.refs_2_, ...), custom_call_target="tpu_custom_call" | custom-call | flops 1610612736 | bytes 2097152 | tf_op jit(solution)/shard_map/begin/pallas_call | solution.py:185
  131.7 3.0 %stage_rows.1 = (bf16[4,256,2048]{2,1,0:T(8,128)(2,1)S(1)}, bf16[4,256,2048]{2,1,0:T(8,128)(2,1)S(1)}) custom-call(s32[4]{0:T(128)S(1)} %pad_add_fusion.place_ref, bf16[1024,4096]{1,0:T(8,128)(2,1)S(1)} %bitcast.11, bf16[1024,4096]{1,0:T(8,128)(2,1)} %collective-permute-done.2.far_ref), custom_call_target="tpu_custom_call" | custom-call | bytes 16777216 | tf_op jit(solution)/shard_map/stage_rows/pallas_call | solution.py:89
  134.7 3.5 %collective-permute-done.17.refs_3_ = bf16[512,256]{1,0:T(8,128)(2,1)} collective-permute-done((bf16[512,256]{1,0:T(8,128)(2,1)}, bf16[512,256]{1,0:T(8,128)(2,1)}, u32[]{:S(2)}, u32[]{:S(2)}) %collective-permute-start.17) | collective-permute-done | bytes 262176 | tf_op jit(solution)/shard_map/ppermute | solution.py:315
  138.1 2.6 %collective-permute-done.18.refs_2_ = bf16[2048,256]{1,0:T(8,128)(2,1)} collective-permute-done((bf16[2048,256]{1,0:T(8,128)(2,1)}, bf16[2048,256]{1,0:T(8,128)(2,1)}, u32[]{:S(2)}, u32[]{:S(2)}) %collective-permute-start.18) | collective-permute-done | bytes 1048608 | tf_op jit(solution)/shard_map/ppermute | solution.py:318
  140.7 3.7 %collective-permute-done.16.refs_2_ = bf16[512,256]{1,0:T(8,128)(2,1)} collective-permute-done((bf16[512,256]{1,0:T(8,128)(2,1)}, bf16[512,256]{1,0:T(8,128)(2,1)}, u32[]{:S(2)}, u32[]{:S(2)}) %collective-permute-start.16) | collective-permute-done | bytes 262176 | tf_op jit(solution)/shard_map/ppermute | solution.py:315
  144.4 1.9 %copy-done.1 = bf16[1,384,4096]{2,1,0:T(8,128)(2,1)S(1)} copy-done((bf16[1,384,4096]{2,1,0:T(8,128)(2,1)S(1)}, bf16[1,384,4096]{2,1,0:T(8,128)(2,1)}, u32[]{:S(2)}) %copy-start.1) | copy-done | bytes 3145752
  146.3 3.5 %keys_values.1 = (bf16[4,384,128]{2,1,0:T(8,128)(2,1)S(1)}, bf16[4,384,128]{2,1,0:T(8,128)(2,1)S(1)}, f32[4,128,128]{2,1,0:T(8,128)S(1)}, f32[2,128,128]{2,1,0:T(8,128)S(1)}) custom-call(s32[4]{0:T(128)S(1)} %pad_add_fusion.place_ref, bf16[3,384,4096]{2,1,0:T(8,128)(2,1)S(1)} %stage.2.stream_ref.refs_0_, bf16[1,384,4096]{2,1,0:T(8,128)(2,1)S(1)} %copy-done.1, ...), custom_call_target="tpu_custom_call" | custom-call | flops 1610612736 | bytes 2097152 | tf_op jit(solution)/shard_map/keys_values/pallas_call | solution.py:185
  149.8 1.6 collective-permute-start.19
  151.4 2.0 %begin.5.refs_4_ = f32[4,384,256]{2,1,0:T(8,128)S(1)} custom-call(s32[4]{0:T(128)S(1)} %pad_add_fusion.place_ref, bf16[3,384,4096]{2,1,0:T(8,128)(2,1)S(1)} %stage.2.stream_ref.refs_0_, bf16[1,384,4096]{2,1,0:T(8,128)(2,1)S(1)} %copy-done.1, bf16[512,256]{1,0:T(8,128)(2,1)} %collective-permute-done.16.refs_2_, ...), custom_call_target="tpu_custom_call" | custom-call | flops 805306368 | bytes 2097152 | tf_op jit(solution)/shard_map/begin/pallas_call | solution.py:185
  153.5 2.3 %queries.1.query_ref = bf16[4,384,256]{2,1,0:T(8,128)(2,1)S(1)} custom-call(s32[4]{0:T(128)S(1)} %pad_add_fusion.place_ref, bf16[3,384,4096]{2,1,0:T(8,128)(2,1)S(1)} %stage.2.stream_ref.refs_0_, bf16[1,384,4096]{2,1,0:T(8,128)(2,1)S(1)} %copy-done.1, bf16[512,256]{1,0:T(8,128)(2,1)} %collective-permute-done.14.refs_2_, ...), custom_call_target="tpu_custom_call" | custom-call | flops 805306368 | bytes 2097152 | tf_op jit(solution)/shard_map/queries/pallas_call | solution.py:185
  155.8 1.6 attend.4
  158.9 2.5 %collective-permute-start.23 = (bf16[384,256]{1,0:T(8,128)(2,1)S(1)}, bf16[384,256]{1,0:T(8,128)(2,1)S(1)}, u32[]{:S(2)}, u32[]{:S(2)}) collective-permute-start(bf16[384,256]{1,0:T(8,128)(2,1)S(1)} %get-tuple-element.132), channel_id=1, source_target_pairs={{0,4},{2,6},{4,0},{6,2},{8,12},{10,14},{12,8},{14,10},{1,5},{3,7},... | collective-permute-start | bytes 589832 | tf_op jit(solution)/shard_map/ppermute | solution.py:315
  164.5 2.4 %collective-permute-done.23.refs_2_ = bf16[384,256]{1,0:T(8,128)(2,1)S(1)} collective-permute-done((bf16[384,256]{1,0:T(8,128)(2,1)S(1)}, bf16[384,256]{1,0:T(8,128)(2,1)S(1)}, u32[]{:S(2)}, u32[]{:S(2)}) %collective-permute-start.23) | collective-permute-done | bytes 196640 | tf_op jit(solution)/shard_map/ppermute | solution.py:315
  166.9 2.7 %collective-permute-done.25.refs_3_ = bf16[384,256]{1,0:T(8,128)(2,1)S(1)} collective-permute-done((bf16[384,256]{1,0:T(8,128)(2,1)S(1)}, bf16[384,256]{1,0:T(8,128)(2,1)S(1)}, u32[]{:S(2)}, u32[]{:S(2)}) %collective-permute-start.25) | collective-permute-done | bytes 196640 | tf_op jit(solution)/shard_map/ppermute | solution.py:315
  169.6 1.8 %add_features.2.refs_5_ = f32[384,2048]{1,0:T(8,128)S(1)} custom-call(bf16[384,256]{1,0:T(8,128)(2,1)S(1)} %attend.3.refs_0_, bf16[384,256]{1,0:T(8,128)(2,1)S(1)} %collective-permute-done.21.refs_1_, bf16[384,256]{1,0:T(8,128)(2,1)S(1)} %collective-permute-done.23.refs_2_, bf16[384,256]{1,0:T(8,128)(2,1)S(1)} %collective-permute-done.25.refs_3_, ...), custom_call_target="tpu_custom_call" | custom-call | flops 1610612736 | bytes 8388608 | tf_op jit(solution)/shard_map/add_features/pallas_call | solution.py:289
  171.4 2.9 %add_features.3 = bf16[384,2048]{1,0:T(8,128)(2,1)} custom-call(bf16[384,256]{1,0:T(8,128)(2,1)S(1)} %collective-permute-done.20.refs_0_, bf16[384,256]{1,0:T(8,128)(2,1)S(1)} %collective-permute-done.22.refs_1_, bf16[384,256]{1,0:T(8,128)(2,1)S(1)} %collective-permute-done.24.refs_2_, bf16[384,256]{1,0:T(8,128)(2,1)S(1)} %collective-permute-done.26.refs_3_, ...), custom_call_target="tpu_custom_call" | custom-call | flops 1610612736 | bytes 8388608 | tf_op jit(solution)/shard_map/add_features/pallas_call | solution.py:289
  (77 shorter events, 24.9 us)
Async XLA Ops:
  0.0 71.4 %collective-permute-start.2 = (bf16[1024,4096]{1,0:T(8,128)(2,1)}, bf16[1024,4096]{1,0:T(8,128)(2,1)}, u32[]{:S(2)}, u32[]{:S(2)}) collective-permute-start(bf16[1024,4096]{1,0:T(8,128)(2,1)} %out_ref.1), channel_id=1, source_target_pairs={{0,1},{1,0},{2,3},{3,2},{4,5},{5,4},{6,7},{7,6},{8,9},{9,8},{10,11... | collective-permute-start | bytes 25165832 | tf_op jit(solution)/shard_map/ppermute | solution.py:321
  5.1 66.3 %copy-start.12 = (bf16[512,1024]{1,0:T(8,128)(2,1)S(1)}, bf16[512,1024]{1,0:T(8,128)(2,1)}, u32[]{:S(2)}) copy-start(bf16[512,1024]{1,0:T(8,128)(2,1)} %query_ref) | copy-start | bytes 3145732
  5.1 77.5 %all-to-all-start = ((bf16[8,512,256]{2,1,0:T(8,128)(2,1)}), bf16[8,512,256]{2,1,0:T(8,128)(2,1)S(1)}, u32[]{:S(2)}, u32[]{:S(2)}) async-start(bf16[8,512,256]{2,1,0:T(8,128)(2,1)} %bitcast.12), calls=%async_computation | async-start | bytes 4194304 | tf_op jit(solution)/shard_map/all_to_all | solution.py:324
  12.1 3.6 %collective-permute-start.1 = (bf16[384,2048]{1,0:T(8,128)(2,1)}, bf16[384,2048]{1,0:T(8,128)(2,1)S(1)}, u32[]{:S(2)}, u32[]{:S(2)}) collective-permute-start(bf16[384,2048]{1,0:T(8,128)(2,1)} %refs_0_.1), channel_id=1, source_target_pairs={{0,1},{1,0},{2,3},{3,2},{4,5},{5,4},{6,7},{7,6},{8,9},{9,8},{10,11... | collective-permute-start | bytes 4718600 | tf_op jit(solution)/shard_map/ppermute | solution.py:321
  12.3 59.1 %collective-permute-start = (bf16[384,2048]{1,0:T(8,128)(2,1)}, bf16[384,2048]{1,0:T(8,128)(2,1)}, u32[]{:S(2)}, u32[]{:S(2)}) collective-permute-start(bf16[384,2048]{1,0:T(8,128)(2,1)} %refs_0_.1), channel_id=1, source_target_pairs={{0,2},{2,0},{4,6},{6,4},{8,10},{10,8},{12,14},{14,12},{1,3},{3,1},... | collective-permute-start | bytes 4718600 | tf_op jit(solution)/shard_map/ppermute | solution.py:315
  14.1 68.6 %collective-permute-start.3 = (bf16[384,2048]{1,0:T(8,128)(2,1)}, bf16[384,2048]{1,0:T(8,128)(2,1)}, u32[]{:S(2)}, u32[]{:S(2)}) collective-permute-start(bf16[384,2048]{1,0:T(8,128)(2,1)} %refs_0_.1), channel_id=1, source_target_pairs={{0,4},{2,6},{4,0},{6,2},{8,12},{10,14},{12,8},{14,10},{1,5},{3,7},... | collective-permute-start | bytes 4718600 | tf_op jit(solution)/shard_map/ppermute | solution.py:315
  71.4 11.3 %collective-permute-start.4 = (bf16[384,2048]{1,0:T(8,128)(2,1)}, bf16[384,2048]{1,0:T(8,128)(2,1)}, u32[]{:S(2)}, u32[]{:S(2)}) collective-permute-start(bf16[384,2048]{1,0:T(8,128)(2,1)} %collective-permute-done.refs_2_), channel_id=1, source_target_pairs={{0,1},{1,0},{2,3},{3,2},{4,5},{5,4},{6,7},{7,6},{8,9},{9,8},{10,11... | collective-permute-start | bytes 4718600 | tf_op jit(solution)/shard_map/ppermute | solution.py:321
  72.9 9.7 %collective-permute-start.5 = (bf16[512,256]{1,0:T(8,128)(2,1)}, bf16[512,256]{1,0:T(8,128)(2,1)S(1)}, u32[]{:S(2)}, u32[]{:S(2)}) collective-permute-start(bf16[512,256]{1,0:T(8,128)(2,1)} %get-tuple-element.93), channel_id=1, source_target_pairs={{0,2},{2,0},{4,6},{6,4},{8,10},{10,8},{12,14},{14,12},{1,3},{3,1},... | collective-permute-start | bytes 786440 | tf_op jit(solution)/shard_map/ppermute | solution.py:315
  82.7 7.7 %collective-permute-start.6 = (bf16[384,2048]{1,0:T(8,128)(2,1)}, bf16[384,2048]{1,0:T(8,128)(2,1)S(1)}, u32[]{:S(2)}, u32[]{:S(2)}) collective-permute-start(bf16[384,2048]{1,0:T(8,128)(2,1)} %collective-permute-done.3.refs_4_), channel_id=1, source_target_pairs={{0,1},{1,0},{2,3},{3,2},{4,5},{5,4},{6,7},{7,6},{8,9},{9,8},{10,11... | collective-permute-start | bytes 4718600 | tf_op jit(solution)/shard_map/ppermute | solution.py:321
  82.7 9.0 %copy-start.9 = (bf16[384,2048]{1,0:T(8,128)(2,1)S(1)}, bf16[384,2048]{1,0:T(8,128)(2,1)}, u32[]{:S(2)}) copy-start(bf16[384,2048]{1,0:T(8,128)(2,1)} %copy-done.8) | copy-start | bytes 4718596
  84.2 29.5 %collective-permute-start.7 = (bf16[384,1408]{1,0:T(8,128)(2,1)S(1)}, bf16[384,1408]{1,0:T(8,128)(2,1)S(1)}, u32[]{:S(2)}, u32[]{:S(2)}) collective-permute-start(bf16[384,1408]{1,0:T(8,128)(2,1)S(1)} %slice.13), channel_id=1, source_target_pairs={{0,2},{2,0},{4,6},{6,4},{8,10},{10,8},{12,14},{14,12},{1,3},{3,1},... | collective-permute-start | bytes 3244040 | tf_op jit(solution)/shard_map/ppermute | solution.py:315
  85.8 27.9 %collective-permute-start.11 = (bf16[2048,256]{1,0:T(8,128)(2,1)S(1)}, bf16[2048,256]{1,0:T(8,128)(2,1)S(1)}, u32[]{:S(2)}, u32[]{:S(2)}) collective-permute-start(bf16[2048,256]{1,0:T(8,128)(2,1)S(1)} %slice.14), channel_id=1, source_target_pairs={{0,16},{16,0},{1,17},{17,1},{2,18},{18,2},{3,19},{19,3},{4,20},{20... | collective-permute-start | bytes 3145736 | tf_op jit(solution)/shard_map/ppermute | solution.py:318
  87.4 26.3 %collective-permute-start.8 = (bf16[384,640]{1,0:T(8,128)(2,1)S(1)}, bf16[384,640]{1,0:T(8,128)(2,1)S(1)}, u32[]{:S(2)}, u32[]{:S(2)}) collective-permute-start(bf16[384,640]{1,0:T(8,128)(2,1)S(1)} %slice.12), channel_id=1, source_target_pairs={{0,4},{2,6},{4,0},{6,2},{8,12},{10,14},{12,8},{14,10},{1,5},{3,7},... | collective-permute-start | bytes 1474568 | tf_op jit(solution)/shard_map/ppermute | solution.py:315
  88.9 17.3 %collective-permute-start.9 = (bf16[512,256]{1,0:T(8,128)(2,1)S(1)}, bf16[512,256]{1,0:T(8,128)(2,1)S(1)}, u32[]{:S(2)}, u32[]{:S(2)}) collective-permute-start(bf16[512,256]{1,0:T(8,128)(2,1)S(1)} %get-tuple-element.99.refs_2_), channel_id=1, source_target_pairs={{0,8},{2,10},{4,12},{6,14},{8,0},{10,2},{12,4},{14,6},{1,9},{3,11}... | collective-permute-start | bytes 786440 | tf_op jit(solution)/shard_map/ppermute | solution.py:315
  90.3 23.4 %collective-permute-start.10 = (bf16[512,256]{1,0:T(8,128)(2,1)}, bf16[512,256]{1,0:T(8,128)(2,1)S(1)}, u32[]{:S(2)}, u32[]{:S(2)}) collective-permute-start(bf16[512,256]{1,0:T(8,128)(2,1)} %get-tuple-element.101), channel_id=1, source_target_pairs={{0,12},{2,14},{4,8},{6,10},{8,4},{10,6},{12,0},{14,2},{1,13},{3,15... | collective-permute-start | bytes 786440 | tf_op jit(solution)/shard_map/ppermute | solution.py:315
  113.7 6.5 %collective-permute-start.12 = (bf16[384,1408]{1,0:T(8,128)(2,1)S(1)}, bf16[384,1408]{1,0:T(8,128)(2,1)S(1)}, u32[]{:S(2)}, u32[]{:S(2)}) collective-permute-start(bf16[384,1408]{1,0:T(8,128)(2,1)S(1)} %collective-permute-done.7.refs_0_), channel_id=1, source_target_pairs={{0,1},{1,0},{2,3},{3,2},{4,5},{5,4},{6,7},{7,6},{8,9},{9,8},{10,11... | collective-permute-start | bytes 3244040 | tf_op jit(solution)/shard_map/ppermute | solution.py:321
  114.9 25.9 %collective-permute-start.18 = (bf16[2048,256]{1,0:T(8,128)(2,1)}, bf16[2048,256]{1,0:T(8,128)(2,1)}, u32[]{:S(2)}, u32[]{:S(2)}) collective-permute-start(bf16[2048,256]{1,0:T(8,128)(2,1)} %slice.15), channel_id=1, source_target_pairs={{0,16},{16,0},{1,17},{17,1},{2,18},{18,2},{3,19},{19,3},{4,20},{20... | collective-permute-start | bytes 3145736 | tf_op jit(solution)/shard_map/ppermute | solution.py:318
  115.4 4.9 %collective-permute-start.13 = (bf16[384,640]{1,0:T(8,128)(2,1)S(1)}, bf16[384,640]{1,0:T(8,128)(2,1)S(1)}, u32[]{:S(2)}, u32[]{:S(2)}) collective-permute-start(bf16[384,640]{1,0:T(8,128)(2,1)S(1)} %collective-permute-done.8.refs_2_), channel_id=1, source_target_pairs={{0,1},{1,0},{2,3},{3,2},{4,5},{5,4},{6,7},{7,6},{8,9},{9,8},{10,11... | collective-permute-start | bytes 1474568 | tf_op jit(solution)/shard_map/ppermute | solution.py:321
  115.6 22.5 %collective-permute-start.17 = (bf16[512,256]{1,0:T(8,128)(2,1)}, bf16[512,256]{1,0:T(8,128)(2,1)}, u32[]{:S(2)}, u32[]{:S(2)}) collective-permute-start(bf16[512,256]{1,0:T(8,128)(2,1)} %get-tuple-element.93), channel_id=1, source_target_pairs={{0,10},{2,8},{4,14},{6,12},{8,2},{10,0},{12,6},{14,4},{1,11},{3,9}... | collective-permute-start | bytes 786440 | tf_op jit(solution)/shard_map/ppermute | solution.py:315
  118.0 35.5 %collective-permute-start.15 = (bf16[512,256]{1,0:T(8,128)(2,1)}, bf16[512,256]{1,0:T(8,128)(2,1)}, u32[]{:S(2)}, u32[]{:S(2)}) collective-permute-start(bf16[512,256]{1,0:T(8,128)(2,1)} %get-tuple-element.98), channel_id=1, source_target_pairs={{0,14},{2,12},{4,10},{6,8},{8,6},{10,4},{12,2},{14,0},{1,15},{3,13... | collective-permute-start | bytes 786440 | tf_op jit(solution)/shard_map/ppermute | solution.py:315
  120.3 33.2 %collective-permute-start.14 = (bf16[512,256]{1,0:T(8,128)(2,1)}, bf16[512,256]{1,0:T(8,128)(2,1)}, u32[]{:S(2)}, u32[]{:S(2)}) collective-permute-start(bf16[512,256]{1,0:T(8,128)(2,1)} %get-tuple-element.98), channel_id=1, source_target_pairs={{0,6},{2,4},{4,2},{6,0},{8,14},{10,12},{12,10},{14,8},{1,7},{3,5},... | collective-permute-start | bytes 786440 | tf_op jit(solution)/shard_map/ppermute | solution.py:315
  120.3 24.1 %collective-permute-start.16 = (bf16[512,256]{1,0:T(8,128)(2,1)}, bf16[512,256]{1,0:T(8,128)(2,1)}, u32[]{:S(2)}, u32[]{:S(2)}) collective-permute-start(bf16[512,256]{1,0:T(8,128)(2,1)} %get-tuple-element.101), channel_id=1, source_target_pairs={{0,4},{2,6},{4,0},{6,2},{8,12},{10,14},{12,8},{14,10},{1,5},{3,7},... | collective-permute-start | bytes 786440 | tf_op jit(solution)/shard_map/ppermute | solution.py:315
  123.3 8.4 %slice-start = ((s8[8388608]{0:T(1024)(128)(4,1)}), s8[4194304]{0:T(1024)(128)(4,1)S(1)}, s32[]{:S(2)}) async-start(s8[8388608]{0:T(1024)(128)(4,1)} %bitcast.10), calls=%async_computation.1 | async-start | bytes 8388608
  131.7 12.8 %copy-start.6 = (f32[4,384,256]{2,1,0:T(8,128)S(1)}, f32[4,384,256]{2,1,0:T(8,128)}, u32[]{:S(2)}) copy-start(f32[4,384,256]{2,1,0:T(8,128)} %copy-done.5) | copy-start | bytes 4718596
  149.8 6.0 %collective-permute-start.19 = (f32[2,128,128]{2,1,0:T(8,128)S(1)}, f32[2,128,128]{2,1,0:T(8,128)S(1)}, u32[]{:S(2)}, u32[]{:S(2)}) collective-permute-start(f32[2,128,128]{2,1,0:T(8,128)S(1)} %get-tuple-element.130), channel_id=1, source_target_pairs={{0,8},{2,10},{4,12},{6,14},{1,9},{3,11},{5,13},{7,15},{16,24},{18,... | collective-permute-start | bytes 393224 | tf_op jit(solution)/shard_map/ppermute | solution.py:295
  157.4 6.6 %collective-permute-start.21 = (bf16[384,256]{1,0:T(8,128)(2,1)S(1)}, bf16[384,256]{1,0:T(8,128)(2,1)S(1)}, u32[]{:S(2)}, u32[]{:S(2)}) collective-permute-start(bf16[384,256]{1,0:T(8,128)(2,1)S(1)} %get-tuple-element.131), channel_id=1, source_target_pairs={{0,2},{2,0},{4,6},{6,4},{8,10},{10,8},{12,14},{14,12},{1,3},{3,1},... | collective-permute-start | bytes 589832 | tf_op jit(solution)/shard_map/ppermute | solution.py:315
  158.9 7.9 %collective-permute-start.23 = (bf16[384,256]{1,0:T(8,128)(2,1)S(1)}, bf16[384,256]{1,0:T(8,128)(2,1)S(1)}, u32[]{:S(2)}, u32[]{:S(2)}) collective-permute-start(bf16[384,256]{1,0:T(8,128)(2,1)S(1)} %get-tuple-element.132), channel_id=1, source_target_pairs={{0,4},{2,6},{4,0},{6,2},{8,12},{10,14},{12,8},{14,10},{1,5},{3,7},... | collective-permute-start | bytes 589832 | tf_op jit(solution)/shard_map/ppermute | solution.py:315
  162.6 7.0 %collective-permute-start.25 = (bf16[384,256]{1,0:T(8,128)(2,1)S(1)}, bf16[384,256]{1,0:T(8,128)(2,1)S(1)}, u32[]{:S(2)}, u32[]{:S(2)}) collective-permute-start(bf16[384,256]{1,0:T(8,128)(2,1)S(1)} %attend.5), channel_id=1, source_target_pairs={{0,6},{2,4},{4,2},{6,0},{8,14},{10,12},{12,10},{14,8},{1,7},{3,5},... | collective-permute-start | bytes 589832 | tf_op jit(solution)/shard_map/ppermute | solution.py:315
  163.9 7.5 %collective-permute-start.20 = (bf16[384,256]{1,0:T(8,128)(2,1)S(1)}, bf16[384,256]{1,0:T(8,128)(2,1)S(1)}, u32[]{:S(2)}, u32[]{:S(2)}) collective-permute-start(bf16[384,256]{1,0:T(8,128)(2,1)S(1)} %attend.3.refs_0_), channel_id=1, source_target_pairs={{0,1},{1,0},{2,3},{3,2},{4,5},{5,4},{6,7},{7,6},{8,9},{9,8},{10,11... | collective-permute-start | bytes 589832 | tf_op jit(solution)/shard_map/ppermute | solution.py:321
  164.0 7.4 %collective-permute-start.22 = (bf16[384,256]{1,0:T(8,128)(2,1)S(1)}, bf16[384,256]{1,0:T(8,128)(2,1)S(1)}, u32[]{:S(2)}, u32[]{:S(2)}) collective-permute-start(bf16[384,256]{1,0:T(8,128)(2,1)S(1)} %collective-permute-done.21.refs_1_), channel_id=1, source_target_pairs={{0,1},{1,0},{2,3},{3,2},{4,5},{5,4},{6,7},{7,6},{8,9},{9,8},{10,11... | collective-permute-start | bytes 589832 | tf_op jit(solution)/shard_map/ppermute | solution.py:321
  166.9 4.5 %collective-permute-start.24 = (bf16[384,256]{1,0:T(8,128)(2,1)S(1)}, bf16[384,256]{1,0:T(8,128)(2,1)S(1)}, u32[]{:S(2)}, u32[]{:S(2)}) collective-permute-start(bf16[384,256]{1,0:T(8,128)(2,1)S(1)} %collective-permute-done.23.refs_2_), channel_id=1, source_target_pairs={{0,1},{1,0},{2,3},{3,2},{4,5},{5,4},{6,7},{7,6},{8,9},{9,8},{10,11... | collective-permute-start | bytes 589832 | tf_op jit(solution)/shard_map/ppermute | solution.py:321
  169.6 1.8 %collective-permute-start.26 = (bf16[384,256]{1,0:T(8,128)(2,1)S(1)}, bf16[384,256]{1,0:T(8,128)(2,1)S(1)}, u32[]{:S(2)}, u32[]{:S(2)}) collective-permute-start(bf16[384,256]{1,0:T(8,128)(2,1)S(1)} %collective-permute-done.25.refs_3_), channel_id=1, source_target_pairs={{0,1},{1,0},{2,3},{3,2},{4,5},{5,4},{6,7},{7,6},{8,9},{9,8},{10,11... | collective-permute-start | bytes 589832 | tf_op jit(solution)/shard_map/ppermute | solution.py:321
  (11 other events, 32.6 us)
